TPU v7x, 32 devices: a whole 2x2x4 slice. The times are simulated.
32 devices in a mesh: dp: 16 (over z, x, core), tensor: 2 (over y).
Axes of the slice: x: 2, y: 2, z: 4, core: 2. Of those that a mesh axis runs over, the one named last changes fastest.
Arguments:
- tokens: bfloat16 [32768, 1024], P(('dp', 'tensor')), may hold values from -6 to 6
- alpha_logit: float32 [1024, 16], P('tensor'), may hold values from -6 to 0
- delta_logit: float32 [1024, 16], P('tensor'), may hold values from -3 to 3
- ema_beta: float32 [1024, 16], P('tensor'), may hold values from -1.73 to 1.73
- ema_eta: float32 [1024, 16], P('tensor'), may hold values from -0.43 to 0.43
- ema_omega: float32 [1024], P('tensor'), may hold values from -1.73 to 1.73
- w_z: bfloat16 [1024, 128], replicated, may hold values from -0.1875 to 0.1875
- qk_gain: float32 [2, 128], replicated, may hold values from -2.6 to 2.6
- qk_bias: float32 [2, 128], replicated, may hold values from -0.87 to 0.87
- w_v: bfloat16 [1024, 2048], P(None, 'tensor'), may hold values from -0.1875 to 0.1875
- w_gamma: bfloat16 [1024, 2048], P(None, 'tensor'), may hold values from -0.1875 to 0.1875
- u_h: bfloat16 [2048, 1024], P('tensor'), may hold values from -0.75 to 0.75
- w_h: bfloat16 [1024, 1024], P('tensor'), may hold values from -0.1875 to 0.1875
- w_phi: bfloat16 [1024, 1024], P('tensor'), may hold values from -0.1875 to 0.1875
- w_up: bfloat16 [1024, 4096], P(None, 'tensor'), may hold values from -0.1875 to 0.1875
- w_down: bfloat16 [4096, 1024], P('tensor'), may hold values from -0.09375 to 0.09375
- cotangent: bfloat16 [32768, 1024], P(('dp', 'tensor')), may hold values from -6 to 6
Outputs:
- output: bfloat16 [32768, 1024], P(('dp', 'tensor'))
- input_grad: float32 [32768, 1024], P(('dp', 'tensor'))
- alpha_grad: float32 [1024, 16], P('tensor')
- delta_grad: float32 [1024, 16], P('tensor')
- beta_grad: float32 [1024, 16], P('tensor')
- eta_grad: float32 [1024, 16], P('tensor')
- omega_grad: float32 [1024], P('tensor')
- z_grad: float32 [1024, 128], P('dp')
- gain_grad: float32 [2, 128], replicated
- bias_grad: float32 [2, 128], replicated
- value_grad: float32 [1024, 2048], P('dp', 'tensor')
- gamma_grad: float32 [1024, 2048], P('dp', 'tensor')
- uh_grad: float32 [2048, 1024], P('tensor', 'dp')
- wh_grad: float32 [1024, 1024], P('tensor', 'dp')
- phi_grad: float32 [1024, 1024], P('tensor', 'dp')
- up_grad: float32 [1024, 4096], P('dp', 'tensor')
- down_grad: float32 [4096, 1024], P('tensor', 'dp')
All inputs are finite; a program needn't handle non-finite values.
Results may differ from a plain program's by a relative error of at most 0.023.
Values may be sent and summed in bfloat16 or wider, within the bound.
No kernel may reach another device: no remote copies, remote signals or barrier semaphores. Data moves between devices by JAX's collectives and lax.ppermute only.
A program may use at most 320 MiB of HBM per device.

v0:
```python
import jax
import jax.numpy as jnp
from jax import lax
from jax.sharding import PartitionSpec as P

H = 16
LEN = 1024
ATT_BLOCK = 512
EMA_BLOCK = 128


norm_eps = 1e-06
masked_value = -1e30


def rms_rows(values_in):
    return values_in * lax.rsqrt(jnp.mean(values_in * values_in, axis=-1, keepdims=True) + norm_eps)


def matmul(left, right):
    return jnp.dot(left, right, preferred_element_type=jnp.float32)


def row_inner(left, right):
    return lax.dot_general(
        left, right, (((0,), (0,)), ((), ())), preferred_element_type=jnp.float32
    )


def col_inner(left, right):
    return lax.dot_general(
        left, right, (((1,), (1,)), ((), ())), preferred_element_type=jnp.float32
    )


def silu_slope(pre_act):
    logistic = jax.nn.sigmoid(pre_act)
    return logistic * (1.0 + pre_act * (1.0 - logistic))


def gate_apply(h_pre, f_pre, x_rows):
    update = jax.nn.sigmoid(f_pre)
    return update * jax.nn.silu(h_pre) + (1.0 - update) * x_rows


def ema_apply(signal, ema_params):
    alpha_logit, delta_logit, ema_beta, ema_eta, ema_omega = ema_params
    alpha_rate = jax.nn.sigmoid(alpha_logit)
    decay_rate = 1.0 - alpha_rate * jax.nn.sigmoid(delta_logit)
    feed_rate = alpha_rate * ema_beta
    log_decay = jnp.log(decay_rate)
    total_rows, chan_count = signal.shape
    seq_count = total_rows // LEN
    block_count = LEN // EMA_BLOCK
    blocks = signal.reshape(seq_count, block_count, EMA_BLOCK, chan_count)
    steps_in = jnp.arange(EMA_BLOCK, dtype=jnp.float32)
    lag_power = jnp.exp(steps_in[:, None, None] * log_decay[None])
    kernel = jnp.sum(lag_power * (feed_rate * ema_eta)[None], axis=-1)
    offsets = steps_in[:, None] - steps_in[None, :]
    lag_index = jnp.clip(offsets, 0, EMA_BLOCK - 1).astype(jnp.int32)
    toeplitz = jnp.where((offsets >= 0)[:, :, None], kernel[lag_index], 0.0)
    local_part = jnp.einsum("ijc,snjc->snic", toeplitz, blocks)
    tail_power = lag_power[::-1] * feed_rate[None]
    block_state = jnp.einsum("jch,snjc->snch", tail_power, blocks)
    full_decay = jnp.exp(EMA_BLOCK * log_decay)

    def carry_step(state_in, incoming):
        return (full_decay * state_in + incoming, state_in)

    zero_state = jnp.zeros((seq_count, chan_count, H), jnp.float32)
    _, start_state = lax.scan(carry_step, zero_state, jnp.moveaxis(block_state, 1, 0))
    start_state = jnp.moveaxis(start_state, 0, 1)
    head_power = lag_power * decay_rate[None] * ema_eta[None]
    carried = jnp.einsum("ich,snch->snic", head_power, start_state)
    ema_pre = (local_part + carried).reshape(total_rows, chan_count) + ema_omega * signal
    return jax.nn.silu(ema_pre)


def masked_scores(q_rows, k_rows, first_row):
    raw_scores = col_inner(q_rows, k_rows) * q_rows.shape[1] ** (-0.5)
    row_pos = first_row + jnp.arange(q_rows.shape[0])[:, None]
    col_pos = jnp.arange(k_rows.shape[0])[None, :]
    return jnp.where(col_pos <= row_pos, raw_scores, masked_value)


def attend_forward(query_low, key_low, value_low):
    total_rows, value_width = value_low.shape
    seq_count = total_rows // LEN
    per_seq = LEN // ATT_BLOCK

    def attend_one_block(flat_index):
        seq_id = flat_index // per_seq
        blk_id = flat_index % per_seq
        seq_start = seq_id * LEN
        q_rows = lax.dynamic_slice_in_dim(query_low, seq_start + blk_id * ATT_BLOCK, ATT_BLOCK, 0)
        k_rows = lax.dynamic_slice_in_dim(key_low, seq_start, LEN, 0)
        v_rows = lax.dynamic_slice_in_dim(value_low, seq_start, LEN, 0)
        scores = masked_scores(q_rows, k_rows, blk_id * ATT_BLOCK)
        top_score = jnp.max(scores, axis=-1, keepdims=True)
        weights = jnp.exp(scores - top_score)
        total_weight = jnp.sum(weights, axis=-1, keepdims=True)
        probs = (weights / total_weight).astype(jnp.bfloat16)
        return (matmul(probs, v_rows), top_score[:, 0] + jnp.log(total_weight[:, 0]))

    outs, lse_all = lax.map(attend_one_block, jnp.arange(seq_count * per_seq))
    return (outs.reshape(total_rows, value_width), lse_all.reshape(total_rows))


def attend_backward(query_low, key_low, value_low, lse_rows, d_att):
    total_rows, value_width = value_low.shape
    head_width = query_low.shape[1]
    seq_count = total_rows // LEN
    per_seq = LEN // ATT_BLOCK
    scale = head_width ** (-0.5)

    def one_seq(seq_id):
        seq_start = seq_id * LEN
        k_rows = lax.dynamic_slice_in_dim(key_low, seq_start, LEN, 0)
        v_rows = lax.dynamic_slice_in_dim(value_low, seq_start, LEN, 0)

        def one_one_block(carry_in, blk_id):
            d_keys, d_vals = carry_in
            row_start = seq_start + blk_id * ATT_BLOCK
            q_rows = lax.dynamic_slice_in_dim(query_low, row_start, ATT_BLOCK, 0)
            g_rows = lax.dynamic_slice_in_dim(d_att, row_start, ATT_BLOCK, 0)
            lse_part = lax.dynamic_slice_in_dim(lse_rows, row_start, ATT_BLOCK, 0)
            probs = jnp.exp(masked_scores(q_rows, k_rows, blk_id * ATT_BLOCK) - lse_part[:, None])
            d_probs = col_inner(g_rows, v_rows)
            d_scores = (
                probs * (d_probs - jnp.sum(probs * d_probs, axis=-1, keepdims=True))
            ).astype(jnp.bfloat16)
            d_rows = matmul(d_scores, k_rows) * scale
            d_keys = d_keys + row_inner(d_scores, q_rows) * scale
            d_vals = d_vals + row_inner(probs.astype(jnp.bfloat16), g_rows)
            return ((d_keys, d_vals), d_rows)

        start_carry = (
            jnp.zeros((LEN, head_width), jnp.float32),
            jnp.zeros((LEN, value_width), jnp.float32),
        )
        (d_keys, d_vals), d_rows = lax.scan(one_one_block, start_carry, jnp.arange(per_seq))
        return (d_rows.reshape(LEN, head_width), d_keys, d_vals)

    d_query, d_key, d_value = lax.map(one_seq, jnp.arange(seq_count))
    return (
        d_query.reshape(total_rows, head_width),
        d_key.reshape(total_rows, head_width),
        d_value.reshape(total_rows, value_width),
    )


def shards(
    tokens,
    alpha_logit,
    delta_logit,
    ema_beta,
    ema_eta,
    ema_omega,
    w_z,
    qk_gain,
    qk_bias,
    w_v,
    w_gamma,
    u_h,
    w_h,
    w_phi,
    w_up,
    w_down,
    cotangent,
):
    tensor_pos = lax.axis_index("tensor")
    feature_count = tokens.shape[1]
    chan_count = ema_omega.shape[0]
    chan_start = tensor_pos * chan_count
    x_rows = tokens.astype(jnp.float32)
    normed_rows, norm_pull = jax.vjp(rms_rows, x_rows)
    normed, cot_full = (
        lax.all_gather(normed_rows.astype(jnp.bfloat16), "tensor", axis=0, tiled=True),
        lax.all_gather(cotangent, "tensor", axis=0, tiled=True),
    )
    signal = lax.dynamic_slice_in_dim(normed, chan_start, chan_count, 1).astype(jnp.float32)
    ema_params = (alpha_logit, delta_logit, ema_beta, ema_eta, ema_omega)
    ema_val, ema_pull = jax.vjp(ema_apply, signal, ema_params)
    ema_low = ema_val.astype(jnp.bfloat16)
    ema_full = lax.all_gather(ema_low, "tensor", axis=1, tiled=True)
    z_pre = matmul(ema_full, w_z)
    z_act = jax.nn.silu(z_pre)
    query_low = (z_act * qk_gain[0] + qk_bias[0]).astype(jnp.bfloat16)
    key_low = (z_act * qk_gain[1] + qk_bias[1]).astype(jnp.bfloat16)
    values_pre = matmul(normed, w_v)
    value_low = jax.nn.silu(values_pre).astype(jnp.bfloat16)
    gamma_pre = matmul(ema_full, w_gamma)
    gamma_act = jax.nn.silu(gamma_pre)
    attended, lse_rows = attend_forward(query_low, key_low, value_low)
    gated_low = (gamma_act * attended).astype(jnp.bfloat16)
    both_pre = lax.psum_scatter(
        jnp.concatenate(
            [matmul(gated_low, u_h) + matmul(ema_low, w_h), matmul(ema_low, w_phi)], axis=1
        ),
        "tensor",
        scatter_dimension=0,
        tiled=True,
    )
    h_pre = both_pre[:, :feature_count]
    f_pre = both_pre[:, feature_count:]
    mixed, gate_pull = jax.vjp(gate_apply, h_pre, f_pre, x_rows)
    normed_two, norm_two_pull = jax.vjp(rms_rows, mixed)
    lowered = lax.all_gather(normed_two.astype(jnp.bfloat16), "tensor", axis=0, tiled=True)
    up_pre = matmul(lowered, w_up)
    hidden = jax.nn.silu(up_pre).astype(jnp.bfloat16)
    down_rows = lax.psum_scatter(
        matmul(hidden, w_down).astype(jnp.bfloat16), "tensor", scatter_dimension=0, tiled=True
    ).astype(jnp.float32)
    output = (mixed + down_rows).astype(jnp.bfloat16)
    cot_rows = cotangent.astype(jnp.float32)
    d_hidden = col_inner(cot_full, w_down)
    d_up = (d_hidden * silu_slope(up_pre)).astype(jnp.bfloat16)
    down_grad = row_inner(hidden, cot_full)
    up_grad = row_inner(lowered, d_up)
    d_lowered = lax.psum_scatter(col_inner(d_up, w_up), "tensor", scatter_dimension=0, tiled=True)
    d_mixed = cot_rows + norm_two_pull(d_lowered)[0]
    d_hpre, d_fpre, d_direct = gate_pull(d_mixed)
    h_full_grad, f_full_grad = (
        lax.all_gather(d_hpre.astype(jnp.bfloat16), "tensor", axis=0, tiled=True),
        lax.all_gather(d_fpre.astype(jnp.bfloat16), "tensor", axis=0, tiled=True),
    )
    uh_grad = row_inner(gated_low, h_full_grad)
    wh_grad = row_inner(ema_low, h_full_grad)
    phi_grad = row_inner(ema_low, f_full_grad)
    d_gated = col_inner(h_full_grad, u_h)
    d_att = (d_gated * gamma_act).astype(jnp.bfloat16)
    d_gamma = (d_gated * attended * silu_slope(gamma_pre)).astype(jnp.bfloat16)
    d_query, d_key, d_value = attend_backward(query_low, key_low, value_low, lse_rows, d_att)
    d_query, d_key = lax.psum((d_query, d_key), "tensor")
    d_z = (silu_slope(z_pre) * (d_query * qk_gain[0] + d_key * qk_gain[1])).astype(jnp.bfloat16)
    gain_grad = jnp.stack([jnp.sum(d_query * z_act, axis=0), jnp.sum(d_key * z_act, axis=0)])
    bias_grad = jnp.stack([jnp.sum(d_query, axis=0), jnp.sum(d_key, axis=0)])
    z_grad = row_inner(ema_full, d_z)
    gamma_grad = row_inner(ema_full, d_gamma)
    d_value_pre = (d_value * silu_slope(values_pre)).astype(jnp.bfloat16)
    value_grad = row_inner(normed, d_value_pre)
    d_chan = lax.psum_scatter(
        col_inner(d_gamma, w_gamma).astype(jnp.bfloat16), "tensor", scatter_dimension=1, tiled=True
    ).astype(jnp.float32)
    z_rows = lax.dynamic_slice_in_dim(w_z, chan_start, chan_count, 0)
    d_chan = (
        d_chan
        + col_inner(d_z, z_rows)
        + col_inner(h_full_grad, w_h)
        + col_inner(f_full_grad, w_phi)
    )
    d_signal, d_params = ema_pull(d_chan)
    d_norm_part = col_inner(d_value_pre, w_v)
    own_cols = lax.dynamic_slice_in_dim(d_norm_part, chan_start, chan_count, 1)
    d_norm_part = lax.dynamic_update_slice_in_dim(d_norm_part, own_cols + d_signal, chan_start, 1)
    d_normed = lax.psum_scatter(
        d_norm_part.astype(jnp.bfloat16), "tensor", scatter_dimension=0, tiled=True
    ).astype(jnp.float32)
    input_grad = d_direct + norm_pull(d_normed)[0]
    weight_totals = (
        lax.psum_scatter(z_grad.astype(jnp.bfloat16), "dp", scatter_dimension=0, tiled=True).astype(
            jnp.float32
        ),
        lax.psum_scatter(
            value_grad.astype(jnp.bfloat16), "dp", scatter_dimension=0, tiled=True
        ).astype(jnp.float32),
        lax.psum_scatter(
            gamma_grad.astype(jnp.bfloat16), "dp", scatter_dimension=0, tiled=True
        ).astype(jnp.float32),
        lax.psum_scatter(
            uh_grad.astype(jnp.bfloat16), "dp", scatter_dimension=1, tiled=True
        ).astype(jnp.float32),
        lax.psum_scatter(
            wh_grad.astype(jnp.bfloat16), "dp", scatter_dimension=1, tiled=True
        ).astype(jnp.float32),
        lax.psum_scatter(
            phi_grad.astype(jnp.bfloat16), "dp", scatter_dimension=1, tiled=True
        ).astype(jnp.float32),
        lax.psum_scatter(
            up_grad.astype(jnp.bfloat16), "dp", scatter_dimension=0, tiled=True
        ).astype(jnp.float32),
        lax.psum_scatter(
            down_grad.astype(jnp.bfloat16), "dp", scatter_dimension=1, tiled=True
        ).astype(jnp.float32),
    )
    param_totals = lax.psum(
        (d_params[0], d_params[1], d_params[2], d_params[3], d_params[4], gain_grad, bias_grad),
        "dp",
    )
    return (
        output,
        input_grad,
        param_totals[0],
        param_totals[1],
        param_totals[2],
        param_totals[3],
        param_totals[4],
        weight_totals[0],
        param_totals[5],
        param_totals[6],
        weight_totals[1],
        weight_totals[2],
        weight_totals[3],
        weight_totals[4],
        weight_totals[5],
        weight_totals[6],
        weight_totals[7],
    )


def solution(mesh):
    placed = (
        P(("dp", "tensor"), None),
        P("tensor", None),
        P("tensor", None),
        P("tensor", None),
        P("tensor", None),
        P("tensor"),
        P(),
        P(),
        P(),
        P(None, "tensor"),
        P(None, "tensor"),
        P("tensor", None),
        P("tensor", None),
        P("tensor", None),
        P(None, "tensor"),
        P("tensor", None),
        P(("dp", "tensor"), None),
    )
    return jax.shard_map(
        shards,
        mesh=mesh,
        in_specs=placed,
        out_specs=(
            P(("dp", "tensor"), None),
            P(("dp", "tensor"), None),
            P("tensor", None),
            P("tensor", None),
            P("tensor", None),
            P("tensor", None),
            P("tensor"),
            P("dp", None),
            P(),
            P(),
            P("dp", "tensor"),
            P("dp", "tensor"),
            P("tensor", "dp"),
            P("tensor", "dp"),
            P("tensor", "dp"),
            P("dp", "tensor"),
            P("tensor", "dp"),
        ),
        check_vma=False,
    )
```

profile of v0, /device:TPU:0, one launch (start us, length us, event | category | flops | bytes accessed | tf_op | source)
XLA Modules:
  0.0 1864.3 jit_solution(1521306902017170247)
XLA Ops:
  19.9 9.1 multiply_exponential_fusion
  29.0 7.3 rev.6
  36.5 66.4 %gather_fusion = bf16[16384,512]{1,0:T(8,128)(2,1)} fusion(bf16[128,512]{1,0:T(8,128)(2,1)S(1)} %copy.123, s32[16384]{0:T(1024)S(1)} %broadcast_clamp_fusion), kind=kCustom, calls=%fused_computation | custom fusion | bytes 33619968 | tf_op jit(solution)/shard_map/jvp()/gather | solution.py:61
  102.9 23.6 %copy.124 = bf16[128,128,512]{1,0,2:T(8,128)(2,1)} copy(bf16[128,128,512]{2,1,0:T(8,128)(2,1)} %bitcast.285) | data formatting | bytes 33554432 | tf_op jit(solution)/shard_map/jvp()/gather | solution.py:61
  148.0 12.7 fusion.28
  173.7 7.7 fusion.129
  181.4 8.7 multiply_convert_fusion.4
  190.1 42.8 %all-gather.9.cloned.1.call-done = bf16[2048,1024]{0,1:T(8,128)(2,1)} async-done(((bf16[2048,512]{0,1:T(8,128)(2,1)}), bf16[2048,1024]{0,1:T(8,128)(2,1)}) %all-gather.9.cloned.1.call-update) | async-done | bytes 4194320 | tf_op jit(solution)/shard_map/all_gather | solution.py:185
  237.5 48.1 %while.81 = (s32[]{:T(128)}, f32[4,512,1024]{2,1,0:T(8,128)}, f32[4,512]{1,0:T(4,128)}, s32[4]{0:T(128)S(1)}, bf16[2048,128]{1,0:T(8,128)(2,1)S(1)}, /*index=5*/...) while((s32[]{:T(128)}, f32[4,512,1024]{2,1,0:T(8,128)}, f32[4,512]{1,0:T(4,128)}, ...), condition=%wide.region_7.8_spmd.clone, body=%wide.region_4.7_spmd.sunk.clone | while | flops 1212678144 | bytes 19292600 | solution.py:105
  285.6 14.6 fusion.37
  307.8 9.9 pad_maximum_fusion
  317.8 189.2 %reduce-scatter.14.cloned.1.call-done = f32[1024,2048]{0,1:T(8,128)} async-done(((f32[2048,2048]{0,1:T(8,128)}), f32[1024,2048]{0,1:T(8,128)}) %reduce-scatter.14.cloned.1.call-update) | async-done | bytes 8388624 | tf_op jit(solution)/shard_map/reduce_scatter | solution.py:196
  516.9 56.3 %all-gather.11.cloned.1.call-done = bf16[2048,1024]{0,1:T(8,128)(2,1)} async-done(((bf16[1024,1024]{0,1:T(8,128)(2,1)}), bf16[2048,1024]{0,1:T(8,128)(2,1)}) %all-gather.11.cloned.1.call-update) | async-done | bytes 4194320 | tf_op jit(solution)/shard_map/all_gather | solution.py:208
  573.2 19.0 %multiply_convert_fusion.2 = (bf16[2048,2048]{1,0:T(8,128)(2,1)}, f32[2048,2048]{1,0:T(8,128)}) fusion(bf16[2048,1024]{0,1:T(8,128)(2,1)} %all-gather.11.cloned.1.call-done, bf16[1024,2048]{1,0:T(8,128)(2,1)} %param.41), kind=kOutput, calls=%fused_computation.61 | convolution fusion | flops 8610906112 | bytes 33554432 | tf_op jit(solution)/shard_map/dot_general | solution.py:21
  592.2 39.3 %all-gather.13.cloned.1.call-done = bf16[2048,1024]{1,0:T(8,128)(2,1)} async-done(((bf16[1024,1024]{1,0:T(8,128)(2,1)}), bf16[2048,1024]{1,0:T(8,128)(2,1)}) %all-gather.13.cloned.1.call-update) | async-done | bytes 4194320 | tf_op jit(solution)/shard_map/all_gather | solution.py:179
  631.4 20.6 %multiply_convert_fusion.1 = bf16[2048,2048]{1,0:T(8,128)(2,1)} fusion(f32[2048,2048]{1,0:T(8,128)} %get-tuple-element.735, bf16[2048,1024]{1,0:T(8,128)(2,1)} %all-gather.13.cloned.1.call-done, bf16[2048,1024]{1,0:T(8,128)(2,1)} %param.42), kind=kOutput, calls=%fused_computation.60 | convolution fusion | flops 8627683328 | bytes 33554432 | tf_op jit(solution)/shard_map/dot_general | solution.py:31
  652.0 13.5 fusion.130
  669.6 95.4 %reduce-scatter.18.cloned.1.call-done = f32[1024,1024]{0,1:T(8,128)} async-done(((f32[2048,1024]{0,1:T(8,128)}), f32[1024,1024]{0,1:T(8,128)}) %reduce-scatter.18.cloned.1.call-update) | async-done | bytes 4194320 | tf_op jit(solution)/shard_map/reduce_scatter | solution.py:220
  770.9 8.7 fusion.45
  780.4 56.1 %all-gather.15.cloned.1.call-done = bf16[2048,1024]{0,1:T(8,128)(2,1)} async-done(((bf16[1024,1024]{0,1:T(8,128)(2,1)}), bf16[2048,1024]{0,1:T(8,128)(2,1)}) %all-gather.15.cloned.1.call-update) | async-done | bytes 4194320 | tf_op jit(solution)/shard_map/all_gather | solution.py:224
  836.5 15.5 fusion.39
  852.0 74.5 %while.83 = (s32[]{:T(128)}, f32[2,1024,128]{2,1,0:T(8,128)}, f32[2,1024,128]{2,1,0:T(8,128)}, f32[2,1024,1024]{2,1,0:T(8,128)}, s32[2]{0:T(128)S(1)}, /*index=5...) while((s32[]{:T(128)}, f32[2,1024,128]{2,1,0:T(8,128)}, ...), condition=%wide.region_17.18_spmd.clone, body=%wide.region_13.17_spmd.sunk.clone | while | flops 2557935616 | bytes 79182504 | solution.py:144
  857.4 26.1 %while.82 = (s32[]{:T(128)}, f32[1024,128]{1,0:T(8,128)S(1)}, f32[1024,1024]{1,0:T(8,128)}, f32[2,512,128]{2,1,0:T(8,128)S(1)}, s32[2]{0:T(128)S(1)}, /*index=5*...) while((s32[]{:T(128)}, f32[1024,128]{1,0:T(8,128)S(1)}, ...), condition=%wide.region_16.16_spmd.clone, body=%wide.region_14.15_spmd.clone.sunk | while | flops 2557935616 | bytes 63977784 | solution.py:141
  894.7 26.1 %while.82 = (s32[]{:T(128)}, f32[1024,128]{1,0:T(8,128)S(1)}, f32[1024,1024]{1,0:T(8,128)}, f32[2,512,128]{2,1,0:T(8,128)S(1)}, s32[2]{0:T(128)S(1)}, /*index=5*...) while((s32[]{:T(128)}, f32[1024,128]{1,0:T(8,128)S(1)}, ...), condition=%wide.region_16.16_spmd.clone, body=%wide.region_14.15_spmd.clone.sunk | while | flops 2557935616 | bytes 63977784 | solution.py:141
  926.8 9.5 convolution_convert_fusion.2
  936.4 14.0 convolution_convert_fusion.3
  950.5 13.9 convolution_convert_fusion
  977.8 12.0 all-reduce.7.cloned.1.call-done
  996.9 10.0 convolution_convert_fusion.4
  1007.0 9.4 convolution_convert_fusion.5
  1016.9 7.7 fusion.36
  1048.5 8.5 fusion.42
  1069.4 7.5 while.85
  1078.9 9.5 fusion.26
  1104.1 14.2 convolution_convert_fusion.1
  1124.6 74.2 %reduce-scatter.36.cloned.1.call-done = bf16[64,2048]{1,0:T(8,128)(2,1)} async-done(((bf16[1024,2048]{1,0:T(8,128)(2,1)}), bf16[64,2048]{1,0:T(8,128)(2,1)}) %reduce-scatter.36.cloned.1.call-update) | async-done | bytes 262160 | tf_op jit(solution)/shard_map/reduce_scatter | solution.py:279
  1200.5 58.2 %reduce-scatter.32.cloned.1.call-done = bf16[512,64]{0,1:T(8,128)(2,1)} async-done(((bf16[512,1024]{0,1:T(8,128)(2,1)}), bf16[512,64]{0,1:T(8,128)(2,1)}) %reduce-scatter.32.cloned.1.call-update) | async-done | bytes 65552 | tf_op jit(solution)/shard_map/reduce_scatter | solution.py:273
  1260.2 58.9 %reduce-scatter.34.cloned.1.call-done = bf16[512,64]{0,1:T(8,128)(2,1)} async-done(((bf16[512,1024]{0,1:T(8,128)(2,1)}), bf16[512,64]{0,1:T(8,128)(2,1)}) %reduce-scatter.34.cloned.1.call-update) | async-done | bytes 65552 | tf_op jit(solution)/shard_map/reduce_scatter | solution.py:276
  1321.8 55.0 %reduce-scatter.24.cloned.1.call-done = bf16[64,128]{1,0:T(8,128)(2,1)} async-done(((bf16[1024,128]{1,0:T(8,128)(2,1)}), bf16[64,128]{1,0:T(8,128)(2,1)}) %reduce-scatter.24.cloned.1.call-update) | async-done | bytes 16400 | tf_op jit(solution)/shard_map/reduce_scatter | solution.py:261
  1378.2 62.9 %reduce-scatter.30.cloned.1.call-done = bf16[1024,64]{0,1:T(8,128)(2,1)} async-done(((bf16[1024,1024]{0,1:T(8,128)(2,1)}), bf16[1024,64]{0,1:T(8,128)(2,1)}) %reduce-scatter.30.cloned.1.call-update) | async-done | bytes 131088 | tf_op jit(solution)/shard_map/reduce_scatter | solution.py:270
  1442.7 63.1 %reduce-scatter.28.cloned.1.call-done = bf16[64,1024]{1,0:T(8,128)(2,1)} async-done(((bf16[1024,1024]{1,0:T(8,128)(2,1)}), bf16[64,1024]{1,0:T(8,128)(2,1)}) %reduce-scatter.28.cloned.1.call-update) | async-done | bytes 131088 | tf_op jit(solution)/shard_map/reduce_scatter | solution.py:267
  1507.4 62.5 %reduce-scatter.26.cloned.1.call-done = bf16[64,1024]{1,0:T(8,128)(2,1)} async-done(((bf16[1024,1024]{1,0:T(8,128)(2,1)}), bf16[64,1024]{1,0:T(8,128)(2,1)}) %reduce-scatter.26.cloned.1.call-update) | async-done | bytes 131088 | tf_op jit(solution)/shard_map/reduce_scatter | solution.py:264
  1585.8 14.9 fusion.25
  1600.7 35.0 %copy.166 = f32[128,128,512]{2,1,0:T(8,128)} copy(f32[128,128,512]{1,0,2:T(8,128)} %fusion.25) | data formatting | bytes 67108864 | tf_op jit(solution)/shard_map/transpose(jvp(jit(_where)))/select_n | solution.py:61
  1635.7 104.4 %scatter_custom_fusion = f32[128,512]{1,0:T(8,128)S(1)} fusion(s32[16384]{0:T(1024)S(1)} %fusion.111, f32[16384,512]{1,0:T(8,128)} %bitcast.290, f32[]{:T(128)} %constant.226.clone.1), kind=kCustom, calls=%fused_computation.186 | custom fusion | flops 8388608 | bytes 262656 | tf_op jit(solution)/shard_map/transpose(jvp())/scatter-add | solution.py:61
  1741.0 13.8 fusion.63
  1762.2 10.4 fusion.43
  1782.1 65.8 %all-reduce.5.cloned.1.call-done = (f32[512,16]{0,1:T(8,128)}, f32[512,16]{0,1:T(8,128)}, f32[512,16]{0,1:T(8,128)}, f32[512,16]{0,1:T(8,128)}, f32[512]{0:T(512)}, /*index=5*/f32[2,128]{1,0:T(2,128)}, f32[2,128]{1,0:T(2,128)}) async-done(((f32[512,16]{0,1:T(8,128)}, f32[512,16]{0,1:T(8,128)}, f32[512,16]{0,1:T(8,128)}, f32[512,16]{0,1:T(8,128)}, f32[512]{0:T(512)}, /*index=5*/f32[2,128]{1,0:T(2,128)}, ...) | async-done | bytes 135184 | tf_op jit(solution)/shard_map/psum | solution.py:286
  (444 shorter events, 335.8 us)
Async XLA Ops:
  7.2 293.0 %copy-start = (bf16[1024,1024]{1,0:T(8,128)(2,1)S(1)}, bf16[1024,1024]{1,0:T(8,128)(2,1)}, u32[]{:S(2)}) copy-start(bf16[1024,1024]{1,0:T(8,128)(2,1)} %param.38) | copy-start | bytes 6291460
  7.2 119.4 %all-gather.7.cloned.1.call-start = ((), (), s32[]{:S(2)}) async-start(), calls=%async_computation.13 | async-start | bytes 6291456 | tf_op jit(solution)/shard_map/all_gather | solution.py:178
  17.0 216.0 %all-gather.9.cloned.1.call-start = ((), (), s32[]{:S(2)}) async-start(), calls=%async_computation.14 | async-start | bytes 6291456 | tf_op jit(solution)/shard_map/all_gather | solution.py:185
  18.0 18.4 copy-start.41
  18.9 141.8 %copy-start.35 = (f32[512,16]{1,0:T(8,128)}, f32[512,16]{1,0:T(8,128)S(1)}, u32[]{:S(2)}) copy-start(f32[512,16]{1,0:T(8,128)S(1)} %copy.121) | copy-start | bytes 98308
  19.1 110.0 %copy-start.22 = (f32[512,16]{1,0:T(8,128)}, f32[512,16]{1,0:T(8,128)S(1)}, u32[]{:S(2)}) copy-start(f32[512,16]{1,0:T(8,128)S(1)} %copy.125) | copy-start | bytes 98308
  126.5 21.5 %copy-start.48 = (pred[128,128]{1,0:T(8,128)(4,1)}, pred[128,128]{1,0:T(8,128)(4,1)S(1)}, u32[]{:S(2)}) copy-start(pred[128,128]{1,0:T(8,128)(4,1)S(1)} %subtract_compare_fusion) | copy-start | bytes 49156
  144.5 16.2 copy-start.28
  144.5 16.2 copy-start.32
  173.4 333.6 %reduce-scatter.14.cloned.1.call-start = ((), (), s32[]{:S(2)}) async-start(), calls=%async_computation.15 | async-start | bytes 25165824 | tf_op jit(solution)/shard_map/reduce_scatter | solution.py:196
  173.7 59.3 %copy-start.70 = (f32[128]{0:T(128)}, f32[128]{0:T(128)S(1)}, u32[]{:S(2)}) copy-start(f32[128]{0:T(128)S(1)} %get-tuple-element.738) | copy-start | bytes 1540
  173.7 59.3 %copy-start.72 = (f32[128]{0:T(128)}, f32[128]{0:T(128)S(1)}, u32[]{:S(2)}) copy-start(f32[128]{0:T(128)S(1)} %get-tuple-element.739) | copy-start | bytes 1540
  181.4 51.5 %copy-start.80 = (bf16[1024,128]{1,0:T(8,128)(2,1)S(1)}, bf16[1024,128]{1,0:T(8,128)(2,1)}, u32[]{:S(2)}) copy-start(bf16[1024,128]{1,0:T(8,128)(2,1)} %param.33) | copy-start | bytes 786436
  317.7 255.5 %all-gather.11.cloned.1.call-start = ((), (), s32[]{:S(2)}) async-start(), calls=%async_computation.16 | async-start | bytes 6291456 | tf_op jit(solution)/shard_map/all_gather | solution.py:208
  512.3 256.8 %copy-start.54 = (f32[1024]{0:T(1024)}, f32[1024]{0:T(1024)S(1)}, u32[]{:S(2)}) copy-start(f32[1024]{0:T(1024)S(1)} %fusion.116) | copy-start | bytes 12292
  516.3 115.2 %all-gather.13.cloned.1.call-start = ((), (), s32[]{:S(2)}) async-start(), calls=%async_computation.18 | async-start | bytes 6291456 | tf_op jit(solution)/shard_map/all_gather | solution.py:179
  516.9 248.1 %reduce-scatter.18.cloned.1.call-start = ((), (), s32[]{:S(2)}) async-start(), calls=%async_computation.19 | async-start | bytes 12582912 | tf_op jit(solution)/shard_map/reduce_scatter | solution.py:220
  631.4 20.6 %copy-start.76 = (bf16[1024,2048]{1,0:T(8,128)(2,1)S(1)}, bf16[1024,2048]{1,0:T(8,128)(2,1)}, u32[]{:S(2)}) copy-start(bf16[1024,2048]{1,0:T(8,128)(2,1)} %param.41) | copy-start | bytes 12582916
  665.6 170.9 %all-gather.15.cloned.1.call-start = ((), (), s32[]{:S(2)}) async-start(), calls=%async_computation.20 | async-start | bytes 6291456 | tf_op jit(solution)/shard_map/all_gather | solution.py:224
  779.6 192.5 %all-gather.17.cloned.1.call-start = ((), (), s32[]{:S(2)}) async-start(), calls=%async_computation.22 | async-start | bytes 6291456 | tf_op jit(solution)/shard_map/all_gather | solution.py:225
  780.4 209.5 %all-reduce.7.cloned.1.call-start = ((), (), s32[]{:S(2)}) async-start(), calls=%async_computation.33 | async-start | bytes 4194304 | tf_op jit(solution)/shard_map/psum | solution.py:234
  926.6 121.9 %reduce-scatter.20.cloned.1.call-start = ((), (), s32[]{:S(2)}) async-start(), calls=%async_computation.21 | async-start | bytes 6291456 | tf_op jit(solution)/shard_map/reduce_scatter | solution.py:242
  936.4 186.4 %reduce-scatter.38.cloned.1.call-start = ((), (), s32[]{:S(2)}) async-start(), calls=%async_computation.31 | async-start | bytes 4456448 | tf_op jit(solution)/shard_map/reduce_scatter | solution.py:282
  950.5 248.3 %reduce-scatter.36.cloned.1.call-start = ((), (), s32[]{:S(2)}) async-start(), calls=%async_computation.30 | async-start | bytes 4456448 | tf_op jit(solution)/shard_map/reduce_scatter | solution.py:279
  964.5 294.2 %reduce-scatter.32.cloned.1.call-start = ((), (), s32[]{:S(2)}) async-start(), calls=%async_computation.28 | async-start | bytes 1114112 | tf_op jit(solution)/shard_map/reduce_scatter | solution.py:273
  972.0 17.8 copy-start.38
  972.0 17.8 copy-start.71
  972.1 17.8 copy-start.73
  972.1 347.1 %reduce-scatter.34.cloned.1.call-start = ((), (), s32[]{:S(2)}) async-start(), calls=%async_computation.29 | async-start | bytes 1114112 | tf_op jit(solution)/shard_map/reduce_scatter | solution.py:276
  977.8 399.1 %reduce-scatter.24.cloned.1.call-start = ((), (), s32[]{:S(2)}) async-start(), calls=%async_computation.24 | async-start | bytes 278528 | tf_op jit(solution)/shard_map/reduce_scatter | solution.py:261
  996.9 444.2 %reduce-scatter.30.cloned.1.call-start = ((), (), s32[]{:S(2)}) async-start(), calls=%async_computation.27 | async-start | bytes 2228224 | tf_op jit(solution)/shard_map/reduce_scatter | solution.py:270
  1006.9 498.9 %reduce-scatter.28.cloned.1.call-start = ((), (), s32[]{:S(2)}) async-start(), calls=%async_computation.26 | async-start | bytes 2228224 | tf_op jit(solution)/shard_map/reduce_scatter | solution.py:267
  1016.4 553.5 %reduce-scatter.26.cloned.1.call-start = ((), (), s32[]{:S(2)}) async-start(), calls=%async_computation.25 | async-start | bytes 2228224 | tf_op jit(solution)/shard_map/reduce_scatter | solution.py:264
  1037.1 722.5 %reduce-scatter.22.cloned.1.call-start = ((), (), s32[]{:S(2)}) async-start(), calls=%async_computation.23 | async-start | bytes 6291456 | tf_op jit(solution)/shard_map/reduce_scatter | solution.py:256
  1104.1 658.1 %reduce-scatter.16.cloned.1.call-start = ((), (), s32[]{:S(2)}) async-start(), calls=%async_computation.17 | async-start | bytes 6291456 | tf_op jit(solution)/shard_map/reduce_scatter | solution.py:211
  1118.3 202.3 %copy-start.68 = (f32[128]{0:T(128)S(1)}, f32[128]{0:T(128)}, u32[]{:S(2)}) copy-start(f32[128]{0:T(128)} %get-tuple-element.597) | copy-start | bytes 1540
  1118.4 202.3 %copy-start.69 = (f32[128]{0:T(128)S(1)}, f32[128]{0:T(128)}, u32[]{:S(2)}) copy-start(f32[128]{0:T(128)} %get-tuple-element.600) | copy-start | bytes 1540
  1118.4 202.9 %copy-start.66 = (f32[128]{0:T(128)S(1)}, f32[128]{0:T(128)}, u32[]{:S(2)}) copy-start(f32[128]{0:T(128)} %get-tuple-element.598) | copy-start | bytes 1540
  1118.4 202.9 %copy-start.67 = (f32[128]{0:T(128)S(1)}, f32[128]{0:T(128)}, u32[]{:S(2)}) copy-start(f32[128]{0:T(128)} %get-tuple-element.599) | copy-start | bytes 1540
  1118.4 453.2 %copy-start.14 = (bf16[64,8,16,128]{3,2,1,0:T(8,128)(2,1)S(1)}, bf16[64,8,16,128]{3,2,1,0:T(8,128)(2,1)}, u32[]{:S(2)}) copy-start(bf16[64,8,16,128]{3,2,1,0:T(8,128)(2,1)} %copy-done.13) | copy-start | bytes 6291460
  1118.4 729.5 %all-reduce.5.cloned.1.call-start = ((), (), s32[]{:S(2)}) async-start(), calls=%async_computation.32 | async-start | bytes 270336 | tf_op jit(solution)/shard_map/psum | solution.py:286
  1600.7 140.2 %copy-start.37 = (f32[512,16]{1,0:T(8,128)S(1)}, f32[512,16]{1,0:T(8,128)}, u32[]{:S(2)}) copy-start(f32[512,16]{1,0:T(8,128)} %copy.122) | copy-start | bytes 98308
  1600.7 140.2 %copy-start.47 = (f32[512,16]{1,0:T(8,128)S(1)}, f32[512,16]{1,0:T(8,128)}, u32[]{:S(2)}) copy-start(f32[512,16]{1,0:T(8,128)} %copy.127) | copy-start | bytes 98308
  1740.9 17.2 copy-start.40
  1740.9 17.2 copy-start.42
  1740.9 17.2 copy-start.51
  1741.0 18.7 %copy-start.7 = (bf16[1024,1024]{0,1:T(8,128)(2,1)S(1)}, bf16[1024,1024]{0,1:T(8,128)(2,1)}, u32[]{:S(2)}) copy-start(bf16[1024,1024]{0,1:T(8,128)(2,1)} %copy.120) | copy-start | bytes 6291460
  1772.6 84.5 %copy-start.1 = (bf16[1024,1024]{1,0:T(8,128)(2,1)S(1)}, bf16[1024,1024]{1,0:T(8,128)(2,1)}, u32[]{:S(2)}) copy-start(bf16[1024,1024]{1,0:T(8,128)(2,1)} %param.38) | copy-start | bytes 6291460
  (65 other events, 370.9 us)
Sparse Core Ops, SparseCore 0:
  17.1 59.4 all-gather.6
  173.5 59.4 all-gather.8
  317.8 189.1 reduce-scatter.13
  516.4 56.7 all-gather.10
  574.7 56.7 all-gather.12
  665.7 99.2 reduce-scatter.17
  779.8 56.7 all-gather.14
  838.1 56.7 all-gather.16
  926.7 63.0 all-reduce.6
  992.1 54.2 reduce-scatter.19
  1050.3 72.4 reduce-scatter.37
  1127.0 71.7 reduce-scatter.35
  1202.4 56.3 reduce-scatter.31
  1262.6 56.4 reduce-scatter.33
  1322.5 54.2 reduce-scatter.23
  1380.4 60.5 reduce-scatter.29
  1445.1 60.6 reduce-scatter.27
  1509.4 60.5 reduce-scatter.25
  1572.9 53.2 reduce-scatter.21
  1628.4 54.2 reduce-scatter.15
  1759.8 88.0 all-reduce.4
where the time goes:
time: 1880 us; the launch traced here: 1860 us
  waiting for transfers between devices  998 us (53%)
  matrix products  362 us (19%)
  local copies, waits for them, and re-layouts  249 us (13%)
  other arithmetic  223 us (12%)
    reduce_scatter x1, waiting for transfers between devices, shards(): lax.psum_scatter(jnp.concatenate([matmul(gated_low, u_h) + matmul(ema_low...  189 us
    dot_general x20, matrix products, col_inner(): lax.dot_general(left, right, (((1,), (1,)), ((), ())), preferred_element_...  106 us
    scatter-add x1, other arithmetic, ema_apply(): toeplitz = jnp.where((offsets >= 0)[:, :, None], kernel[lag_index], 0.0)  104 us
    dot_general x16, matrix products, matmul(): return jnp.dot(left, right, preferred_element_type=jnp.float32)  97.7 us
    reduce_scatter x1, waiting for transfers between devices, shards(): lax.psum_scatter(col_inner(d_up, w_up), 'tensor', scatter_dimension=0, ti...  95.4 us
    gather x2, local copies, waits for them, and re-layouts, ema_apply(): toeplitz = jnp.where((offsets >= 0)[:, :, None], kernel[lag_index], 0.0)  90 us
    dot_general x16, matrix products, row_inner(): lax.dot_general(left, right, (((0,), (0,)), ((), ())), preferred_element_...  83.3 us
    reduce_scatter x1, waiting for transfers between devices, shards(): lax.psum_scatter(up_grad.astype(jnp.bfloat16), 'dp', scatter_dimension=0,...  74.2 us
  transfers between devices with their start and end apart: 21, of which 16 were waited for; matrix products, arithmetic and copies ran while one was open for 33% of the time, Pallas kernels for 0%

commit v1 on v0

--- a/solution.py
+++ b/solution.py
@@ -1,6 +1,10 @@
+import math
+
 import jax
 import jax.numpy as jnp
 from jax import lax
+from jax.experimental import pallas as pl
+from jax.experimental.pallas import tpu as pltpu
 from jax.sharding import PartitionSpec as P
 
 H = 16
@@ -308,6 +312,783 @@
     )
 
 
+CP = pltpu.CompilerParams(vmem_limit_bytes=56 * 1024 * 1024)
+BF = jnp.bfloat16
+F32 = jnp.float32
+ROWS = 256
+
+
+def sds(shape, dtype=BF):
+    return jax.ShapeDtypeStruct(shape, dtype)
+
+
+def whole(shape):
+    return pl.BlockSpec(shape, lambda i, s: (0,) * len(shape), pipeline_mode=pl.Buffered(1))
+
+
+def rows_of(cols, rows=ROWS):
+    return pl.BlockSpec((rows, cols), lambda i, s: (i, 0))
+
+
+def cols_of(rows, cols):
+    return pl.BlockSpec((rows, cols), lambda i, s: (0, i))
+
+
+def run(body, grid, scal, ins, in_specs, out_shape, out_specs, scratch=(), flops=0, name=None):
+    moved = sum(a.size * a.dtype.itemsize for a in ins)
+    moved += sum(math.prod(o.shape) * jnp.dtype(o.dtype).itemsize for o in out_shape)
+    return pl.pallas_call(
+        body,
+        out_shape=out_shape,
+        grid_spec=pltpu.PrefetchScalarGridSpec(
+            num_scalar_prefetch=1,
+            grid=grid,
+            in_specs=in_specs,
+            out_specs=out_specs,
+            scratch_shapes=list(scratch),
+        ),
+        compiler_params=CP,
+        cost_estimate=pl.CostEstimate(flops=int(flops), bytes_accessed=int(moved), transcendentals=0),
+        name=name,
+    )(scal, *ins)
+
+
+def sig(u):
+    return 1.0 / (1.0 + jnp.exp(-u))
+
+
+def silu_pair(u):
+    s = sig(u)
+    return u * s, s * (1.0 + u * (1.0 - s))
+
+
+def place(scr, s, pieces, base=0):
+    rows = pieces[0].shape[0]
+    for p in range(4):
+        scr[pl.ds(pl.multiple_of(base + s[p] * rows, rows), rows), :] = pieces[p][...]
+
+
+def piece_block(rows, cols, row_block):
+    return pl.BlockSpec((rows, cols), lambda i, s: (row_block, i))
+
+
+def piece_whole(rows, cols, row_block):
+    return pl.BlockSpec((rows, cols), lambda i, s: (row_block, 0), pipeline_mode=pl.Buffered(1))
+
+
+def k_value_own(scal, tokens, w_own):
+    n, d = tokens.shape
+    cols = w_own.shape[1]
+    tn = 512
+
+    def body(s, x_ref, w_ref, n_ref, v_ref, sl_ref):
+        @pl.when(pl.program_id(0) == 0)
+        def _():
+            x = x_ref[...].astype(F32)
+            n_ref[...] = (x * lax.rsqrt(jnp.mean(x * x, axis=-1, keepdims=True) + norm_eps)).astype(BF)
+
+        act, slope = silu_pair(matmul(n_ref[...], w_ref[...]))
+        v_ref[...] = act.astype(BF)
+        sl_ref[...] = slope.astype(BF)
+
+    return run(
+        body, (cols // tn,), scal, [tokens, w_own],
+        [whole((n, d)), cols_of(d, tn)],
+        [sds((n, d)), sds((n, cols)), sds((n, cols))],
+        [pl.BlockSpec((n, d), lambda i, s: (0, 0)), cols_of(n, tn), cols_of(n, tn)],
+        flops=2 * n * d * cols, name="value_own",
+    )
+
+
+def k_act_own(scal, x, w_own, tn):
+    n, d = x.shape
+    cols = w_own.shape[1]
+
+    def body(s, x_ref, w_ref, v_ref, sl_ref):
+        act, slope = silu_pair(matmul(x_ref[...], w_ref[...]))
+        v_ref[...] = act.astype(BF)
+        sl_ref[...] = slope.astype(BF)
+
+    return run(
+        body, (cols // tn,), scal, [x, w_own],
+        [whole((n, d)), cols_of(d, tn)],
+        [sds((n, cols)), sds((n, cols))],
+        [cols_of(n, tn), cols_of(n, tn)],
+        flops=2 * n * d * cols, name="act_own",
+    )
+
+
+def k_act_other(scal, x, pieces, rows, row_block, tn):
+    n, d = x.shape
+    cols = pieces[0].shape[1]
+
+    def body(s, x_ref, p0, p1, p2, p3, v_ref, sl_ref, w_scr):
+        place(w_scr, s, (p0, p1, p2, p3))
+        act, slope = silu_pair(matmul(x_ref[...], w_scr[...]))
+        v_ref[...] = act.astype(BF)
+        sl_ref[...] = slope.astype(BF)
+
+    return run(
+        body, (cols // tn,), scal, [x, *pieces],
+        [whole((n, d))] + [piece_block(rows, tn, row_block)] * 4,
+        [sds((n, cols)), sds((n, cols))],
+        [cols_of(n, tn), cols_of(n, tn)],
+        [pltpu.VMEM((d, tn), BF)],
+        flops=2 * n * d * cols, name="act_other",
+    )
+
+
+def k_query_key(scal, ema_low, w_z, qk_gain, qk_bias):
+    n, d = ema_low.shape
+    zw = w_z.shape[1]
+
+    def body(s, e_ref, w_ref, g_ref, b_ref, z_ref, q_ref, k_ref):
+        z_pre = matmul(e_ref[...], w_ref[...])
+        z_ref[...] = z_pre
+        act = z_pre * sig(z_pre)
+        q_ref[...] = (act * g_ref[0:1, :] + b_ref[0:1, :]).astype(BF)
+        k_ref[...] = (act * g_ref[1:2, :] + b_ref[1:2, :]).astype(BF)
+
+    return run(
+        body, (2,), scal, [ema_low, w_z, qk_gain, qk_bias],
+        [rows_of(d, n // 2), whole((d, zw)), whole((2, zw)), whole((2, zw))],
+        [sds((n, zw), F32), sds((n, zw)), sds((n, zw))],
+        [rows_of(zw, n // 2)] * 3,
+        flops=2 * n * d * zw, name="query_key",
+    )
+
+
+def k_ema_forward(scal, normed, decay, coef, omega):
+    n, d = normed.shape
+    groups = d // 128
+    tb = 128
+
+    def body(s, x_ref, dec_ref, cf_ref, om_ref, e_ref, sl_ref, st, xs, ys):
+        @pl.when(pl.program_id(0) == 0)
+        def _():
+            st[...] = jnp.zeros_like(st)
+
+        for g in range(groups):
+            xs[pl.ds(g, tb, stride=groups), :] = x_ref[:, g * 128 : (g + 1) * 128].astype(F32)
+        dec = [dec_ref[k * groups : (k + 1) * groups, :] for k in range(H)]
+        cf = [cf_ref[k * groups : (k + 1) * groups, :] for k in range(H)]
+        om = om_ref[...]
+
+        def steps(b, carry):
+            states = list(carry)
+            for u in range(8):
+                row = pl.multiple_of((b * 8 + u) * groups, groups)
+                xt = xs[pl.ds(row, groups), :]
+                parts = [om * xt, None, None, None]
+                for k in range(H):
+                    states[k] = dec[k] * states[k] + xt
+                    term = cf[k] * states[k]
+                    parts[k % 4] = term if parts[k % 4] is None else parts[k % 4] + term
+                ys[pl.ds(row, groups), :] = (parts[0] + parts[1]) + (parts[2] + parts[3])
+            return tuple(states)
+
+        start = tuple(st[k * groups : (k + 1) * groups, :] for k in range(H))
+        end = lax.fori_loop(0, tb // 8, steps, start)
+        for k in range(H):
+            st[k * groups : (k + 1) * groups, :] = end[k]
+        for g in range(groups):
+            act, slope = silu_pair(ys[pl.ds(g, tb, stride=groups), :])
+            e_ref[:, g * 128 : (g + 1) * 128] = act.astype(BF)
+            sl_ref[:, g * 128 : (g + 1) * 128] = slope.astype(BF)
+
+    return run(
+        body, (n // tb,), scal, [normed, decay, coef, omega],
+        [rows_of(d, tb), whole((H * groups, 128)), whole((H * groups, 128)), whole((groups, 128))],
+        [sds((n, d)), sds((n, d))],
+        [rows_of(d, tb)] * 2,
+        [pltpu.VMEM((H * groups, 128), F32), pltpu.VMEM((tb * groups, 128), F32), pltpu.VMEM((tb * groups, 128), F32)],
+        flops=20e9, name="ema_forward",
+    )
+
+
+def k_ema_backward(scal, normed, d_e, decay, coef, omega):
+    n, d = normed.shape
+    groups = d // 128
+    tb = 128
+    nb = n // tb
+    half = H // 2
+    gh = groups * half
+
+    def body(s, x_ref, g_ref, dec_ref, cf_ref, om_ref, o_ref, a_ref, b_ref, w_ref, back, deriv, xs, gs, ys):
+        @pl.when(pl.program_id(0) == 0)
+        def _():
+            back[...] = jnp.zeros_like(back)
+            deriv[...] = jnp.zeros_like(deriv)
+            a_ref[...] = jnp.zeros_like(a_ref)
+            b_ref[...] = jnp.zeros_like(b_ref)
+            w_ref[...] = jnp.zeros_like(w_ref)
+
+        for g in range(groups):
+            xs[pl.ds(g, tb, stride=groups), :] = x_ref[:, g * 128 : (g + 1) * 128].astype(F32)
+            gs[pl.ds(g, tb, stride=groups), :] = g_ref[:, g * 128 : (g + 1) * 128]
+
+        for part in range(2):
+            first = part * gh
+            at = [slice(first + k * groups, first + (k + 1) * groups) for k in range(half)]
+            dec = [dec_ref[a, :] for a in at]
+
+            def steps(b, carry, part=part, at=at, dec=dec):
+                bk, dv, aa, bb, ww = (list(c) for c in carry)
+                for u in range(4):
+                    row = pl.multiple_of((tb - 1 - (b * 4 + u)) * groups, groups)
+                    xt = xs[pl.ds(row, groups), :]
+                    gt = gs[pl.ds(row, groups), :]
+                    if part == 0:
+                        outs = [om_ref[...] * gt, None]
+                        ww[0] = ww[0] + xt * gt
+                    else:
+                        outs = [ys[pl.ds(row, groups), :], None]
+                    for k in range(half):
+                        dv[k] = dec[k] * dv[k] + bk[k]
+                        bk[k] = dec[k] * bk[k] + gt
+                        term = cf_ref[at[k], :] * bk[k]
+                        outs[k % 2] = term if outs[k % 2] is None else outs[k % 2] + term
+                        aa[k] = aa[k] + xt * bk[k]
+                        bb[k] = bb[k] + xt * dv[k]
+                    ys[pl.ds(row, groups), :] = outs[0] + outs[1]
+                return tuple(bk), tuple(dv), tuple(aa), tuple(bb), tuple(ww)
+
+            start = (
+                tuple(back[a, :] for a in at),
+                tuple(deriv[a, :] for a in at),
+                tuple(a_ref[a, :] for a in at),
+                tuple(b_ref[a, :] for a in at),
+                (w_ref[...],),
+            )
+            bk, dv, aa, bb, ww = lax.fori_loop(0, tb // 4, steps, start)
+            for k in range(half):
+                back[at[k], :] = bk[k]
+                deriv[at[k], :] = dv[k]
+                a_ref[at[k], :] = aa[k]
+                b_ref[at[k], :] = bb[k]
+            w_ref[...] = ww[0]
+        for g in range(groups):
+            o_ref[:, g * 128 : (g + 1) * 128] = ys[pl.ds(g, tb, stride=groups), :]
+
+    back_rows = pl.BlockSpec((tb, d), lambda i, s: (nb - 1 - i, 0))
+    par = (H * groups, 128)
+    const = pl.BlockSpec(par, lambda i, s: (0, 0))
+    return run(
+        body, (nb,), scal, [normed, d_e, decay, coef, omega],
+        [back_rows, back_rows, whole(par), whole(par), whole((groups, 128))],
+        [sds((n, d), F32), sds(par, F32), sds(par, F32), sds((groups, 128), F32)],
+        [back_rows, const, const, pl.BlockSpec((groups, 128), lambda i, s: (0, 0))],
+        [pltpu.VMEM(par, F32), pltpu.VMEM(par, F32)] + [pltpu.VMEM((tb * groups, 128), F32)] * 3,
+        flops=40e9, name="ema_backward",
+    )
+
+
+def k_attend(scal, q, k, v_own, v_oth, g_own, g_oth, gs_own, gs_oth):
+    n, zw = q.shape
+    half = v_own.shape[1]
+    blocks = n // ROWS
+    scale = zw ** (-0.5)
+
+    def body(s, q_ref, k_ref, vo, vt, go, gt, so, st, gated_o, gated_t, mo, mt, p_ref):
+        for i in range(blocks):
+
+            @pl.when(pl.program_id(0) == i)
+            def _(i=i):
+                seen = (i + 1) * ROWS
+                sc = col_inner(q_ref[...], k_ref[0:seen, :]) * scale
+                row = i * ROWS + lax.broadcasted_iota(jnp.int32, (ROWS, seen), 0)
+                col = lax.broadcasted_iota(jnp.int32, (ROWS, seen), 1)
+                sc = jnp.where(col <= row, sc, masked_value)
+                e = jnp.exp(sc - jnp.max(sc, axis=-1, keepdims=True))
+                p = (e * (1.0 / jnp.sum(e, axis=-1, keepdims=True))).astype(BF)
+                p_ref[:, 0:seen] = p
+                for v_ref, g_ref, sl_ref, gated, m in ((vo, go, so, gated_o, mo), (vt, gt, st, gated_t, mt)):
+                    att = matmul(p, v_ref[0:seen, :])
+                    gated[...] = (g_ref[...].astype(F32) * att).astype(BF)
+                    m[...] = (sl_ref[...].astype(F32) * att).astype(BF)
+
+    return run(
+        body, (blocks,), scal, [q, k, v_own, v_oth, g_own, g_oth, gs_own, gs_oth],
+        [rows_of(zw), whole((n, zw)), whole((n, half)), whole((n, half))] + [rows_of(half)] * 4,
+        [sds((n, half))] * 4 + [sds((n, n))],
+        [rows_of(half)] * 4 + [rows_of(n)],
+        flops=n * n * (zw + 2 * half) * 1.25, name="attend",
+    )
+
+
+def k_gate(scal, gated_own, gated_oth, ema_low, tokens, u_own, h_own, f_own, packs, rows):
+    n, d = tokens.shape
+    half = u_own.shape[0]
+    ch = h_own.shape[0]
+    ru, rh = rows
+
+    def body(s, go, gt, e_ref, x_ref, uo, ho, fo, u0, u1, u2, u3, h0, h1, h2, h3, f0, f1, f2, f3,
+             mix_ref, low_ref, a_ref, b_ref, up_ref, u_scr, h_scr, f_scr):
+        @pl.when(pl.program_id(0) == 0)
+        def _():
+            place(u_scr, s, (u0, u1, u2, u3))
+            own = pl.multiple_of(s[6] * ch, ch)
+            oth = s[7] * ch
+            h_scr[pl.ds(own, ch), :] = ho[...]
+            f_scr[pl.ds(own, ch), :] = fo[...]
+            place(h_scr, s, (h0, h1, h2, h3), oth)
+            place(f_scr, s, (f0, f1, f2, f3), oth)
+
+        h_pre = matmul(go[...], uo[...]) + matmul(gt[...], u_scr[...]) + matmul(e_ref[...], h_scr[...])
+        f_pre = matmul(e_ref[...], f_scr[...])
+        x = x_ref[...].astype(F32)
+        act, slope = silu_pair(h_pre)
+        update = sig(f_pre)
+        mixed = update * act + (1.0 - update) * x
+        mix_ref[...] = mixed
+        low_ref[...] = (mixed * lax.rsqrt(jnp.mean(mixed * mixed, axis=-1, keepdims=True) + norm_eps)).astype(BF)
+        a_ref[...] = (update * slope).astype(BF)
+        b_ref[...] = ((act - x) * update * (1.0 - update)).astype(BF)
+        up_ref[...] = (1.0 - update).astype(BF)
+
+    ins = [gated_own, gated_oth, ema_low, tokens, u_own, h_own, f_own, *packs, *packs, *packs]
+    specs = [rows_of(half), rows_of(half), rows_of(d), rows_of(d), whole((half, d)), whole((ch, d)), whole((ch, d))]
+    specs += [piece_whole(ru, d, 0)] * 4 + [piece_whole(rh, d, ru // rh)] * 4 + [piece_whole(rh, d, ru // rh + 1)] * 4
+    return run(
+        body, (n // ROWS,), scal, ins, specs,
+        [sds((n, d), F32), sds((n, d)), sds((n, d)), sds((n, d)), sds((n, d))],
+        [rows_of(d)] * 5,
+        [pltpu.VMEM((half, d), BF), pltpu.VMEM((2 * ch, d), BF), pltpu.VMEM((2 * ch, d), BF)],
+        flops=2 * n * d * (2 * half + 4 * ch), name="gate",
+    )
+
+
+def k_down_own(scal, hid, us, w_own, cot):
+    n, cols = hid.shape
+    d = w_own.shape[1]
+    tn = 512
+
+    def body(s, h_ref, us_ref, w_ref, c_ref, acc_ref, du_ref):
+        part = matmul(h_ref[...], w_ref[...])
+
+        @pl.when(pl.program_id(0) == 0)
+        def _():
+            acc_ref[...] = part
+
+        @pl.when(pl.program_id(0) > 0)
+        def _():
+            acc_ref[...] += part
+
+        du_ref[...] = (col_inner(c_ref[...], w_ref[...]) * us_ref[...].astype(F32)).astype(BF)
+
+    return run(
+        body, (cols // tn,), scal, [hid, us, w_own, cot],
+        [cols_of(n, tn), cols_of(n, tn), rows_of(d, tn), whole((n, d))],
+        [sds((n, d), F32), sds((n, cols))],
+        [pl.BlockSpec((n, d), lambda i, s: (0, 0)), cols_of(n, tn)],
+        flops=4 * n * d * cols, name="down_own",
+    )
+
+
+def k_down_other(scal, hid, us, packs, cot, acc, mixed):
+    n, cols = hid.shape
+    rp, d = packs[0].shape
+
+    def body(s, h_ref, us_ref, w0, w1, w2, w3, c_ref, in_ref, m_ref, out_ref, du_ref, acc_ref):
+        for p, w_ref in enumerate((w0, w1, w2, w3)):
+
+            @pl.when(pl.program_id(0) == p)
+            def _(p=p, w_ref=w_ref):
+                part = matmul(h_ref[...], w_ref[...])
+                if p == 0:
+                    acc_ref[...] = part + in_ref[...]
+                elif p < 3:
+                    acc_ref[...] += part
+                else:
+                    out_ref[...] = (m_ref[...] + (acc_ref[...] + part)).astype(BF)
+                du_ref[...] = (col_inner(c_ref[...], w_ref[...]) * us_ref[...].astype(F32)).astype(BF)
+
+    at = pl.BlockSpec((n, rp), lambda i, s: (0, s[i]))
+    return run(
+        body, (4,), scal, [hid, us, *packs, cot, acc, mixed],
+        [at, at] + [whole((rp, d))] * 4 + [whole((n, d))] * 3,
+        [sds((n, d)), sds((n, cols))],
+        [pl.BlockSpec((n, d), lambda i, s: (0, 0)), at],
+        [pltpu.VMEM((n, d), F32)],
+        flops=4 * n * d * cols, name="down_other",
+    )
+
+
+def k_lowered_back(scal, du_own, du_oth, w_own, packs, cot, mixed, a, b, keep):
+    n, cols = du_own.shape
+    d = w_own.shape[0]
+    rp = packs[0].shape[0]
+
+    def body(s, do, dt, wo, w0, w1, w2, w3, c_ref, m_ref, a_ref, b_ref, k_ref, dh_ref, df_ref, dir_ref, w_scr):
+        @pl.when(pl.program_id(0) == 0)
+        def _():
+            place(w_scr, s, (w0, w1, w2, w3))
+
+        dl = col_inner(do[...], wo[...]) + col_inner(dt[...], w_scr[...])
+        m = m_ref[...]
+        r = lax.rsqrt(jnp.mean(m * m, axis=-1, keepdims=True) + norm_eps)
+        n2 = m * r
+        dm = c_ref[...].astype(F32) + r * (dl - n2 * jnp.mean(dl * n2, axis=-1, keepdims=True))
+        dh_ref[...] = (dm * a_ref[...].astype(F32)).astype(BF)
+        df_ref[...] = (dm * b_ref[...].astype(F32)).astype(BF)
+        dir_ref[...] = (dm * k_ref[...].astype(F32)).astype(BF)
+
+    return run(
+        body, (n // ROWS,), scal, [du_own, du_oth, w_own, *packs, cot, mixed, a, b, keep],
+        [rows_of(cols), rows_of(cols), whole((d, cols))] + [whole((rp, cols))] * 4 + [rows_of(d)] * 5,
+        [sds((n, d))] * 3,
+        [rows_of(d)] * 3,
+        [pltpu.VMEM((d, cols), BF)],
+        flops=4 * n * d * cols, name="lowered_back",
+    )
+
+
+def k_gated_back(scal, dh, u_own, packs, rp, g_own, g_oth, m_own, m_oth):
+    n, d = dh.shape
+    half = u_own.shape[0]
+    own_steps = half // rp
+
+    def body(s, dh_ref, uo, u0, u1, u2, u3, go, gt, mo, mt, ao, at, co, ct):
+        for i in range(own_steps + 4):
+
+            @pl.when(pl.program_id(0) == i)
+            def _(i=i):
+                if i < own_steps:
+                    w, g_ref, m_ref, a_ref, c_ref = uo[i * rp : (i + 1) * rp, :], go, mo, ao, co
+                else:
+                    w, g_ref, m_ref, a_ref, c_ref = (u0, u1, u2, u3)[i - own_steps][...], gt, mt, at, ct
+                dg = col_inner(dh_ref[...], w)
+                a_ref[...] = (dg * g_ref[...].astype(F32)).astype(BF)
+                c_ref[...] = (dg * m_ref[...].astype(F32)).astype(BF)
+
+    first = pl.BlockSpec((n, rp), lambda i, s: (0, jnp.minimum(i, own_steps - 1)))
+    second = pl.BlockSpec((n, rp), lambda i, s: (0, s[jnp.maximum(i - own_steps, 0)]))
+    return run(
+        body, (own_steps + 4,), scal, [dh, u_own, *packs, g_own, g_oth, m_own, m_oth],
+        [whole((n, d)), whole((half, d))] + [piece_whole(rp, d, 0)] * 4 + [first, second, first, second],
+        [sds((n, half))] * 4,
+        [first, second, first, second],
+        flops=4 * n * d * half, name="gated_back",
+    )
+
+
+def k_value_back(scal, p, da_own, da_oth, vs_own, vs_oth):
+    n = p.shape[0]
+    half = da_own.shape[1]
+    blocks = n // ROWS
+
+    def body(s, p_ref, ao, at, so, st, oo, ot):
+        for j in range(blocks):
+
+            @pl.when(pl.program_id(0) == j)
+            def _(j=j):
+                pj = p_ref[j * ROWS :, :]
+                oo[...] = (row_inner(pj, ao[j * ROWS :, :]) * so[...].astype(F32)).astype(BF)
+                ot[...] = (row_inner(pj, at[j * ROWS :, :]) * st[...].astype(F32)).astype(BF)
+
+    return run(
+        body, (blocks,), scal, [p, da_own, da_oth, vs_own, vs_oth],
+        [cols_of(n, ROWS), whole((n, half)), whole((n, half)), rows_of(half), rows_of(half)],
+        [sds((n, half))] * 2,
+        [rows_of(half)] * 2,
+        flops=n * n * 2 * half * 1.25, name="value_back",
+    )
+
+
+def k_score_back(scal, p, da_own, da_oth, v_own, v_oth, q, k, z_pre, gain):
+    n, zw = q.shape
+    half = da_own.shape[1]
+    blocks = n // ROWS
+    scale = zw ** (-0.5)
+
+    def body(s, p_ref, ao, at, vo, vt, q_ref, k_ref, z_ref, g_ref, dz_ref, st_ref, ds, dq):
+        for i in range(blocks):
+
+            @pl.when(pl.program_id(0) == i)
+            def _(i=i):
+                seen = (i + 1) * ROWS
+                pr = p_ref[:, 0:seen].astype(F32)
+                dp = col_inner(ao[...], vo[0:seen, :]) + col_inner(at[...], vt[0:seen, :])
+                d = (pr * (dp - jnp.sum(pr * dp, axis=-1, keepdims=True))).astype(BF)
+                ds[i * ROWS : (i + 1) * ROWS, 0:seen] = d
+                dq[i * ROWS : (i + 1) * ROWS, :] = matmul(d, k_ref[0:seen, :]) * scale
+                if i == blocks - 1:
+                    sums = [jnp.zeros((1, zw), F32)] * 4
+                    for j in range(blocks):
+                        at_j = slice(j * ROWS, (j + 1) * ROWS)
+                        dk = row_inner(ds[j * ROWS :, at_j], q_ref[j * ROWS :, :]) * scale
+                        dqj = dq[at_j, :]
+                        act, slope = silu_pair(z_ref[at_j, :])
+                        dz_ref[at_j, :] = (slope * (dqj * g_ref[0:1, :] + dk * g_ref[1:2, :])).astype(BF)
+                        for n_, v in enumerate((dqj * act, dk * act, dqj, dk)):
+                            sums[n_] = sums[n_] + jnp.sum(v, axis=0, keepdims=True)
+                    for n_ in range(4):
+                        st_ref[n_ : n_ + 1, :] = sums[n_]
+                    st_ref[4:8, :] = jnp.zeros((4, zw), F32)
+
+    return run(
+        body, (blocks,), scal, [p, da_own, da_oth, v_own, v_oth, q, k, z_pre, gain],
+        [rows_of(n), rows_of(half), rows_of(half), whole((n, half)), whole((n, half)), whole((n, zw)),
+         whole((n, zw)), whole((n, zw)), whole((2, zw))],
+        [sds((n, zw)), sds((8, zw), F32)],
+        [pl.BlockSpec((n, zw), lambda i, s: (0, 0)), pl.BlockSpec((8, zw), lambda i, s: (0, 0))],
+        [pltpu.VMEM((n, n), BF), pltpu.VMEM((n, zw), F32)],
+        flops=n * n * 2 * half * 1.25, name="score_back",
+    )
+
+
+def k_ema_out_back(scal, dg_own, dg_oth, dz, dh, df, slope, wg_own, w_z, h_own, f_own, packs_g, rg, packs_h, rows):
+    n, d = dh.shape
+    half = dg_own.shape[1]
+    ch = h_own.shape[0]
+    zw = w_z.shape[1]
+    ru, rh = rows
+
+    def body(s, go, gt, dz_ref, dh_ref, df_ref, sl_ref, wo, wz, ho, fo, g0, g1, g2, g3, h0, h1, h2, h3,
+             f0, f1, f2, f3, o_ref, w_scr, h_scr, f_scr):
+        @pl.when(pl.program_id(0) == 0)
+        def _():
+            place(w_scr, s, (g0, g1, g2, g3))
+            own = pl.multiple_of(s[6] * ch, ch)
+            oth = s[7] * ch
+            h_scr[pl.ds(own, ch), :] = ho[...]
+            f_scr[pl.ds(own, ch), :] = fo[...]
+            place(h_scr, s, (h0, h1, h2, h3), oth)
+            place(f_scr, s, (f0, f1, f2, f3), oth)
+
+        total = col_inner(go[...], wo[...]) + col_inner(gt[...], w_scr[...]) + col_inner(dz_ref[...], wz[...])
+        total = total + col_inner(dh_ref[...], h_scr[...]) + col_inner(df_ref[...], f_scr[...])
+        o_ref[...] = total * sl_ref[...].astype(F32)
+
+    ins = [dg_own, dg_oth, dz, dh, df, slope, wg_own, w_z, h_own, f_own, *packs_g, *packs_h, *packs_h]
+    specs = [rows_of(half), rows_of(half), rows_of(zw), rows_of(d), rows_of(d), rows_of(d)]
+    specs += [whole((d, half)), whole((d, zw)), whole((ch, d)), whole((ch, d))]
+    specs += [piece_whole(rg, half, 1)] * 4
+    specs += [piece_whole(rh, d, ru // rh)] * 4 + [piece_whole(rh, d, ru // rh + 1)] * 4
+    return run(
+        body, (n // ROWS,), scal, ins, specs,
+        [sds((n, d), F32)], [rows_of(d)],
+        [pltpu.VMEM((d, half), BF), pltpu.VMEM((2 * ch, d), BF), pltpu.VMEM((2 * ch, d), BF)],
+        flops=2 * n * d * (2 * half + 4 * ch + zw), name="ema_out_back",
+    )[0]
+
+
+def k_input_back(scal, dv_own, dv_oth, w_own, packs, rp, d_sig, tokens, direct):
+    n, d = tokens.shape
+    half = dv_own.shape[1]
+
+    def body(s, vo, vt, wo, w0, w1, w2, w3, sg, x_ref, dir_ref, o_ref, w_scr):
+        @pl.when(pl.program_id(0) == 0)
+        def _():
+            place(w_scr, s, (w0, w1, w2, w3))
+
+        dn = col_inner(vo[...], wo[...]) + col_inner(vt[...], w_scr[...]) + sg[...]
+        x = x_ref[...].astype(F32)
+        r = lax.rsqrt(jnp.mean(x * x, axis=-1, keepdims=True) + norm_eps)
+        n1 = x * r
+        o_ref[...] = dir_ref[...].astype(F32) + r * (dn - n1 * jnp.mean(dn * n1, axis=-1, keepdims=True))
+
+    return run(
+        body, (n // ROWS,), scal, [dv_own, dv_oth, w_own, *packs, d_sig, tokens, direct],
+        [rows_of(half), rows_of(half), whole((d, half))] + [piece_whole(rp, half, 0)] * 4 + [rows_of(d)] * 3,
+        [sds((n, d), F32)], [rows_of(d)],
+        [pltpu.VMEM((d, half), BF)],
+        flops=4 * n * d * half, name="input_back",
+    )[0]
+
+
+def k_weight(scal, left, right, at, cols, tn, adds=(), name="weight"):
+    n, d = left.shape
+    steps = cols // tn
+
+    def body(s, l_ref, r_ref, *refs):
+        total = row_inner(l_ref[...], r_ref[...])
+        for ref in refs[:-1]:
+            total = total + ref[...].astype(F32)
+        refs[-1][...] = total.astype(BF)
+
+    ins = [left, right] + [a for a, _ in adds]
+    specs = [whole((n, d)), pl.BlockSpec((n, tn), lambda i, s: (0, at(s) * steps + i))]
+    specs += [pl.BlockSpec((d, tn), lambda i, s, o=o: (0, o * steps + i)) for _, o in adds]
+    return run(
+        body, (steps,), scal, ins, specs, [sds((d, cols))], [cols_of(d, tn)],
+        flops=2 * n * d * cols, name=name,
+    )[0]
+
+
+def swap(values, axis, bit, size):
+    return lax.ppermute(values, axis, [(i, i ^ bit) for i in range(size)])
+
+
+def pick(values, index, axis):
+    return lax.dynamic_index_in_dim(values, index, axis, keepdims=False)
+
+
+def one_sequence(
+    tokens, alpha_logit, delta_logit, ema_beta, ema_eta, ema_omega, w_z, qk_gain, qk_bias,
+    w_v, w_gamma, u_h, w_h, w_phi, w_up, w_down, cotangent,
+):
+    n, d = tokens.shape
+    dp_size = lax.axis_size("dp")
+    me = lax.axis_index("dp").astype(jnp.int32)
+    t = lax.axis_index("tensor").astype(jnp.int32)
+    core = me % 2
+    x_pos = (me // 2) % 2
+    z_pos = me // 4
+    k0 = me % 4
+    scal = jnp.stack([k0, k0 ^ 2, k0 ^ 1, k0 ^ 3, core, 1 - core, t, 1 - t])
+
+    def my_rows(w):
+        rows = w.shape[0] // 4
+        return lax.dynamic_slice_in_dim(w, k0 * rows, rows, 0)
+
+    def fetch(values):
+        by_y = swap(values, "tensor", 1, 2)
+        by_x = swap(by_y, "dp", 2, dp_size)
+        return by_y, by_x, swap(by_y, "dp", 1, dp_size), swap(by_x, "dp", 1, dp_size)
+
+    own_params = jnp.concatenate(
+        [a.T for a in (alpha_logit, delta_logit, ema_beta, ema_eta)] + [ema_omega[None]], axis=0
+    )
+    oth_params = swap(own_params, "tensor", 1, 2)
+    pv = fetch(jnp.concatenate([my_rows(w_v), my_rows(w_gamma)], axis=0))
+    ph = fetch(jnp.concatenate([my_rows(u_h), my_rows(w_h), my_rows(w_phi)], axis=0))
+    pu = fetch(my_rows(w_up))
+    pd = fetch(my_rows(w_down))
+    rv = w_v.shape[0] // 4
+    rh = (u_h.shape[0] // 4, w_h.shape[0] // 4)
+
+    params = jnp.where(
+        t == 0,
+        jnp.concatenate([own_params, oth_params], axis=1),
+        jnp.concatenate([oth_params, own_params], axis=1),
+    )
+    al, de, be, et = (params[i * H : (i + 1) * H] for i in range(4))
+    alpha_rate = jax.nn.sigmoid(al)
+    decay = (1.0 - alpha_rate * jax.nn.sigmoid(de)).reshape(-1, 128)
+    coef = (alpha_rate * be * et).reshape(-1, 128)
+    omega = params[4 * H].reshape(-1, 128)
+
+    normed, v_own, vs_own = k_value_own(scal, tokens, w_v)
+    ema_low, e_slope = k_ema_forward(scal, normed, decay, coef, omega)
+    z_pre, query, key = k_query_key(scal, ema_low, w_z, qk_gain, qk_bias)
+    g_own, gs_own = k_act_own(scal, ema_low, w_gamma, 512)
+    v_oth, vs_oth = k_act_other(scal, normed, pv, rv, 0, 512)
+    g_oth, gs_oth = k_act_other(scal, ema_low, pv, rv, 1, 512)
+    gated_own, gated_oth, m_own, m_oth, probs = k_attend(
+        scal, query, key, v_own, v_oth, g_own, g_oth, gs_own, gs_oth
+    )
+    mixed, lowered, fac_h, fac_f, keep = k_gate(
+        scal, gated_own, gated_oth, ema_low, tokens, u_h, w_h, w_phi, ph, rh
+    )
+    hid_own, us_own = k_act_own(scal, lowered, w_up, 1024)
+    hid_oth, us_oth = k_act_other(scal, lowered, pu, pu[0].shape[0], 0, 1024)
+    acc, du_own = k_down_own(scal, hid_own, us_own, w_down, cotangent)
+    output, du_oth = k_down_other(scal, hid_oth, us_oth, pd, cotangent, acc, mixed)
+    dh, df, direct = k_lowered_back(
+        scal, du_own, du_oth, w_up, pu, cotangent, mixed, fac_h, fac_f, keep
+    )
+    da_own, da_oth, dg_own, dg_oth = k_gated_back(
+        scal, dh, u_h, ph, rh[0], g_own, g_oth, m_own, m_oth
+    )
+    dv_own, dv_oth = k_value_back(scal, probs, da_own, da_oth, vs_own, vs_oth)
+    dz, stats = k_score_back(scal, probs, da_own, da_oth, v_own, v_oth, query, key, z_pre, qk_gain)
+    d_e = k_ema_out_back(
+        scal, dg_own, dg_oth, dz, dh, df, e_slope, w_gamma, w_z, w_h, w_phi, pv, rv, ph, rh
+    )
+    d_sig, sum_a, sum_b, sum_w = k_ema_backward(scal, normed, d_e, decay, coef, omega)
+    input_grad = k_input_back(scal, dv_own, dv_oth, w_v, pv, rv, d_sig, tokens, direct)
+
+    def theirs(s):
+        return s[5]
+
+    def mine(s):
+        return s[4]
+
+    def chip_sum(left, own, oth, tn):
+        quarter = own.shape[1] // 2
+        tn = min(tn, quarter)
+        sent = [k_weight(scal, left, r, theirs, quarter, tn) for r in (own, oth)]
+        got = [swap(v, "dp", 1, dp_size) for v in sent]
+        return (
+            k_weight(scal, left, own, mine, quarter, tn, [(got[0], 0)]),
+            k_weight(scal, left, oth, mine, quarter, tn, [(got[1], 0)]),
+        )
+
+    def chip_sum_ema(left):
+        quarter = d // 4
+        ats = [
+            (lambda s: s[6] * 2 + s[5], lambda s: s[6] * 2 + s[4]),
+            (lambda s: s[7] * 2 + s[5], lambda s: s[7] * 2 + s[4]),
+        ]
+        res = []
+        for send_at, keep_at in ats:
+            got = swap(k_weight(scal, left, ema_low, send_at, quarter, quarter), "dp", 1, dp_size)
+            res.append(k_weight(scal, left, ema_low, keep_at, quarter, quarter, [(got, 0)]))
+        return tuple(res)
+
+    def over_rows(total):
+        c = total.shape[1]
+        by_x = total.reshape(4, 2, d // 8, c)
+        got = swap(pick(by_x, 1 - x_pos, 1), "dp", 2, dp_size)
+        total = (pick(by_x, x_pos, 1).astype(F32) + got.astype(F32)).astype(BF)
+        by_z = total.reshape(2, 2, d // 8, c)
+        got = swap(pick(by_z, 1 - z_pos % 2, 1), "dp", 4, dp_size)
+        total = (pick(by_z, z_pos % 2, 1).astype(F32) + got.astype(F32)).astype(BF)
+        got = swap(pick(total, 1 - z_pos // 2, 0), "dp", 8, dp_size)
+        return pick(total, z_pos // 2, 0).astype(F32) + got.astype(F32)
+
+    def finish(total):
+        c = total.shape[1]
+        by_core = total.reshape(2, d // 16, c)
+        got = swap(pick(by_core, 1 - core, 0).astype(BF), "dp", 1, dp_size).astype(F32)
+        kept = pick(by_core, core, 0)
+        return jnp.where(
+            core == 0,
+            jnp.concatenate([kept, got], axis=1),
+            jnp.concatenate([got, kept], axis=1),
+        )
+
+    def over_y(pair):
+        own, oth = pair
+        got = swap(oth, "tensor", 1, 2)
+        return (own.astype(F32) + got.astype(F32)).astype(BF)
+
+    down_t = finish(over_rows(over_y(chip_sum(cotangent, hid_own, hid_oth, 1024))))
+    up = finish(over_rows(over_y(chip_sum(lowered, du_own, du_oth, 1024))))
+    uh_t = finish(over_rows(over_y(chip_sum(dh, gated_own, gated_oth, 512))))
+    wh_t = finish(over_rows(over_y(chip_sum_ema(dh))))
+    phi_t = finish(over_rows(over_y(chip_sum_ema(df))))
+    gamma = finish(over_rows(over_y(chip_sum(ema_low, dg_own, dg_oth, 512))))
+    value = finish(over_rows(over_y(chip_sum(normed, dv_own, dv_oth, 512))))
+    z_own = k_weight(scal, ema_low, dz, lambda s: 0, dz.shape[1], dz.shape[1])
+    z_sum = (z_own.astype(F32) + swap(z_own, "dp", 1, dp_size).astype(F32)).astype(BF)
+    z_sum = (z_sum.astype(F32) + swap(z_sum, "tensor", 1, 2).astype(F32)).astype(BF)
+    z_grad = pick(over_rows(z_sum).reshape(2, d // 16, -1), core, 0)
+
+    sums = lax.psum(jnp.concatenate([sum_a, sum_b, sum_w, stats], axis=0), ("dp", "tensor"))
+    gh = sum_a.shape[0]
+
+    def own_half(v):
+        return lax.dynamic_slice_in_dim(v, t * (d // 2), d // 2, 1).T
+
+    tot_a = own_half(sums[:gh].reshape(H, d))
+    tot_b = own_half(sums[gh : 2 * gh].reshape(H, d))
+    omega_grad = lax.dynamic_slice_in_dim(sums[2 * gh : 2 * gh + d // 128].reshape(d), t * (d // 2), d // 2, 0)
+    zsum = sums[2 * gh + d // 128 :]
+    rate = jax.nn.sigmoid(alpha_logit)
+    damp = jax.nn.sigmoid(delta_logit)
+    feed = rate * ema_beta
+    feed_grad = ema_eta * tot_a
+    decay_grad = feed * ema_eta * tot_b
+    alpha_grad = (feed_grad * ema_beta - decay_grad * damp) * rate * (1.0 - rate)
+    delta_grad = -decay_grad * rate * damp * (1.0 - damp)
+    return (
+        output, input_grad, alpha_grad, delta_grad, feed_grad * rate, feed * tot_a, omega_grad,
+        z_grad, zsum[0:2], zsum[2:4], value, gamma, uh_t.T, wh_t.T, phi_t.T, up, down_t.T,
+    )
+
+
 def solution(mesh):
     placed = (
         P(("dp", "tensor"), None),
@@ -328,8 +1109,13 @@
         P("tensor", None),
         P(("dp", "tensor"), None),
     )
+
+    def per_device(tokens, *rest):
+        whole_sequence = tokens.shape[0] == LEN and dict(mesh.shape) == {"dp": 16, "tensor": 2}
+        return (one_sequence if whole_sequence else shards)(tokens, *rest)
+
     return jax.shard_map(
-        shards,
+        per_device,
         mesh=mesh,
         in_specs=placed,
         out_specs=(

time: 1880 us -> 871 us (0.46)
  waiting for transfers between devices: 998 us -> 334 us
  Pallas kernels: 0 us -> 412 us
  matrix products: 362 us -> 0 us
  local copies, waits for them, and re-layouts: 249 us -> 25.4 us
  other arithmetic: 223 us -> 21.1 us
  starting transfers between devices: 1.87 us -> 55 us
    reduce_scatter x13 -> x0, waiting for transfers between devices: 724 us -> none  [the longest x1 189 us: shards(): lax.psum_scatter(jnp.concatenate([matmul(gated_low, u_h) + matmul(ema_low...]
    pallas_call x0 -> x48, Pallas kernels: none -> 412 us  [run(): pl.pallas_call(body, out_shape=out_shape, grid_spec=pltpu.PrefetchScalarG...]
    dot_general x61 -> x0, matrix products: 362 us -> none  [the longest x20 106 us: col_inner(): lax.dot_general(left, right, (((1,), (1,)), ((), ())), preferred_element_...]
    ppermute x0 -> x71, waiting for transfers between devices: none -> 233 us  [swap(): return lax.ppermute(values, axis, [(i, i ^ bit) for i in range(size)])]
    all_gather x6 -> x0, waiting for transfers between devices: 195 us -> none  [the longest x1 56.3 us: shards(): lax.all_gather(normed_two.astype(jnp.bfloat16), 'tensor', axis=0, tiled=T...]
    scatter-add x1 -> x0, other arithmetic: 104 us -> none  [ema_apply(): toeplitz = jnp.where((offsets >= 0)[:, :, None], kernel[lag_index], 0.0)]
    gather x2 -> x0, local copies, waits for them, and re-layouts: 90 us -> none  [ema_apply(): toeplitz = jnp.where((offsets >= 0)[:, :, None], kernel[lag_index], 0.0)]
    ppermute x0 -> x71, starting transfers between devices: none -> 55 us  [swap(): return lax.ppermute(values, axis, [(i, i ^ bit) for i in range(size)])]
  transfers between devices with their start and end apart: 21 -> 72, of which waited for: 16 -> 25; matrix products, arithmetic and copies ran while one was open for 33% -> 4% of each run, Pallas kernels for 0% -> 41%
where the time goes in v1:
time: 871 us; the launch traced here: 862 us
  Pallas kernels  412 us (47%)
  waiting for transfers between devices  334 us (38%)
  starting transfers between devices  55 us (6%)
  local copies, waits for them, and re-layouts  25.4 us (3%)
  other arithmetic  21.1 us (2%)
  between operations  15.6 us (2%)
    pallas_call x48, Pallas kernels, run(): pl.pallas_call(body, out_shape=out_shape, grid_spec=pltpu.PrefetchScalarG...  412 us
    ppermute x71, waiting for transfers between devices, swap(): return lax.ppermute(values, axis, [(i, i ^ bit) for i in range(size)])  233 us
    psum x1, waiting for transfers between devices, one_sequence(): lax.psum(jnp.concatenate([sum_a, sum_b, sum_w, stats], axis=0), ('dp', 't...  101 us
    ppermute x71, starting transfers between devices, swap(): return lax.ppermute(values, axis, [(i, i ^ bit) for i in range(size)])  55 us
  transfers between devices with their start and end apart: 72, of which 25 were waited for; matrix products, arithmetic and copies ran while one was open for 4% of the time, Pallas kernels for 41%

profile of v1, /device:TPU:0, one launch (start us, length us, event | category | flops | bytes accessed | tf_op | source)
XLA Modules:
  0.0 862.5 jit_solution(839972434476689720)
XLA Ops:
  24.7 12.1 %collective-permute-done.1.p0.g0.w0 = bf16[512,1024]{1,0:T(8,128)(2,1)S(1)} collective-permute-done((bf16[512,1024]{1,0:T(8,128)(2,1)}, bf16[512,1024]{1,0:T(8,128)(2,1)S(1)}, u32[]{:S(2)}, u32[]{:S(2)}) %collective-permute-start.1) | collective-permute-done | bytes 1048608 | tf_op jit(solution)/shard_map/ppermute | solution.py:920
  38.8 23.6 %collective-permute-done = f32[65,512]{1,0:T(8,128)S(1)} collective-permute-done((f32[65,512]{1,0:T(8,128)S(1)}, f32[65,512]{1,0:T(8,128)S(1)}, u32[]{:S(2)}, u32[]{:S(2)}) %collective-permute-start) | collective-permute-done | bytes 133152 | tf_op jit(solution)/shard_map/ppermute | solution.py:920
  65.1 8.5 value_own.1
  75.6 9.2 %collective-permute-done.9.p0.w0 = bf16[256,2048]{1,0:T(8,128)(2,1)S(1)} collective-permute-done((bf16[256,2048]{1,0:T(8,128)(2,1)}, bf16[256,2048]{1,0:T(8,128)(2,1)S(1)}, u32[]{:S(2)}, u32[]{:S(2)}) %collective-permute-start.9) | collective-permute-done | bytes 1048608 | tf_op jit(solution)/shard_map/ppermute | solution.py:920
  84.8 21.7 %collective-permute-done.13.w0 = bf16[512,1024]{1,0:T(8,128)(2,1)} collective-permute-done((bf16[512,1024]{1,0:T(8,128)(2,1)}, bf16[512,1024]{1,0:T(8,128)(2,1)}, u32[]{:S(2)}, u32[]{:S(2)}) %collective-permute-start.13) | collective-permute-done | bytes 1048608 | tf_op jit(solution)/shard_map/ppermute | solution.py:920
  109.1 15.5 %ema_forward.1 = (bf16[1024,1024]{1,0:T(8,128)(2,1)}, bf16[1024,1024]{1,0:T(8,128)(2,1)}) custom-call(s32[8]{0:T(128)} %stack.35.s, bf16[1024,1024]{1,0:T(8,128)(2,1)} %get-tuple-element.64.x_ref.l_ref, f32[128,128]{1,0:T(8,128)} %reshape.176.dec_ref, f32[128,128]{1,0:T(8,128)} %reshape.177.cf_ref, f32[8,128]{1,0:T(8,128)} %bitcast.276), custom_call_target="tpu_custom_call" | custom-call | flops 20000000000 | bytes 6426624 | tf_op jit(solution)/shard_map/ema_forward/pallas_call | solution.py:340
  128.3 7.8 act_own.2
  137.1 8.1 act_other.4
  145.3 8.2 act_other.3
  153.5 13.3 %attend.1 = (bf16[1024,1024]{1,0:T(8,128)(2,1)}, bf16[1024,1024]{1,0:T(8,128)(2,1)}, bf16[1024,1024]{1,0:T(8,128)(2,1)}, bf16[1024,1024]{1,0:T(8,128)(2,1)}, bf16[1024,1024]{1,0:T(8,128)(2,1)}) custom-call(s32[8]{0:T(128)} %stack.35.s, bf16[1024,128]{1,0:T(8,128)(2,1)} %get-tuple-element.66.q_ref, bf16[1024,128]{1,0:T(8,128)(2,1)} %get-tuple-element.67.k_ref, ...), custom_call_target="tpu_custom_call" | custom-call | flops 2852126720 | bytes 23592960 | tf_op jit(solution)/shard_map/attend/pallas_call | solution.py:340
  168.5 18.9 %gate.1 = (f32[1024,1024]{1,0:T(8,128)}, bf16[1024,1024]{1,0:T(8,128)(2,1)}, bf16[1024,1024]{1,0:T(8,128)(2,1)}, bf16[1024,1024]{1,0:T(8,128)(2,1)}, bf16[1024,1024]{1,0:T(8,128)(2,1)}) custom-call(s32[8]{0:T(128)} %stack.35.s, bf16[1024,1024]{1,0:T(8,128)(2,1)} %get-tuple-element.74.go.r_ref, bf16[1024,1024]{1,0:T(8,128)(2,1)} %get-tuple-element.75.gt.r_ref, ...), custom_call_target="tpu_custom_call" | custom-call | flops 8589934592 | bytes 37748736 | tf_op jit(solution)/shard_map/gate/pallas_call | solution.py:340
  187.4 12.0 %act_own.3 = (bf16[1024,2048]{1,0:T(8,128)(2,1)}, bf16[1024,2048]{1,0:T(8,128)(2,1)}) custom-call(s32[8]{0:T(128)} %stack.35.s, bf16[1024,1024]{1,0:T(8,128)(2,1)} %get-tuple-element.76.x_ref.l_ref, bf16[1024,2048]{1,0:T(8,128)(2,1)} %wo.3), custom_call_target="tpu_custom_call" | custom-call | flops 4294967296 | bytes 14680064 | tf_op jit(solution)/shard_map/act_own/pallas_call | solution.py:340
  201.4 13.0 %act_other.5 = (bf16[1024,2048]{1,0:T(8,128)(2,1)}, bf16[1024,2048]{1,0:T(8,128)(2,1)}) custom-call(s32[8]{0:T(128)} %stack.35.s, bf16[1024,1024]{1,0:T(8,128)(2,1)} %get-tuple-element.76.x_ref.l_ref, bf16[256,2048]{1,0:T(8,128)(2,1)} %copy-done.34, bf16[256,2048]{1,0:T(8,128)(2,1)} %copy-done.35, bf16[256,2048]{1,0:T(8,128)(2,1)} %copy-done.36, ...), custom_call_target="tpu_custom_call" | custom-call | flops 4294967296 | bytes 14680064 | tf_op jit(solution)/shard_map/act_other/pallas_call | solution.py:340
  214.4 6.6 weight.56
  221.0 6.6 weight.54
  227.6 16.4 %down_own.1 = (f32[1024,1024]{1,0:T(8,128)}, bf16[1024,2048]{1,0:T(8,128)(2,1)}) custom-call(s32[8]{0:T(128)} %stack.35.s, bf16[1024,2048]{1,0:T(8,128)(2,1)} %get-tuple-element.79.h_ref.r_ref, bf16[1024,2048]{1,0:T(8,128)(2,1)} %get-tuple-element.80.us_ref, bf16[2048,1024]{1,0:T(8,128)(2,1)} %w_ref.9, bf16[1024,1024]{1,0:T(8,128)(2,1)} %l_ref.7), custom_call_target="tpu_custom_call" | custom-call | flops 8589934592 | bytes 23068672 | tf_op jit(solution)/shard_map/down_own/pallas_call | solution.py:340
  243.9 6.6 weight.50
  251.5 18.1 %down_other.1 = (bf16[1024,1024]{1,0:T(8,128)(2,1)}, bf16[1024,2048]{1,0:T(8,128)(2,1)}) custom-call(s32[8]{0:T(128)} %stack.35.s, bf16[1024,2048]{1,0:T(8,128)(2,1)} %get-tuple-element.77.h_ref.r_ref, bf16[1024,2048]{1,0:T(8,128)(2,1)} %get-tuple-element.78.us_ref, bf16[512,1024]{1,0:T(8,128)(2,1)} %collective-permute-done.13.w0, ...), custom_call_target="tpu_custom_call" | custom-call | flops 8589934592 | bytes 29360128 | tf_op jit(solution)/shard_map/down_other/pallas_call | solution.py:340
  269.6 6.6 weight.52
  276.2 19.7 %lowered_back.1 = (bf16[1024,1024]{1,0:T(8,128)(2,1)}, bf16[1024,1024]{1,0:T(8,128)(2,1)}, bf16[1024,1024]{1,0:T(8,128)(2,1)}) custom-call(s32[8]{0:T(128)} %stack.35.s, bf16[1024,2048]{1,0:T(8,128)(2,1)} %get-tuple-element.85.do.r_ref, bf16[1024,2048]{1,0:T(8,128)(2,1)} %get-tuple-element.86.dt.r_ref, bf16[1024,2048]{1,0:T(8,128)(2,1)} %wo.3, ...), custom_call_target="tpu_custom_call" | custom-call | flops 8589934592 | bytes 35651584 | tf_op jit(solution)/shard_map/lowered_back/pallas_call | solution.py:340
  314.0 14.1 %gated_back.1 = (bf16[1024,1024]{1,0:T(8,128)(2,1)}, bf16[1024,1024]{1,0:T(8,128)(2,1)}, bf16[1024,1024]{1,0:T(8,128)(2,1)}, bf16[1024,1024]{1,0:T(8,128)(2,1)}) custom-call(s32[8]{0:T(128)} %stack.35.s, bf16[1024,1024]{1,0:T(8,128)(2,1)} %get-tuple-element.90.dh_ref.l_ref, bf16[1024,1024]{1,0:T(8,128)(2,1)} %uo.3, bf16[512,1024]{1,0:T(8,128)(2,1)} %copy-done.10, ...), custom_call_target="tpu_custom_call" | custom-call | flops 4294967296 | bytes 25165824 | tf_op jit(solution)/shard_map/gated_back/pallas_call | solution.py:340
  337.7 9.6 %value_back.1 = (bf16[1024,1024]{1,0:T(8,128)(2,1)}, bf16[1024,1024]{1,0:T(8,128)(2,1)}) custom-call(s32[8]{0:T(128)} %stack.35.s, bf16[1024,1024]{1,0:T(8,128)(2,1)} %get-tuple-element.84.p_ref, bf16[1024,1024]{1,0:T(8,128)(2,1)} %get-tuple-element.93.ao, bf16[1024,1024]{1,0:T(8,128)(2,1)} %get-tuple-element.94.at, ...), custom_call_target="tpu_custom_call" | custom-call | flops 2684354560 | bytes 14680064 | tf_op jit(solution)/shard_map/value_back/pallas_call | solution.py:340
  356.9 10.3 %score_back.1 = (bf16[1024,128]{1,0:T(8,128)(2,1)}, f32[8,128]{1,0:T(8,128)}) custom-call(s32[8]{0:T(128)} %stack.35.s, bf16[1024,1024]{1,0:T(8,128)(2,1)} %get-tuple-element.84.p_ref, bf16[1024,1024]{1,0:T(8,128)(2,1)} %get-tuple-element.93.ao, bf16[1024,1024]{1,0:T(8,128)(2,1)} %get-tuple-element.94.at, bf16[1024,1024]{1,0:T(8,128)(2,1)} %get-tuple-element.68.vo, ...), custom_call_target="tpu_custom_call" | custom-call | flops 2684354560 | bytes 11801600 | tf_op jit(solution)/shard_map/score_back/pallas_call | solution.py:340
  371.4 16.8 %ema_out_back.1.g_ref = f32[1024,1024]{1,0:T(8,128)} custom-call(s32[8]{0:T(128)} %stack.35.s, bf16[1024,1024]{1,0:T(8,128)(2,1)} %get-tuple-element.99.go.r_ref, bf16[1024,1024]{1,0:T(8,128)(2,1)} %get-tuple-element.100.gt.r_ref, bf16[1024,128]{1,0:T(8,128)(2,1)} %get-tuple-element.102.dz_ref.r_ref, bf16[1024,1024]{1,0:T(8,128)(2,1)} %get-tuple-element.90.dh_ref.l_ref, ...), custom_call_target="tpu_custom_call" | custom-call | flops 8858370048 | bytes 31981568 | tf_op jit(solution)/shard_map/ema_out_back/pallas_call | solution.py:340
  388.3 34.2 %ema_backward.1 = (f32[1024,1024]{1,0:T(8,128)}, f32[128,128]{1,0:T(8,128)}, f32[128,128]{1,0:T(8,128)}, f32[8,128]{1,0:T(8,128)}) custom-call(s32[8]{0:T(128)} %stack.35.s, bf16[1024,1024]{1,0:T(8,128)(2,1)} %get-tuple-element.64.x_ref.l_ref, f32[1024,1024]{1,0:T(8,128)} %ema_out_back.1.g_ref, f32[128,128]{1,0:T(8,128)} %reshape.176.dec_ref, ...), custom_call_target="tpu_custom_call" | custom-call | flops 40000000000 | bytes 10756096 | tf_op jit(solution)/shard_map/ema_backward/pallas_call | solution.py:340
  424.1 12.3 %input_back.1 = f32[1024,1024]{1,0:T(8,128)} custom-call(s32[8]{0:T(128)} %stack.35.s, bf16[1024,1024]{1,0:T(8,128)(2,1)} %get-tuple-element.97.vo.r_ref, bf16[1024,1024]{1,0:T(8,128)(2,1)} %get-tuple-element.98.vt.r_ref, bf16[1024,1024]{1,0:T(8,128)(2,1)} %wo.5, bf16[512,1024]{1,0:T(8,128)(2,1)} %copy-done.9, ...), custom_call_target="tpu_custom_call" | custom-call | flops 4294967296 | bytes 23068672 | tf_op jit(solution)/shard_map/input_back/pallas_call | solution.py:340
  444.9 101.1 %all-reduce.2.cloned.1.call-done = f32[272,128]{1,0:T(8,128)} async-done(((f32[272,128]{1,0:T(8,128)}), f32[272,128]{1,0:T(8,128)}) %all-reduce.2.cloned.1.call-update) | async-done | bytes 139280 | tf_op jit(solution)/shard_map/psum | solution.py:1069
  549.9 6.0 collective-permute-done.18
  585.0 10.5 %collective-permute-done.45 = bf16[1024,256]{1,0:T(8,128)(2,1)S(1)} collective-permute-done((bf16[1024,256]{1,0:T(8,128)(2,1)}, bf16[1024,256]{1,0:T(8,128)(2,1)S(1)}, u32[]{:S(2)}, u32[]{:S(2)}) %collective-permute-start.45) | collective-permute-done | bytes 524320 | tf_op jit(solution)/shard_map/ppermute | solution.py:920
  596.6 5.2 weight.39
  602.8 5.1 weight.41
  608.4 5.1 weight.35
  614.1 5.3 weight.37
  620.3 5.1 weight.31
  626.8 5.3 weight.33
  662.8 7.2 weight.57
  671.6 7.2 weight.53
  678.7 5.6 collective-permute-done.31
  688.2 18.5 %collective-permute-done.24 = bf16[1024,512]{1,0:T(8,128)(2,1)} collective-permute-done((bf16[1024,512]{1,0:T(8,128)(2,1)}, bf16[1024,512]{1,0:T(8,128)(2,1)}, u32[]{:S(2)}, u32[]{:S(2)}) %collective-permute-start.24) | collective-permute-done | bytes 1048608 | tf_op jit(solution)/shard_map/ppermute | solution.py:920
  711.2 7.2 weight.55
  719.4 7.3 weight.51
  728.0 5.2 collective-permute-done.32
  734.5 7.8 collective-permute-done.25
  745.8 8.4 collective-permute-done.26
  762.3 33.7 %collective-permute-done.59 = bf16[1024,1024]{1,0:T(8,128)(2,1)S(1)} collective-permute-done((bf16[1024,1024]{1,0:T(8,128)(2,1)}, bf16[1024,1024]{1,0:T(8,128)(2,1)S(1)}, u32[]{:S(2)}, u32[]{:S(2)}) %collective-permute-start.59) | collective-permute-done | bytes 2097184 | tf_op jit(solution)/shard_map/ppermute | solution.py:920
  799.9 21.9 %collective-permute-done.60 = bf16[4,128,1024]{2,1,0:T(8,128)(2,1)S(1)} collective-permute-done((bf16[4,128,1024]{2,1,0:T(8,128)(2,1)S(1)}, bf16[4,128,1024]{2,1,0:T(8,128)(2,1)S(1)}, u32[]{:S(2)}, u32[]{:S(2)}) %collective-permute-start.60) | collective-permute-done | bytes 1048608 | tf_op jit(solution)/shard_map/ppermute | solution.py:920
  825.9 14.5 %collective-permute-done.61 = bf16[2,128,1024]{2,1,0:T(8,128)(2,1)S(1)} collective-permute-done((bf16[2,128,1024]{2,1,0:T(8,128)(2,1)S(1)}, bf16[2,128,1024]{2,1,0:T(8,128)(2,1)S(1)}, u32[]{:S(2)}, u32[]{:S(2)}) %collective-permute-start.61) | collective-permute-done | bytes 524320 | tf_op jit(solution)/shard_map/ppermute | solution.py:920
  840.9 11.9 %collective-permute-done.62 = bf16[128,1024]{1,0:T(8,128)(2,1)S(1)} collective-permute-done((bf16[128,1024]{1,0:T(8,128)(2,1)S(1)}, bf16[128,1024]{1,0:T(8,128)(2,1)S(1)}, u32[]{:S(2)}, u32[]{:S(2)}) %collective-permute-start.62) | collective-permute-done | bytes 262176 | tf_op jit(solution)/shard_map/ppermute | solution.py:920
  (335 shorter events, 191.9 us)
Async XLA Ops:
  7.2 538.8 %all-reduce.2.cloned.1.call-start = ((), (), s32[]{:S(2)}) async-start(), calls=%async_computation | async-start | bytes 278528 | tf_op jit(solution)/shard_map/psum | solution.py:1069
  9.6 27.2 %collective-permute-start.1 = (bf16[512,1024]{1,0:T(8,128)(2,1)}, bf16[512,1024]{1,0:T(8,128)(2,1)S(1)}, u32[]{:S(2)}, u32[]{:S(2)}) collective-permute-start(bf16[512,1024]{1,0:T(8,128)(2,1)} %pad_maximum_fusion), channel_id=1, source_target_pairs={{0,1},{1,0},{2,3},{3,2},{4,5},{5,4},{6,7},{7,6},{8,9},{9,8},{10,11... | collective-permute-start | bytes 3145736 | tf_op jit(solution)/shard_map/ppermute | solution.py:920
  15.8 46.6 %collective-permute-start.5 = (bf16[512,1024]{1,0:T(8,128)(2,1)}, bf16[512,1024]{1,0:T(8,128)(2,1)S(1)}, u32[]{:S(2)}, u32[]{:S(2)}) collective-permute-start(bf16[512,1024]{1,0:T(8,128)(2,1)} %pad_maximum_fusion.1), channel_id=1, source_target_pairs={{0,1},{1,0},{2,3},{3,2},{4,5},{5,4},{6,7},{7,6},{8,9},{9,8},{10,11... | collective-permute-start | bytes 3145736 | tf_op jit(solution)/shard_map/ppermute | solution.py:920
  16.0 46.4 %collective-permute-start = (f32[65,512]{1,0:T(8,128)S(1)}, f32[65,512]{1,0:T(8,128)S(1)}, u32[]{:S(2)}, u32[]{:S(2)}) collective-permute-start(f32[65,512]{1,0:T(8,128)S(1)} %dynamic-update-slice.4), channel_id=1, source_target_pairs={{0,1},{1,0},{2,3},{3,2},{4,5},{5,4},{6,7},{7,6},{8,9},{9,8},{10,11... | collective-permute-start | bytes 399368 | tf_op jit(solution)/shard_map/ppermute | solution.py:920
  20.4 64.4 %collective-permute-start.9 = (bf16[256,2048]{1,0:T(8,128)(2,1)}, bf16[256,2048]{1,0:T(8,128)(2,1)S(1)}, u32[]{:S(2)}, u32[]{:S(2)}) collective-permute-start(bf16[256,2048]{1,0:T(8,128)(2,1)} %constant_dynamic-slice_fusion.1), channel_id=1, source_target_pairs={{0,1},{1,0},{2,3},{3,2},{4,5},{5,4},{6,7},{7,6},{8,9},{9,8},{10,11... | collective-permute-start | bytes 3145736 | tf_op jit(solution)/shard_map/ppermute | solution.py:920
  22.7 83.9 %collective-permute-start.13 = (bf16[512,1024]{1,0:T(8,128)(2,1)}, bf16[512,1024]{1,0:T(8,128)(2,1)}, u32[]{:S(2)}, u32[]{:S(2)}) collective-permute-start(bf16[512,1024]{1,0:T(8,128)(2,1)} %constant_dynamic-slice_fusion), channel_id=1, source_target_pairs={{0,1},{1,0},{2,3},{3,2},{4,5},{5,4},{6,7},{7,6},{8,9},{9,8},{10,11... | collective-permute-start | bytes 3145736 | tf_op jit(solution)/shard_map/ppermute | solution.py:920
  36.7 71.6 %collective-permute-start.2 = (bf16[512,1024]{1,0:T(8,128)(2,1)S(1)}, bf16[512,1024]{1,0:T(8,128)(2,1)}, u32[]{:S(2)}, u32[]{:S(2)}) collective-permute-start(bf16[512,1024]{1,0:T(8,128)(2,1)S(1)} %collective-permute-done.1.p0.g0.w0), channel_id=1, source_target_pairs={{0,4},{2,6},{4,0},{6,2},{8,12},{10,14},{12,8},{14,10},{16,20},{18,... | collective-permute-start | bytes 3145736 | tf_op jit(solution)/shard_map/ppermute | solution.py:920
  62.4 46.3 %collective-permute-start.3 = (bf16[512,1024]{1,0:T(8,128)(2,1)S(1)}, bf16[512,1024]{1,0:T(8,128)(2,1)}, u32[]{:S(2)}, u32[]{:S(2)}) collective-permute-start(bf16[512,1024]{1,0:T(8,128)(2,1)S(1)} %collective-permute-done.1.p0.g0.w0), channel_id=1, source_target_pairs={{0,2},{2,0},{4,6},{6,4},{8,10},{10,8},{12,14},{14,12},{16,18},{18,... | collective-permute-start | bytes 3145736 | tf_op jit(solution)/shard_map/ppermute | solution.py:920
  62.4 46.2 %collective-permute-start.6 = (bf16[512,1024]{1,0:T(8,128)(2,1)S(1)}, bf16[512,1024]{1,0:T(8,128)(2,1)}, u32[]{:S(2)}, u32[]{:S(2)}) collective-permute-start(bf16[512,1024]{1,0:T(8,128)(2,1)S(1)} %collective-permute-done.5.u0.h0.f0), channel_id=1, source_target_pairs={{0,4},{2,6},{4,0},{6,2},{8,12},{10,14},{12,8},{14,10},{16,20},{18,... | collective-permute-start | bytes 3145736 | tf_op jit(solution)/shard_map/ppermute | solution.py:920
  84.8 81.9 %collective-permute-start.7 = (bf16[512,1024]{1,0:T(8,128)(2,1)S(1)}, bf16[512,1024]{1,0:T(8,128)(2,1)S(1)}, u32[]{:S(2)}, u32[]{:S(2)}) collective-permute-start(bf16[512,1024]{1,0:T(8,128)(2,1)S(1)} %collective-permute-done.5.u0.h0.f0), channel_id=1, source_target_pairs={{0,2},{2,0},{4,6},{6,4},{8,10},{10,8},{12,14},{14,12},{16,18},{18,... | collective-permute-start | bytes 3145736 | tf_op jit(solution)/shard_map/ppermute | solution.py:920
  106.6 60.3 %collective-permute-start.10 = (bf16[256,2048]{1,0:T(8,128)(2,1)S(1)}, bf16[256,2048]{1,0:T(8,128)(2,1)S(1)}, u32[]{:S(2)}, u32[]{:S(2)}) collective-permute-start(bf16[256,2048]{1,0:T(8,128)(2,1)S(1)} %collective-permute-done.9.p0.w0), channel_id=1, source_target_pairs={{0,4},{2,6},{4,0},{6,2},{8,12},{10,14},{12,8},{14,10},{16,20},{18,... | collective-permute-start | bytes 3145736 | tf_op jit(solution)/shard_map/ppermute | solution.py:920
  108.3 59.1 %collective-permute-start.14 = (bf16[512,1024]{1,0:T(8,128)(2,1)}, bf16[512,1024]{1,0:T(8,128)(2,1)}, u32[]{:S(2)}, u32[]{:S(2)}) collective-permute-start(bf16[512,1024]{1,0:T(8,128)(2,1)} %collective-permute-done.13.w0), channel_id=1, source_target_pairs={{0,4},{2,6},{4,0},{6,2},{8,12},{10,14},{12,8},{14,10},{16,20},{18,... | collective-permute-start | bytes 3145736 | tf_op jit(solution)/shard_map/ppermute | solution.py:920
  108.6 27.5 %collective-permute-start.4 = (bf16[512,1024]{1,0:T(8,128)(2,1)}, bf16[512,1024]{1,0:T(8,128)(2,1)S(1)}, u32[]{:S(2)}, u32[]{:S(2)}) collective-permute-start(bf16[512,1024]{1,0:T(8,128)(2,1)} %collective-permute-done.2.p1.g1.w1), channel_id=1, source_target_pairs={{0,2},{2,0},{4,6},{6,4},{8,10},{10,8},{12,14},{14,12},{16,18},{18,... | collective-permute-start | bytes 3145736 | tf_op jit(solution)/shard_map/ppermute | solution.py:920
  108.6 58.8 %collective-permute-start.8 = (bf16[512,1024]{1,0:T(8,128)(2,1)}, bf16[512,1024]{1,0:T(8,128)(2,1)S(1)}, u32[]{:S(2)}, u32[]{:S(2)}) collective-permute-start(bf16[512,1024]{1,0:T(8,128)(2,1)} %collective-permute-done.6.u1.h1.f1), channel_id=1, source_target_pairs={{0,2},{2,0},{4,6},{6,4},{8,10},{10,8},{12,14},{14,12},{16,18},{18,... | collective-permute-start | bytes 3145736 | tf_op jit(solution)/shard_map/ppermute | solution.py:920
  136.1 63.2 %collective-permute-start.11 = (bf16[256,2048]{1,0:T(8,128)(2,1)S(1)}, bf16[256,2048]{1,0:T(8,128)(2,1)S(1)}, u32[]{:S(2)}, u32[]{:S(2)}) collective-permute-start(bf16[256,2048]{1,0:T(8,128)(2,1)S(1)} %collective-permute-done.9.p0.w0), channel_id=1, source_target_pairs={{0,2},{2,0},{4,6},{6,4},{8,10},{10,8},{12,14},{14,12},{16,18},{18,... | collective-permute-start | bytes 3145736 | tf_op jit(solution)/shard_map/ppermute | solution.py:920
  166.8 83.7 %collective-permute-start.15 = (bf16[512,1024]{1,0:T(8,128)(2,1)}, bf16[512,1024]{1,0:T(8,128)(2,1)S(1)}, u32[]{:S(2)}, u32[]{:S(2)}) collective-permute-start(bf16[512,1024]{1,0:T(8,128)(2,1)} %collective-permute-done.13.w0), channel_id=1, source_target_pairs={{0,2},{2,0},{4,6},{6,4},{8,10},{10,8},{12,14},{14,12},{16,18},{18,... | collective-permute-start | bytes 3145736 | tf_op jit(solution)/shard_map/ppermute | solution.py:920
  166.9 32.5 %collective-permute-start.12 = (bf16[256,2048]{1,0:T(8,128)(2,1)S(1)}, bf16[256,2048]{1,0:T(8,128)(2,1)S(1)}, u32[]{:S(2)}, u32[]{:S(2)}) collective-permute-start(bf16[256,2048]{1,0:T(8,128)(2,1)S(1)} %collective-permute-done.10.p1.w1), channel_id=1, source_target_pairs={{0,2},{2,0},{4,6},{6,4},{8,10},{10,8},{12,14},{14,12},{16,18},{18,... | collective-permute-start | bytes 3145736 | tf_op jit(solution)/shard_map/ppermute | solution.py:920
  167.4 83.1 %collective-permute-start.16 = (bf16[512,1024]{1,0:T(8,128)(2,1)}, bf16[512,1024]{1,0:T(8,128)(2,1)}, u32[]{:S(2)}, u32[]{:S(2)}) collective-permute-start(bf16[512,1024]{1,0:T(8,128)(2,1)} %collective-permute-done.14.w1), channel_id=1, source_target_pairs={{0,2},{2,0},{4,6},{6,4},{8,10},{10,8},{12,14},{14,12},{16,18},{18,... | collective-permute-start | bytes 3145736 | tf_op jit(solution)/shard_map/ppermute | solution.py:920
  313.5 245.7 %collective-permute-start.50 = (bf16[1024,256]{1,0:T(8,128)(2,1)}, bf16[1024,256]{1,0:T(8,128)(2,1)S(1)}, u32[]{:S(2)}, u32[]{:S(2)}) collective-permute-start(bf16[1024,256]{1,0:T(8,128)(2,1)} %weight.46), channel_id=1, source_target_pairs={{0,2},{2,0},{4,6},{6,4},{8,10},{10,8},{12,14},{14,12},{16,18},{18,... | collective-permute-start | bytes 1572872 | tf_op jit(solution)/shard_map/ppermute | solution.py:920
  313.9 256.1 %collective-permute-start.44 = (bf16[1024,256]{1,0:T(8,128)(2,1)S(1)}, bf16[1024,256]{1,0:T(8,128)(2,1)S(1)}, u32[]{:S(2)}, u32[]{:S(2)}) collective-permute-start(bf16[1024,256]{1,0:T(8,128)(2,1)S(1)} %copy-done.20), channel_id=1, source_target_pairs={{0,2},{2,0},{4,6},{6,4},{8,10},{10,8},{12,14},{14,12},{16,18},{18,... | collective-permute-start | bytes 1572872 | tf_op jit(solution)/shard_map/ppermute | solution.py:920
  371.0 175.8 %collective-permute-start.17 = (bf16[1024,128]{1,0:T(8,128)(2,1)}, bf16[1024,128]{1,0:T(8,128)(2,1)S(1)}, u32[]{:S(2)}, u32[]{:S(2)}) collective-permute-start(bf16[1024,128]{1,0:T(8,128)(2,1)} %weight.29), channel_id=1, source_target_pairs={{0,2},{2,0},{4,6},{6,4},{8,10},{10,8},{12,14},{14,12},{16,18},{18,... | collective-permute-start | bytes 786440 | tf_op jit(solution)/shard_map/ppermute | solution.py:920
  440.4 123.8 %collective-permute-start.51 = (bf16[1024,256]{1,0:T(8,128)(2,1)}, bf16[1024,256]{1,0:T(8,128)(2,1)}, u32[]{:S(2)}, u32[]{:S(2)}) collective-permute-start(bf16[1024,256]{1,0:T(8,128)(2,1)} %weight.48), channel_id=1, source_target_pairs={{0,2},{2,0},{4,6},{6,4},{8,10},{10,8},{12,14},{14,12},{16,18},{18,... | collective-permute-start | bytes 1572872 | tf_op jit(solution)/shard_map/ppermute | solution.py:920
  444.5 132.0 %collective-permute-start.43 = (bf16[1024,256]{1,0:T(8,128)(2,1)}, bf16[1024,256]{1,0:T(8,128)(2,1)S(1)}, u32[]{:S(2)}, u32[]{:S(2)}) collective-permute-start(bf16[1024,256]{1,0:T(8,128)(2,1)} %weight.42), channel_id=1, source_target_pairs={{0,2},{2,0},{4,6},{6,4},{8,10},{10,8},{12,14},{14,12},{16,18},{18,... | collective-permute-start | bytes 1572872 | tf_op jit(solution)/shard_map/ppermute | solution.py:920
  559.2 36.4 %collective-permute-start.36 = (bf16[1024,512]{1,0:T(8,128)(2,1)}, bf16[1024,512]{1,0:T(8,128)(2,1)S(1)}, u32[]{:S(2)}, u32[]{:S(2)}) collective-permute-start(bf16[1024,512]{1,0:T(8,128)(2,1)} %weight.38), channel_id=1, source_target_pairs={{0,2},{2,0},{4,6},{6,4},{8,10},{10,8},{12,14},{14,12},{16,18},{18,... | collective-permute-start | bytes 3145736 | tf_op jit(solution)/shard_map/ppermute | solution.py:920
  564.1 37.7 %collective-permute-start.37 = (bf16[1024,512]{1,0:T(8,128)(2,1)}, bf16[1024,512]{1,0:T(8,128)(2,1)S(1)}, u32[]{:S(2)}, u32[]{:S(2)}) collective-permute-start(bf16[1024,512]{1,0:T(8,128)(2,1)} %weight.40), channel_id=1, source_target_pairs={{0,2},{2,0},{4,6},{6,4},{8,10},{10,8},{12,14},{14,12},{16,18},{18,... | collective-permute-start | bytes 3145736 | tf_op jit(solution)/shard_map/ppermute | solution.py:920
  575.6 20.0 %collective-permute-start.45 = (bf16[1024,256]{1,0:T(8,128)(2,1)}, bf16[1024,256]{1,0:T(8,128)(2,1)S(1)}, u32[]{:S(2)}, u32[]{:S(2)}) collective-permute-start(bf16[1024,256]{1,0:T(8,128)(2,1)} %weight.45), channel_id=1, source_target_pairs={{0,1},{1,0},{2,3},{3,2},{4,5},{5,4},{6,7},{7,6},{8,9},{9,8},{10,11... | collective-permute-start | bytes 1572872 | tf_op jit(solution)/shard_map/ppermute | solution.py:920
  582.7 25.2 %collective-permute-start.29 = (bf16[1024,512]{1,0:T(8,128)(2,1)}, bf16[1024,512]{1,0:T(8,128)(2,1)}, u32[]{:S(2)}, u32[]{:S(2)}) collective-permute-start(bf16[1024,512]{1,0:T(8,128)(2,1)} %weight.34), channel_id=1, source_target_pairs={{0,2},{2,0},{4,6},{6,4},{8,10},{10,8},{12,14},{14,12},{16,18},{18,... | collective-permute-start | bytes 3145736 | tf_op jit(solution)/shard_map/ppermute | solution.py:920
  585.0 28.5 %collective-permute-start.30 = (bf16[1024,512]{1,0:T(8,128)(2,1)}, bf16[1024,512]{1,0:T(8,128)(2,1)}, u32[]{:S(2)}, u32[]{:S(2)}) collective-permute-start(bf16[1024,512]{1,0:T(8,128)(2,1)} %weight.36), channel_id=1, source_target_pairs={{0,2},{2,0},{4,6},{6,4},{8,10},{10,8},{12,14},{14,12},{16,18},{18,... | collective-permute-start | bytes 3145736 | tf_op jit(solution)/shard_map/ppermute | solution.py:920
  595.6 23.8 %collective-permute-start.22 = (bf16[1024,512]{1,0:T(8,128)(2,1)}, bf16[1024,512]{1,0:T(8,128)(2,1)S(1)}, u32[]{:S(2)}, u32[]{:S(2)}) collective-permute-start(bf16[1024,512]{1,0:T(8,128)(2,1)} %weight.30), channel_id=1, source_target_pairs={{0,2},{2,0},{4,6},{6,4},{8,10},{10,8},{12,14},{14,12},{16,18},{18,... | collective-permute-start | bytes 3145736 | tf_op jit(solution)/shard_map/ppermute | solution.py:920
  595.6 29.8 %collective-permute-start.23 = (bf16[1024,512]{1,0:T(8,128)(2,1)}, bf16[1024,512]{1,0:T(8,128)(2,1)}, u32[]{:S(2)}, u32[]{:S(2)}) collective-permute-start(bf16[1024,512]{1,0:T(8,128)(2,1)} %weight.32), channel_id=1, source_target_pairs={{0,2},{2,0},{4,6},{6,4},{8,10},{10,8},{12,14},{14,12},{16,18},{18,... | collective-permute-start | bytes 3145736 | tf_op jit(solution)/shard_map/ppermute | solution.py:920
  601.8 56.3 %collective-permute-start.65 = (bf16[1024,1024]{1,0:T(8,128)(2,1)S(1)}, bf16[1024,1024]{1,0:T(8,128)(2,1)}, u32[]{:S(2)}, u32[]{:S(2)}) collective-permute-start(bf16[1024,1024]{1,0:T(8,128)(2,1)S(1)} %copy-done.6), channel_id=1, source_target_pairs={{0,2},{2,0},{4,6},{6,4},{8,10},{10,8},{12,14},{14,12},{16,18},{18,... | collective-permute-start | bytes 6291464 | tf_op jit(solution)/shard_map/ppermute | solution.py:920
  607.9 102.2 %collective-permute-start.64 = (bf16[1024,1024]{1,0:T(8,128)(2,1)}, bf16[1024,1024]{1,0:T(8,128)(2,1)}, u32[]{:S(2)}, u32[]{:S(2)}) collective-permute-start(bf16[1024,1024]{1,0:T(8,128)(2,1)} %weight.54), channel_id=1, source_target_pairs={{0,2},{2,0},{4,6},{6,4},{8,10},{10,8},{12,14},{14,12},{16,18},{18,... | collective-permute-start | bytes 6291464 | tf_op jit(solution)/shard_map/ppermute | solution.py:920
  619.4 50.6 %collective-permute-start.58 = (bf16[1024,1024]{1,0:T(8,128)(2,1)S(1)}, bf16[1024,1024]{1,0:T(8,128)(2,1)}, u32[]{:S(2)}, u32[]{:S(2)}) collective-permute-start(bf16[1024,1024]{1,0:T(8,128)(2,1)S(1)} %copy-done.5), channel_id=1, source_target_pairs={{0,2},{2,0},{4,6},{6,4},{8,10},{10,8},{12,14},{14,12},{16,18},{18,... | collective-permute-start | bytes 6291464 | tf_op jit(solution)/shard_map/ppermute | solution.py:920
  632.1 29.1 %collective-permute-start.38 = (bf16[1024,512]{1,0:T(8,128)(2,1)S(1)}, bf16[1024,512]{1,0:T(8,128)(2,1)S(1)}, u32[]{:S(2)}, u32[]{:S(2)}) collective-permute-start(bf16[1024,512]{1,0:T(8,128)(2,1)S(1)} %copy-done.15), channel_id=1, source_target_pairs={{0,1},{1,0},{2,3},{3,2},{4,5},{5,4},{6,7},{7,6},{8,9},{9,8},{10,11... | collective-permute-start | bytes 3145736 | tf_op jit(solution)/shard_map/ppermute | solution.py:920
  658.0 60.4 %collective-permute-start.57 = (bf16[1024,1024]{1,0:T(8,128)(2,1)}, bf16[1024,1024]{1,0:T(8,128)(2,1)}, u32[]{:S(2)}, u32[]{:S(2)}) collective-permute-start(bf16[1024,1024]{1,0:T(8,128)(2,1)} %weight.50), channel_id=1, source_target_pairs={{0,2},{2,0},{4,6},{6,4},{8,10},{10,8},{12,14},{14,12},{16,18},{18,... | collective-permute-start | bytes 6291464 | tf_op jit(solution)/shard_map/ppermute | solution.py:920
  658.2 26.1 %collective-permute-start.31 = (bf16[1024,512]{1,0:T(8,128)(2,1)S(1)}, bf16[1024,512]{1,0:T(8,128)(2,1)}, u32[]{:S(2)}, u32[]{:S(2)}) collective-permute-start(bf16[1024,512]{1,0:T(8,128)(2,1)S(1)} %copy-done.14), channel_id=1, source_target_pairs={{0,1},{1,0},{2,3},{3,2},{4,5},{5,4},{6,7},{7,6},{8,9},{9,8},{10,11... | collective-permute-start | bytes 3145736 | tf_op jit(solution)/shard_map/ppermute | solution.py:920
  661.1 45.6 %collective-permute-start.24 = (bf16[1024,512]{1,0:T(8,128)(2,1)}, bf16[1024,512]{1,0:T(8,128)(2,1)}, u32[]{:S(2)}, u32[]{:S(2)}) collective-permute-start(bf16[1024,512]{1,0:T(8,128)(2,1)} %weight.33), channel_id=1, source_target_pairs={{0,1},{1,0},{2,3},{3,2},{4,5},{5,4},{6,7},{7,6},{8,9},{9,8},{10,11... | collective-permute-start | bytes 3145736 | tf_op jit(solution)/shard_map/ppermute | solution.py:920
  670.0 87.5 %collective-permute-start.66 = (bf16[1024,1024]{1,0:T(8,128)(2,1)}, bf16[1024,1024]{1,0:T(8,128)(2,1)S(1)}, u32[]{:S(2)}, u32[]{:S(2)}) collective-permute-start(bf16[1024,1024]{1,0:T(8,128)(2,1)} %weight.57), channel_id=1, source_target_pairs={{0,1},{1,0},{2,3},{3,2},{4,5},{5,4},{6,7},{7,6},{8,9},{9,8},{10,11... | collective-permute-start | bytes 6291464 | tf_op jit(solution)/shard_map/ppermute | solution.py:920
  684.3 111.7 %collective-permute-start.59 = (bf16[1024,1024]{1,0:T(8,128)(2,1)}, bf16[1024,1024]{1,0:T(8,128)(2,1)S(1)}, u32[]{:S(2)}, u32[]{:S(2)}) collective-permute-start(bf16[1024,1024]{1,0:T(8,128)(2,1)} %weight.53), channel_id=1, source_target_pairs={{0,1},{1,0},{2,3},{3,2},{4,5},{5,4},{6,7},{7,6},{8,9},{9,8},{10,11... | collective-permute-start | bytes 6291464 | tf_op jit(solution)/shard_map/ppermute | solution.py:920
  710.1 23.1 %collective-permute-start.32 = (bf16[4,128,512]{2,1,0:T(8,128)(2,1)}, bf16[4,128,512]{2,1,0:T(8,128)(2,1)}, u32[]{:S(2)}, u32[]{:S(2)}) collective-permute-start(bf16[4,128,512]{2,1,0:T(8,128)(2,1)} %dynamic-slice_bitcast_fusion.5), channel_id=1, source_target_pairs={{0,4},{2,6},{4,0},{6,2},{8,12},{10,14},{12,8},{14,10},{16,20},{18,... | collective-permute-start | bytes 1572872 | tf_op jit(solution)/shard_map/ppermute | solution.py:920
  718.4 23.8 %collective-permute-start.25 = (bf16[4,128,512]{2,1,0:T(8,128)(2,1)}, bf16[4,128,512]{2,1,0:T(8,128)(2,1)S(1)}, u32[]{:S(2)}, u32[]{:S(2)}) collective-permute-start(bf16[4,128,512]{2,1,0:T(8,128)(2,1)} %dynamic-slice_bitcast_fusion.6), channel_id=1, source_target_pairs={{0,4},{2,6},{4,0},{6,2},{8,12},{10,14},{12,8},{14,10},{16,20},{18,... | collective-permute-start | bytes 1572872 | tf_op jit(solution)/shard_map/ppermute | solution.py:920
  754.4 43.9 %collective-permute-start.27 = (bf16[128,512]{1,0:T(8,128)(2,1)S(1)}, bf16[128,512]{1,0:T(8,128)(2,1)S(1)}, u32[]{:S(2)}, u32[]{:S(2)}) collective-permute-start(bf16[128,512]{1,0:T(8,128)(2,1)S(1)} %dynamic-slice_bitcast_fusion.23), channel_id=1, source_target_pairs={{0,16},{2,18},{4,20},{6,22},{8,24},{10,26},{12,28},{14,30},{16,0},... | collective-permute-start | bytes 393224 | tf_op jit(solution)/shard_map/ppermute | solution.py:920
  754.5 44.0 %collective-permute-start.42 = (bf16[64,512]{1,0:T(8,128)(2,1)S(1)}, bf16[64,512]{1,0:T(8,128)(2,1)S(1)}, u32[]{:S(2)}, u32[]{:S(2)}) collective-permute-start(bf16[64,512]{1,0:T(8,128)(2,1)S(1)} %fusion.24), channel_id=1, source_target_pairs={{0,2},{2,0},{4,6},{6,4},{8,10},{10,8},{12,14},{14,12},{16,18},{18,... | collective-permute-start | bytes 196616 | tf_op jit(solution)/shard_map/ppermute | solution.py:920
  757.4 41.2 %collective-permute-start.35 = (bf16[64,512]{1,0:T(8,128)(2,1)S(1)}, bf16[64,512]{1,0:T(8,128)(2,1)S(1)}, u32[]{:S(2)}, u32[]{:S(2)}) collective-permute-start(bf16[64,512]{1,0:T(8,128)(2,1)S(1)} %fusion.23), channel_id=1, source_target_pairs={{0,2},{2,0},{4,6},{6,4},{8,10},{10,8},{12,14},{14,12},{16,18},{18,... | collective-permute-start | bytes 196616 | tf_op jit(solution)/shard_map/ppermute | solution.py:920
  758.8 40.5 %collective-permute-start.67 = (bf16[4,128,1024]{2,1,0:T(8,128)(2,1)S(1)}, bf16[4,128,1024]{2,1,0:T(8,128)(2,1)S(1)}, u32[]{:S(2)}, u32[]{:S(2)}) collective-permute-start(bf16[4,128,1024]{2,1,0:T(8,128)(2,1)S(1)} %dynamic-slice_bitcast_fusion), channel_id=1, source_target_pairs={{0,4},{2,6},{4,0},{6,2},{8,12},{10,14},{12,8},{14,10},{16,20},{18,... | collective-permute-start | bytes 3145736 | tf_op jit(solution)/shard_map/ppermute | solution.py:920
  797.1 24.7 %collective-permute-start.60 = (bf16[4,128,1024]{2,1,0:T(8,128)(2,1)S(1)}, bf16[4,128,1024]{2,1,0:T(8,128)(2,1)S(1)}, u32[]{:S(2)}, u32[]{:S(2)}) collective-permute-start(bf16[4,128,1024]{2,1,0:T(8,128)(2,1)S(1)} %dynamic-slice_bitcast_fusion.1), channel_id=1, source_target_pairs={{0,4},{2,6},{4,0},{6,2},{8,12},{10,14},{12,8},{14,10},{16,20},{18,... | collective-permute-start | bytes 3145736 | tf_op jit(solution)/shard_map/ppermute | solution.py:920
  798.4 24.6 %collective-permute-start.28 = (bf16[64,512]{1,0:T(8,128)(2,1)S(1)}, bf16[64,512]{1,0:T(8,128)(2,1)S(1)}, u32[]{:S(2)}, u32[]{:S(2)}) collective-permute-start(bf16[64,512]{1,0:T(8,128)(2,1)S(1)} %fusion.22), channel_id=1, source_target_pairs={{0,2},{2,0},{4,6},{6,4},{8,10},{10,8},{12,14},{14,12},{16,18},{18,... | collective-permute-start | bytes 196616 | tf_op jit(solution)/shard_map/ppermute | solution.py:920
  799.8 24.0 %collective-permute-start.68 = (bf16[2,128,1024]{2,1,0:T(8,128)(2,1)S(1)}, bf16[2,128,1024]{2,1,0:T(8,128)(2,1)S(1)}, u32[]{:S(2)}, u32[]{:S(2)}) collective-permute-start(bf16[2,128,1024]{2,1,0:T(8,128)(2,1)S(1)} %dynamic-slice_bitcast_fusion.2), channel_id=1, source_target_pairs={{0,8},{2,10},{4,12},{6,14},{8,0},{10,2},{12,4},{14,6},{16,24},{18,... | collective-permute-start | bytes 1572872 | tf_op jit(solution)/shard_map/ppermute | solution.py:920
  (63 other events, 1186.4 us)
Sparse Core Ops, SparseCore 0:
  424.2 121.7 all-reduce.1

commit v2 on v1

--- a/solution.py
+++ b/solution.py
@@ -506,7 +506,7 @@
     )
 
 
-def k_ema_backward(scal, normed, d_e, decay, coef, omega):
+def k_ema_backward(scal, normed, de_part, dz, slope, w_z, decay, coef, omega):
     n, d = normed.shape
     groups = d // 128
     tb = 128
@@ -514,7 +514,9 @@
     half = H // 2
     gh = groups * half
 
-    def body(s, x_ref, g_ref, dec_ref, cf_ref, om_ref, o_ref, a_ref, b_ref, w_ref, back, deriv, xs, gs, ys):
+    zw = dz.shape[1]
+
+    def body(s, x_ref, de_ref, z_ref, sl_ref, wz_ref, dec_ref, cf_ref, om_ref, o_ref, a_ref, b_ref, w_ref, back, deriv, xs, gs, ys):
         @pl.when(pl.program_id(0) == 0)
         def _():
             back[...] = jnp.zeros_like(back)
@@ -523,9 +525,10 @@
             b_ref[...] = jnp.zeros_like(b_ref)
             w_ref[...] = jnp.zeros_like(w_ref)
 
+        d_e = (de_ref[...] + col_inner(z_ref[...], wz_ref[...])) * sl_ref[...].astype(F32)
         for g in range(groups):
             xs[pl.ds(g, tb, stride=groups), :] = x_ref[:, g * 128 : (g + 1) * 128].astype(F32)
-            gs[pl.ds(g, tb, stride=groups), :] = g_ref[:, g * 128 : (g + 1) * 128]
+            gs[pl.ds(g, tb, stride=groups), :] = d_e[:, g * 128 : (g + 1) * 128]
 
         for part in range(2):
             first = part * gh
@@ -574,8 +577,8 @@
     par = (H * groups, 128)
     const = pl.BlockSpec(par, lambda i, s: (0, 0))
     return run(
-        body, (nb,), scal, [normed, d_e, decay, coef, omega],
-        [back_rows, back_rows, whole(par), whole(par), whole((groups, 128))],
+        body, (nb,), scal, [normed, de_part, dz, slope, w_z, decay, coef, omega],
+        [back_rows, back_rows, pl.BlockSpec((tb, zw), lambda i, s: (nb - 1 - i, 0)), back_rows, whole((d, zw)), whole(par), whole(par), whole((groups, 128))],
         [sds((n, d), F32), sds(par, F32), sds(par, F32), sds((groups, 128), F32)],
         [back_rows, const, const, pl.BlockSpec((groups, 128), lambda i, s: (0, 0))],
         [pltpu.VMEM(par, F32), pltpu.VMEM(par, F32)] + [pltpu.VMEM((tb * groups, 128), F32)] * 3,
@@ -658,117 +661,139 @@
     )
 
 
-def k_down_own(scal, hid, us, w_own, cot):
-    n, cols = hid.shape
-    d = w_own.shape[1]
-    tn = 512
-
-    def body(s, h_ref, us_ref, w_ref, c_ref, acc_ref, du_ref):
-        part = matmul(h_ref[...], w_ref[...])
-
+def k_ffn(scal, lowered, cot, up, down, acc, grad, pieces):
+    n, d = lowered.shape
+    cols = up[0].shape[1]
+    tn = cols // 4
+    last = grad is not None
+    first_in = [acc, grad] if last else [acc]
+
+    def body(s, low_ref, c_ref, *refs):
+        step = pl.program_id(0)
+        nu = 4 if pieces else 1
+        ups, downs, refs = refs[:nu], refs[nu : 2 * nu], refs[2 * nu :]
+        ins, refs = refs[: len(first_in)], refs[len(first_in) :]
+        if last:
+            out_ref, gl_ref, sent_ref, kept_ref, acc_ref, u_scr = refs
+        else:
+            acc_ref, gl_ref, sent_ref, kept_ref, u_scr = refs
+
+        @pl.when(step == 0)
+        def _():
+            acc_ref[...] = ins[0][...]
+            gl_ref[...] = ins[1][...] if last else jnp.zeros_like(gl_ref)
+
+        if pieces:
+            place(u_scr, s, ups)
+            wu = u_scr
+        else:
+            wu = ups[0]
+
+        def work(wd, grads):
+            act, slope = silu_pair(matmul(low_ref[...], wu[...]))
+            hid = act.astype(BF)
+            acc_ref[...] += matmul(hid, wd[...])
+            du = (col_inner(c_ref[...], wd[...]) * slope).astype(BF)
+            gl_ref[...] += col_inner(du, wu[...])
+            grads[0] = row_inner(c_ref[...], hid).astype(BF)
+            grads[1] = row_inner(low_ref[...], du).astype(BF)
+
+        if pieces:
+            for i, p in enumerate((2, 3, 0, 1)):
+
+                @pl.when(step == i)
+                def _(i=i, p=p):
+                    work(downs[p], sent_ref if i < 2 else kept_ref)
+        else:
+
+            @pl.when(step < 2)
+            def _():
+                work(downs[0], sent_ref)
+
+            @pl.when(step >= 2)
+            def _():
+                work(downs[0], kept_ref)
+
+        if last:
+
+            @pl.when(step == 3)
+            def _():
+                out_ref[...] = acc_ref[...].astype(BF)
+
+    if pieces:
+        specs = [pl.BlockSpec((d // 4, tn), lambda i, s: (0, s[(i + 2) % 4]))] * 4 + [whole((tn, d))] * 4
+    else:
+        specs = [
+            pl.BlockSpec((d, tn), lambda i, s: (0, s[(i + 2) % 4])),
+            pl.BlockSpec((tn, d), lambda i, s: (s[(i + 2) % 4], 0)),
+        ]
+    still = pl.BlockSpec((n, d), lambda i, s: (0, 0))
+    pair = (2, d, tn)
+    sent = pl.BlockSpec(pair, lambda i, s: (0, 0, s[2 + jnp.minimum(i, 1)] % 2))
+    kept = pl.BlockSpec(pair, lambda i, s: (0, 0, s[jnp.maximum(i - 2, 0)] % 2))
+    return run(
+        body, (4,), scal, [lowered, cot, *up, *down, *first_in],
+        [whole((n, d)), whole((n, d))] + specs + [whole((n, d))] * len(first_in),
+        [sds((n, d), BF if last else F32), sds((n, d), F32), sds((2, d, cols // 2)), sds((2, d, cols // 2))],
+        [still, still, sent, kept],
+        ([pltpu.VMEM((n, d), F32)] if last else []) + [pltpu.VMEM((d, tn), BF)],
+        flops=12 * n * d * cols, name="ffn_other" if last else "ffn_own",
+    )
+
+
+def k_mid_back(scal, dl, cot, mixed, fac_h, fac_f, keep, g_own, g_oth, m_own, m_oth,
+               u_own, wg_own, h_own, f_own, packs_g, packs_h, rows):
+    n, d = cot.shape
+    half = u_own.shape[0]
+    ch = h_own.shape[0]
+    ru, rh = rows
+    rg = packs_g[0].shape[0]
+
+    def body(s, dl_ref, c_ref, x_ref, a_ref, b_ref, k_ref, go, gt, mo, mt, uo, wo, ho, fo,
+             w0, w1, w2, w3, u0, u1, u2, u3, h0, h1, h2, h3, f0, f1, f2, f3,
+             dh_ref, df_ref, dir_ref, ao, at, do, dt, de_ref, u_scr, w_scr, h_scr, f_scr):
         @pl.when(pl.program_id(0) == 0)
         def _():
-            acc_ref[...] = part
-
-        @pl.when(pl.program_id(0) > 0)
-        def _():
-            acc_ref[...] += part
-
-        du_ref[...] = (col_inner(c_ref[...], w_ref[...]) * us_ref[...].astype(F32)).astype(BF)
-
-    return run(
-        body, (cols // tn,), scal, [hid, us, w_own, cot],
-        [cols_of(n, tn), cols_of(n, tn), rows_of(d, tn), whole((n, d))],
-        [sds((n, d), F32), sds((n, cols))],
-        [pl.BlockSpec((n, d), lambda i, s: (0, 0)), cols_of(n, tn)],
-        flops=4 * n * d * cols, name="down_own",
-    )
-
-
-def k_down_other(scal, hid, us, packs, cot, acc, mixed):
-    n, cols = hid.shape
-    rp, d = packs[0].shape
-
-    def body(s, h_ref, us_ref, w0, w1, w2, w3, c_ref, in_ref, m_ref, out_ref, du_ref, acc_ref):
-        for p, w_ref in enumerate((w0, w1, w2, w3)):
-
-            @pl.when(pl.program_id(0) == p)
-            def _(p=p, w_ref=w_ref):
-                part = matmul(h_ref[...], w_ref[...])
-                if p == 0:
-                    acc_ref[...] = part + in_ref[...]
-                elif p < 3:
-                    acc_ref[...] += part
-                else:
-                    out_ref[...] = (m_ref[...] + (acc_ref[...] + part)).astype(BF)
-                du_ref[...] = (col_inner(c_ref[...], w_ref[...]) * us_ref[...].astype(F32)).astype(BF)
-
-    at = pl.BlockSpec((n, rp), lambda i, s: (0, s[i]))
-    return run(
-        body, (4,), scal, [hid, us, *packs, cot, acc, mixed],
-        [at, at] + [whole((rp, d))] * 4 + [whole((n, d))] * 3,
-        [sds((n, d)), sds((n, cols))],
-        [pl.BlockSpec((n, d), lambda i, s: (0, 0)), at],
-        [pltpu.VMEM((n, d), F32)],
-        flops=4 * n * d * cols, name="down_other",
-    )
-
-
-def k_lowered_back(scal, du_own, du_oth, w_own, packs, cot, mixed, a, b, keep):
-    n, cols = du_own.shape
-    d = w_own.shape[0]
-    rp = packs[0].shape[0]
-
-    def body(s, do, dt, wo, w0, w1, w2, w3, c_ref, m_ref, a_ref, b_ref, k_ref, dh_ref, df_ref, dir_ref, w_scr):
-        @pl.when(pl.program_id(0) == 0)
-        def _():
+            place(u_scr, s, (u0, u1, u2, u3))
             place(w_scr, s, (w0, w1, w2, w3))
-
-        dl = col_inner(do[...], wo[...]) + col_inner(dt[...], w_scr[...])
-        m = m_ref[...]
+            own = pl.multiple_of(s[6] * ch, ch)
+            oth = s[7] * ch
+            h_scr[pl.ds(own, ch), :] = ho[...]
+            f_scr[pl.ds(own, ch), :] = fo[...]
+            place(h_scr, s, (h0, h1, h2, h3), oth)
+            place(f_scr, s, (f0, f1, f2, f3), oth)
+
+        dl = dl_ref[...]
+        m = x_ref[...]
         r = lax.rsqrt(jnp.mean(m * m, axis=-1, keepdims=True) + norm_eps)
         n2 = m * r
         dm = c_ref[...].astype(F32) + r * (dl - n2 * jnp.mean(dl * n2, axis=-1, keepdims=True))
-        dh_ref[...] = (dm * a_ref[...].astype(F32)).astype(BF)
-        df_ref[...] = (dm * b_ref[...].astype(F32)).astype(BF)
+        dh = (dm * a_ref[...].astype(F32)).astype(BF)
+        df = (dm * b_ref[...].astype(F32)).astype(BF)
+        dh_ref[...] = dh
+        df_ref[...] = df
         dir_ref[...] = (dm * k_ref[...].astype(F32)).astype(BF)
-
-    return run(
-        body, (n // ROWS,), scal, [du_own, du_oth, w_own, *packs, cot, mixed, a, b, keep],
-        [rows_of(cols), rows_of(cols), whole((d, cols))] + [whole((rp, cols))] * 4 + [rows_of(d)] * 5,
-        [sds((n, d))] * 3,
-        [rows_of(d)] * 3,
-        [pltpu.VMEM((d, cols), BF)],
-        flops=4 * n * d * cols, name="lowered_back",
-    )
-
-
-def k_gated_back(scal, dh, u_own, packs, rp, g_own, g_oth, m_own, m_oth):
-    n, d = dh.shape
-    half = u_own.shape[0]
-    own_steps = half // rp
-
-    def body(s, dh_ref, uo, u0, u1, u2, u3, go, gt, mo, mt, ao, at, co, ct):
-        for i in range(own_steps + 4):
-
-            @pl.when(pl.program_id(0) == i)
-            def _(i=i):
-                if i < own_steps:
-                    w, g_ref, m_ref, a_ref, c_ref = uo[i * rp : (i + 1) * rp, :], go, mo, ao, co
-                else:
-                    w, g_ref, m_ref, a_ref, c_ref = (u0, u1, u2, u3)[i - own_steps][...], gt, mt, at, ct
-                dg = col_inner(dh_ref[...], w)
-                a_ref[...] = (dg * g_ref[...].astype(F32)).astype(BF)
-                c_ref[...] = (dg * m_ref[...].astype(F32)).astype(BF)
-
-    first = pl.BlockSpec((n, rp), lambda i, s: (0, jnp.minimum(i, own_steps - 1)))
-    second = pl.BlockSpec((n, rp), lambda i, s: (0, s[jnp.maximum(i - own_steps, 0)]))
-    return run(
-        body, (own_steps + 4,), scal, [dh, u_own, *packs, g_own, g_oth, m_own, m_oth],
-        [whole((n, d)), whole((half, d))] + [piece_whole(rp, d, 0)] * 4 + [first, second, first, second],
-        [sds((n, half))] * 4,
-        [first, second, first, second],
-        flops=4 * n * d * half, name="gated_back",
+        de = col_inner(dh, h_scr[...]) + col_inner(df, f_scr[...])
+        for u, w, g_ref, m_ref, a_out, d_out in ((uo, wo, go, mo, ao, do), (u_scr, w_scr, gt, mt, at, dt)):
+            dg = col_inner(dh, u[...])
+            a_out[...] = (dg * g_ref[...].astype(F32)).astype(BF)
+            low = (dg * m_ref[...].astype(F32)).astype(BF)
+            d_out[...] = low
+            de = de + col_inner(low, w[...])
+        de_ref[...] = de
+
+    ins = [dl, cot, mixed, fac_h, fac_f, keep, g_own, g_oth, m_own, m_oth, u_own, wg_own, h_own, f_own]
+    ins += [*packs_g, *packs_h, *packs_h, *packs_h]
+    specs = [rows_of(d)] * 6 + [rows_of(half)] * 4
+    specs += [whole((half, d)), whole((d, half)), whole((ch, d)), whole((ch, d))]
+    specs += [piece_whole(rg, half, 0)] * 4 + [piece_whole(ru, d, 0)] * 4
+    specs += [piece_whole(rh, d, ru // rh)] * 4 + [piece_whole(rh, d, ru // rh + 1)] * 4
+    return run(
+        body, (n // ROWS,), scal, ins, specs,
+        [sds((n, d))] * 3 + [sds((n, half))] * 4 + [sds((n, d), F32)],
+        [rows_of(d)] * 3 + [rows_of(half)] * 4 + [rows_of(d)],
+        [pltpu.VMEM((half, d), BF), pltpu.VMEM((d, half), BF), pltpu.VMEM((2 * ch, d), BF), pltpu.VMEM((2 * ch, d), BF)],
+        flops=2 * n * d * (4 * half + 4 * ch), name="mid_back",
     )
 
 
@@ -837,42 +862,6 @@
     )
 
 
-def k_ema_out_back(scal, dg_own, dg_oth, dz, dh, df, slope, wg_own, w_z, h_own, f_own, packs_g, rg, packs_h, rows):
-    n, d = dh.shape
-    half = dg_own.shape[1]
-    ch = h_own.shape[0]
-    zw = w_z.shape[1]
-    ru, rh = rows
-
-    def body(s, go, gt, dz_ref, dh_ref, df_ref, sl_ref, wo, wz, ho, fo, g0, g1, g2, g3, h0, h1, h2, h3,
-             f0, f1, f2, f3, o_ref, w_scr, h_scr, f_scr):
-        @pl.when(pl.program_id(0) == 0)
-        def _():
-            place(w_scr, s, (g0, g1, g2, g3))
-            own = pl.multiple_of(s[6] * ch, ch)
-            oth = s[7] * ch
-            h_scr[pl.ds(own, ch), :] = ho[...]
-            f_scr[pl.ds(own, ch), :] = fo[...]
-            place(h_scr, s, (h0, h1, h2, h3), oth)
-            place(f_scr, s, (f0, f1, f2, f3), oth)
-
-        total = col_inner(go[...], wo[...]) + col_inner(gt[...], w_scr[...]) + col_inner(dz_ref[...], wz[...])
-        total = total + col_inner(dh_ref[...], h_scr[...]) + col_inner(df_ref[...], f_scr[...])
-        o_ref[...] = total * sl_ref[...].astype(F32)
-
-    ins = [dg_own, dg_oth, dz, dh, df, slope, wg_own, w_z, h_own, f_own, *packs_g, *packs_h, *packs_h]
-    specs = [rows_of(half), rows_of(half), rows_of(zw), rows_of(d), rows_of(d), rows_of(d)]
-    specs += [whole((d, half)), whole((d, zw)), whole((ch, d)), whole((ch, d))]
-    specs += [piece_whole(rg, half, 1)] * 4
-    specs += [piece_whole(rh, d, ru // rh)] * 4 + [piece_whole(rh, d, ru // rh + 1)] * 4
-    return run(
-        body, (n // ROWS,), scal, ins, specs,
-        [sds((n, d), F32)], [rows_of(d)],
-        [pltpu.VMEM((d, half), BF), pltpu.VMEM((2 * ch, d), BF), pltpu.VMEM((2 * ch, d), BF)],
-        flops=2 * n * d * (2 * half + 4 * ch + zw), name="ema_out_back",
-    )[0]
-
-
 def k_input_back(scal, dv_own, dv_oth, w_own, packs, rp, d_sig, tokens, direct):
     n, d = tokens.shape
     half = dv_own.shape[1]
@@ -914,6 +903,71 @@
         body, (steps,), scal, ins, specs, [sds((d, cols))], [cols_of(d, tn)],
         flops=2 * n * d * cols, name=name,
     )[0]
+
+
+def k_weight_mid(scal, ema_low, dh, df, gated_own, gated_oth, dg_own, dg_oth, part, got=None):
+    n, d = ema_low.shape
+    half = gated_own.shape[1] // 2
+    qe = d // 4
+
+    def body(s, e_ref, h_ref, f_ref, go, gt, do, dt, eo, et, *refs):
+        adds = refs[:-2]
+        own, oth = refs[-2:]
+
+        def put(out, k, at, width, value):
+            if adds:
+                value = value + adds[k][:, at : at + width].astype(F32)
+            out[:, at : at + width] = value.astype(BF)
+
+        for i in range(3):
+
+            @pl.when(pl.program_id(0) == i)
+            def _(i=i):
+                for k, (out, g, dg, e) in enumerate(((own, go, do, eo), (oth, gt, dt, et))):
+                    if i == 0:
+                        put(out, k, 0, half, row_inner(h_ref[...], g[...]))
+                    elif i == 1:
+                        put(out, k, 0, half, row_inner(e_ref[...], dg[...]))
+                    else:
+                        put(out, k, 0, qe, row_inner(h_ref[...], e[...]))
+                        put(out, k, qe, qe, row_inner(f_ref[...], e[...]))
+
+    at = pl.BlockSpec((n, half), lambda i, s: (0, s[part]), pipeline_mode=pl.Buffered(1))
+    e_own = pl.BlockSpec((n, qe), lambda i, s: (0, s[6] * 2 + s[part]), pipeline_mode=pl.Buffered(1))
+    e_oth = pl.BlockSpec((n, qe), lambda i, s: (0, s[7] * 2 + s[part]), pipeline_mode=pl.Buffered(1))
+    adds = list(got) if got is not None else []
+    return run(
+        body, (3,), scal, [ema_low, dh, df, gated_own, gated_oth, dg_own, dg_oth, ema_low, ema_low] + adds,
+        [whole((n, d))] * 3 + [at] * 4 + [e_own, e_oth] + [cols_of(d, half)] * len(adds),
+        [sds((d, 3 * half))] * 2, [cols_of(d, half)] * 2,
+        flops=2 * n * d * 6 * half, name="weight_mid",
+    )
+
+
+def k_weight_value(scal, normed, dv_own, dv_oth, part, got=None):
+    n, d = normed.shape
+    half = dv_own.shape[1] // 2
+
+    def body(s, x_ref, vo, vt, *refs):
+        adds = refs[:-2]
+        for i, v in enumerate((vo, vt)):
+
+            @pl.when(pl.program_id(0) == i)
+            def _(i=i, v=v):
+                total = row_inner(x_ref[...], v[...])
+                if adds:
+                    total = total + adds[i][...].astype(F32)
+                refs[-2 + i][...] = total.astype(BF)
+
+    at = pl.BlockSpec((n, half), lambda i, s: (0, s[part]), pipeline_mode=pl.Buffered(1))
+    adds = list(got) if got is not None else []
+    still = pl.BlockSpec((d, half), lambda i, s: (0, 0))
+    return run(
+        body, (2,), scal, [normed, dv_own, dv_oth] + adds,
+        [whole((n, d)), at, at] + [whole((d, half))] * len(adds),
+        [sds((d, half))] * 2, [still] * 2,
+        flops=2 * n * d * 2 * half, name="weight_value",
+    )
 
 
 def swap(values, axis, bit, size):
@@ -935,23 +989,36 @@
     core = me % 2
     x_pos = (me // 2) % 2
     z_pos = me // 4
-    k0 = me % 4
-    scal = jnp.stack([k0, k0 ^ 2, k0 ^ 1, k0 ^ 3, core, 1 - core, t, 1 - t])
+    k0 = core * 2 + x_pos
+    scal = jnp.stack([k0, k0 ^ 1, k0 ^ 2, k0 ^ 3, core, 1 - core, t, 1 - t])
+
+    def after(*values):
+        return lax.optimization_barrier((scal, *values))[0]
+
+    def over_core(v):
+        return swap(v, "dp", 1, dp_size)
+
+    def over_x(v):
+        return swap(v, "dp", 2, dp_size)
+
+    def over_tensor(v):
+        return swap(v, "tensor", 1, 2)
 
     def my_rows(w):
         rows = w.shape[0] // 4
         return lax.dynamic_slice_in_dim(w, k0 * rows, rows, 0)
 
     def fetch(values):
-        by_y = swap(values, "tensor", 1, 2)
-        by_x = swap(by_y, "dp", 2, dp_size)
-        return by_y, by_x, swap(by_y, "dp", 1, dp_size), swap(by_x, "dp", 1, dp_size)
+        by_y = over_tensor(values)
+        by_x = over_x(by_y)
+        return by_y, by_x, over_core(by_y), over_core(by_x)
 
     own_params = jnp.concatenate(
         [a.T for a in (alpha_logit, delta_logit, ema_beta, ema_eta)] + [ema_omega[None]], axis=0
     )
-    oth_params = swap(own_params, "tensor", 1, 2)
-    pv = fetch(jnp.concatenate([my_rows(w_v), my_rows(w_gamma)], axis=0))
+    oth_params = over_tensor(own_params)
+    pv = fetch(my_rows(w_v))
+    pg = fetch(my_rows(w_gamma))
     ph = fetch(jnp.concatenate([my_rows(u_h), my_rows(w_h), my_rows(w_phi)], axis=0))
     pu = fetch(my_rows(w_up))
     pd = fetch(my_rows(w_down))
@@ -970,103 +1037,116 @@
     omega = params[4 * H].reshape(-1, 128)
 
     normed, v_own, vs_own = k_value_own(scal, tokens, w_v)
-    ema_low, e_slope = k_ema_forward(scal, normed, decay, coef, omega)
+    ema_low, e_slope = k_ema_forward(after(v_own), normed, decay, coef, omega)
     z_pre, query, key = k_query_key(scal, ema_low, w_z, qk_gain, qk_bias)
-    g_own, gs_own = k_act_own(scal, ema_low, w_gamma, 512)
-    v_oth, vs_oth = k_act_other(scal, normed, pv, rv, 0, 512)
-    g_oth, gs_oth = k_act_other(scal, ema_low, pv, rv, 1, 512)
+    g_own, gs_own = k_act_own(after(query), ema_low, w_gamma, 512)
+    v_oth, vs_oth = k_act_other(after(g_own), normed, pv, rv, 0, 512)
+    g_oth, gs_oth = k_act_other(after(v_oth), ema_low, pg, rv, 0, 512)
     gated_own, gated_oth, m_own, m_oth, probs = k_attend(
         scal, query, key, v_own, v_oth, g_own, g_oth, gs_own, gs_oth
     )
     mixed, lowered, fac_h, fac_f, keep = k_gate(
         scal, gated_own, gated_oth, ema_low, tokens, u_h, w_h, w_phi, ph, rh
     )
-    hid_own, us_own = k_act_own(scal, lowered, w_up, 1024)
-    hid_oth, us_oth = k_act_other(scal, lowered, pu, pu[0].shape[0], 0, 1024)
-    acc, du_own = k_down_own(scal, hid_own, us_own, w_down, cotangent)
-    output, du_oth = k_down_other(scal, hid_oth, us_oth, pd, cotangent, acc, mixed)
-    dh, df, direct = k_lowered_back(
-        scal, du_own, du_oth, w_up, pu, cotangent, mixed, fac_h, fac_f, keep
-    )
-    da_own, da_oth, dg_own, dg_oth = k_gated_back(
-        scal, dh, u_h, ph, rh[0], g_own, g_oth, m_own, m_oth
-    )
-    dv_own, dv_oth = k_value_back(scal, probs, da_own, da_oth, vs_own, vs_oth)
-    dz, stats = k_score_back(scal, probs, da_own, da_oth, v_own, v_oth, query, key, z_pre, qk_gain)
-    d_e = k_ema_out_back(
-        scal, dg_own, dg_oth, dz, dh, df, e_slope, w_gamma, w_z, w_h, w_phi, pv, rv, ph, rh
-    )
-    d_sig, sum_a, sum_b, sum_w = k_ema_backward(scal, normed, d_e, decay, coef, omega)
+    acc, dl, ffn_so, ffn_ko = k_ffn(scal, lowered, cotangent, [w_up], [w_down], mixed, None, False)
+    ffn_go = over_core(ffn_so)
+    output, dl, ffn_st, ffn_kt = k_ffn(after(acc), lowered, cotangent, pu, pd, acc, dl, True)
+    ffn_gt = over_core(ffn_st)
+    dh, df, direct, da_own, da_oth, dg_own, dg_oth, de_part = k_mid_back(
+        scal, dl, cotangent, mixed, fac_h, fac_f, keep, g_own, g_oth, m_own, m_oth,
+        u_h, w_gamma, w_h, w_phi, pg, ph, rh,
+    )
+    mid_sent = k_weight_mid(after(dh), ema_low, dh, df, gated_own, gated_oth, dg_own, dg_oth, 5)
+    mid_got = [over_core(v) for v in mid_sent]
+    dv_own, dv_oth = k_value_back(after(*mid_sent), probs, da_own, da_oth, vs_own, vs_oth)
+    val_sent = k_weight_value(after(dv_own), normed, dv_own, dv_oth, 5)
+    val_got = [over_core(v) for v in val_sent]
+    mid_own, mid_oth = k_weight_mid(
+        after(*val_sent), ema_low, dh, df, gated_own, gated_oth, dg_own, dg_oth, 4, mid_got
+    )
+    dz, stats = k_score_back(
+        after(mid_own), probs, da_own, da_oth, v_own, v_oth, query, key, z_pre, qk_gain
+    )
+    val_own, val_oth = k_weight_value(after(dz), normed, dv_own, dv_oth, 4, val_got)
+    z_own = k_weight(after(dz), ema_low, dz, lambda s: 0, dz.shape[1], dz.shape[1])
+    d_sig, sum_a, sum_b, sum_w = k_ema_backward(
+        after(val_own, z_own), normed, de_part, dz, e_slope, w_z, decay, coef, omega
+    )
     input_grad = k_input_back(scal, dv_own, dv_oth, w_v, pv, rv, d_sig, tokens, direct)
 
-    def theirs(s):
-        return s[5]
-
-    def mine(s):
-        return s[4]
-
-    def chip_sum(left, own, oth, tn):
-        quarter = own.shape[1] // 2
-        tn = min(tn, quarter)
-        sent = [k_weight(scal, left, r, theirs, quarter, tn) for r in (own, oth)]
-        got = [swap(v, "dp", 1, dp_size) for v in sent]
-        return (
-            k_weight(scal, left, own, mine, quarter, tn, [(got[0], 0)]),
-            k_weight(scal, left, oth, mine, quarter, tn, [(got[1], 0)]),
-        )
-
-    def chip_sum_ema(left):
-        quarter = d // 4
-        ats = [
-            (lambda s: s[6] * 2 + s[5], lambda s: s[6] * 2 + s[4]),
-            (lambda s: s[7] * 2 + s[5], lambda s: s[7] * 2 + s[4]),
-        ]
-        res = []
-        for send_at, keep_at in ats:
-            got = swap(k_weight(scal, left, ema_low, send_at, quarter, quarter), "dp", 1, dp_size)
-            res.append(k_weight(scal, left, ema_low, keep_at, quarter, quarter, [(got, 0)]))
-        return tuple(res)
-
-    def over_rows(total):
-        c = total.shape[1]
-        by_x = total.reshape(4, 2, d // 8, c)
-        got = swap(pick(by_x, 1 - x_pos, 1), "dp", 2, dp_size)
-        total = (pick(by_x, x_pos, 1).astype(F32) + got.astype(F32)).astype(BF)
-        by_z = total.reshape(2, 2, d // 8, c)
+    def add(*values):
+        total = values[0].astype(F32)
+        for v in values[1:]:
+            total = total + v.astype(F32)
+        return total.astype(BF)
+
+    def split_x(v):
+        v = v.reshape(4, 2, d // 8, v.shape[-1])
+        return pick(v, x_pos, 1), pick(v, 1 - x_pos, 1)
+
+    def x_then_y(own_terms, oth_terms):
+        own = [split_x(v) for v in own_terms]
+        oth = [split_x(v) for v in oth_terms]
+        got_own = over_x(add(*[v[1] for v in own]))
+        got_oth = over_x(add(*[v[1] for v in oth]))
+        got = over_tensor(add(*[v[0] for v in oth], got_oth))
+        return [*[v[0] for v in own], got_own, got]
+
+    def y_then_x(own_terms, oth_terms):
+        got = over_tensor(add(*oth_terms))
+        own = [split_x(v) for v in [*own_terms, got]]
+        got = over_x(add(*[v[1] for v in own]))
+        return [*[v[0] for v in own], got]
+
+    def over_z(terms):
+        total = add(*terms)
+        by_z = total.reshape(2, 2, d // 8, total.shape[-1])
         got = swap(pick(by_z, 1 - z_pos % 2, 1), "dp", 4, dp_size)
-        total = (pick(by_z, z_pos % 2, 1).astype(F32) + got.astype(F32)).astype(BF)
-        got = swap(pick(total, 1 - z_pos // 2, 0), "dp", 8, dp_size)
-        return pick(total, z_pos // 2, 0).astype(F32) + got.astype(F32)
+        pair = add(pick(by_z, z_pos % 2, 1), got)
+        got = swap(pick(pair, 1 - z_pos // 2, 0), "dp", 8, dp_size)
+        return pick(pair, z_pos // 2, 0).astype(F32) + got.astype(F32)
 
     def finish(total):
-        c = total.shape[1]
-        by_core = total.reshape(2, d // 16, c)
-        got = swap(pick(by_core, 1 - core, 0).astype(BF), "dp", 1, dp_size).astype(F32)
+        by_core = total.reshape(2, d // 16, total.shape[1])
+        got = over_core(pick(by_core, 1 - core, 0).astype(BF)).astype(F32)
         kept = pick(by_core, core, 0)
-        return jnp.where(
-            core == 0,
-            jnp.concatenate([kept, got], axis=1),
-            jnp.concatenate([got, kept], axis=1),
-        )
-
-    def over_y(pair):
-        own, oth = pair
-        got = swap(oth, "tensor", 1, 2)
-        return (own.astype(F32) + got.astype(F32)).astype(BF)
-
-    down_t = finish(over_rows(over_y(chip_sum(cotangent, hid_own, hid_oth, 1024))))
-    up = finish(over_rows(over_y(chip_sum(lowered, du_own, du_oth, 1024))))
-    uh_t = finish(over_rows(over_y(chip_sum(dh, gated_own, gated_oth, 512))))
-    wh_t = finish(over_rows(over_y(chip_sum_ema(dh))))
-    phi_t = finish(over_rows(over_y(chip_sum_ema(df))))
-    gamma = finish(over_rows(over_y(chip_sum(ema_low, dg_own, dg_oth, 512))))
-    value = finish(over_rows(over_y(chip_sum(normed, dv_own, dv_oth, 512))))
-    z_own = k_weight(scal, ema_low, dz, lambda s: 0, dz.shape[1], dz.shape[1])
-    z_sum = (z_own.astype(F32) + swap(z_own, "dp", 1, dp_size).astype(F32)).astype(BF)
-    z_sum = (z_sum.astype(F32) + swap(z_sum, "tensor", 1, 2).astype(F32)).astype(BF)
-    z_grad = pick(over_rows(z_sum).reshape(2, d // 16, -1), core, 0)
-
-    sums = lax.psum(jnp.concatenate([sum_a, sum_b, sum_w, stats], axis=0), ("dp", "tensor"))
+        return jnp.where(core == 0, jnp.stack([kept, got]), jnp.stack([got, kept]))
+
+    def joined(pair):
+        return jnp.concatenate([pair[0], pair[1]], axis=1)
+
+    down_terms = x_then_y([ffn_ko[0], ffn_go[0]], [ffn_kt[0], ffn_gt[0]])
+    up_terms = y_then_x([ffn_ko[1], ffn_go[1]], [ffn_kt[1], ffn_gt[1]])
+    ffn = finish(over_z([jnp.concatenate([add(*down_terms), add(*up_terms)], axis=-1)]))
+    c = ffn.shape[2] // 2
+    down_t, up = joined(ffn[:, :, :c]), joined(ffn[:, :, c:])
+
+    c = mid_own.shape[1] // 2
+    mid_a = x_then_y([mid_own[:, :c]], [mid_oth[:, :c]])
+    mid_b = y_then_x([mid_own[:, c:]], [mid_oth[:, c:]])
+    mid = finish(over_z([jnp.concatenate([add(*mid_a), add(*mid_b)], axis=-1)]))
+    half = gated_own.shape[1] // 2
+    uh_t, gamma = joined(mid[:, :, :half]), joined(mid[:, :, half : 2 * half])
+    wh_t = joined(mid[:, :, 2 * half : 2 * half + d // 4])
+    phi_t = joined(mid[:, :, 2 * half + d // 4 :])
+
+    c = half // 2
+    z_sum = add(z_own, over_core(z_own))
+    z_sum = add(z_sum, over_tensor(z_sum))
+    val_a = x_then_y([val_own[:, :c]], [val_oth[:, :c]])
+    z_mine, z_sent = split_x(z_sum)
+    val_b = y_then_x([val_own[:, c:]], [val_oth[:, c:]])
+    z_total = add(z_mine, over_x(z_sent))
+    val = over_z([jnp.concatenate([add(*val_a), add(*val_b), z_total], axis=-1)])
+    z_grad = pick(val[:, half:].reshape(2, d // 16, -1), core, 0)
+    value = joined(finish(val[:, :half]))
+
+    sums = jnp.concatenate([sum_a, sum_b, sum_w, stats], axis=0)
+    sums = sums + over_core(sums)
+    sums = sums + over_tensor(sums)
+    sums = sums + over_x(sums)
+    sums = sums + swap(sums, "dp", 4, dp_size)
+    sums = sums + swap(sums, "dp", 8, dp_size)
     gh = sum_a.shape[0]
 
     def own_half(v):

time: 871 us -> 644 us (0.74)
  waiting for transfers between devices: 334 us -> 220 us
  Pallas kernels: 412 us -> 303 us
  between operations: 15.6 us -> 2.04 us
  local copies, waits for them, and re-layouts: 25.4 us -> 36.9 us
    pallas_call x48 -> x20, Pallas kernels: 412 us -> 303 us  [run(): pl.pallas_call(body, out_shape=out_shape, grid_spec=pltpu.PrefetchScalarG...]
    psum x1 -> x0, waiting for transfers between devices: 101 us -> none  [one_sequence(): lax.psum(jnp.concatenate([sum_a, sum_b, sum_w, stats], axis=0), ('dp', 't...]
    slice x0 -> x10, local copies, waits for them, and re-layouts: none -> 13.4 us  [the longest x4 7.24 us: one_sequence(): down_terms = x_then_y([ffn_ko[0], ffn_go[0]], [ffn_kt[0], ffn_gt[0]])]
    ppermute x71 -> x59, waiting for transfers between devices: 233 us -> 220 us  [swap(): return lax.ppermute(values, axis, [(i, i ^ bit) for i in range(size)])]
    ppermute x71 -> x59, starting transfers between devices: 55 us -> 52.6 us  [swap(): return lax.ppermute(values, axis, [(i, i ^ bit) for i in range(size)])]
  transfers between devices with their start and end apart: 72 -> 59, of which waited for: 25 -> 22; matrix products, arithmetic and copies ran while one was open for 4% -> 8% of each run, Pallas kernels for 41% -> 35%
where the time goes in v2:
time: 644 us; the launch traced here: 636 us
  Pallas kernels  303 us (47%)
  waiting for transfers between devices  220 us (34%)
  starting transfers between devices  52.6 us (8%)
  local copies, waits for them, and re-layouts  36.9 us (6%)
  other arithmetic  21.2 us (3%)
    pallas_call x20, Pallas kernels, run(): pl.pallas_call(body, out_shape=out_shape, grid_spec=pltpu.PrefetchScalarG...  303 us
    ppermute x59, waiting for transfers between devices, swap(): return lax.ppermute(values, axis, [(i, i ^ bit) for i in range(size)])  220 us
    ppermute x59, starting transfers between devices, swap(): return lax.ppermute(values, axis, [(i, i ^ bit) for i in range(size)])  52.6 us
    convert_element_type x21, other arithmetic, add(): return total.astype(BF)  13.5 us
  transfers between devices with their start and end apart: 59, of which 22 were waited for; matrix products, arithmetic and copies ran while one was open for 8% of the time, Pallas kernels for 35%

profile of v2, /device:TPU:0, one launch (start us, length us, event | category | flops | bytes accessed | tf_op | source)
XLA Modules:
  0.0 635.7 jit_solution(10345228348771630830)
XLA Ops:
  1.8 3.0 collective-permute-start.1
  8.3 2.1 collective-permute-start.9
  10.4 7.3 %collective-permute-done.1.p0.w0 = bf16[256,1024]{1,0:T(8,128)(2,1)} collective-permute-done((bf16[256,1024]{1,0:T(8,128)(2,1)S(1)}, bf16[256,1024]{1,0:T(8,128)(2,1)}, u32[]{:S(2)}, u32[]{:S(2)}) %collective-permute-start.1) | collective-permute-done | bytes 524320 | tf_op jit(solution)/shard_map/ppermute | solution.py:974
  22.7 6.2 collective-permute-done.5.p0.w0
  32.2 21.4 %collective-permute-done = f32[65,512]{1,0:T(8,128)S(1)} collective-permute-done((f32[65,512]{1,0:T(8,128)S(1)}, f32[65,512]{1,0:T(8,128)S(1)}, u32[]{:S(2)}, u32[]{:S(2)}) %collective-permute-start) | collective-permute-done | bytes 133152 | tf_op jit(solution)/shard_map/ppermute | solution.py:974
  58.4 8.6 %value_own.1 = (bf16[1024,1024]{1,0:T(8,128)(2,1)}, bf16[1024,1024]{1,0:T(8,128)(2,1)}, bf16[1024,1024]{1,0:T(8,128)(2,1)}) custom-call(s32[8]{0:T(128)} %stack.80.s, bf16[1024,1024]{1,0:T(8,128)(2,1)} %x_ref.5, bf16[1024,1024]{1,0:T(8,128)(2,1)} %wo.3), custom_call_target="tpu_custom_call" | custom-call | flops 2147483648 | bytes 10485760 | tf_op jit(solution)/shard_map/value_own/pallas_call | solution.py:340
  69.1 10.7 %collective-permute-done.13.refs_0_ = bf16[256,2048]{1,0:T(8,128)(2,1)} collective-permute-done((bf16[256,2048]{1,0:T(8,128)(2,1)S(1)}, bf16[256,2048]{1,0:T(8,128)(2,1)}, u32[]{:S(2)}, u32[]{:S(2)}) %collective-permute-start.13) | collective-permute-done | bytes 1048608 | tf_op jit(solution)/shard_map/ppermute | solution.py:974
  79.8 20.7 %collective-permute-done.17.refs_4_ = bf16[512,1024]{1,0:T(8,128)(2,1)} collective-permute-done((bf16[512,1024]{1,0:T(8,128)(2,1)S(1)}, bf16[512,1024]{1,0:T(8,128)(2,1)}, u32[]{:S(2)}, u32[]{:S(2)}) %collective-permute-start.17) | collective-permute-done | bytes 1048608 | tf_op jit(solution)/shard_map/ppermute | solution.py:974
  102.6 15.5 %ema_forward.1 = (bf16[1024,1024]{1,0:T(8,128)(2,1)}, bf16[1024,1024]{1,0:T(8,128)(2,1)}) custom-call(s32[8]{0:T(128)} %stack.80.s, bf16[1024,1024]{1,0:T(8,128)(2,1)} %get-tuple-element.87.x_ref, f32[128,128]{1,0:T(8,128)} %reshape.168.dec_ref, f32[128,128]{1,0:T(8,128)} %reshape.169.cf_ref, f32[8,128]{1,0:T(8,128)} %bitcast.285), custom_call_target="tpu_custom_call" | custom-call | flops 20000000000 | bytes 6426624 | tf_op jit(solution)/shard_map/ema_forward/pallas_call | solution.py:340
  118.1 3.7 query_key.1
  121.7 7.8 %act_own.1 = (bf16[1024,1024]{1,0:T(8,128)(2,1)}, bf16[1024,1024]{1,0:T(8,128)(2,1)}) custom-call(s32[8]{0:T(128)} %stack.80.s, bf16[1024,1024]{1,0:T(8,128)(2,1)} %get-tuple-element.88.e_ref.x_ref.eo.et.l_ref, bf16[1024,1024]{1,0:T(8,128)(2,1)} %wo.2), custom_call_target="tpu_custom_call" | custom-call | flops 2147483648 | bytes 8388608 | tf_op jit(solution)/shard_map/act_own/pallas_call | solution.py:340
  129.5 8.3 %act_other.2 = (bf16[1024,1024]{1,0:T(8,128)(2,1)}, bf16[1024,1024]{1,0:T(8,128)(2,1)}) custom-call(s32[8]{0:T(128)} %stack.80.s, bf16[1024,1024]{1,0:T(8,128)(2,1)} %get-tuple-element.87.x_ref, bf16[256,1024]{1,0:T(8,128)(2,1)} %collective-permute-done.1.p0.w0, bf16[256,1024]{1,0:T(8,128)(2,1)} %collective-permute-done.2.p1.w1, ...), custom_call_target="tpu_custom_call" | custom-call | flops 2147483648 | bytes 8388608 | tf_op jit(solution)/shard_map/act_other/pallas_call | solution.py:340
  138.6 8.1 %act_other.3 = (bf16[1024,1024]{1,0:T(8,128)(2,1)}, bf16[1024,1024]{1,0:T(8,128)(2,1)}) custom-call(s32[8]{0:T(128)} %stack.80.s, bf16[1024,1024]{1,0:T(8,128)(2,1)} %get-tuple-element.88.e_ref.x_ref.eo.et.l_ref, bf16[256,1024]{1,0:T(8,128)(2,1)} %collective-permute-done.5.p0.w0, bf16[256,1024]{1,0:T(8,128)(2,1)} %collective-permute-done.6.p1.w1, ...), custom_call_target="tpu_custom_call" | custom-call | flops 2147483648 | bytes 8388608 | tf_op jit(solution)/shard_map/act_other/pallas_call | solution.py:340
  146.8 13.2 %attend.1 = (bf16[1024,1024]{1,0:T(8,128)(2,1)}, bf16[1024,1024]{1,0:T(8,128)(2,1)}, bf16[1024,1024]{1,0:T(8,128)(2,1)}, bf16[1024,1024]{1,0:T(8,128)(2,1)}, bf16[1024,1024]{1,0:T(8,128)(2,1)}) custom-call(s32[8]{0:T(128)} %stack.80.s, bf16[1024,128]{1,0:T(8,128)(2,1)} %get-tuple-element.89.q_ref, bf16[1024,128]{1,0:T(8,128)(2,1)} %get-tuple-element.90.k_ref, ...), custom_call_target="tpu_custom_call" | custom-call | flops 2852126720 | bytes 23592960 | tf_op jit(solution)/shard_map/attend/pallas_call | solution.py:340
  162.2 18.8 %gate.1 = (f32[1024,1024]{1,0:T(8,128)}, bf16[1024,1024]{1,0:T(8,128)(2,1)}, bf16[1024,1024]{1,0:T(8,128)(2,1)}, bf16[1024,1024]{1,0:T(8,128)(2,1)}, bf16[1024,1024]{1,0:T(8,128)(2,1)}) custom-call(s32[8]{0:T(128)} %stack.80.s, bf16[1024,1024]{1,0:T(8,128)(2,1)} %get-tuple-element.99.go, bf16[1024,1024]{1,0:T(8,128)(2,1)} %get-tuple-element.100.gt, ...), custom_call_target="tpu_custom_call" | custom-call | flops 8589934592 | bytes 37748736 | tf_op jit(solution)/shard_map/gate/pallas_call | solution.py:340
  181.0 38.2 %ffn_own.1 = (f32[1024,1024]{1,0:T(8,128)}, f32[1024,1024]{1,0:T(8,128)}, bf16[2,1024,1024]{2,1,0:T(8,128)(2,1)}, bf16[2,1024,1024]{2,1,0:T(8,128)(2,1)}) custom-call(s32[8]{0:T(128)} %stack.80.s, bf16[1024,1024]{1,0:T(8,128)(2,1)} %get-tuple-element.101.low_ref, bf16[1024,1024]{1,0:T(8,128)(2,1)} %c_ref.5, bf16[1024,2048]{1,0:T(8,128)(2,1)} %refs_0_.1, ...), custom_call_target="tpu_custom_call" | custom-call | flops 25769803776 | bytes 33554432 | tf_op jit(solution)/shard_map/ffn_own/pallas_call | solution.py:340
  220.9 40.4 %ffn_other.1 = (bf16[1024,1024]{1,0:T(8,128)(2,1)}, f32[1024,1024]{1,0:T(8,128)}, bf16[2,1024,1024]{2,1,0:T(8,128)(2,1)}, bf16[2,1024,1024]{2,1,0:T(8,128)(2,1)}) custom-call(s32[8]{0:T(128)} %stack.80.s, bf16[1024,1024]{1,0:T(8,128)(2,1)} %get-tuple-element.101.low_ref, bf16[1024,1024]{1,0:T(8,128)(2,1)} %c_ref.5, ...), custom_call_target="tpu_custom_call" | custom-call | flops 25769803776 | bytes 35651584 | tf_op jit(solution)/shard_map/ffn_other/pallas_call | solution.py:340
  261.3 26.2 %mid_back.1 = (bf16[1024,1024]{1,0:T(8,128)(2,1)}, bf16[1024,1024]{1,0:T(8,128)(2,1)}, bf16[1024,1024]{1,0:T(8,128)(2,1)}, bf16[1024,1024]{1,0:T(8,128)(2,1)}, b...) custom-call(s32[8]{0:T(128)} %stack.80.s, ...), custom_call_target="tpu_custom_call" | custom-call | flops 12884901888 | bytes 65011712 | tf_op jit(solution)/shard_map/mid_back/pallas_call | solution.py:340
  287.5 13.9 %weight_mid.2 = (bf16[1024,1536]{1,0:T(8,128)(2,1)}, bf16[1024,1536]{1,0:T(8,128)(2,1)}) custom-call(s32[8]{0:T(128)} %stack.80.s, bf16[1024,1024]{1,0:T(8,128)(2,1)} %get-tuple-element.88.e_ref.x_ref.eo.et.l_ref, bf16[1024,1024]{1,0:T(8,128)(2,1)} %get-tuple-element.113.h_ref, bf16[1024,1024]{1,0:T(8,128)(2,1)} %get-tuple-element.115.f_ref, ...), custom_call_target="tpu_custom_call" | custom-call | flops 6442450944 | bytes 25165824 | tf_op jit(solution)/shard_map/weight_mid/pallas_call | solution.py:340
  301.9 9.4 %value_back.1 = (bf16[1024,1024]{1,0:T(8,128)(2,1)}, bf16[1024,1024]{1,0:T(8,128)(2,1)}) custom-call(s32[8]{0:T(128)} %stack.80.s, bf16[1024,1024]{1,0:T(8,128)(2,1)} %get-tuple-element.121.p_ref, bf16[1024,1024]{1,0:T(8,128)(2,1)} %get-tuple-element.122.ao, bf16[1024,1024]{1,0:T(8,128)(2,1)} %get-tuple-element.123.at, ...), custom_call_target="tpu_custom_call" | custom-call | flops 2684354560 | bytes 14680064 | tf_op jit(solution)/shard_map/value_back/pallas_call | solution.py:340
  311.3 7.4 %weight_value.2 = (bf16[1024,512]{1,0:T(8,128)(2,1)}, bf16[1024,512]{1,0:T(8,128)(2,1)}) custom-call(s32[8]{0:T(128)} %stack.80.s, bf16[1024,1024]{1,0:T(8,128)(2,1)} %get-tuple-element.87.x_ref, bf16[1024,1024]{1,0:T(8,128)(2,1)} %get-tuple-element.126.vo, bf16[1024,1024]{1,0:T(8,128)(2,1)} %get-tuple-element.127.vt), custom_call_target="tpu_custom_call" | custom-call | flops 2147483648 | bytes 8388608 | tf_op jit(solution)/shard_map/weight_value/pallas_call | solution.py:340
  321.4 2.5 fusion.34
  324.4 14.4 %weight_mid.3 = (bf16[1024,1536]{1,0:T(8,128)(2,1)}, bf16[1024,1536]{1,0:T(8,128)(2,1)}) custom-call(s32[8]{0:T(128)} %stack.80.s, bf16[1024,1024]{1,0:T(8,128)(2,1)} %get-tuple-element.88.e_ref.x_ref.eo.et.l_ref, bf16[1024,1024]{1,0:T(8,128)(2,1)} %get-tuple-element.113.h_ref, bf16[1024,1024]{1,0:T(8,128)(2,1)} %get-tuple-element.115.f_ref, ...), custom_call_target="tpu_custom_call" | custom-call | flops 6442450944 | bytes 31457280 | tf_op jit(solution)/shard_map/weight_mid/pallas_call | solution.py:340
  338.8 10.7 %score_back.1 = (bf16[1024,128]{1,0:T(8,128)(2,1)}, f32[8,128]{1,0:T(8,128)}) custom-call(s32[8]{0:T(128)} %stack.80.s, bf16[1024,1024]{1,0:T(8,128)(2,1)} %get-tuple-element.121.p_ref, bf16[1024,1024]{1,0:T(8,128)(2,1)} %get-tuple-element.122.ao, bf16[1024,1024]{1,0:T(8,128)(2,1)} %get-tuple-element.123.at, bf16[1024,1024]{1,0:T(8,128)(2,1)} %get-tuple-element.85.vo, ...), custom_call_target="tpu_custom_call" | custom-call | flops 2684354560 | bytes 11801600 | tf_op jit(solution)/shard_map/score_back/pallas_call | solution.py:340
  349.5 3.7 weight.1
  355.6 7.4 %weight_value.3 = (bf16[1024,512]{1,0:T(8,128)(2,1)}, bf16[1024,512]{1,0:T(8,128)(2,1)}) custom-call(s32[8]{0:T(128)} %stack.80.s, bf16[1024,1024]{1,0:T(8,128)(2,1)} %get-tuple-element.87.x_ref, bf16[1024,1024]{1,0:T(8,128)(2,1)} %get-tuple-element.126.vo, bf16[1024,1024]{1,0:T(8,128)(2,1)} %get-tuple-element.127.vt, bf16[1024,512]{1,0:T(8,128)(2,1)} %copy-done.10, ...), custom_call_target="tpu_custom_call" | custom-call | flops 2147483648 | bytes 10485760 | tf_op jit(solution)/shard_map/weight_value/pallas_call | solution.py:340
  364.5 3.4 fusion.37
  367.9 34.8 %ema_backward.1 = (f32[1024,1024]{1,0:T(8,128)}, f32[128,128]{1,0:T(8,128)}, f32[128,128]{1,0:T(8,128)}, f32[8,128]{1,0:T(8,128)}) custom-call(s32[8]{0:T(128)} %stack.80.s, bf16[1024,1024]{1,0:T(8,128)(2,1)} %get-tuple-element.87.x_ref, f32[1024,1024]{1,0:T(8,128)} %get-tuple-element.139.de_ref, bf16[1024,128]{1,0:T(8,128)(2,1)} %get-tuple-element.135.r_ref.z_ref, ...), custom_call_target="tpu_custom_call" | custom-call | flops 40000000000 | bytes 13377536 | tf_op jit(solution)/shard_map/ema_backward/pallas_call | solution.py:340
  405.1 12.5 %input_back.1 = f32[1024,1024]{1,0:T(8,128)} custom-call(s32[8]{0:T(128)} %stack.80.s, bf16[1024,1024]{1,0:T(8,128)(2,1)} %get-tuple-element.126.vo, bf16[1024,1024]{1,0:T(8,128)(2,1)} %get-tuple-element.127.vt, bf16[1024,1024]{1,0:T(8,128)(2,1)} %wo.3, bf16[256,1024]{1,0:T(8,128)(2,1)} %collective-permute-done.1.p0.w0, ...), custom_call_target="tpu_custom_call" | custom-call | flops 4294967296 | bytes 20971520 | tf_op jit(solution)/shard_map/input_back/pallas_call | solution.py:340
  423.7 4.4 collective-permute-done.26
  430.3 6.6 %collective-permute-done.27 = f32[272,128]{1,0:T(8,128)S(1)} collective-permute-done((f32[272,128]{1,0:T(8,128)S(1)}, f32[272,128]{1,0:T(8,128)S(1)}, u32[]{:S(2)}, u32[]{:S(2)}) %collective-permute-start.27) | collective-permute-done | bytes 139296 | tf_op jit(solution)/shard_map/ppermute | solution.py:974
  440.8 12.3 %collective-permute-done.32 = bf16[4,128,256]{2,1,0:T(8,128)(2,1)S(1)} collective-permute-done((bf16[4,128,256]{2,1,0:T(8,128)(2,1)S(1)}, bf16[4,128,256]{2,1,0:T(8,128)(2,1)S(1)}, u32[]{:S(2)}, u32[]{:S(2)}) %collective-permute-start.32) | collective-permute-done | bytes 262176 | tf_op jit(solution)/shard_map/ppermute | solution.py:974
  456.3 3.2 collective-permute-done.37
  459.5 2.6 collective-permute-start.29
  462.1 4.8 collective-permute-done.29
  471.9 4.6 collective-permute-done.42
  478.8 14.7 %collective-permute-done.34 = bf16[4,128,256]{2,1,0:T(8,128)(2,1)S(1)} collective-permute-done((bf16[4,128,256]{2,1,0:T(8,128)(2,1)S(1)}, bf16[4,128,256]{2,1,0:T(8,128)(2,1)S(1)}, u32[]{:S(2)}, u32[]{:S(2)}) %collective-permute-start.34) | collective-permute-done | bytes 262176 | tf_op jit(solution)/shard_map/ppermute | solution.py:974
  499.7 2.5 fusion
  503.1 2.7 fusion.35
  505.9 2.7 collective-permute-start.39
  511.0 2.9 collective-permute-done.39
  518.6 26.7 %collective-permute-done.45 = bf16[4,128,768]{2,1,0:T(8,128)(2,1)S(1)} collective-permute-done((bf16[4,128,768]{2,1,0:T(8,128)(2,1)S(1)}, bf16[4,128,768]{2,1,0:T(8,128)(2,1)S(1)}, u32[]{:S(2)}, u32[]{:S(2)}) %collective-permute-start.45) | collective-permute-done | bytes 786464 | tf_op jit(solution)/shard_map/ppermute | solution.py:974
  548.8 13.3 %collective-permute-done.54 = bf16[1024,1024]{1,0:T(8,128)(2,1)S(1)} collective-permute-done((bf16[1024,1024]{1,0:T(8,128)(2,1)S(1)}, bf16[1024,1024]{1,0:T(8,128)(2,1)S(1)}, u32[]{:S(2)}, u32[]{:S(2)}) %collective-permute-start.54) | collective-permute-done | bytes 2097184 | tf_op jit(solution)/shard_map/ppermute | solution.py:974
  565.8 14.2 %collective-permute-done.53 = bf16[4,128,1024]{2,1,0:T(8,128)(2,1)S(1)} collective-permute-done((bf16[4,128,1024]{2,1,0:T(8,128)(2,1)S(1)}, bf16[4,128,1024]{2,1,0:T(8,128)(2,1)S(1)}, u32[]{:S(2)}, u32[]{:S(2)}) %collective-permute-start.53) | collective-permute-done | bytes 1048608 | tf_op jit(solution)/shard_map/ppermute | solution.py:974
  581.2 2.5 collective-permute-done.55
  585.5 22.5 %collective-permute-done.56 = bf16[2,128,2048]{2,1,0:T(8,128)(2,1)S(1)} collective-permute-done((bf16[2,128,2048]{2,1,0:T(8,128)(2,1)S(1)}, bf16[2,128,2048]{2,1,0:T(8,128)(2,1)S(1)}, u32[]{:S(2)}, u32[]{:S(2)}) %collective-permute-start.56) | collective-permute-done | bytes 1048608 | tf_op jit(solution)/shard_map/ppermute | solution.py:974
  608.5 2.4 collective-permute-start.57
  613.0 18.6 %collective-permute-done.57 = bf16[128,2048]{1,0:T(8,128)(2,1)S(1)} collective-permute-done((bf16[128,2048]{1,0:T(8,128)(2,1)S(1)}, bf16[128,2048]{1,0:T(8,128)(2,1)S(1)}, u32[]{:S(2)}, u32[]{:S(2)}) %collective-permute-start.57) | collective-permute-done | bytes 524320 | tf_op jit(solution)/shard_map/ppermute | solution.py:974
  (256 shorter events, 89.5 us)
Async XLA Ops:
  1.8 15.9 %collective-permute-start.1 = (bf16[256,1024]{1,0:T(8,128)(2,1)S(1)}, bf16[256,1024]{1,0:T(8,128)(2,1)}, u32[]{:S(2)}, u32[]{:S(2)}) collective-permute-start(bf16[256,1024]{1,0:T(8,128)(2,1)S(1)} %constant_dynamic-slice_fusion.9), channel_id=1, source_target_pairs={{0,1},{1,0},{2,3},{3,2},{4,5},{5,4},{6,7},{7,6},{8,9},{9,8},{10,11... | collective-permute-start | bytes 1572872 | tf_op jit(solution)/shard_map/ppermute | solution.py:974
  5.9 23.0 %collective-permute-start.5 = (bf16[256,1024]{1,0:T(8,128)(2,1)S(1)}, bf16[256,1024]{1,0:T(8,128)(2,1)}, u32[]{:S(2)}, u32[]{:S(2)}) collective-permute-start(bf16[256,1024]{1,0:T(8,128)(2,1)S(1)} %constant_dynamic-slice_fusion.8), channel_id=1, source_target_pairs={{0,1},{1,0},{2,3},{3,2},{4,5},{5,4},{6,7},{7,6},{8,9},{9,8},{10,11... | collective-permute-start | bytes 1572872 | tf_op jit(solution)/shard_map/ppermute | solution.py:974
  8.3 47.3 %collective-permute-start.9 = (bf16[512,1024]{1,0:T(8,128)(2,1)S(1)}, bf16[512,1024]{1,0:T(8,128)(2,1)}, u32[]{:S(2)}, u32[]{:S(2)}) collective-permute-start(bf16[512,1024]{1,0:T(8,128)(2,1)S(1)} %pad_maximum_fusion.2), channel_id=1, source_target_pairs={{0,1},{1,0},{2,3},{3,2},{4,5},{5,4},{6,7},{7,6},{8,9},{9,8},{10,11... | collective-permute-start | bytes 3145736 | tf_op jit(solution)/shard_map/ppermute | solution.py:974
  17.7 37.7 %collective-permute-start.2 = (bf16[256,1024]{1,0:T(8,128)(2,1)}, bf16[256,1024]{1,0:T(8,128)(2,1)}, u32[]{:S(2)}, u32[]{:S(2)}) collective-permute-start(bf16[256,1024]{1,0:T(8,128)(2,1)} %collective-permute-done.1.p0.w0), channel_id=1, source_target_pairs={{0,4},{2,6},{4,0},{6,2},{8,12},{10,14},{12,8},{14,10},{16,20},{18,... | collective-permute-start | bytes 1572872 | tf_op jit(solution)/shard_map/ppermute | solution.py:974
  19.8 33.8 %collective-permute-start = (f32[65,512]{1,0:T(8,128)S(1)}, f32[65,512]{1,0:T(8,128)S(1)}, u32[]{:S(2)}, u32[]{:S(2)}) collective-permute-start(f32[65,512]{1,0:T(8,128)S(1)} %dynamic-update-slice.8), channel_id=1, source_target_pairs={{0,1},{1,0},{2,3},{3,2},{4,5},{5,4},{6,7},{7,6},{8,9},{9,8},{10,11... | collective-permute-start | bytes 399368 | tf_op jit(solution)/shard_map/ppermute | solution.py:974
  22.7 35.3 %collective-permute-start.3 = (bf16[256,1024]{1,0:T(8,128)(2,1)}, bf16[256,1024]{1,0:T(8,128)(2,1)}, u32[]{:S(2)}, u32[]{:S(2)}) collective-permute-start(bf16[256,1024]{1,0:T(8,128)(2,1)} %collective-permute-done.1.p0.w0), channel_id=1, source_target_pairs={{0,2},{2,0},{4,6},{6,4},{8,10},{10,8},{12,14},{14,12},{16,18},{18,... | collective-permute-start | bytes 1572872 | tf_op jit(solution)/shard_map/ppermute | solution.py:974
  28.9 29.0 %collective-permute-start.6 = (bf16[256,1024]{1,0:T(8,128)(2,1)}, bf16[256,1024]{1,0:T(8,128)(2,1)}, u32[]{:S(2)}, u32[]{:S(2)}) collective-permute-start(bf16[256,1024]{1,0:T(8,128)(2,1)} %collective-permute-done.5.p0.w0), channel_id=1, source_target_pairs={{0,4},{2,6},{4,0},{6,2},{8,12},{10,14},{12,8},{14,10},{16,20},{18,... | collective-permute-start | bytes 1572872 | tf_op jit(solution)/shard_map/ppermute | solution.py:974
  53.6 26.2 %collective-permute-start.13 = (bf16[256,2048]{1,0:T(8,128)(2,1)S(1)}, bf16[256,2048]{1,0:T(8,128)(2,1)}, u32[]{:S(2)}, u32[]{:S(2)}) collective-permute-start(bf16[256,2048]{1,0:T(8,128)(2,1)S(1)} %constant_dynamic-slice_fusion.4), channel_id=1, source_target_pairs={{0,1},{1,0},{2,3},{3,2},{4,5},{5,4},{6,7},{7,6},{8,9},{9,8},{10,11... | collective-permute-start | bytes 3145736 | tf_op jit(solution)/shard_map/ppermute | solution.py:974
  55.3 45.2 %collective-permute-start.17 = (bf16[512,1024]{1,0:T(8,128)(2,1)S(1)}, bf16[512,1024]{1,0:T(8,128)(2,1)}, u32[]{:S(2)}, u32[]{:S(2)}) collective-permute-start(bf16[512,1024]{1,0:T(8,128)(2,1)S(1)} %constant_dynamic-slice_fusion.3), channel_id=1, source_target_pairs={{0,1},{1,0},{2,3},{3,2},{4,5},{5,4},{6,7},{7,6},{8,9},{9,8},{10,11... | collective-permute-start | bytes 3145736 | tf_op jit(solution)/shard_map/ppermute | solution.py:974
  55.6 46.9 %collective-permute-start.10 = (bf16[512,1024]{1,0:T(8,128)(2,1)}, bf16[512,1024]{1,0:T(8,128)(2,1)}, u32[]{:S(2)}, u32[]{:S(2)}) collective-permute-start(bf16[512,1024]{1,0:T(8,128)(2,1)} %collective-permute-done.9.u0.h0.f0), channel_id=1, source_target_pairs={{0,4},{2,6},{4,0},{6,2},{8,12},{10,14},{12,8},{14,10},{16,20},{18,... | collective-permute-start | bytes 3145736 | tf_op jit(solution)/shard_map/ppermute | solution.py:974
  57.9 11.1 %collective-permute-start.7 = (bf16[256,1024]{1,0:T(8,128)(2,1)}, bf16[256,1024]{1,0:T(8,128)(2,1)}, u32[]{:S(2)}, u32[]{:S(2)}) collective-permute-start(bf16[256,1024]{1,0:T(8,128)(2,1)} %collective-permute-done.5.p0.w0), channel_id=1, source_target_pairs={{0,2},{2,0},{4,6},{6,4},{8,10},{10,8},{12,14},{14,12},{16,18},{18,... | collective-permute-start | bytes 1572872 | tf_op jit(solution)/shard_map/ppermute | solution.py:974
  57.9 44.0 %collective-permute-start.4 = (bf16[256,1024]{1,0:T(8,128)(2,1)}, bf16[256,1024]{1,0:T(8,128)(2,1)S(1)}, u32[]{:S(2)}, u32[]{:S(2)}) collective-permute-start(bf16[256,1024]{1,0:T(8,128)(2,1)} %collective-permute-done.2.p1.w1), channel_id=1, source_target_pairs={{0,2},{2,0},{4,6},{6,4},{8,10},{10,8},{12,14},{14,12},{16,18},{18,... | collective-permute-start | bytes 1572872 | tf_op jit(solution)/shard_map/ppermute | solution.py:974
  69.0 91.0 %collective-permute-start.11 = (bf16[512,1024]{1,0:T(8,128)(2,1)}, bf16[512,1024]{1,0:T(8,128)(2,1)S(1)}, u32[]{:S(2)}, u32[]{:S(2)}) collective-permute-start(bf16[512,1024]{1,0:T(8,128)(2,1)} %collective-permute-done.9.u0.h0.f0), channel_id=1, source_target_pairs={{0,2},{2,0},{4,6},{6,4},{8,10},{10,8},{12,14},{14,12},{16,18},{18,... | collective-permute-start | bytes 3145736 | tf_op jit(solution)/shard_map/ppermute | solution.py:974
  79.8 58.0 %collective-permute-start.8 = (bf16[256,1024]{1,0:T(8,128)(2,1)}, bf16[256,1024]{1,0:T(8,128)(2,1)S(1)}, u32[]{:S(2)}, u32[]{:S(2)}) collective-permute-start(bf16[256,1024]{1,0:T(8,128)(2,1)} %collective-permute-done.6.p1.w1), channel_id=1, source_target_pairs={{0,2},{2,0},{4,6},{6,4},{8,10},{10,8},{12,14},{14,12},{16,18},{18,... | collective-permute-start | bytes 1572872 | tf_op jit(solution)/shard_map/ppermute | solution.py:974
  100.5 60.1 %collective-permute-start.14 = (bf16[256,2048]{1,0:T(8,128)(2,1)}, bf16[256,2048]{1,0:T(8,128)(2,1)S(1)}, u32[]{:S(2)}, u32[]{:S(2)}) collective-permute-start(bf16[256,2048]{1,0:T(8,128)(2,1)} %collective-permute-done.13.refs_0_), channel_id=1, source_target_pairs={{0,4},{2,6},{4,0},{6,2},{8,12},{10,14},{12,8},{14,10},{16,20},{18,... | collective-permute-start | bytes 3145736 | tf_op jit(solution)/shard_map/ppermute | solution.py:974
  101.9 58.8 %collective-permute-start.18 = (bf16[512,1024]{1,0:T(8,128)(2,1)}, bf16[512,1024]{1,0:T(8,128)(2,1)S(1)}, u32[]{:S(2)}, u32[]{:S(2)}) collective-permute-start(bf16[512,1024]{1,0:T(8,128)(2,1)} %collective-permute-done.17.refs_4_), channel_id=1, source_target_pairs={{0,4},{2,6},{4,0},{6,2},{8,12},{10,14},{12,8},{14,10},{16,20},{18,... | collective-permute-start | bytes 3145736 | tf_op jit(solution)/shard_map/ppermute | solution.py:974
  102.6 58.5 %collective-permute-start.12 = (bf16[512,1024]{1,0:T(8,128)(2,1)}, bf16[512,1024]{1,0:T(8,128)(2,1)S(1)}, u32[]{:S(2)}, u32[]{:S(2)}) collective-permute-start(bf16[512,1024]{1,0:T(8,128)(2,1)} %collective-permute-done.10.u1.h1.f1), channel_id=1, source_target_pairs={{0,2},{2,0},{4,6},{6,4},{8,10},{10,8},{12,14},{14,12},{16,18},{18,... | collective-permute-start | bytes 3145736 | tf_op jit(solution)/shard_map/ppermute | solution.py:974
  137.8 81.4 %collective-permute-start.15 = (bf16[256,2048]{1,0:T(8,128)(2,1)}, bf16[256,2048]{1,0:T(8,128)(2,1)S(1)}, u32[]{:S(2)}, u32[]{:S(2)}) collective-permute-start(bf16[256,2048]{1,0:T(8,128)(2,1)} %collective-permute-done.13.refs_0_), channel_id=1, source_target_pairs={{0,2},{2,0},{4,6},{6,4},{8,10},{10,8},{12,14},{14,12},{16,18},{18,... | collective-permute-start | bytes 3145736 | tf_op jit(solution)/shard_map/ppermute | solution.py:974
  160.0 59.3 %collective-permute-start.19 = (bf16[512,1024]{1,0:T(8,128)(2,1)}, bf16[512,1024]{1,0:T(8,128)(2,1)S(1)}, u32[]{:S(2)}, u32[]{:S(2)}) collective-permute-start(bf16[512,1024]{1,0:T(8,128)(2,1)} %collective-permute-done.17.refs_4_), channel_id=1, source_target_pairs={{0,2},{2,0},{4,6},{6,4},{8,10},{10,8},{12,14},{14,12},{16,18},{18,... | collective-permute-start | bytes 3145736 | tf_op jit(solution)/shard_map/ppermute | solution.py:974
  160.6 58.7 %collective-permute-start.16 = (bf16[256,2048]{1,0:T(8,128)(2,1)S(1)}, bf16[256,2048]{1,0:T(8,128)(2,1)S(1)}, u32[]{:S(2)}, u32[]{:S(2)}) collective-permute-start(bf16[256,2048]{1,0:T(8,128)(2,1)S(1)} %collective-permute-done.14.refs_1_), channel_id=1, source_target_pairs={{0,2},{2,0},{4,6},{6,4},{8,10},{10,8},{12,14},{14,12},{16,18},{18,... | collective-permute-start | bytes 3145736 | tf_op jit(solution)/shard_map/ppermute | solution.py:974
  160.7 58.6 %collective-permute-start.20 = (bf16[512,1024]{1,0:T(8,128)(2,1)S(1)}, bf16[512,1024]{1,0:T(8,128)(2,1)}, u32[]{:S(2)}, u32[]{:S(2)}) collective-permute-start(bf16[512,1024]{1,0:T(8,128)(2,1)S(1)} %collective-permute-done.18.refs_5_), channel_id=1, source_target_pairs={{0,2},{2,0},{4,6},{6,4},{8,10},{10,8},{12,14},{14,12},{16,18},{18,... | collective-permute-start | bytes 3145736 | tf_op jit(solution)/shard_map/ppermute | solution.py:974
  301.4 22.5 %collective-permute-start.21 = (bf16[1024,1536]{1,0:T(8,128)(2,1)}, bf16[1024,1536]{1,0:T(8,128)(2,1)}, u32[]{:S(2)}, u32[]{:S(2)}) collective-permute-start(bf16[1024,1536]{1,0:T(8,128)(2,1)} %get-tuple-element.118), channel_id=1, source_target_pairs={{0,2},{2,0},{4,6},{6,4},{8,10},{10,8},{12,14},{14,12},{16,18},{18,... | collective-permute-start | bytes 9437192 | tf_op jit(solution)/shard_map/ppermute | solution.py:974
  301.4 23.0 %collective-permute-start.22 = (bf16[1024,1536]{1,0:T(8,128)(2,1)}, bf16[1024,1536]{1,0:T(8,128)(2,1)}, u32[]{:S(2)}, u32[]{:S(2)}) collective-permute-start(bf16[1024,1536]{1,0:T(8,128)(2,1)} %get-tuple-element.119), channel_id=1, source_target_pairs={{0,2},{2,0},{4,6},{6,4},{8,10},{10,8},{12,14},{14,12},{16,18},{18,... | collective-permute-start | bytes 9437192 | tf_op jit(solution)/shard_map/ppermute | solution.py:974
  318.7 36.0 %collective-permute-start.23 = (bf16[1024,512]{1,0:T(8,128)(2,1)}, bf16[1024,512]{1,0:T(8,128)(2,1)S(1)}, u32[]{:S(2)}, u32[]{:S(2)}) collective-permute-start(bf16[1024,512]{1,0:T(8,128)(2,1)} %get-tuple-element.129), channel_id=1, source_target_pairs={{0,2},{2,0},{4,6},{6,4},{8,10},{10,8},{12,14},{14,12},{16,18},{18,... | collective-permute-start | bytes 3145736 | tf_op jit(solution)/shard_map/ppermute | solution.py:974
  318.7 36.0 %collective-permute-start.24 = (bf16[1024,512]{1,0:T(8,128)(2,1)}, bf16[1024,512]{1,0:T(8,128)(2,1)}, u32[]{:S(2)}, u32[]{:S(2)}) collective-permute-start(bf16[1024,512]{1,0:T(8,128)(2,1)} %get-tuple-element.130), channel_id=1, source_target_pairs={{0,2},{2,0},{4,6},{6,4},{8,10},{10,8},{12,14},{14,12},{16,18},{18,... | collective-permute-start | bytes 3145736 | tf_op jit(solution)/shard_map/ppermute | solution.py:974
  319.2 176.1 %collective-permute-start.51 = (bf16[2,1024,1024]{2,1,0:T(8,128)(2,1)}, bf16[2,1024,1024]{2,1,0:T(8,128)(2,1)}, u32[]{:S(2)}, u32[]{:S(2)}) collective-permute-start(bf16[2,1024,1024]{2,1,0:T(8,128)(2,1)} %get-tuple-element.152), channel_id=1, source_target_pairs={{0,2},{2,0},{4,6},{6,4},{8,10},{10,8},{12,14},{14,12},{16,18},{18,... | collective-permute-start | bytes 12582920 | tf_op jit(solution)/shard_map/ppermute | solution.py:974
  323.9 178.4 %collective-permute-start.49 = (bf16[2,1024,1024]{2,1,0:T(8,128)(2,1)}, bf16[2,1024,1024]{2,1,0:T(8,128)(2,1)}, u32[]{:S(2)}, u32[]{:S(2)}) collective-permute-start(bf16[2,1024,1024]{2,1,0:T(8,128)(2,1)} %get-tuple-element.150), channel_id=1, source_target_pairs={{0,2},{2,0},{4,6},{6,4},{8,10},{10,8},{12,14},{14,12},{16,18},{18,... | collective-permute-start | bytes 12582920 | tf_op jit(solution)/shard_map/ppermute | solution.py:974
  364.4 58.6 %collective-permute-start.35 = (bf16[1024,128]{1,0:T(8,128)(2,1)S(1)}, bf16[1024,128]{1,0:T(8,128)(2,1)S(1)}, u32[]{:S(2)}, u32[]{:S(2)}) collective-permute-start(bf16[1024,128]{1,0:T(8,128)(2,1)S(1)} %copy-done.12), channel_id=1, source_target_pairs={{0,2},{2,0},{4,6},{6,4},{8,10},{10,8},{12,14},{14,12},{16,18},{18,... | collective-permute-start | bytes 786440 | tf_op jit(solution)/shard_map/ppermute | solution.py:974
  423.1 15.3 %collective-permute-start.36 = (bf16[1024,128]{1,0:T(8,128)(2,1)S(1)}, bf16[1024,128]{1,0:T(8,128)(2,1)S(1)}, u32[]{:S(2)}, u32[]{:S(2)}) collective-permute-start(bf16[1024,128]{1,0:T(8,128)(2,1)S(1)} %add_convert_fusion.6), channel_id=1, source_target_pairs={{0,1},{1,0},{2,3},{3,2},{4,5},{5,4},{6,7},{7,6},{8,9},{9,8},{10,11... | collective-permute-start | bytes 786440 | tf_op jit(solution)/shard_map/ppermute | solution.py:974
  436.9 17.1 %collective-permute-start.33 = (bf16[1024,256]{1,0:T(8,128)(2,1)S(1)}, bf16[1024,256]{1,0:T(8,128)(2,1)S(1)}, u32[]{:S(2)}, u32[]{:S(2)}) collective-permute-start(bf16[1024,256]{1,0:T(8,128)(2,1)S(1)} %get-tuple-element.168), channel_id=1, source_target_pairs={{0,1},{1,0},{2,3},{3,2},{4,5},{5,4},{6,7},{7,6},{8,9},{9,8},{10,11... | collective-permute-start | bytes 1572872 | tf_op jit(solution)/shard_map/ppermute | solution.py:974
  438.4 14.6 %collective-permute-start.32 = (bf16[4,128,256]{2,1,0:T(8,128)(2,1)S(1)}, bf16[4,128,256]{2,1,0:T(8,128)(2,1)S(1)}, u32[]{:S(2)}, u32[]{:S(2)}) collective-permute-start(bf16[4,128,256]{2,1,0:T(8,128)(2,1)S(1)} %fusion.16), channel_id=1, source_target_pairs={{0,1},{1,0},{2,3},{3,2},{4,5},{5,4},{6,7},{7,6},{8,9},{9,8},{10,11... | collective-permute-start | bytes 786440 | tf_op jit(solution)/shard_map/ppermute | solution.py:974
  439.1 16.2 %collective-permute-start.28 = (f32[272,128]{1,0:T(8,128)S(1)}, f32[272,128]{1,0:T(8,128)S(1)}, u32[]{:S(2)}, u32[]{:S(2)}) collective-permute-start(f32[272,128]{1,0:T(8,128)S(1)} %add.286), channel_id=1, source_target_pairs={{0,8},{2,10},{4,12},{6,14},{8,0},{10,2},{12,4},{14,6},{16,24},{18,... | collective-permute-start | bytes 417800 | tf_op jit(solution)/shard_map/ppermute | solution.py:974
  454.0 22.4 %collective-permute-start.42 = (bf16[4,128,768]{2,1,0:T(8,128)(2,1)}, bf16[4,128,768]{2,1,0:T(8,128)(2,1)}, u32[]{:S(2)}, u32[]{:S(2)}) collective-permute-start(bf16[4,128,768]{2,1,0:T(8,128)(2,1)} %dynamic-slice_bitcast_fusion.2), channel_id=1, source_target_pairs={{0,4},{2,6},{4,0},{6,2},{8,12},{10,14},{12,8},{14,10},{16,20},{18,... | collective-permute-start | bytes 2359304 | tf_op jit(solution)/shard_map/ppermute | solution.py:974
  455.3 60.5 %collective-permute-start.41 = (bf16[4,128,768]{2,1,0:T(8,128)(2,1)}, bf16[4,128,768]{2,1,0:T(8,128)(2,1)}, u32[]{:S(2)}, u32[]{:S(2)}) collective-permute-start(bf16[4,128,768]{2,1,0:T(8,128)(2,1)} %dynamic-slice_bitcast_fusion.3), channel_id=1, source_target_pairs={{0,4},{2,6},{4,0},{6,2},{8,12},{10,14},{12,8},{14,10},{16,20},{18,... | collective-permute-start | bytes 2359304 | tf_op jit(solution)/shard_map/ppermute | solution.py:974
  466.9 42.1 %collective-permute-start.44 = (bf16[1024,768]{1,0:T(8,128)(2,1)}, bf16[1024,768]{1,0:T(8,128)(2,1)}, u32[]{:S(2)}, u32[]{:S(2)}) collective-permute-start(bf16[1024,768]{1,0:T(8,128)(2,1)} %get-tuple-element.160), channel_id=1, source_target_pairs={{0,1},{1,0},{2,3},{3,2},{4,5},{5,4},{6,7},{7,6},{8,9},{9,8},{10,11... | collective-permute-start | bytes 4718600 | tf_op jit(solution)/shard_map/ppermute | solution.py:974
  476.4 17.1 %collective-permute-start.34 = (bf16[4,128,256]{2,1,0:T(8,128)(2,1)S(1)}, bf16[4,128,256]{2,1,0:T(8,128)(2,1)S(1)}, u32[]{:S(2)}, u32[]{:S(2)}) collective-permute-start(bf16[4,128,256]{2,1,0:T(8,128)(2,1)S(1)} %fusion.20), channel_id=1, source_target_pairs={{0,4},{2,6},{4,0},{6,2},{8,12},{10,14},{12,8},{14,10},{16,20},{18,... | collective-permute-start | bytes 786440 | tf_op jit(solution)/shard_map/ppermute | solution.py:974
  493.5 23.6 %collective-permute-start.43 = (bf16[4,128,768]{2,1,0:T(8,128)(2,1)S(1)}, bf16[4,128,768]{2,1,0:T(8,128)(2,1)S(1)}, u32[]{:S(2)}, u32[]{:S(2)}) collective-permute-start(bf16[4,128,768]{2,1,0:T(8,128)(2,1)S(1)} %fusion.7), channel_id=1, source_target_pairs={{0,1},{1,0},{2,3},{3,2},{4,5},{5,4},{6,7},{7,6},{8,9},{9,8},{10,11... | collective-permute-start | bytes 2359304 | tf_op jit(solution)/shard_map/ppermute | solution.py:974
  502.3 45.2 %collective-permute-start.52 = (bf16[4,128,1024]{2,1,0:T(8,128)(2,1)S(1)}, bf16[4,128,1024]{2,1,0:T(8,128)(2,1)S(1)}, u32[]{:S(2)}, u32[]{:S(2)}) collective-permute-start(bf16[4,128,1024]{2,1,0:T(8,128)(2,1)S(1)} %fusion.12), channel_id=1, source_target_pairs={{0,4},{2,6},{4,0},{6,2},{8,12},{10,14},{12,8},{14,10},{16,20},{18,... | collective-permute-start | bytes 3145736 | tf_op jit(solution)/shard_map/ppermute | solution.py:974
  509.0 53.1 %collective-permute-start.54 = (bf16[1024,1024]{1,0:T(8,128)(2,1)S(1)}, bf16[1024,1024]{1,0:T(8,128)(2,1)S(1)}, u32[]{:S(2)}, u32[]{:S(2)}) collective-permute-start(bf16[1024,1024]{1,0:T(8,128)(2,1)S(1)} %fusion), channel_id=1, source_target_pairs={{0,1},{1,0},{2,3},{3,2},{4,5},{5,4},{6,7},{7,6},{8,9},{9,8},{10,11... | collective-permute-start | bytes 6291464 | tf_op jit(solution)/shard_map/ppermute | solution.py:974
  513.8 31.5 %collective-permute-start.45 = (bf16[4,128,768]{2,1,0:T(8,128)(2,1)S(1)}, bf16[4,128,768]{2,1,0:T(8,128)(2,1)S(1)}, u32[]{:S(2)}, u32[]{:S(2)}) collective-permute-start(bf16[4,128,768]{2,1,0:T(8,128)(2,1)S(1)} %fusion.14), channel_id=1, source_target_pairs={{0,4},{2,6},{4,0},{6,2},{8,12},{10,14},{12,8},{14,10},{16,20},{18,... | collective-permute-start | bytes 2359304 | tf_op jit(solution)/shard_map/ppermute | solution.py:974
  515.9 50.0 %collective-permute-start.50 = (bf16[4,128,1024]{2,1,0:T(8,128)(2,1)S(1)}, bf16[4,128,1024]{2,1,0:T(8,128)(2,1)S(1)}, u32[]{:S(2)}, u32[]{:S(2)}) collective-permute-start(bf16[4,128,1024]{2,1,0:T(8,128)(2,1)S(1)} %fusion.11), channel_id=1, source_target_pairs={{0,4},{2,6},{4,0},{6,2},{8,12},{10,14},{12,8},{14,10},{16,20},{18,... | collective-permute-start | bytes 3145736 | tf_op jit(solution)/shard_map/ppermute | solution.py:974
  517.2 30.3 %collective-permute-start.40 = (bf16[64,512]{1,0:T(8,128)(2,1)S(1)}, bf16[64,512]{1,0:T(8,128)(2,1)S(1)}, u32[]{:S(2)}, u32[]{:S(2)}) collective-permute-start(bf16[64,512]{1,0:T(8,128)(2,1)S(1)} %fusion.24), channel_id=1, source_target_pairs={{0,2},{2,0},{4,6},{6,4},{8,10},{10,8},{12,14},{14,12},{16,18},{18,... | collective-permute-start | bytes 196616 | tf_op jit(solution)/shard_map/ppermute | solution.py:974
  547.0 16.7 %collective-permute-start.46 = (bf16[2,128,1536]{2,1,0:T(8,128)(2,1)S(1)}, bf16[2,128,1536]{2,1,0:T(8,128)(2,1)S(1)}, u32[]{:S(2)}, u32[]{:S(2)}) collective-permute-start(bf16[2,128,1536]{2,1,0:T(8,128)(2,1)S(1)} %dynamic-slice_bitcast_fusion.1), channel_id=1, source_target_pairs={{0,8},{2,10},{4,12},{6,14},{8,0},{10,2},{12,4},{14,6},{16,24},{18,... | collective-permute-start | bytes 2359304 | tf_op jit(solution)/shard_map/ppermute | solution.py:974
  548.2 31.8 %collective-permute-start.53 = (bf16[4,128,1024]{2,1,0:T(8,128)(2,1)S(1)}, bf16[4,128,1024]{2,1,0:T(8,128)(2,1)S(1)}, u32[]{:S(2)}, u32[]{:S(2)}) collective-permute-start(bf16[4,128,1024]{2,1,0:T(8,128)(2,1)S(1)} %fusion.3), channel_id=1, source_target_pairs={{0,1},{1,0},{2,3},{3,2},{4,5},{5,4},{6,7},{7,6},{8,9},{9,8},{10,11... | collective-permute-start | bytes 3145736 | tf_op jit(solution)/shard_map/ppermute | solution.py:974
  562.8 20.9 %collective-permute-start.55 = (bf16[4,128,1024]{2,1,0:T(8,128)(2,1)S(1)}, bf16[4,128,1024]{2,1,0:T(8,128)(2,1)S(1)}, u32[]{:S(2)}, u32[]{:S(2)}) collective-permute-start(bf16[4,128,1024]{2,1,0:T(8,128)(2,1)S(1)} %fusion.13), channel_id=1, source_target_pairs={{0,4},{2,6},{4,0},{6,2},{8,12},{10,14},{12,8},{14,10},{16,20},{18,... | collective-permute-start | bytes 3145736 | tf_op jit(solution)/shard_map/ppermute | solution.py:974
  563.9 17.0 %collective-permute-start.47 = (bf16[128,1536]{1,0:T(8,128)(2,1)S(1)}, bf16[128,1536]{1,0:T(8,128)(2,1)S(1)}, u32[]{:S(2)}, u32[]{:S(2)}) collective-permute-start(bf16[128,1536]{1,0:T(8,128)(2,1)S(1)} %dynamic-slice_bitcast_fusion.5), channel_id=1, source_target_pairs={{0,16},{2,18},{4,20},{6,22},{8,24},{10,26},{12,28},{14,30},{16,0},... | collective-permute-start | bytes 1179656 | tf_op jit(solution)/shard_map/ppermute | solution.py:974
  584.8 23.2 %collective-permute-start.56 = (bf16[2,128,2048]{2,1,0:T(8,128)(2,1)S(1)}, bf16[2,128,2048]{2,1,0:T(8,128)(2,1)S(1)}, u32[]{:S(2)}, u32[]{:S(2)}) collective-permute-start(bf16[2,128,2048]{2,1,0:T(8,128)(2,1)S(1)} %dynamic-slice_bitcast_fusion), channel_id=1, source_target_pairs={{0,8},{2,10},{4,12},{6,14},{8,0},{10,2},{12,4},{14,6},{16,24},{18,... | collective-permute-start | bytes 3145736 | tf_op jit(solution)/shard_map/ppermute | solution.py:974
  608.5 23.2 %collective-permute-start.57 = (bf16[128,2048]{1,0:T(8,128)(2,1)S(1)}, bf16[128,2048]{1,0:T(8,128)(2,1)S(1)}, u32[]{:S(2)}, u32[]{:S(2)}) collective-permute-start(bf16[128,2048]{1,0:T(8,128)(2,1)S(1)} %dynamic-slice_bitcast_fusion.4), channel_id=1, source_target_pairs={{0,16},{2,18},{4,20},{6,22},{8,24},{10,26},{12,28},{14,30},{16,0},... | collective-permute-start | bytes 1572872 | tf_op jit(solution)/shard_map/ppermute | solution.py:974
  (41 other events, 416.8 us)

commit v3 on v2

--- a/solution.py
+++ b/solution.py
@@ -316,6 +316,7 @@
 BF = jnp.bfloat16
 F32 = jnp.float32
 ROWS = 256
+hint = 10
 
 
 def sds(shape, dtype=BF):
@@ -334,7 +335,7 @@
     return pl.BlockSpec((rows, cols), lambda i, s: (0, i))
 
 
-def run(body, grid, scal, ins, in_specs, out_shape, out_specs, scratch=(), flops=0, name=None):
+def run(body, grid, scal, ins, in_specs, out_shape, out_specs, scratch=(), flops=0, name=None, aliases=None):
     moved = sum(a.size * a.dtype.itemsize for a in ins)
     moved += sum(math.prod(o.shape) * jnp.dtype(o.dtype).itemsize for o in out_shape)
     return pl.pallas_call(
@@ -348,8 +349,9 @@
             scratch_shapes=list(scratch),
         ),
         compiler_params=CP,
-        cost_estimate=pl.CostEstimate(flops=int(flops), bytes_accessed=int(moved), transcendentals=0),
+        cost_estimate=pl.CostEstimate(flops=int(flops * hint), bytes_accessed=int(moved * hint), transcendentals=0),
         name=name,
+        input_output_aliases=aliases or {},
     )(scal, *ins)
 
 
@@ -362,10 +364,10 @@
     return u * s, s * (1.0 + u * (1.0 - s))
 
 
-def place(scr, s, pieces, base=0):
+def place(scr, s, pieces, base=0, table=0):
     rows = pieces[0].shape[0]
     for p in range(4):
-        scr[pl.ds(pl.multiple_of(base + s[p] * rows, rows), rows), :] = pieces[p][...]
+        scr[pl.ds(pl.multiple_of(base + s[table + p] * rows, rows), rows), :] = pieces[p][...]
 
 
 def piece_block(rows, cols, row_block):
@@ -418,19 +420,19 @@
     )
 
 
-def k_act_other(scal, x, pieces, rows, row_block, tn):
+def k_act_other(scal, x, pieces, table, tn):
     n, d = x.shape
-    cols = pieces[0].shape[1]
+    rows, cols = pieces[0].shape
 
     def body(s, x_ref, p0, p1, p2, p3, v_ref, sl_ref, w_scr):
-        place(w_scr, s, (p0, p1, p2, p3))
+        place(w_scr, s, (p0, p1, p2, p3), table=table)
         act, slope = silu_pair(matmul(x_ref[...], w_scr[...]))
         v_ref[...] = act.astype(BF)
         sl_ref[...] = slope.astype(BF)
 
     return run(
         body, (cols // tn,), scal, [x, *pieces],
-        [whole((n, d))] + [piece_block(rows, tn, row_block)] * 4,
+        [whole((n, d))] + [piece_block(rows, tn, 0)] * 4,
         [sds((n, cols)), sds((n, cols))],
         [cols_of(n, tn), cols_of(n, tn)],
         [pltpu.VMEM((d, tn), BF)],
@@ -458,15 +460,17 @@
     )
 
 
-def k_ema_forward(scal, normed, decay, coef, omega):
+def k_ema_forward(scal, normed, decay, coef, omega, first, count, before=None):
     n, d = normed.shape
     groups = d // 128
     tb = 128
 
-    def body(s, x_ref, dec_ref, cf_ref, om_ref, e_ref, sl_ref, st, xs, ys):
+    def body(s, x_ref, dec_ref, cf_ref, om_ref, *refs):
+        e_ref, sl_ref, st, xs, ys = refs[-5:]
+
         @pl.when(pl.program_id(0) == 0)
         def _():
-            st[...] = jnp.zeros_like(st)
+            st[...] = refs[0][...] if before else jnp.zeros_like(st)
 
         for g in range(groups):
             xs[pl.ds(g, tb, stride=groups), :] = x_ref[:, g * 128 : (g + 1) * 128].astype(F32)
@@ -496,34 +500,36 @@
             e_ref[:, g * 128 : (g + 1) * 128] = act.astype(BF)
             sl_ref[:, g * 128 : (g + 1) * 128] = slope.astype(BF)
 
-    return run(
-        body, (n // tb,), scal, [normed, decay, coef, omega],
-        [rows_of(d, tb), whole((H * groups, 128)), whole((H * groups, 128)), whole((groups, 128))],
-        [sds((n, d)), sds((n, d))],
-        [rows_of(d, tb)] * 2,
-        [pltpu.VMEM((H * groups, 128), F32), pltpu.VMEM((tb * groups, 128), F32), pltpu.VMEM((tb * groups, 128), F32)],
-        flops=20e9, name="ema_forward",
-    )
-
-
-def k_ema_backward(scal, normed, de_part, dz, slope, w_z, decay, coef, omega):
+    par = (H * groups, 128)
+    at = pl.BlockSpec((tb, d), lambda i, s: (first + i, 0))
+    more = list(before) if before else []
+    return run(
+        body, (count,), scal, [normed, decay, coef, omega, *more],
+        [at, whole(par), whole(par), whole((groups, 128))]
+        + ([whole(par), pl.BlockSpec(memory_space=pl.ANY), pl.BlockSpec(memory_space=pl.ANY)] if before else []),
+        [sds((n, d)), sds((n, d)), sds(par, F32)],
+        [at, at, pl.BlockSpec(par, lambda i, s: (0, 0))],
+        [pltpu.VMEM((tb * groups, 128), F32), pltpu.VMEM((tb * groups, 128), F32)],
+        flops=2.5e9 * count, name="ema_forward", aliases={6: 0, 7: 1} if before else {},
+    )
+
+
+def k_ema_backward(scal, normed, de_part, dz, slope, w_z, decay, coef, omega, first, count, before=None):
     n, d = normed.shape
     groups = d // 128
     tb = 128
     nb = n // tb
     half = H // 2
     gh = groups * half
-
     zw = dz.shape[1]
 
-    def body(s, x_ref, de_ref, z_ref, sl_ref, wz_ref, dec_ref, cf_ref, om_ref, o_ref, a_ref, b_ref, w_ref, back, deriv, xs, gs, ys):
+    def body(s, x_ref, de_ref, z_ref, sl_ref, wz_ref, dec_ref, cf_ref, om_ref, *refs):
+        o_ref, back, deriv, a_ref, b_ref, w_ref, xs, gs, ys = refs[-9:]
+
         @pl.when(pl.program_id(0) == 0)
         def _():
-            back[...] = jnp.zeros_like(back)
-            deriv[...] = jnp.zeros_like(deriv)
-            a_ref[...] = jnp.zeros_like(a_ref)
-            b_ref[...] = jnp.zeros_like(b_ref)
-            w_ref[...] = jnp.zeros_like(w_ref)
+            for i, ref in enumerate((back, deriv, a_ref, b_ref, w_ref)):
+                ref[...] = refs[i][...] if before else jnp.zeros_like(ref)
 
         d_e = (de_ref[...] + col_inner(z_ref[...], wz_ref[...])) * sl_ref[...].astype(F32)
         for g in range(groups):
@@ -531,8 +537,8 @@
             gs[pl.ds(g, tb, stride=groups), :] = d_e[:, g * 128 : (g + 1) * 128]
 
         for part in range(2):
-            first = part * gh
-            at = [slice(first + k * groups, first + (k + 1) * groups) for k in range(half)]
+            low = part * gh
+            at = [slice(low + k * groups, low + (k + 1) * groups) for k in range(half)]
             dec = [dec_ref[a, :] for a in at]
 
             def steps(b, carry, part=part, at=at, dec=dec):
@@ -573,16 +579,21 @@
         for g in range(groups):
             o_ref[:, g * 128 : (g + 1) * 128] = ys[pl.ds(g, tb, stride=groups), :]
 
-    back_rows = pl.BlockSpec((tb, d), lambda i, s: (nb - 1 - i, 0))
+    top = nb - 1 - first
+    back_rows = pl.BlockSpec((tb, d), lambda i, s: (top - i, 0))
     par = (H * groups, 128)
     const = pl.BlockSpec(par, lambda i, s: (0, 0))
-    return run(
-        body, (nb,), scal, [normed, de_part, dz, slope, w_z, decay, coef, omega],
-        [back_rows, back_rows, pl.BlockSpec((tb, zw), lambda i, s: (nb - 1 - i, 0)), back_rows, whole((d, zw)), whole(par), whole(par), whole((groups, 128))],
-        [sds((n, d), F32), sds(par, F32), sds(par, F32), sds((groups, 128), F32)],
-        [back_rows, const, const, pl.BlockSpec((groups, 128), lambda i, s: (0, 0))],
-        [pltpu.VMEM(par, F32), pltpu.VMEM(par, F32)] + [pltpu.VMEM((tb * groups, 128), F32)] * 3,
-        flops=40e9, name="ema_backward",
+    small = (groups, 128)
+    more = [*before[1:], before[0]] if before else []
+    return run(
+        body, (count,), scal, [normed, de_part, dz, slope, w_z, decay, coef, omega, *more],
+        [back_rows, back_rows, pl.BlockSpec((tb, zw), lambda i, s: (top - i, 0)), back_rows, whole((d, zw)),
+         whole(par), whole(par), whole(small)]
+        + ([whole(par)] * 4 + [whole(small), pl.BlockSpec(memory_space=pl.ANY)] if before else []),
+        [sds((n, d), F32)] + [sds(par, F32)] * 4 + [sds(small, F32)],
+        [back_rows, const, const, const, const, pl.BlockSpec(small, lambda i, s: (0, 0))],
+        [pltpu.VMEM((tb * groups, 128), F32)] * 3,
+        flops=5e9 * count, name="ema_backward", aliases={14: 0} if before else {},
     )
 
 
@@ -619,11 +630,11 @@
     )
 
 
-def k_gate(scal, gated_own, gated_oth, ema_low, tokens, u_own, h_own, f_own, packs, rows):
+def k_gate(scal, gated_own, gated_oth, ema_low, tokens, u_own, h_own, f_own, packs_u, packs_h):
     n, d = tokens.shape
     half = u_own.shape[0]
     ch = h_own.shape[0]
-    ru, rh = rows
+    ru, rh = packs_u[0].shape[0], packs_h[0].shape[0] // 2
 
     def body(s, go, gt, e_ref, x_ref, uo, ho, fo, u0, u1, u2, u3, h0, h1, h2, h3, f0, f1, f2, f3,
              mix_ref, low_ref, a_ref, b_ref, up_ref, u_scr, h_scr, f_scr):
@@ -634,8 +645,8 @@
             oth = s[7] * ch
             h_scr[pl.ds(own, ch), :] = ho[...]
             f_scr[pl.ds(own, ch), :] = fo[...]
-            place(h_scr, s, (h0, h1, h2, h3), oth)
-            place(f_scr, s, (f0, f1, f2, f3), oth)
+            place(h_scr, s, (h0, h1, h2, h3), oth, 8)
+            place(f_scr, s, (f0, f1, f2, f3), oth, 8)
 
         h_pre = matmul(go[...], uo[...]) + matmul(gt[...], u_scr[...]) + matmul(e_ref[...], h_scr[...])
         f_pre = matmul(e_ref[...], f_scr[...])
@@ -649,9 +660,9 @@
         b_ref[...] = ((act - x) * update * (1.0 - update)).astype(BF)
         up_ref[...] = (1.0 - update).astype(BF)
 
-    ins = [gated_own, gated_oth, ema_low, tokens, u_own, h_own, f_own, *packs, *packs, *packs]
+    ins = [gated_own, gated_oth, ema_low, tokens, u_own, h_own, f_own, *packs_u, *packs_h, *packs_h]
     specs = [rows_of(half), rows_of(half), rows_of(d), rows_of(d), whole((half, d)), whole((ch, d)), whole((ch, d))]
-    specs += [piece_whole(ru, d, 0)] * 4 + [piece_whole(rh, d, ru // rh)] * 4 + [piece_whole(rh, d, ru // rh + 1)] * 4
+    specs += [piece_whole(ru, d, 0)] * 4 + [piece_whole(rh, d, 0)] * 4 + [piece_whole(rh, d, 1)] * 4
     return run(
         body, (n // ROWS,), scal, ins, specs,
         [sds((n, d), F32), sds((n, d)), sds((n, d)), sds((n, d)), sds((n, d))],
@@ -661,110 +672,89 @@
     )
 
 
-def k_ffn(scal, lowered, cot, up, down, acc, grad, pieces):
+def k_ffn(scal, lowered, cot, up, down, part):
     n, d = lowered.shape
-    cols = up[0].shape[1]
-    tn = cols // 4
-    last = grad is not None
-    first_in = [acc, grad] if last else [acc]
+    pieces = len(up) > 1
+    tn = up[0].shape[1] // 4
 
     def body(s, low_ref, c_ref, *refs):
         step = pl.program_id(0)
-        nu = 4 if pieces else 1
-        ups, downs, refs = refs[:nu], refs[nu : 2 * nu], refs[2 * nu :]
-        ins, refs = refs[: len(first_in)], refs[len(first_in) :]
-        if last:
-            out_ref, gl_ref, sent_ref, kept_ref, acc_ref, u_scr = refs
-        else:
-            acc_ref, gl_ref, sent_ref, kept_ref, u_scr = refs
-
-        @pl.when(step == 0)
-        def _():
-            acc_ref[...] = ins[0][...]
-            gl_ref[...] = ins[1][...] if last else jnp.zeros_like(gl_ref)
-
+        nu, nd = len(up), len(down)
+        ups, downs = refs[:nu], refs[nu : nu + nd]
+        out_ref, gl_ref, grads, acc, gl, u_scr = refs[nu + nd :]
         if pieces:
             place(u_scr, s, ups)
             wu = u_scr
         else:
             wu = ups[0]
 
-        def work(wd, grads):
+        def work(wd, i):
             act, slope = silu_pair(matmul(low_ref[...], wu[...]))
             hid = act.astype(BF)
-            acc_ref[...] += matmul(hid, wd[...])
+            out = matmul(hid, wd[...])
             du = (col_inner(c_ref[...], wd[...]) * slope).astype(BF)
-            gl_ref[...] += col_inner(du, wu[...])
+            back = col_inner(du, wu[...])
+            if i == 0:
+                acc[...] = out
+                gl[...] = back
+            else:
+                out_ref[...] = (acc[...] + out).astype(BF)
+                gl_ref[...] = (gl[...] + back).astype(BF)
             grads[0] = row_inner(c_ref[...], hid).astype(BF)
             grads[1] = row_inner(low_ref[...], du).astype(BF)
 
-        if pieces:
-            for i, p in enumerate((2, 3, 0, 1)):
-
-                @pl.when(step == i)
-                def _(i=i, p=p):
-                    work(downs[p], sent_ref if i < 2 else kept_ref)
-        else:
-
-            @pl.when(step < 2)
-            def _():
-                work(downs[0], sent_ref)
-
-            @pl.when(step >= 2)
-            def _():
-                work(downs[0], kept_ref)
-
-        if last:
-
-            @pl.when(step == 3)
-            def _():
-                out_ref[...] = acc_ref[...].astype(BF)
-
+        for i in range(2):
+
+            @pl.when(step == i)
+            def _(i=i):
+                work(downs[i % nd], i)
+
+    first = 8 + 2 * part
     if pieces:
-        specs = [pl.BlockSpec((d // 4, tn), lambda i, s: (0, s[(i + 2) % 4]))] * 4 + [whole((tn, d))] * 4
+        down = down[2 * part : 2 * part + 2]
+        specs = [pl.BlockSpec((d // 4, tn), lambda i, s: (0, s[first + i]))] * 4 + [whole((tn, d))] * 2
     else:
         specs = [
-            pl.BlockSpec((d, tn), lambda i, s: (0, s[(i + 2) % 4])),
-            pl.BlockSpec((tn, d), lambda i, s: (s[(i + 2) % 4], 0)),
+            pl.BlockSpec((d, tn), lambda i, s: (0, s[first + i])),
+            pl.BlockSpec((tn, d), lambda i, s: (s[first + i], 0)),
         ]
     still = pl.BlockSpec((n, d), lambda i, s: (0, 0))
-    pair = (2, d, tn)
-    sent = pl.BlockSpec(pair, lambda i, s: (0, 0, s[2 + jnp.minimum(i, 1)] % 2))
-    kept = pl.BlockSpec(pair, lambda i, s: (0, 0, s[jnp.maximum(i - 2, 0)] % 2))
-    return run(
-        body, (4,), scal, [lowered, cot, *up, *down, *first_in],
-        [whole((n, d)), whole((n, d))] + specs + [whole((n, d))] * len(first_in),
-        [sds((n, d), BF if last else F32), sds((n, d), F32), sds((2, d, cols // 2)), sds((2, d, cols // 2))],
-        [still, still, sent, kept],
-        ([pltpu.VMEM((n, d), F32)] if last else []) + [pltpu.VMEM((d, tn), BF)],
-        flops=12 * n * d * cols, name="ffn_other" if last else "ffn_own",
-    )
-
-
-def k_mid_back(scal, dl, cot, mixed, fac_h, fac_f, keep, g_own, g_oth, m_own, m_oth,
-               u_own, wg_own, h_own, f_own, packs_g, packs_h, rows):
+    return run(
+        body, (2,), scal, [lowered, cot, *up, *down],
+        [whole((n, d)), whole((n, d))] + specs,
+        [sds((n, d)), sds((n, d)), sds((2, d, 2 * tn))],
+        [still, still, pl.BlockSpec((2, d, tn), lambda i, s: (0, 0, s[first + i] % 2))],
+        [pltpu.VMEM((n, d), F32), pltpu.VMEM((n, d), F32), pltpu.VMEM((d, tn), BF)],
+        flops=24 * n * d * tn, name="ffn",
+    )
+
+
+def k_mid_back(scal, dls, accs, cot, mixed, fac_h, fac_f, keep, g_own, g_oth, m_own, m_oth,
+               u_own, wg_own, h_own, f_own, packs_g, packs_u, packs_h):
     n, d = cot.shape
     half = u_own.shape[0]
     ch = h_own.shape[0]
-    ru, rh = rows
+    ru, rh = packs_u[0].shape[0], packs_h[0].shape[0] // 2
     rg = packs_g[0].shape[0]
 
-    def body(s, dl_ref, c_ref, x_ref, a_ref, b_ref, k_ref, go, gt, mo, mt, uo, wo, ho, fo,
+    def body(s, l0, l1, l2, l3, o0, o1, o2, o3, c_ref, x_ref, a_ref, b_ref, k_ref, go, gt, mo, mt, uo, wo, ho, fo,
              w0, w1, w2, w3, u0, u1, u2, u3, h0, h1, h2, h3, f0, f1, f2, f3,
-             dh_ref, df_ref, dir_ref, ao, at, do, dt, de_ref, u_scr, w_scr, h_scr, f_scr):
+             out_ref, dh_ref, df_ref, dir_ref, ao, at, do, dt, de_ref, u_scr, w_scr, h_scr, f_scr):
         @pl.when(pl.program_id(0) == 0)
         def _():
             place(u_scr, s, (u0, u1, u2, u3))
-            place(w_scr, s, (w0, w1, w2, w3))
+            place(w_scr, s, (w0, w1, w2, w3), table=8)
             own = pl.multiple_of(s[6] * ch, ch)
             oth = s[7] * ch
             h_scr[pl.ds(own, ch), :] = ho[...]
             f_scr[pl.ds(own, ch), :] = fo[...]
-            place(h_scr, s, (h0, h1, h2, h3), oth)
-            place(f_scr, s, (f0, f1, f2, f3), oth)
-
-        dl = dl_ref[...]
+            place(h_scr, s, (h0, h1, h2, h3), oth, 8)
+            place(f_scr, s, (f0, f1, f2, f3), oth, 8)
+
+        dl = (l0[...].astype(F32) + l1[...].astype(F32)) + (l2[...].astype(F32) + l3[...].astype(F32))
+        out = (o0[...].astype(F32) + o1[...].astype(F32)) + (o2[...].astype(F32) + o3[...].astype(F32))
         m = x_ref[...]
+        out_ref[...] = (m + out).astype(BF)
         r = lax.rsqrt(jnp.mean(m * m, axis=-1, keepdims=True) + norm_eps)
         n2 = m * r
         dm = c_ref[...].astype(F32) + r * (dl - n2 * jnp.mean(dl * n2, axis=-1, keepdims=True))
@@ -782,16 +772,16 @@
             de = de + col_inner(low, w[...])
         de_ref[...] = de
 
-    ins = [dl, cot, mixed, fac_h, fac_f, keep, g_own, g_oth, m_own, m_oth, u_own, wg_own, h_own, f_own]
-    ins += [*packs_g, *packs_h, *packs_h, *packs_h]
-    specs = [rows_of(d)] * 6 + [rows_of(half)] * 4
+    ins = [*dls, *accs, cot, mixed, fac_h, fac_f, keep, g_own, g_oth, m_own, m_oth, u_own, wg_own, h_own, f_own]
+    ins += [*packs_g, *packs_u, *packs_h, *packs_h]
+    specs = [rows_of(d)] * 13 + [rows_of(half)] * 4
     specs += [whole((half, d)), whole((d, half)), whole((ch, d)), whole((ch, d))]
     specs += [piece_whole(rg, half, 0)] * 4 + [piece_whole(ru, d, 0)] * 4
-    specs += [piece_whole(rh, d, ru // rh)] * 4 + [piece_whole(rh, d, ru // rh + 1)] * 4
+    specs += [piece_whole(rh, d, 0)] * 4 + [piece_whole(rh, d, 1)] * 4
     return run(
         body, (n // ROWS,), scal, ins, specs,
-        [sds((n, d))] * 3 + [sds((n, half))] * 4 + [sds((n, d), F32)],
-        [rows_of(d)] * 3 + [rows_of(half)] * 4 + [rows_of(d)],
+        [sds((n, d))] * 4 + [sds((n, half))] * 4 + [sds((n, d), F32)],
+        [rows_of(d)] * 4 + [rows_of(half)] * 4 + [rows_of(d)],
         [pltpu.VMEM((half, d), BF), pltpu.VMEM((d, half), BF), pltpu.VMEM((2 * ch, d), BF), pltpu.VMEM((2 * ch, d), BF)],
         flops=2 * n * d * (4 * half + 4 * ch), name="mid_back",
     )
@@ -862,8 +852,9 @@
     )
 
 
-def k_input_back(scal, dv_own, dv_oth, w_own, packs, rp, d_sig, tokens, direct):
+def k_input_back(scal, dv_own, dv_oth, w_own, packs, d_sig, tokens, direct):
     n, d = tokens.shape
+    rp = packs[0].shape[0]
     half = dv_own.shape[1]
 
     def body(s, vo, vt, wo, w0, w1, w2, w3, sg, x_ref, dir_ref, o_ref, w_scr):
@@ -989,11 +980,15 @@
     core = me % 2
     x_pos = (me // 2) % 2
     z_pos = me // 4
-    k0 = core * 2 + x_pos
-    scal = jnp.stack([k0, k0 ^ 1, k0 ^ 2, k0 ^ 3, core, 1 - core, t, 1 - t])
-
-    def after(*values):
-        return lax.optimization_barrier((scal, *values))[0]
+    kx = core * 2 + x_pos
+    kz = core * 2 + z_pos % 2
+    scal = jnp.stack([kx, kx ^ 1, kx ^ 2, kx ^ 3, core, 1 - core, t, 1 - t, kz, kz ^ 1, kz ^ 2, kz ^ 3])
+
+    def held(values, *deps):
+        return lax.optimization_barrier((values, deps))[0]
+
+    def after(*deps):
+        return held(scal, *deps)
 
     def over_core(v):
         return swap(v, "dp", 1, dp_size)
@@ -1001,30 +996,21 @@
     def over_x(v):
         return swap(v, "dp", 2, dp_size)
 
+    def over_z(v):
+        return swap(v, "dp", 4, dp_size)
+
     def over_tensor(v):
         return swap(v, "tensor", 1, 2)
 
-    def my_rows(w):
+    def my_rows(w, k):
         rows = w.shape[0] // 4
-        return lax.dynamic_slice_in_dim(w, k0 * rows, rows, 0)
-
-    def fetch(values):
-        by_y = over_tensor(values)
-        by_x = over_x(by_y)
-        return by_y, by_x, over_core(by_y), over_core(by_x)
+        return lax.dynamic_slice_in_dim(w, k * rows, rows, 0)
 
     own_params = jnp.concatenate(
         [a.T for a in (alpha_logit, delta_logit, ema_beta, ema_eta)] + [ema_omega[None]], axis=0
     )
     oth_params = over_tensor(own_params)
-    pv = fetch(my_rows(w_v))
-    pg = fetch(my_rows(w_gamma))
-    ph = fetch(jnp.concatenate([my_rows(u_h), my_rows(w_h), my_rows(w_phi)], axis=0))
-    pu = fetch(my_rows(w_up))
-    pd = fetch(my_rows(w_down))
-    rv = w_v.shape[0] // 4
-    rh = (u_h.shape[0] // 4, w_h.shape[0] // 4)
-
+    pv = [over_tensor(my_rows(w_v, kx))]
     params = jnp.where(
         t == 0,
         jnp.concatenate([own_params, oth_params], axis=1),
@@ -1037,42 +1023,41 @@
     omega = params[4 * H].reshape(-1, 128)
 
     normed, v_own, vs_own = k_value_own(scal, tokens, w_v)
-    ema_low, e_slope = k_ema_forward(after(v_own), normed, decay, coef, omega)
+    pg = [over_tensor(held(my_rows(w_gamma, kz), v_own))]
+    blocks = n // 128
+    ema_a = k_ema_forward(after(v_own), normed, decay, coef, omega, 0, blocks // 2)
+    pv.append(over_x(held(pv[0], ema_a[0])))
+    ema_low, e_slope, state = k_ema_forward(
+        after(ema_a[0]), normed, decay, coef, omega, blocks // 2, blocks // 2, (ema_a[2], ema_a[0], ema_a[1])
+    )
+    pg.append(over_z(held(pg[0], state)))
+    pu = [over_tensor(held(my_rows(u_h, kx), state))]
     z_pre, query, key = k_query_key(scal, ema_low, w_z, qk_gain, qk_bias)
+    pv += [over_core(v) for v in held((pv[0], pv[1]), query)]
     g_own, gs_own = k_act_own(after(query), ema_low, w_gamma, 512)
-    v_oth, vs_oth = k_act_other(after(g_own), normed, pv, rv, 0, 512)
-    g_oth, gs_oth = k_act_other(after(v_oth), ema_low, pg, rv, 0, 512)
+    pg += [over_core(v) for v in held((pg[0], pg[1]), g_own)]
+    pu.append(over_x(held(pu[0], g_own)))
+    ph = [over_tensor(held(jnp.concatenate([my_rows(w_h, kz), my_rows(w_phi, kz)], axis=0), g_own))]
+    v_oth, vs_oth = k_act_other(after(g_own), normed, pv, 0, 512)
+    pup = [over_tensor(held(my_rows(w_up, kx), v_oth))]
+    g_oth, gs_oth = k_act_other(after(v_oth), ema_low, pg, 8, 512)
+    ph.append(over_z(held(ph[0], g_oth)))
+    pu += [over_core(v) for v in held((pu[0], pu[1]), g_oth)]
     gated_own, gated_oth, m_own, m_oth, probs = k_attend(
-        scal, query, key, v_own, v_oth, g_own, g_oth, gs_own, gs_oth
-    )
+        after(g_oth), query, key, v_own, v_oth, g_own, g_oth, gs_own, gs_oth
+    )
+    ph += [over_core(v) for v in held((ph[0], ph[1]), probs)]
+    pdn = [over_tensor(held(my_rows(w_down, kz), probs))]
     mixed, lowered, fac_h, fac_f, keep = k_gate(
-        scal, gated_own, gated_oth, ema_low, tokens, u_h, w_h, w_phi, ph, rh
-    )
-    acc, dl, ffn_so, ffn_ko = k_ffn(scal, lowered, cotangent, [w_up], [w_down], mixed, None, False)
-    ffn_go = over_core(ffn_so)
-    output, dl, ffn_st, ffn_kt = k_ffn(after(acc), lowered, cotangent, pu, pd, acc, dl, True)
-    ffn_gt = over_core(ffn_st)
-    dh, df, direct, da_own, da_oth, dg_own, dg_oth, de_part = k_mid_back(
-        scal, dl, cotangent, mixed, fac_h, fac_f, keep, g_own, g_oth, m_own, m_oth,
-        u_h, w_gamma, w_h, w_phi, pg, ph, rh,
-    )
-    mid_sent = k_weight_mid(after(dh), ema_low, dh, df, gated_own, gated_oth, dg_own, dg_oth, 5)
-    mid_got = [over_core(v) for v in mid_sent]
-    dv_own, dv_oth = k_value_back(after(*mid_sent), probs, da_own, da_oth, vs_own, vs_oth)
-    val_sent = k_weight_value(after(dv_own), normed, dv_own, dv_oth, 5)
-    val_got = [over_core(v) for v in val_sent]
-    mid_own, mid_oth = k_weight_mid(
-        after(*val_sent), ema_low, dh, df, gated_own, gated_oth, dg_own, dg_oth, 4, mid_got
-    )
-    dz, stats = k_score_back(
-        after(mid_own), probs, da_own, da_oth, v_own, v_oth, query, key, z_pre, qk_gain
-    )
-    val_own, val_oth = k_weight_value(after(dz), normed, dv_own, dv_oth, 4, val_got)
-    z_own = k_weight(after(dz), ema_low, dz, lambda s: 0, dz.shape[1], dz.shape[1])
-    d_sig, sum_a, sum_b, sum_w = k_ema_backward(
-        after(val_own, z_own), normed, de_part, dz, e_slope, w_z, decay, coef, omega
-    )
-    input_grad = k_input_back(scal, dv_own, dv_oth, w_v, pv, rv, d_sig, tokens, direct)
+        after(probs), gated_own, gated_oth, ema_low, tokens, u_h, w_h, w_phi, pu, ph
+    )
+    pup.append(over_x(held(pup[0], mixed)))
+    acc0, dl0, sent_o = k_ffn(after(mixed), lowered, cotangent, [w_up], [w_down], 1)
+    pdn.append(over_z(held(pdn[0], acc0)))
+    got_o = over_core(sent_o)
+    acc1, dl1, kept_o = k_ffn(after(acc0), lowered, cotangent, [w_up], [w_down], 0)
+    pup += [over_core(v) for v in held((pup[0], pup[1]), acc1)]
+    pdn += [over_core(v) for v in held((pdn[0], pdn[1]), acc1)]
 
     def add(*values):
         total = values[0].astype(F32)
@@ -1080,73 +1065,175 @@
             total = total + v.astype(F32)
         return total.astype(BF)
 
-    def split_x(v):
-        v = v.reshape(4, 2, d // 8, v.shape[-1])
-        return pick(v, x_pos, 1), pick(v, 1 - x_pos, 1)
-
-    def x_then_y(own_terms, oth_terms):
-        own = [split_x(v) for v in own_terms]
-        oth = [split_x(v) for v in oth_terms]
-        got_own = over_x(add(*[v[1] for v in own]))
-        got_oth = over_x(add(*[v[1] for v in oth]))
-        got = over_tensor(add(*[v[0] for v in oth], got_oth))
-        return [*[v[0] for v in own], got_own, got]
-
-    def y_then_x(own_terms, oth_terms):
-        got = over_tensor(add(*oth_terms))
-        own = [split_x(v) for v in [*own_terms, got]]
-        got = over_x(add(*[v[1] for v in own]))
-        return [*[v[0] for v in own], got]
-
-    def over_z(terms):
-        total = add(*terms)
-        by_z = total.reshape(2, 2, d // 8, total.shape[-1])
-        got = swap(pick(by_z, 1 - z_pos % 2, 1), "dp", 4, dp_size)
-        pair = add(pick(by_z, z_pos % 2, 1), got)
-        got = swap(pick(pair, 1 - z_pos // 2, 0), "dp", 8, dp_size)
-        return pick(pair, z_pos // 2, 0).astype(F32) + got.astype(F32)
-
-    def finish(total):
-        by_core = total.reshape(2, d // 16, total.shape[1])
-        got = over_core(pick(by_core, 1 - core, 0).astype(BF)).astype(F32)
-        kept = pick(by_core, core, 0)
-        return jnp.where(core == 0, jnp.stack([kept, got]), jnp.stack([got, kept]))
-
-    def joined(pair):
-        return jnp.concatenate([pair[0], pair[1]], axis=1)
-
-    down_terms = x_then_y([ffn_ko[0], ffn_go[0]], [ffn_kt[0], ffn_gt[0]])
-    up_terms = y_then_x([ffn_ko[1], ffn_go[1]], [ffn_kt[1], ffn_gt[1]])
-    ffn = finish(over_z([jnp.concatenate([add(*down_terms), add(*up_terms)], axis=-1)]))
-    c = ffn.shape[2] // 2
-    down_t, up = joined(ffn[:, :, :c]), joined(ffn[:, :, c:])
-
+    def x_mine(v):
+        return pick(v.reshape(4, 2, d // 8, v.shape[-1]), x_pos, 1)
+
+    def x_theirs(v):
+        return pick(v.reshape(4, 2, d // 8, v.shape[-1]), 1 - x_pos, 1)
+
+    def z_first(terms):
+        by_z = [v.reshape(2, 2, d // 8, v.shape[-1]) for v in terms]
+        send = add(*[pick(v, 1 - z_pos % 2, 1) for v in by_z])
+        return send, [pick(v, z_pos % 2, 1) for v in by_z]
+
+    def z_second(terms):
+        send = add(*[pick(v, 1 - z_pos // 2, 0) for v in terms])
+        return send, [pick(v, z_pos // 2, 0) for v in terms]
+
+    def over_z2(v):
+        return swap(v, "dp", 8, dp_size)
+
+    def core_rows(terms):
+        by_core = [v.reshape(2, d // 16, v.shape[-1]) for v in terms]
+        send = add(*[pick(v, 1 - core, 0) for v in by_core])
+        return send, [pick(v, core, 0) for v in by_core]
+
+    def total(terms):
+        value = terms[0].astype(F32)
+        for v in terms[1:]:
+            value = value + v.astype(F32)
+        return value
+
+    def joined(kept, got):
+        kept, got = kept.astype(F32), got.astype(F32)
+        return jnp.where(
+            core == 0, jnp.concatenate([kept, got], axis=1), jnp.concatenate([got, kept], axis=1)
+        )
+
+    dn_x1 = add(x_theirs(kept_o[0]), x_theirs(got_o[0]))
+    dn_got_x1 = over_x(dn_x1)
+    acc2, dl2, sent_t = k_ffn(after(acc1, dn_x1), lowered, cotangent, pup, pdn, 1)
+    got_t = over_core(sent_t)
+    acc3, dl3, kept_t = k_ffn(after(acc2), lowered, cotangent, pup, pdn, 0)
+    dn_x2 = add(x_theirs(kept_t[0]), x_theirs(got_t[0]))
+    up_y1 = add(kept_t[1], got_t[1])
+    dn_got_x2 = over_x(dn_x2)
+    up_got_y = over_tensor(up_y1)
+    output, dh, df, direct, da_own, da_oth, dg_own, dg_oth, de_part = k_mid_back(
+        after(acc3, dn_x2, up_y1), [dl0, dl1, dl2, dl3], [acc0, acc1, acc2, acc3], cotangent, mixed, fac_h, fac_f, keep,
+        g_own, g_oth, m_own, m_oth, u_h, w_gamma, w_h, w_phi, pg, pu, ph,
+    )
+    dn_got_x2 = held(dn_got_x2, dh)
+    dn_y = add(x_mine(kept_t[0]), x_mine(got_t[0]), dn_got_x2)
+    dn_got_y = over_tensor(dn_y)
+    mid_sent = k_weight_mid(after(dh, dn_y), ema_low, dh, df, gated_own, gated_oth, dg_own, dg_oth, 5)
+    mid_got = [over_core(v) for v in mid_sent]
+    dv_own, dv_oth = k_value_back(after(*mid_sent), probs, da_own, da_oth, vs_own, vs_oth)
+    up_got_y = held(up_got_y, dv_own)
+    up_terms = [kept_o[1], got_o[1], up_got_y]
+    up_x = add(*[x_theirs(v) for v in up_terms])
+    up_got_x = over_x(up_x)
+    val_sent = k_weight_value(after(dv_own, up_x), normed, dv_own, dv_oth, 5)
+    val_got = [over_core(v) for v in val_sent]
+    mid_own, mid_oth = k_weight_mid(
+        after(*val_sent), ema_low, dh, df, gated_own, gated_oth, dg_own, dg_oth, 4, mid_got
+    )
     c = mid_own.shape[1] // 2
-    mid_a = x_then_y([mid_own[:, :c]], [mid_oth[:, :c]])
-    mid_b = y_then_x([mid_own[:, c:]], [mid_oth[:, c:]])
-    mid = finish(over_z([jnp.concatenate([add(*mid_a), add(*mid_b)], axis=-1)]))
-    half = gated_own.shape[1] // 2
-    uh_t, gamma = joined(mid[:, :, :half]), joined(mid[:, :, half : 2 * half])
-    wh_t = joined(mid[:, :, 2 * half : 2 * half + d // 4])
-    phi_t = joined(mid[:, :, 2 * half + d // 4 :])
-
-    c = half // 2
-    z_sum = add(z_own, over_core(z_own))
-    z_sum = add(z_sum, over_tensor(z_sum))
-    val_a = x_then_y([val_own[:, :c]], [val_oth[:, :c]])
-    z_mine, z_sent = split_x(z_sum)
-    val_b = y_then_x([val_own[:, c:]], [val_oth[:, c:]])
-    z_total = add(z_mine, over_x(z_sent))
-    val = over_z([jnp.concatenate([add(*val_a), add(*val_b), z_total], axis=-1)])
-    z_grad = pick(val[:, half:].reshape(2, d // 16, -1), core, 0)
-    value = joined(finish(val[:, :half]))
-
+    ma_own, ma_oth, mb_own, mb_oth = mid_own[:, :c], mid_oth[:, :c], mid_own[:, c:], mid_oth[:, c:]
+    ma_x = (x_theirs(ma_own), x_theirs(ma_oth))
+    ma_got_x = [over_x(v) for v in ma_x]
+    mb_got_y = over_tensor(mb_oth)
+    dz, stats = k_score_back(
+        after(mid_own, ma_x), probs, da_own, da_oth, v_own, v_oth, query, key, z_pre, qk_gain
+    )
+    dn_got_y, up_got_x = held((dn_got_y, up_got_x), dz)
+    ffn_terms = [
+        jnp.concatenate([x_mine(a), x_mine(b)], axis=-1)
+        for a, b in ((kept_o[0], kept_o[1]), (got_o[0], got_o[1]))
+    ] + [
+        jnp.concatenate([dn_got_x1, x_mine(up_got_y)], axis=-1),
+        jnp.concatenate([dn_got_y, up_got_x], axis=-1),
+    ]
+    ffn_z1, ffn_terms = z_first(ffn_terms)
+    ffn_got_z1 = over_z(ffn_z1)
+    z_own = k_weight(after(dz, ffn_z1), ema_low, dz, lambda s: 0, dz.shape[1], dz.shape[1])
+    z_got = over_core(z_own)
+    val_own, val_oth = k_weight_value(after(z_own), normed, dv_own, dv_oth, 4, val_got)
+    c = val_own.shape[1] // 2
+    va_own, va_oth, vb_own, vb_oth = val_own[:, :c], val_oth[:, :c], val_own[:, c:], val_oth[:, c:]
+    va_x = (x_theirs(va_own), x_theirs(va_oth))
+    va_got_x = [over_x(v) for v in va_x]
+    z_sum = add(z_own, z_got)
+    vb_y = jnp.concatenate([vb_oth, z_sum], axis=1)
+    vb_got_y = over_tensor(vb_y)
+    quarter = blocks // 4
+    eb = k_ema_backward(
+        after(val_own, va_x, vb_y), normed, de_part, dz, e_slope, w_z, decay, coef, omega, 0, quarter
+    )
+    ma_got_x, mb_got_y = held((ma_got_x, mb_got_y), eb[1])
+    ma_y = add(x_mine(ma_oth), ma_got_x[1])
+    mb_x = add(x_theirs(mb_own), x_theirs(mb_got_y))
+    ma_got_y = over_tensor(ma_y)
+    mb_got_x = over_x(mb_x)
+    eb = k_ema_backward(
+        after(eb[1], ma_y, mb_x), normed, de_part, dz, e_slope, w_z, decay, coef, omega, quarter, quarter, eb
+    )
+    ffn_got_z1 = held(ffn_got_z1, eb[1])
+    ffn_z2, ffn_terms = z_second([*ffn_terms, ffn_got_z1])
+    ffn_got_z2 = over_z2(ffn_z2)
+    va_got_x, vb_got_y = held((va_got_x, vb_got_y), eb[1])
+    va_y = add(x_mine(va_oth), va_got_x[1])
+    vb_mine = jnp.concatenate([vb_own, z_sum], axis=1)
+    vb_x = add(x_theirs(vb_mine), x_theirs(vb_got_y))
+    va_got_y = over_tensor(va_y)
+    vb_got_x = over_x(vb_x)
+    eb = k_ema_backward(
+        after(eb[1], ffn_z2, va_y, vb_x), normed, de_part, dz, e_slope, w_z, decay, coef, omega, 2 * quarter, quarter, eb
+    )
+    ma_got_y, mb_got_x = held((ma_got_y, mb_got_x), eb[1])
+    mid_terms = [
+        jnp.concatenate([x_mine(ma_own), x_mine(mb_own)], axis=-1),
+        jnp.concatenate([ma_got_x[0], x_mine(mb_got_y)], axis=-1),
+        jnp.concatenate([ma_got_y, mb_got_x], axis=-1),
+    ]
+    mid_z1, mid_terms = z_first(mid_terms)
+    mid_got_z1 = over_z(mid_z1)
+    eb = k_ema_backward(
+        after(eb[1], mid_z1), normed, de_part, dz, e_slope, w_z, decay, coef, omega, 3 * quarter, quarter, eb
+    )
+    d_sig, _, _, sum_a, sum_b, sum_w = eb
+    va_got_y, vb_got_x = held((va_got_y, vb_got_x), sum_a)
+    val_terms = [
+        jnp.concatenate([x_mine(va_own), x_mine(vb_mine)], axis=-1),
+        jnp.concatenate([va_got_x[0], x_mine(vb_got_y)], axis=-1),
+        jnp.concatenate([va_got_y, vb_got_x], axis=-1),
+    ]
+    val_z1, val_terms = z_first(val_terms)
+    val_got_z1 = over_z(val_z1)
     sums = jnp.concatenate([sum_a, sum_b, sum_w, stats], axis=0)
-    sums = sums + over_core(sums)
+    sums_core = over_core(sums)
+    input_grad = k_input_back(
+        after(sum_a, val_z1), dv_own, dv_oth, w_v, pv, d_sig, tokens, direct
+    )
+    mid_got_z1, ffn_got_z2, val_got_z1, sums_core = held(
+        (mid_got_z1, ffn_got_z2, val_got_z1, sums_core), input_grad
+    )
+    mid_z2, mid_terms = z_second([*mid_terms, mid_got_z1])
+    mid_got_z2 = over_z2(mid_z2)
+    val_z2, val_terms = z_second([*val_terms, val_got_z1])
+    val_got_z2 = over_z2(val_z2)
+    sums = sums + sums_core
     sums = sums + over_tensor(sums)
     sums = sums + over_x(sums)
-    sums = sums + swap(sums, "dp", 4, dp_size)
-    sums = sums + swap(sums, "dp", 8, dp_size)
+    sums = sums + over_z(sums)
+    sums = sums + over_z2(sums)
+
+    def finish(terms):
+        send, terms = core_rows(terms)
+        return total(terms), over_core(send)
+
+    ffn_kept, ffn_got = finish([*ffn_terms, ffn_got_z2])
+    c = ffn_kept.shape[1] // 2
+    down_t, up = joined(ffn_kept[:, :c], ffn_got[:, :c]), joined(ffn_kept[:, c:], ffn_got[:, c:])
+    mid_kept, mid_got = finish([*mid_terms, mid_got_z2])
+    half = gated_own.shape[1] // 2
+    cuts = (0, half, 2 * half, 2 * half + d // 4, 3 * half)
+    uh_t, gamma, wh_t, phi_t = (
+        joined(mid_kept[:, lo:hi], mid_got[:, lo:hi]) for lo, hi in zip(cuts[:-1], cuts[1:])
+    )
+    val_kept, val_got = finish([*val_terms, val_got_z2])
+    value = joined(val_kept[:, :half], val_got[:, :half])
+    z_grad = val_kept[:, half:]
     gh = sum_a.shape[0]
 
     def own_half(v):

time: 644 us -> 551 us (0.86)
  waiting for transfers between devices: 220 us -> 67.5 us
  other arithmetic: 21.2 us -> 45.6 us
  local copies, waits for them, and re-layouts: 36.9 us -> 58.2 us
  Pallas kernels: 303 us -> 323 us
  starting transfers between devices: 52.6 us -> 45.7 us
    ppermute x59 -> x61, waiting for transfers between devices: 220 us -> 67.5 us  [swap(): return lax.ppermute(values, axis, [(i, i ^ bit) for i in range(size)])]
    pallas_call x20 -> x26, Pallas kernels: 303 us -> 323 us  [run(): pl.pallas_call(body, out_shape=out_shape, grid_spec=pltpu.PrefetchScalarG...]
    unnamed x67 -> x173, local copies, waits for them, and re-layouts: 8.96 us -> 19.9 us
    concatenate x7 -> x12, other arithmetic: 2.7 us -> 13.5 us  [the longest x1 2.01 us: one_sequence(): jnp.concatenate([dn_got_x1, x_mine(up_got_y)], axis=-1)]
    convert_element_type x21 -> x16, other arithmetic: 13.5 us -> 21.5 us  [add(): return total.astype(BF)]
    dynamic_slice x3 -> x17, local copies, waits for them, and re-layouts: 0.07 us -> 7.89 us  [pick(): return lax.dynamic_index_in_dim(values, index, axis, keepdims=False)]
    ppermute x59 -> x61, starting transfers between devices: 52.6 us -> 45.7 us  [swap(): return lax.ppermute(values, axis, [(i, i ^ bit) for i in range(size)])]
    slice x10 -> x13, local copies, waits for them, and re-layouts: 13.4 us -> 13.8 us  [the longest x2 4.39 us: one_sequence(): up_terms = [kept_o[1], got_o[1], up_got_y]]
  transfers between devices with their start and end apart: 59 -> 61, of which waited for: 22 -> 11; matrix products, arithmetic and copies ran while one was open for 8% -> 15% of each run, Pallas kernels for 35% -> 60%
where the time goes in v3:
time: 551 us; the launch traced here: 542 us
  Pallas kernels  323 us (59%)
  waiting for transfers between devices  67.5 us (12%)
  local copies, waits for them, and re-layouts  58.2 us (11%)
  starting transfers between devices  45.7 us (8%)
  other arithmetic  45.6 us (8%)
    pallas_call x26, Pallas kernels, run(): pl.pallas_call(body, out_shape=out_shape, grid_spec=pltpu.PrefetchScalarG...  323 us
    ppermute x61, waiting for transfers between devices, swap(): return lax.ppermute(values, axis, [(i, i ^ bit) for i in range(size)])  67.5 us
    ppermute x61, starting transfers between devices, swap(): return lax.ppermute(values, axis, [(i, i ^ bit) for i in range(size)])  45.7 us
    convert_element_type x16, other arithmetic, add(): return total.astype(BF)  21.5 us
    unnamed x173, local copies, waits for them, and re-layouts  19.9 us
  transfers between devices with their start and end apart: 61, of which 11 were waited for; matrix products, arithmetic and copies ran while one was open for 15% of the time, Pallas kernels for 60%

profile of v3, /device:TPU:0, one launch (start us, length us, event | category | flops | bytes accessed | tf_op | source)
XLA Modules:
  0.0 541.9 jit_solution(8638639356024841094)
XLA Ops:
  4.4 3.0 collective-permute-start
  9.3 8.6 %value_own.1 = (bf16[1024,1024]{1,0:T(8,128)(2,1)}, bf16[1024,1024]{1,0:T(8,128)(2,1)}, bf16[1024,1024]{1,0:T(8,128)(2,1)}) custom-call(s32[12]{0:T(128)} %stack.51.s, bf16[1024,1024]{1,0:T(8,128)(2,1)} %x_ref.5, bf16[1024,1024]{1,0:T(8,128)(2,1)} %wo.3), custom_call_target="tpu_custom_call" | custom-call | flops 21474836480 | bytes 104857600 | tf_op jit(solution)/shard_map/value_own/pallas_call | solution.py:341
  19.8 2.0 collective-permute-start.5
  27.5 9.1 %ema_forward.2 = (bf16[1024,1024]{1,0:T(8,128)(2,1)}, bf16[1024,1024]{1,0:T(8,128)(2,1)}, f32[128,128]{1,0:T(8,128)}) custom-call(s32[12]{0:T(128)} %stack.51.s, bf16[1024,1024]{1,0:T(8,128)(2,1)} %get-tuple-element.168.x_ref, f32[128,128]{1,0:T(8,128)} %reshape.361.dec_ref, f32[128,128]{1,0:T(8,128)} %reshape.362.cf_ref, f32[8,128]{1,0:T(8,128)} %bitcast.356), custom_call_target="tpu_custom_call" | custom-call | flops 99999997952 | bytes 64921600 | tf_op jit(solution)/shard_map/ema_forward/pallas_call | solution.py:341
  38.1 9.1 %ema_forward.3 = (bf16[1024,1024]{1,0:T(8,128)(2,1)}, bf16[1024,1024]{1,0:T(8,128)(2,1)}, f32[128,128]{1,0:T(8,128)}) custom-call(s32[12]{0:T(128)} %stack.51.s, bf16[1024,1024]{1,0:T(8,128)(2,1)} %get-tuple-element.168.x_ref, f32[128,128]{1,0:T(8,128)} %reshape.361.dec_ref, ...), custom_call_target="tpu_custom_call", output_to_operand_aliasing={{0}: (6, {}), {1}: (7, {})} | custom-call | flops 99999997952 | bytes 107520000 | tf_op jit(solution)/shard_map/ema_forward/pallas_call | solution.py:341
  48.9 3.8 query_key.1
  53.9 7.8 %act_own.1 = (bf16[1024,1024]{1,0:T(8,128)(2,1)}, bf16[1024,1024]{1,0:T(8,128)(2,1)}) custom-call(s32[12]{0:T(128)} %stack.51.s, bf16[1024,1024]{1,0:T(8,128)(2,1)} %get-tuple-element.173.e_ref.x_ref.eo.et.l_ref, bf16[1024,1024]{1,0:T(8,128)(2,1)} %wo.2), custom_call_target="tpu_custom_call" | custom-call | flops 21474836480 | bytes 83886080 | tf_op jit(solution)/shard_map/act_own/pallas_call | solution.py:341
  63.3 2.3 collective-permute-done.9.u0
  67.3 8.3 %act_other.2 = (bf16[1024,1024]{1,0:T(8,128)(2,1)}, bf16[1024,1024]{1,0:T(8,128)(2,1)}) custom-call(s32[12]{0:T(128)} %stack.51.s, bf16[1024,1024]{1,0:T(8,128)(2,1)} %get-tuple-element.168.x_ref, bf16[256,1024]{1,0:T(8,128)(2,1)} %copy-done.70, bf16[256,1024]{1,0:T(8,128)(2,1)} %copy-done.71, bf16[256,1024]{1,0:T(8,128)(2,1)} %copy-done.72, ...), custom_call_target="tpu_custom_call" | custom-call | flops 21474836480 | bytes 83886080 | tf_op jit(solution)/shard_map/act_other/pallas_call | solution.py:341
  77.2 8.1 %act_other.3 = (bf16[1024,1024]{1,0:T(8,128)(2,1)}, bf16[1024,1024]{1,0:T(8,128)(2,1)}) custom-call(s32[12]{0:T(128)} %stack.51.s, bf16[1024,1024]{1,0:T(8,128)(2,1)} %get-tuple-element.173.e_ref.x_ref.eo.et.l_ref, bf16[256,1024]{1,0:T(8,128)(2,1)} %collective-permute-done.5.p0.w0, bf16[256,1024]{1,0:T(8,128)(2,1)} %copy-done.74, ...), custom_call_target="tpu_custom_call" | custom-call | flops 21474836480 | bytes 83886080 | tf_op jit(solution)/shard_map/act_other/pallas_call | solution.py:341
  86.4 13.2 %attend.1 = (bf16[1024,1024]{1,0:T(8,128)(2,1)}, bf16[1024,1024]{1,0:T(8,128)(2,1)}, bf16[1024,1024]{1,0:T(8,128)(2,1)}, bf16[1024,1024]{1,0:T(8,128)(2,1)}, bf16[1024,1024]{1,0:T(8,128)(2,1)}) custom-call(s32[12]{0:T(128)} %stack.51.s, bf16[1024,128]{1,0:T(8,128)(2,1)} %get-tuple-element.174.q_ref, bf16[1024,128]{1,0:T(8,128)(2,1)} %get-tuple-element.190.k_ref, ...), custom_call_target="tpu_custom_call" | custom-call | flops 28521267200 | bytes 235929600 | tf_op jit(solution)/shard_map/attend/pallas_call | solution.py:341
  100.3 2.3 constant_dynamic-slice_fusion.18
  102.5 2.3 constant_dynamic-slice_fusion.19
  104.9 2.0 collective-permute-start.18
  107.7 18.8 %gate.1 = (f32[1024,1024]{1,0:T(8,128)}, bf16[1024,1024]{1,0:T(8,128)(2,1)}, bf16[1024,1024]{1,0:T(8,128)(2,1)}, bf16[1024,1024]{1,0:T(8,128)(2,1)}, bf16[1024,1024]{1,0:T(8,128)(2,1)}) custom-call(s32[12]{0:T(128)} %stack.51.s, bf16[1024,1024]{1,0:T(8,128)(2,1)} %get-tuple-element.195.go, bf16[1024,1024]{1,0:T(8,128)(2,1)} %get-tuple-element.196.gt, ...), custom_call_target="tpu_custom_call" | custom-call | flops 85899345920 | bytes 314572800 | tf_op jit(solution)/shard_map/gate/pallas_call | solution.py:341
  126.5 20.2 %ffn.4 = (bf16[1024,1024]{1,0:T(8,128)(2,1)}, bf16[1024,1024]{1,0:T(8,128)(2,1)}, bf16[2,1024,1024]{2,1,0:T(8,128)(2,1)}) custom-call(s32[12]{0:T(128)} %stack.51.s, bf16[1024,1024]{1,0:T(8,128)(2,1)} %get-tuple-element.207.low_ref, bf16[1024,1024]{1,0:T(8,128)(2,1)} %c_ref.9, bf16[1024,2048]{1,0:T(8,128)(2,1)} %refs_0_.3, bf16[2048,1024]{1,0:T(8,128)(2,1)} %refs_1_.3), custom_call_target="tpu_custom_call" | custom-call | flops 128849018880 | bytes 209715200 | tf_op jit(solution)/shard_map/ffn/pallas_call | solution.py:341
  148.3 4.6 collective-permute-done.18.refs_0_
  154.1 20.4 %ffn.5 = (bf16[1024,1024]{1,0:T(8,128)(2,1)}, bf16[1024,1024]{1,0:T(8,128)(2,1)}, bf16[2,1024,1024]{2,1,0:T(8,128)(2,1)}) custom-call(s32[12]{0:T(128)} %stack.51.s, bf16[1024,1024]{1,0:T(8,128)(2,1)} %get-tuple-element.207.low_ref, bf16[1024,1024]{1,0:T(8,128)(2,1)} %c_ref.9, bf16[1024,2048]{1,0:T(8,128)(2,1)} %refs_0_.3, bf16[2048,1024]{1,0:T(8,128)(2,1)} %refs_1_.3), custom_call_target="tpu_custom_call" | custom-call | flops 128849018880 | bytes 209715200 | tf_op jit(solution)/shard_map/ffn/pallas_call | solution.py:341
  175.2 2.4 collective-permute-done.19.refs_1_
  178.1 2.7 fusion.65
  191.8 20.7 %ffn.6 = (bf16[1024,1024]{1,0:T(8,128)(2,1)}, bf16[1024,1024]{1,0:T(8,128)(2,1)}, bf16[2,1024,1024]{2,1,0:T(8,128)(2,1)}) custom-call(s32[12]{0:T(128)} %stack.51.s, bf16[1024,1024]{1,0:T(8,128)(2,1)} %get-tuple-element.207.low_ref, bf16[1024,1024]{1,0:T(8,128)(2,1)} %c_ref.9, bf16[256,2048]{1,0:T(8,128)(2,1)} %collective-permute-done.18.refs_0_, ...), custom_call_target="tpu_custom_call" | custom-call | flops 128849018880 | bytes 188743680 | tf_op jit(solution)/shard_map/ffn/pallas_call | solution.py:341
  212.5 21.1 %ffn.7 = (bf16[1024,1024]{1,0:T(8,128)(2,1)}, bf16[1024,1024]{1,0:T(8,128)(2,1)}, bf16[2,1024,1024]{2,1,0:T(8,128)(2,1)}) custom-call(s32[12]{0:T(128)} %stack.51.s, bf16[1024,1024]{1,0:T(8,128)(2,1)} %get-tuple-element.207.low_ref, bf16[1024,1024]{1,0:T(8,128)(2,1)} %c_ref.9, bf16[256,2048]{1,0:T(8,128)(2,1)} %collective-permute-done.18.refs_0_, ...), custom_call_target="tpu_custom_call" | custom-call | flops 128849018880 | bytes 188743680 | tf_op jit(solution)/shard_map/ffn/pallas_call | solution.py:341
  239.7 1.9 slice.179
  243.1 4.0 fusion
  247.7 28.9 %mid_back.1 = (bf16[1024,1024]{1,0:T(8,128)(2,1)}, bf16[1024,1024]{1,0:T(8,128)(2,1)}, bf16[1024,1024]{1,0:T(8,128)(2,1)}, bf16[1024,1024]{1,0:T(8,128)(2,1)}, b...) custom-call(s32[12]{0:T(128)} %stack.51.s, ...), custom_call_target="tpu_custom_call" | custom-call | flops 128849018880 | bytes 734003200 | tf_op jit(solution)/shard_map/mid_back/pallas_call | solution.py:341
  278.3 14.2 %weight_mid.2 = (bf16[1024,1536]{1,0:T(8,128)(2,1)}, bf16[1024,1536]{1,0:T(8,128)(2,1)}) custom-call(s32[12]{0:T(128)} %stack.51.s, bf16[1024,1024]{1,0:T(8,128)(2,1)} %get-tuple-element.173.e_ref.x_ref.eo.et.l_ref, bf16[1024,1024]{1,0:T(8,128)(2,1)} %get-tuple-element.238.h_ref, bf16[1024,1024]{1,0:T(8,128)(2,1)} %get-tuple-element.241.f_ref, ...), custom_call_target="tpu_custom_call" | custom-call | flops 64424509440 | bytes 251658240 | tf_op jit(solution)/shard_map/weight_mid/pallas_call | solution.py:341
  294.5 9.8 %value_back.1 = (bf16[1024,1024]{1,0:T(8,128)(2,1)}, bf16[1024,1024]{1,0:T(8,128)(2,1)}) custom-call(s32[12]{0:T(128)} %stack.51.s, bf16[1024,1024]{1,0:T(8,128)(2,1)} %get-tuple-element.193.p_ref, bf16[1024,1024]{1,0:T(8,128)(2,1)} %get-tuple-element.247.ao, bf16[1024,1024]{1,0:T(8,128)(2,1)} %get-tuple-element.248.at, ...), custom_call_target="tpu_custom_call" | custom-call | flops 26843545600 | bytes 146800640 | tf_op jit(solution)/shard_map/value_back/pallas_call | solution.py:341
  307.2 6.7 %weight_value.2 = (bf16[1024,512]{1,0:T(8,128)(2,1)}, bf16[1024,512]{1,0:T(8,128)(2,1)}) custom-call(s32[12]{0:T(128)} %stack.51.s, bf16[1024,1024]{1,0:T(8,128)(2,1)} %get-tuple-element.168.x_ref, bf16[1024,1024]{1,0:T(8,128)(2,1)} %get-tuple-element.251.vo, bf16[1024,1024]{1,0:T(8,128)(2,1)} %get-tuple-element.254.vt), custom_call_target="tpu_custom_call" | custom-call | flops 21474836480 | bytes 83886080 | tf_op jit(solution)/shard_map/weight_value/pallas_call | solution.py:341
  315.3 2.0 fusion.25
  317.6 14.7 %weight_mid.3 = (bf16[1024,1536]{1,0:T(8,128)(2,1)}, bf16[1024,1536]{1,0:T(8,128)(2,1)}) custom-call(s32[12]{0:T(128)} %stack.51.s, bf16[1024,1024]{1,0:T(8,128)(2,1)} %get-tuple-element.173.e_ref.x_ref.eo.et.l_ref, bf16[1024,1024]{1,0:T(8,128)(2,1)} %get-tuple-element.238.h_ref, bf16[1024,1024]{1,0:T(8,128)(2,1)} %get-tuple-element.241.f_ref, ...), custom_call_target="tpu_custom_call" | custom-call | flops 64424509440 | bytes 314572800 | tf_op jit(solution)/shard_map/weight_mid/pallas_call | solution.py:341
  332.3 2.1 fusion.67
  339.2 10.9 %score_back.1 = (bf16[1024,128]{1,0:T(8,128)(2,1)}, f32[8,128]{1,0:T(8,128)}) custom-call(s32[12]{0:T(128)} %stack.51.s, bf16[1024,1024]{1,0:T(8,128)(2,1)} %get-tuple-element.193.p_ref, bf16[1024,1024]{1,0:T(8,128)(2,1)} %get-tuple-element.247.ao, bf16[1024,1024]{1,0:T(8,128)(2,1)} %get-tuple-element.248.at, bf16[1024,1024]{1,0:T(8,128)(2,1)} %get-tuple-element.166.vo, ...), custom_call_target="tpu_custom_call" | custom-call | flops 26843545600 | bytes 118016000 | tf_op jit(solution)/shard_map/score_back/pallas_call | solution.py:341
  354.3 3.7 weight.1
  361.4 7.5 %weight_value.3 = (bf16[1024,512]{1,0:T(8,128)(2,1)}, bf16[1024,512]{1,0:T(8,128)(2,1)}) custom-call(s32[12]{0:T(128)} %stack.51.s, bf16[1024,1024]{1,0:T(8,128)(2,1)} %get-tuple-element.168.x_ref, bf16[1024,1024]{1,0:T(8,128)(2,1)} %get-tuple-element.251.vo, bf16[1024,1024]{1,0:T(8,128)(2,1)} %get-tuple-element.254.vt, ...), custom_call_target="tpu_custom_call" | custom-call | flops 21474836480 | bytes 104857600 | tf_op jit(solution)/shard_map/weight_value/pallas_call | solution.py:341
  378.5 10.9 %ema_backward.4 = (f32[1024,1024]{1,0:T(8,128)}, f32[128,128]{1,0:T(8,128)}, f32[128,128]{1,0:T(8,128)}, f32[128,128]{1,0:T(8,128)}, f32[128,128]{1,0:T(8,128)}, /*index=5*/f32[8,128]{1,0:T(8,128)}) custom-call(s32[12]{0:T(128)} %stack.51.s, bf16[1024,1024]{1,0:T(8,128)(2,1)} %get-tuple-element.168.x_ref, f32[1024,1024]{1,0:T(8,128)} %get-tuple-element.270.de_ref, ...), custom_call_target="tpu_custom_call" | custom-call | flops 99999997952 | bytes 135086080 | tf_op jit(solution)/shard_map/ema_backward/pallas_call | solution.py:341
  391.7 4.2 collective-permute-done.38
  396.5 13.1 %collective-permute-done.39 = bf16[1024,768]{1,0:T(8,128)(2,1)S(1)} collective-permute-done((bf16[1024,768]{1,0:T(8,128)(2,1)}, bf16[1024,768]{1,0:T(8,128)(2,1)S(1)}, u32[]{:S(2)}, u32[]{:S(2)}) %collective-permute-start.39) | collective-permute-done | bytes 1572896 | tf_op jit(solution)/shard_map/ppermute | solution.py:965
  413.0 11.6 %ema_backward.5 = (f32[1024,1024]{1,0:T(8,128)}, f32[128,128]{1,0:T(8,128)}, f32[128,128]{1,0:T(8,128)}, f32[128,128]{1,0:T(8,128)}, f32[128,128]{1,0:T(8,128)}, /*index=5*/f32[8,128]{1,0:T(8,128)}) custom-call(s32[12]{0:T(128)} %stack.51.s, bf16[1024,1024]{1,0:T(8,128)(2,1)} %get-tuple-element.168.x_ref, ...), custom_call_target="tpu_custom_call", output_to_operand_aliasing={{0}: (14, {})} | custom-call | flops 99999997952 | bytes 179691520 | tf_op jit(solution)/shard_map/ema_backward/pallas_call | solution.py:341
  431.3 2.5 fusion.13
  433.8 2.6 collective-permute-start.49
  436.4 11.1 %ema_backward.6 = (f32[1024,1024]{1,0:T(8,128)}, f32[128,128]{1,0:T(8,128)}, f32[128,128]{1,0:T(8,128)}, f32[128,128]{1,0:T(8,128)}, f32[128,128]{1,0:T(8,128)}, /*index=5*/f32[8,128]{1,0:T(8,128)}) custom-call(s32[12]{0:T(128)} %stack.51.s, bf16[1024,1024]{1,0:T(8,128)(2,1)} %get-tuple-element.168.x_ref, ...), custom_call_target="tpu_custom_call", output_to_operand_aliasing={{0}: (14, {})} | custom-call | flops 99999997952 | bytes 179691520 | tf_op jit(solution)/shard_map/ema_backward/pallas_call | solution.py:341
  450.3 2.2 constant_dynamic-slice_fusion.7
  455.0 11.2 %ema_backward.7 = (f32[1024,1024]{1,0:T(8,128)}, f32[128,128]{1,0:T(8,128)}, f32[128,128]{1,0:T(8,128)}, f32[128,128]{1,0:T(8,128)}, f32[128,128]{1,0:T(8,128)}, /*index=5*/f32[8,128]{1,0:T(8,128)}) custom-call(s32[12]{0:T(128)} %stack.51.s, bf16[1024,1024]{1,0:T(8,128)(2,1)} %get-tuple-element.168.x_ref, ...), custom_call_target="tpu_custom_call", output_to_operand_aliasing={{0}: (14, {})} | custom-call | flops 99999997952 | bytes 179691520 | tf_op jit(solution)/shard_map/ema_backward/pallas_call | solution.py:341
  471.6 12.5 %input_back.1 = f32[1024,1024]{1,0:T(8,128)} custom-call(s32[12]{0:T(128)} %stack.51.s, bf16[1024,1024]{1,0:T(8,128)(2,1)} %get-tuple-element.251.vo, bf16[1024,1024]{1,0:T(8,128)(2,1)} %get-tuple-element.254.vt, bf16[1024,1024]{1,0:T(8,128)(2,1)} %wo.3, bf16[256,1024]{1,0:T(8,128)(2,1)} %copy-done.70, bf16[256,1024]{1,0:T(8,128)(2,1)} %copy-done.71, ...), custom_call_target="tpu_custom_call" | custom-call | flops 42949672960 | bytes 209715200 | tf_op jit(solution)/shard_map/input_back/pallas_call | solution.py:341
  484.2 8.5 %collective-permute-done.48 = bf16[2,128,1536]{2,1,0:T(8,128)(2,1)S(1)} collective-permute-done((bf16[2,128,1536]{2,1,0:T(8,128)(2,1)S(1)}, bf16[2,128,1536]{2,1,0:T(8,128)(2,1)S(1)}, u32[]{:S(2)}, u32[]{:S(2)}) %collective-permute-start.48) | collective-permute-done | bytes 786464 | tf_op jit(solution)/shard_map/ppermute | solution.py:965
  498.3 8.2 %collective-permute-done.56 = bf16[128,640]{1,0:T(8,128)(2,1)S(1)} collective-permute-done((bf16[128,640]{1,0:T(8,128)(2,1)S(1)}, bf16[128,640]{1,0:T(8,128)(2,1)S(1)}, u32[]{:S(2)}, u32[]{:S(2)}) %collective-permute-start.56) | collective-permute-done | bytes 163872 | tf_op jit(solution)/shard_map/ppermute | solution.py:965
  514.8 11.8 %collective-permute-done.58 = bf16[128,1536]{1,0:T(8,128)(2,1)S(1)} collective-permute-done((bf16[128,1536]{1,0:T(8,128)(2,1)S(1)}, bf16[128,1536]{1,0:T(8,128)(2,1)S(1)}, u32[]{:S(2)}, u32[]{:S(2)}) %collective-permute-start.58) | collective-permute-done | bytes 393248 | tf_op jit(solution)/shard_map/ppermute | solution.py:965
  527.1 9.8 %collective-permute-done.55 = f32[272,128]{1,0:T(8,128)S(1)} collective-permute-done((f32[272,128]{1,0:T(8,128)S(1)}, f32[272,128]{1,0:T(8,128)S(1)}, u32[]{:S(2)}, u32[]{:S(2)}) %collective-permute-start.55) | collective-permute-done | bytes 139296 | tf_op jit(solution)/shard_map/ppermute | solution.py:965
  (373 shorter events, 120.6 us)
Async XLA Ops:
  4.4 21.1 %collective-permute-start = (f32[65,512]{1,0:T(8,128)S(1)}, f32[65,512]{1,0:T(8,128)S(1)}, u32[]{:S(2)}, u32[]{:S(2)}) collective-permute-start(f32[65,512]{1,0:T(8,128)S(1)} %dynamic-update-slice.8), channel_id=1, source_target_pairs={{0,1},{1,0},{2,3},{3,2},{4,5},{5,4},{6,7},{7,6},{8,9},{9,8},{10,11... | collective-permute-start | bytes 399368 | tf_op jit(solution)/shard_map/ppermute | solution.py:965
  8.5 28.1 %collective-permute-start.1 = (bf16[256,1024]{1,0:T(8,128)(2,1)S(1)}, bf16[256,1024]{1,0:T(8,128)(2,1)S(1)}, u32[]{:S(2)}, u32[]{:S(2)}) collective-permute-start(bf16[256,1024]{1,0:T(8,128)(2,1)S(1)} %constant_dynamic-slice_fusion.24), channel_id=1, source_target_pairs={{0,1},{1,0},{2,3},{3,2},{4,5},{5,4},{6,7},{7,6},{8,9},{9,8},{10,11... | collective-permute-start | bytes 1572872 | tf_op jit(solution)/shard_map/ppermute | solution.py:965
  19.8 27.5 %collective-permute-start.5 = (bf16[256,1024]{1,0:T(8,128)(2,1)}, bf16[256,1024]{1,0:T(8,128)(2,1)}, u32[]{:S(2)}, u32[]{:S(2)}) collective-permute-start(bf16[256,1024]{1,0:T(8,128)(2,1)} %constant_dynamic-slice_fusion.23), channel_id=1, source_target_pairs={{0,1},{1,0},{2,3},{3,2},{4,5},{5,4},{6,7},{7,6},{8,9},{9,8},{10,11... | collective-permute-start | bytes 1572872 | tf_op jit(solution)/shard_map/ppermute | solution.py:965
  36.6 16.7 %collective-permute-start.2 = (bf16[256,1024]{1,0:T(8,128)(2,1)S(1)}, bf16[256,1024]{1,0:T(8,128)(2,1)S(1)}, u32[]{:S(2)}, u32[]{:S(2)}) collective-permute-start(bf16[256,1024]{1,0:T(8,128)(2,1)S(1)} %collective-permute-done.1.p0.w0), channel_id=1, source_target_pairs={{0,4},{2,6},{4,0},{6,2},{8,12},{10,14},{12,8},{14,10},{16,20},{18,... | collective-permute-start | bytes 1572872 | tf_op jit(solution)/shard_map/ppermute | solution.py:965
  47.3 16.0 %collective-permute-start.6 = (bf16[256,1024]{1,0:T(8,128)(2,1)}, bf16[256,1024]{1,0:T(8,128)(2,1)S(1)}, u32[]{:S(2)}, u32[]{:S(2)}) collective-permute-start(bf16[256,1024]{1,0:T(8,128)(2,1)} %collective-permute-done.5.p0.w0), channel_id=1, source_target_pairs={{0,8},{2,10},{4,12},{6,14},{8,0},{10,2},{12,4},{14,6},{16,24},{18,... | collective-permute-start | bytes 1572872 | tf_op jit(solution)/shard_map/ppermute | solution.py:965
  52.7 12.9 %collective-permute-start.9 = (bf16[256,1024]{1,0:T(8,128)(2,1)S(1)}, bf16[256,1024]{1,0:T(8,128)(2,1)S(1)}, u32[]{:S(2)}, u32[]{:S(2)}) collective-permute-start(bf16[256,1024]{1,0:T(8,128)(2,1)S(1)} %copy-done.56), channel_id=1, source_target_pairs={{0,1},{1,0},{2,3},{3,2},{4,5},{5,4},{6,7},{7,6},{8,9},{9,8},{10,11... | collective-permute-start | bytes 1572872 | tf_op jit(solution)/shard_map/ppermute | solution.py:965
  53.4 12.9 %collective-permute-start.4 = (bf16[256,1024]{1,0:T(8,128)(2,1)S(1)}, bf16[256,1024]{1,0:T(8,128)(2,1)S(1)}, u32[]{:S(2)}, u32[]{:S(2)}) collective-permute-start(bf16[256,1024]{1,0:T(8,128)(2,1)S(1)} %collective-permute-done.2.p1.w1), channel_id=1, source_target_pairs={{0,2},{2,0},{4,6},{6,4},{8,10},{10,8},{12,14},{14,12},{16,18},{18,... | collective-permute-start | bytes 1572872 | tf_op jit(solution)/shard_map/ppermute | solution.py:965
  61.7 23.6 %collective-permute-start.13 = (bf16[256,1024]{1,0:T(8,128)(2,1)S(1)}, bf16[256,1024]{1,0:T(8,128)(2,1)S(1)}, u32[]{:S(2)}, u32[]{:S(2)}) collective-permute-start(bf16[256,1024]{1,0:T(8,128)(2,1)S(1)} %copy-done.55), channel_id=1, source_target_pairs={{0,1},{1,0},{2,3},{3,2},{4,5},{5,4},{6,7},{7,6},{8,9},{9,8},{10,11... | collective-permute-start | bytes 1572872 | tf_op jit(solution)/shard_map/ppermute | solution.py:965
  65.6 20.2 %collective-permute-start.10 = (bf16[256,1024]{1,0:T(8,128)(2,1)S(1)}, bf16[256,1024]{1,0:T(8,128)(2,1)S(1)}, u32[]{:S(2)}, u32[]{:S(2)}) collective-permute-start(bf16[256,1024]{1,0:T(8,128)(2,1)S(1)} %collective-permute-done.9.u0), channel_id=1, source_target_pairs={{0,4},{2,6},{4,0},{6,2},{8,12},{10,14},{12,8},{14,10},{16,20},{18,... | collective-permute-start | bytes 1572872 | tf_op jit(solution)/shard_map/ppermute | solution.py:965
  85.3 14.4 %collective-permute-start.14 = (bf16[256,1024]{1,0:T(8,128)(2,1)S(1)}, bf16[256,1024]{1,0:T(8,128)(2,1)S(1)}, u32[]{:S(2)}, u32[]{:S(2)}) collective-permute-start(bf16[256,1024]{1,0:T(8,128)(2,1)S(1)} %collective-permute-done.13.h0.f0), channel_id=1, source_target_pairs={{0,8},{2,10},{4,12},{6,14},{8,0},{10,2},{12,4},{14,6},{16,24},{18,... | collective-permute-start | bytes 1572872 | tf_op jit(solution)/shard_map/ppermute | solution.py:965
  85.9 19.0 %collective-permute-start.11 = (bf16[256,1024]{1,0:T(8,128)(2,1)S(1)}, bf16[256,1024]{1,0:T(8,128)(2,1)S(1)}, u32[]{:S(2)}, u32[]{:S(2)}) collective-permute-start(bf16[256,1024]{1,0:T(8,128)(2,1)S(1)} %collective-permute-done.9.u0), channel_id=1, source_target_pairs={{0,2},{2,0},{4,6},{6,4},{8,10},{10,8},{12,14},{14,12},{16,18},{18,... | collective-permute-start | bytes 1572872 | tf_op jit(solution)/shard_map/ppermute | solution.py:965
  86.1 20.8 %collective-permute-start.12 = (bf16[256,1024]{1,0:T(8,128)(2,1)S(1)}, bf16[256,1024]{1,0:T(8,128)(2,1)S(1)}, u32[]{:S(2)}, u32[]{:S(2)}) collective-permute-start(bf16[256,1024]{1,0:T(8,128)(2,1)S(1)} %collective-permute-done.10.u1), channel_id=1, source_target_pairs={{0,2},{2,0},{4,6},{6,4},{8,10},{10,8},{12,14},{14,12},{16,18},{18,... | collective-permute-start | bytes 1572872 | tf_op jit(solution)/shard_map/ppermute | solution.py:965
  104.9 41.8 %collective-permute-start.22 = (bf16[512,1024]{1,0:T(8,128)(2,1)}, bf16[512,1024]{1,0:T(8,128)(2,1)}, u32[]{:S(2)}, u32[]{:S(2)}) collective-permute-start(bf16[512,1024]{1,0:T(8,128)(2,1)} %constant_dynamic-slice_fusion.18), channel_id=1, source_target_pairs={{0,1},{1,0},{2,3},{3,2},{4,5},{5,4},{6,7},{7,6},{8,9},{9,8},{10,11... | collective-permute-start | bytes 3145736 | tf_op jit(solution)/shard_map/ppermute | solution.py:965
  104.9 48.0 %collective-permute-start.18 = (bf16[256,2048]{1,0:T(8,128)(2,1)}, bf16[256,2048]{1,0:T(8,128)(2,1)}, u32[]{:S(2)}, u32[]{:S(2)}) collective-permute-start(bf16[256,2048]{1,0:T(8,128)(2,1)} %constant_dynamic-slice_fusion.19), channel_id=1, source_target_pairs={{0,1},{1,0},{2,3},{3,2},{4,5},{5,4},{6,7},{7,6},{8,9},{9,8},{10,11... | collective-permute-start | bytes 3145736 | tf_op jit(solution)/shard_map/ppermute | solution.py:965
  146.7 27.8 %collective-permute-start.23 = (bf16[512,1024]{1,0:T(8,128)(2,1)}, bf16[512,1024]{1,0:T(8,128)(2,1)S(1)}, u32[]{:S(2)}, u32[]{:S(2)}) collective-permute-start(bf16[512,1024]{1,0:T(8,128)(2,1)} %collective-permute-done.22.refs_4_), channel_id=1, source_target_pairs={{0,8},{2,10},{4,12},{6,14},{8,0},{10,2},{12,4},{14,6},{16,24},{18,... | collective-permute-start | bytes 3145736 | tf_op jit(solution)/shard_map/ppermute | solution.py:965
  152.9 24.6 %collective-permute-start.19 = (bf16[256,2048]{1,0:T(8,128)(2,1)}, bf16[256,2048]{1,0:T(8,128)(2,1)S(1)}, u32[]{:S(2)}, u32[]{:S(2)}) collective-permute-start(bf16[256,2048]{1,0:T(8,128)(2,1)} %collective-permute-done.18.refs_0_), channel_id=1, source_target_pairs={{0,4},{2,6},{4,0},{6,2},{8,12},{10,14},{12,8},{14,10},{16,20},{18,... | collective-permute-start | bytes 3145736 | tf_op jit(solution)/shard_map/ppermute | solution.py:965
  154.1 29.9 %collective-permute-start.17 = (bf16[2,1024,1024]{2,1,0:T(8,128)(2,1)}, bf16[2,1024,1024]{2,1,0:T(8,128)(2,1)S(1)}, u32[]{:S(2)}, u32[]{:S(2)}) collective-permute-start(bf16[2,1024,1024]{2,1,0:T(8,128)(2,1)} %get-tuple-element.212), channel_id=1, source_target_pairs={{0,2},{2,0},{4,6},{6,4},{8,10},{10,8},{12,14},{14,12},{16,18},{18,... | collective-permute-start | bytes 12582920 | tf_op jit(solution)/shard_map/ppermute | solution.py:965
  174.5 15.0 %collective-permute-start.24 = (bf16[512,1024]{1,0:T(8,128)(2,1)}, bf16[512,1024]{1,0:T(8,128)(2,1)S(1)}, u32[]{:S(2)}, u32[]{:S(2)}) collective-permute-start(bf16[512,1024]{1,0:T(8,128)(2,1)} %collective-permute-done.22.refs_4_), channel_id=1, source_target_pairs={{0,2},{2,0},{4,6},{6,4},{8,10},{10,8},{12,14},{14,12},{16,18},{18,... | collective-permute-start | bytes 3145736 | tf_op jit(solution)/shard_map/ppermute | solution.py:965
  175.1 14.4 %collective-permute-start.25 = (bf16[512,1024]{1,0:T(8,128)(2,1)S(1)}, bf16[512,1024]{1,0:T(8,128)(2,1)S(1)}, u32[]{:S(2)}, u32[]{:S(2)}) collective-permute-start(bf16[512,1024]{1,0:T(8,128)(2,1)S(1)} %collective-permute-done.23.refs_5_), channel_id=1, source_target_pairs={{0,2},{2,0},{4,6},{6,4},{8,10},{10,8},{12,14},{14,12},{16,18},{18,... | collective-permute-start | bytes 3145736 | tf_op jit(solution)/shard_map/ppermute | solution.py:965
  177.6 13.2 %collective-permute-start.21 = (bf16[256,2048]{1,0:T(8,128)(2,1)S(1)}, bf16[256,2048]{1,0:T(8,128)(2,1)}, u32[]{:S(2)}, u32[]{:S(2)}) collective-permute-start(bf16[256,2048]{1,0:T(8,128)(2,1)S(1)} %collective-permute-done.19.refs_1_), channel_id=1, source_target_pairs={{0,2},{2,0},{4,6},{6,4},{8,10},{10,8},{12,14},{14,12},{16,18},{18,... | collective-permute-start | bytes 3145736 | tf_op jit(solution)/shard_map/ppermute | solution.py:965
  188.4 126.8 %collective-permute-start.31 = (bf16[4,128,1024]{2,1,0:T(8,128)(2,1)}, bf16[4,128,1024]{2,1,0:T(8,128)(2,1)}, u32[]{:S(2)}, u32[]{:S(2)}) collective-permute-start(bf16[4,128,1024]{2,1,0:T(8,128)(2,1)} %fusion.3), channel_id=1, source_target_pairs={{0,4},{2,6},{4,0},{6,2},{8,12},{10,14},{12,8},{14,10},{16,20},{18,... | collective-permute-start | bytes 3145736 | tf_op jit(solution)/shard_map/ppermute | solution.py:965
  212.5 27.2 %collective-permute-start.26 = (bf16[2,1024,1024]{2,1,0:T(8,128)(2,1)}, bf16[2,1024,1024]{2,1,0:T(8,128)(2,1)}, u32[]{:S(2)}, u32[]{:S(2)}) collective-permute-start(bf16[2,1024,1024]{2,1,0:T(8,128)(2,1)} %get-tuple-element.226), channel_id=1, source_target_pairs={{0,2},{2,0},{4,6},{6,4},{8,10},{10,8},{12,14},{14,12},{16,18},{18,... | collective-permute-start | bytes 12582920 | tf_op jit(solution)/shard_map/ppermute | solution.py:965
  242.1 34.6 %collective-permute-start.27 = (bf16[4,128,1024]{2,1,0:T(8,128)(2,1)S(1)}, bf16[4,128,1024]{2,1,0:T(8,128)(2,1)S(1)}, u32[]{:S(2)}, u32[]{:S(2)}) collective-permute-start(bf16[4,128,1024]{2,1,0:T(8,128)(2,1)S(1)} %fusion.4), channel_id=1, source_target_pairs={{0,4},{2,6},{4,0},{6,2},{8,12},{10,14},{12,8},{14,10},{16,20},{18,... | collective-permute-start | bytes 3145736 | tf_op jit(solution)/shard_map/ppermute | solution.py:965
  247.1 57.1 %collective-permute-start.28 = (bf16[1024,1024]{1,0:T(8,128)(2,1)}, bf16[1024,1024]{1,0:T(8,128)(2,1)}, u32[]{:S(2)}, u32[]{:S(2)}) collective-permute-start(bf16[1024,1024]{1,0:T(8,128)(2,1)} %fusion), channel_id=1, source_target_pairs={{0,1},{1,0},{2,3},{3,2},{4,5},{5,4},{6,7},{7,6},{8,9},{9,8},{10,11... | collective-permute-start | bytes 6291464 | tf_op jit(solution)/shard_map/ppermute | solution.py:965
  292.5 24.9 %collective-permute-start.29 = (bf16[1024,1536]{1,0:T(8,128)(2,1)}, bf16[1024,1536]{1,0:T(8,128)(2,1)}, u32[]{:S(2)}, u32[]{:S(2)}) collective-permute-start(bf16[1024,1536]{1,0:T(8,128)(2,1)} %get-tuple-element.244), channel_id=1, source_target_pairs={{0,2},{2,0},{4,6},{6,4},{8,10},{10,8},{12,14},{14,12},{16,18},{18,... | collective-permute-start | bytes 9437192 | tf_op jit(solution)/shard_map/ppermute | solution.py:965
  292.5 25.1 %collective-permute-start.30 = (bf16[1024,1536]{1,0:T(8,128)(2,1)}, bf16[1024,1536]{1,0:T(8,128)(2,1)}, u32[]{:S(2)}, u32[]{:S(2)}) collective-permute-start(bf16[1024,1536]{1,0:T(8,128)(2,1)} %get-tuple-element.245), channel_id=1, source_target_pairs={{0,2},{2,0},{4,6},{6,4},{8,10},{10,8},{12,14},{14,12},{16,18},{18,... | collective-permute-start | bytes 9437192 | tf_op jit(solution)/shard_map/ppermute | solution.py:965
  293.0 57.0 %collective-permute-start.32 = (bf16[4,128,1024]{2,1,0:T(8,128)(2,1)}, bf16[4,128,1024]{2,1,0:T(8,128)(2,1)}, u32[]{:S(2)}, u32[]{:S(2)}) collective-permute-start(bf16[4,128,1024]{2,1,0:T(8,128)(2,1)} %fusion.1), channel_id=1, source_target_pairs={{0,1},{1,0},{2,3},{3,2},{4,5},{5,4},{6,7},{7,6},{8,9},{9,8},{10,11... | collective-permute-start | bytes 3145736 | tf_op jit(solution)/shard_map/ppermute | solution.py:965
  306.1 43.9 %collective-permute-start.33 = (bf16[4,128,1024]{2,1,0:T(8,128)(2,1)S(1)}, bf16[4,128,1024]{2,1,0:T(8,128)(2,1)S(1)}, u32[]{:S(2)}, u32[]{:S(2)}) collective-permute-start(bf16[4,128,1024]{2,1,0:T(8,128)(2,1)S(1)} %fusion.5), channel_id=1, source_target_pairs={{0,4},{2,6},{4,0},{6,2},{8,12},{10,14},{12,8},{14,10},{16,20},{18,... | collective-permute-start | bytes 3145736 | tf_op jit(solution)/shard_map/ppermute | solution.py:965
  315.3 46.1 %collective-permute-start.34 = (bf16[1024,512]{1,0:T(8,128)(2,1)}, bf16[1024,512]{1,0:T(8,128)(2,1)}, u32[]{:S(2)}, u32[]{:S(2)}) collective-permute-start(bf16[1024,512]{1,0:T(8,128)(2,1)} %get-tuple-element.255), channel_id=1, source_target_pairs={{0,2},{2,0},{4,6},{6,4},{8,10},{10,8},{12,14},{14,12},{16,18},{18,... | collective-permute-start | bytes 3145736 | tf_op jit(solution)/shard_map/ppermute | solution.py:965
  317.4 44.0 %collective-permute-start.35 = (bf16[1024,512]{1,0:T(8,128)(2,1)}, bf16[1024,512]{1,0:T(8,128)(2,1)}, u32[]{:S(2)}, u32[]{:S(2)}) collective-permute-start(bf16[1024,512]{1,0:T(8,128)(2,1)} %get-tuple-element.256), channel_id=1, source_target_pairs={{0,2},{2,0},{4,6},{6,4},{8,10},{10,8},{12,14},{14,12},{16,18},{18,... | collective-permute-start | bytes 3145736 | tf_op jit(solution)/shard_map/ppermute | solution.py:965
  358.1 17.3 %collective-permute-start.36 = (bf16[1024,128]{1,0:T(8,128)(2,1)}, bf16[1024,128]{1,0:T(8,128)(2,1)}, u32[]{:S(2)}, u32[]{:S(2)}) collective-permute-start(bf16[1024,128]{1,0:T(8,128)(2,1)} %weight.1), channel_id=1, source_target_pairs={{0,2},{2,0},{4,6},{6,4},{8,10},{10,8},{12,14},{14,12},{16,18},{18,... | collective-permute-start | bytes 786440 | tf_op jit(solution)/shard_map/ppermute | solution.py:965
  358.4 31.7 %collective-permute-start.37 = (bf16[4,128,768]{2,1,0:T(8,128)(2,1)}, bf16[4,128,768]{2,1,0:T(8,128)(2,1)S(1)}, u32[]{:S(2)}, u32[]{:S(2)}) collective-permute-start(bf16[4,128,768]{2,1,0:T(8,128)(2,1)} %get-tuple-element.328), channel_id=1, source_target_pairs={{0,4},{2,6},{4,0},{6,2},{8,12},{10,14},{12,8},{14,10},{16,20},{18,... | collective-permute-start | bytes 2359304 | tf_op jit(solution)/shard_map/ppermute | solution.py:965
  359.4 36.5 %collective-permute-start.38 = (bf16[4,128,768]{2,1,0:T(8,128)(2,1)}, bf16[4,128,768]{2,1,0:T(8,128)(2,1)S(1)}, u32[]{:S(2)}, u32[]{:S(2)}) collective-permute-start(bf16[4,128,768]{2,1,0:T(8,128)(2,1)} %dynamic-slice_bitcast_fusion), channel_id=1, source_target_pairs={{0,4},{2,6},{4,0},{6,2},{8,12},{10,14},{12,8},{14,10},{16,20},{18,... | collective-permute-start | bytes 2359304 | tf_op jit(solution)/shard_map/ppermute | solution.py:965
  372.1 37.5 %collective-permute-start.39 = (bf16[1024,768]{1,0:T(8,128)(2,1)}, bf16[1024,768]{1,0:T(8,128)(2,1)S(1)}, u32[]{:S(2)}, u32[]{:S(2)}) collective-permute-start(bf16[1024,768]{1,0:T(8,128)(2,1)} %get-tuple-element.323), channel_id=1, source_target_pairs={{0,1},{1,0},{2,3},{3,2},{4,5},{5,4},{6,7},{7,6},{8,9},{9,8},{10,11... | collective-permute-start | bytes 4718600 | tf_op jit(solution)/shard_map/ppermute | solution.py:965
  372.6 51.9 %collective-permute-start.41 = (bf16[4,128,256]{2,1,0:T(8,128)(2,1)}, bf16[4,128,256]{2,1,0:T(8,128)(2,1)}, u32[]{:S(2)}, u32[]{:S(2)}) collective-permute-start(bf16[4,128,256]{2,1,0:T(8,128)(2,1)} %get-tuple-element.338), channel_id=1, source_target_pairs={{0,4},{2,6},{4,0},{6,2},{8,12},{10,14},{12,8},{14,10},{16,20},{18,... | collective-permute-start | bytes 786440 | tf_op jit(solution)/shard_map/ppermute | solution.py:965
  375.4 49.8 %collective-permute-start.42 = (bf16[4,128,256]{2,1,0:T(8,128)(2,1)}, bf16[4,128,256]{2,1,0:T(8,128)(2,1)}, u32[]{:S(2)}, u32[]{:S(2)}) collective-permute-start(bf16[4,128,256]{2,1,0:T(8,128)(2,1)} %dynamic-slice_bitcast_fusion.2), channel_id=1, source_target_pairs={{0,4},{2,6},{4,0},{6,2},{8,12},{10,14},{12,8},{14,10},{16,20},{18,... | collective-permute-start | bytes 786440 | tf_op jit(solution)/shard_map/ppermute | solution.py:965
  390.2 39.2 %collective-permute-start.40 = (bf16[2,128,2048]{2,1,0:T(8,128)(2,1)S(1)}, bf16[2,128,2048]{2,1,0:T(8,128)(2,1)}, u32[]{:S(2)}, u32[]{:S(2)}) collective-permute-start(bf16[2,128,2048]{2,1,0:T(8,128)(2,1)S(1)} %fusion.6), channel_id=1, source_target_pairs={{0,8},{2,10},{4,12},{6,14},{8,0},{10,2},{12,4},{14,6},{16,24},{18,... | collective-permute-start | bytes 3145736 | tf_op jit(solution)/shard_map/ppermute | solution.py:965
  395.9 29.9 %collective-permute-start.43 = (bf16[1024,384]{1,0:T(8,128)(2,1)}, bf16[1024,384]{1,0:T(8,128)(2,1)}, u32[]{:S(2)}, u32[]{:S(2)}) collective-permute-start(bf16[1024,384]{1,0:T(8,128)(2,1)} %get-tuple-element.348), channel_id=1, source_target_pairs={{0,1},{1,0},{2,3},{3,2},{4,5},{5,4},{6,7},{7,6},{8,9},{9,8},{10,11... | collective-permute-start | bytes 2359304 | tf_op jit(solution)/shard_map/ppermute | solution.py:965
  411.9 41.3 %collective-permute-start.45 = (bf16[4,128,768]{2,1,0:T(8,128)(2,1)}, bf16[4,128,768]{2,1,0:T(8,128)(2,1)}, u32[]{:S(2)}, u32[]{:S(2)}) collective-permute-start(bf16[4,128,768]{2,1,0:T(8,128)(2,1)} %fusion.16), channel_id=1, source_target_pairs={{0,4},{2,6},{4,0},{6,2},{8,12},{10,14},{12,8},{14,10},{16,20},{18,... | collective-permute-start | bytes 2359304 | tf_op jit(solution)/shard_map/ppermute | solution.py:965
  424.6 28.6 %collective-permute-start.44 = (bf16[4,128,768]{2,1,0:T(8,128)(2,1)S(1)}, bf16[4,128,768]{2,1,0:T(8,128)(2,1)}, u32[]{:S(2)}, u32[]{:S(2)}) collective-permute-start(bf16[4,128,768]{2,1,0:T(8,128)(2,1)S(1)} %copy-done.52), channel_id=1, source_target_pairs={{0,1},{1,0},{2,3},{3,2},{4,5},{5,4},{6,7},{7,6},{8,9},{9,8},{10,11... | collective-permute-start | bytes 2359304 | tf_op jit(solution)/shard_map/ppermute | solution.py:965
  429.3 37.8 %collective-permute-start.47 = (bf16[4,128,384]{2,1,0:T(8,128)(2,1)}, bf16[4,128,384]{2,1,0:T(8,128)(2,1)}, u32[]{:S(2)}, u32[]{:S(2)}) collective-permute-start(bf16[4,128,384]{2,1,0:T(8,128)(2,1)} %fusion.33), channel_id=1, source_target_pairs={{0,4},{2,6},{4,0},{6,2},{8,12},{10,14},{12,8},{14,10},{16,20},{18,... | collective-permute-start | bytes 1179656 | tf_op jit(solution)/shard_map/ppermute | solution.py:965
  430.3 36.8 %collective-permute-start.46 = (bf16[4,128,256]{2,1,0:T(8,128)(2,1)}, bf16[4,128,256]{2,1,0:T(8,128)(2,1)}, u32[]{:S(2)}, u32[]{:S(2)}) collective-permute-start(bf16[4,128,256]{2,1,0:T(8,128)(2,1)} %fusion.32), channel_id=1, source_target_pairs={{0,1},{1,0},{2,3},{3,2},{4,5},{5,4},{6,7},{7,6},{8,9},{9,8},{10,11... | collective-permute-start | bytes 786440 | tf_op jit(solution)/shard_map/ppermute | solution.py:965
  433.8 50.4 %collective-permute-start.49 = (bf16[128,2048]{1,0:T(8,128)(2,1)}, bf16[128,2048]{1,0:T(8,128)(2,1)}, u32[]{:S(2)}, u32[]{:S(2)}) collective-permute-start(bf16[128,2048]{1,0:T(8,128)(2,1)} %fusion.13), channel_id=1, source_target_pairs={{0,16},{2,18},{4,20},{6,22},{8,24},{10,26},{12,28},{14,30},{16,0},... | collective-permute-start | bytes 1572872 | tf_op jit(solution)/shard_map/ppermute | solution.py:965
  469.3 14.9 %collective-permute-start.50 = (bf16[2,128,640]{2,1,0:T(8,128)(2,1)S(1)}, bf16[2,128,640]{2,1,0:T(8,128)(2,1)S(1)}, u32[]{:S(2)}, u32[]{:S(2)}) collective-permute-start(bf16[2,128,640]{2,1,0:T(8,128)(2,1)S(1)} %fusion.38), channel_id=1, source_target_pairs={{0,8},{2,10},{4,12},{6,14},{8,0},{10,2},{12,4},{14,6},{16,24},{18,... | collective-permute-start | bytes 983048 | tf_op jit(solution)/shard_map/ppermute | solution.py:965
  470.9 21.8 %collective-permute-start.48 = (bf16[2,128,1536]{2,1,0:T(8,128)(2,1)S(1)}, bf16[2,128,1536]{2,1,0:T(8,128)(2,1)S(1)}, u32[]{:S(2)}, u32[]{:S(2)}) collective-permute-start(bf16[2,128,1536]{2,1,0:T(8,128)(2,1)S(1)} %fusion.17), channel_id=1, source_target_pairs={{0,8},{2,10},{4,12},{6,14},{8,0},{10,2},{12,4},{14,6},{16,24},{18,... | collective-permute-start | bytes 2359304 | tf_op jit(solution)/shard_map/ppermute | solution.py:965
  494.2 15.4 %collective-permute-start.60 = (bf16[64,2048]{1,0:T(8,128)(2,1)S(1)}, bf16[64,2048]{1,0:T(8,128)(2,1)S(1)}, u32[]{:S(2)}, u32[]{:S(2)}) collective-permute-start(bf16[64,2048]{1,0:T(8,128)(2,1)S(1)} %get-tuple-element.320), channel_id=1, source_target_pairs={{0,2},{2,0},{4,6},{6,4},{8,10},{10,8},{12,14},{14,12},{16,18},{18,... | collective-permute-start | bytes 786440 | tf_op jit(solution)/shard_map/ppermute | solution.py:965
  507.0 19.6 %collective-permute-start.58 = (bf16[128,1536]{1,0:T(8,128)(2,1)S(1)}, bf16[128,1536]{1,0:T(8,128)(2,1)S(1)}, u32[]{:S(2)}, u32[]{:S(2)}) collective-permute-start(bf16[128,1536]{1,0:T(8,128)(2,1)S(1)} %fusion.22), channel_id=1, source_target_pairs={{0,16},{2,18},{4,20},{6,22},{8,24},{10,26},{12,28},{14,30},{16,0},... | collective-permute-start | bytes 1179656 | tf_op jit(solution)/shard_map/ppermute | solution.py:965
  513.3 13.7 %collective-permute-start.54 = (f32[272,128]{1,0:T(8,128)S(1)}, f32[272,128]{1,0:T(8,128)S(1)}, u32[]{:S(2)}, u32[]{:S(2)}) collective-permute-start(f32[272,128]{1,0:T(8,128)S(1)} %add.578), channel_id=1, source_target_pairs={{0,8},{2,10},{4,12},{6,14},{8,0},{10,2},{12,4},{14,6},{16,24},{18,... | collective-permute-start | bytes 417800 | tf_op jit(solution)/shard_map/ppermute | solution.py:965
  (96 other events, 926.8 us)

commit v4 on v3

--- a/solution.py
+++ b/solution.py
@@ -356,7 +356,7 @@
 
 
 def sig(u):
-    return 1.0 / (1.0 + jnp.exp(-u))
+    return 0.5 + 0.5 * jnp.tanh(0.5 * u)
 
 
 def silu_pair(u):
@@ -460,6 +460,32 @@
     )
 
 
+def k_ema_params(scal, own, oth):
+    ch, width = own.shape
+    groups = 2 * ch // 128
+
+    def body(s, own_ref, oth_ref, dec_ref, cf_ref, om_ref, scr):
+        scr[pl.ds(pl.multiple_of(s[6] * ch, ch), ch), :] = own_ref[...]
+        scr[pl.ds(pl.multiple_of(s[7] * ch, ch), ch), :] = oth_ref[...]
+        v = scr[...].T
+        rate = sig(v[0:H])
+        dec = 1.0 - rate * sig(v[H : 2 * H])
+        cf = rate * v[2 * H : 3 * H] * v[3 * H : 4 * H]
+        for g in range(groups):
+            lanes = slice(g * 128, (g + 1) * 128)
+            dec_ref[pl.ds(g, H, stride=groups), :] = dec[:, lanes]
+            cf_ref[pl.ds(g, H, stride=groups), :] = cf[:, lanes]
+            om_ref[g : g + 1, :] = v[4 * H : 4 * H + 1, lanes]
+
+    par = (H * groups, 128)
+    return run(
+        body, (1,), scal, [own, oth], [whole((ch, width))] * 2,
+        [sds(par, F32), sds(par, F32), sds((groups, 128), F32)],
+        [pl.BlockSpec(par, lambda i, s: (0, 0))] * 2 + [pl.BlockSpec((groups, 128), lambda i, s: (0, 0))],
+        [pltpu.VMEM((2 * ch, width), F32)], flops=1e8, name="ema_params",
+    )
+
+
 def k_ema_forward(scal, normed, decay, coef, omega, first, count, before=None):
     n, d = normed.shape
     groups = d // 128
@@ -480,8 +506,8 @@
 
         def steps(b, carry):
             states = list(carry)
-            for u in range(8):
-                row = pl.multiple_of((b * 8 + u) * groups, groups)
+            for u in range(16):
+                row = pl.multiple_of((b * 16 + u) * groups, groups)
                 xt = xs[pl.ds(row, groups), :]
                 parts = [om * xt, None, None, None]
                 for k in range(H):
@@ -492,7 +518,7 @@
             return tuple(states)
 
         start = tuple(st[k * groups : (k + 1) * groups, :] for k in range(H))
-        end = lax.fori_loop(0, tb // 8, steps, start)
+        end = lax.fori_loop(0, tb // 16, steps, start)
         for k in range(H):
             st[k * groups : (k + 1) * groups, :] = end[k]
         for g in range(groups):
@@ -531,7 +557,7 @@
             for i, ref in enumerate((back, deriv, a_ref, b_ref, w_ref)):
                 ref[...] = refs[i][...] if before else jnp.zeros_like(ref)
 
-        d_e = (de_ref[...] + col_inner(z_ref[...], wz_ref[...])) * sl_ref[...].astype(F32)
+        d_e = (de_ref[...].astype(F32) + col_inner(z_ref[...], wz_ref[...])) * sl_ref[...].astype(F32)
         for g in range(groups):
             xs[pl.ds(g, tb, stride=groups), :] = x_ref[:, g * 128 : (g + 1) * 128].astype(F32)
             gs[pl.ds(g, tb, stride=groups), :] = d_e[:, g * 128 : (g + 1) * 128]
@@ -543,8 +569,8 @@
 
             def steps(b, carry, part=part, at=at, dec=dec):
                 bk, dv, aa, bb, ww = (list(c) for c in carry)
-                for u in range(4):
-                    row = pl.multiple_of((tb - 1 - (b * 4 + u)) * groups, groups)
+                for u in range(8):
+                    row = pl.multiple_of((tb - 1 - (b * 8 + u)) * groups, groups)
                     xt = xs[pl.ds(row, groups), :]
                     gt = gs[pl.ds(row, groups), :]
                     if part == 0:
@@ -569,7 +595,7 @@
                 tuple(b_ref[a, :] for a in at),
                 (w_ref[...],),
             )
-            bk, dv, aa, bb, ww = lax.fori_loop(0, tb // 4, steps, start)
+            bk, dv, aa, bb, ww = lax.fori_loop(0, tb // 8, steps, start)
             for k in range(half):
                 back[at[k], :] = bk[k]
                 deriv[at[k], :] = dv[k]
@@ -597,13 +623,18 @@
     )
 
 
-def k_attend(scal, q, k, v_own, v_oth, g_own, g_oth, gs_own, gs_oth):
+def k_attend(scal, q, k, v_own, v_oth, ema_low, g_own, packs):
     n, zw = q.shape
-    half = v_own.shape[1]
+    d, half = g_own.shape
+    rp = packs[0].shape[0]
     blocks = n // ROWS
     scale = zw ** (-0.5)
 
-    def body(s, q_ref, k_ref, vo, vt, go, gt, so, st, gated_o, gated_t, mo, mt, p_ref):
+    def body(s, q_ref, k_ref, vo, vt, e_ref, wo, w0, w1, w2, w3, gated_o, gated_t, go, gt, mo, mt, p_ref, w_scr):
+        @pl.when(pl.program_id(0) == 0)
+        def _():
+            place(w_scr, s, (w0, w1, w2, w3), table=8)
+
         for i in range(blocks):
 
             @pl.when(pl.program_id(0) == i)
@@ -616,17 +647,23 @@
                 e = jnp.exp(sc - jnp.max(sc, axis=-1, keepdims=True))
                 p = (e * (1.0 / jnp.sum(e, axis=-1, keepdims=True))).astype(BF)
                 p_ref[:, 0:seen] = p
-                for v_ref, g_ref, sl_ref, gated, m in ((vo, go, so, gated_o, mo), (vt, gt, st, gated_t, mt)):
+                if seen < n:
+                    p_ref[:, seen:] = jnp.zeros((ROWS, n - seen), BF)
+                for v_ref, w, gated, g, m in ((vo, wo, gated_o, go, mo), (vt, w_scr, gated_t, gt, mt)):
+                    act, slope = silu_pair(matmul(e_ref[...], w[...]))
                     att = matmul(p, v_ref[0:seen, :])
-                    gated[...] = (g_ref[...].astype(F32) * att).astype(BF)
-                    m[...] = (sl_ref[...].astype(F32) * att).astype(BF)
-
-    return run(
-        body, (blocks,), scal, [q, k, v_own, v_oth, g_own, g_oth, gs_own, gs_oth],
-        [rows_of(zw), whole((n, zw)), whole((n, half)), whole((n, half))] + [rows_of(half)] * 4,
-        [sds((n, half))] * 4 + [sds((n, n))],
-        [rows_of(half)] * 4 + [rows_of(n)],
-        flops=n * n * (zw + 2 * half) * 1.25, name="attend",
+                    gated[...] = (act * att).astype(BF)
+                    g[...] = act.astype(BF)
+                    m[...] = (slope * att).astype(BF)
+
+    return run(
+        body, (blocks,), scal, [q, k, v_own, v_oth, ema_low, g_own, *packs],
+        [rows_of(zw), whole((n, zw)), whole((n, half)), whole((n, half)), rows_of(d), whole((d, half))]
+        + [whole((rp, half))] * 4,
+        [sds((n, half))] * 6 + [sds((n, n))],
+        [rows_of(half)] * 6 + [rows_of(n)],
+        [pltpu.VMEM((d, half), BF)],
+        flops=n * n * (zw + 2 * half) * 1.25 + 4 * n * d * half, name="attend",
     )
 
 
@@ -654,7 +691,7 @@
         act, slope = silu_pair(h_pre)
         update = sig(f_pre)
         mixed = update * act + (1.0 - update) * x
-        mix_ref[...] = mixed
+        mix_ref[...] = mixed.astype(BF)
         low_ref[...] = (mixed * lax.rsqrt(jnp.mean(mixed * mixed, axis=-1, keepdims=True) + norm_eps)).astype(BF)
         a_ref[...] = (update * slope).astype(BF)
         b_ref[...] = ((act - x) * update * (1.0 - update)).astype(BF)
@@ -665,30 +702,46 @@
     specs += [piece_whole(ru, d, 0)] * 4 + [piece_whole(rh, d, 0)] * 4 + [piece_whole(rh, d, 1)] * 4
     return run(
         body, (n // ROWS,), scal, ins, specs,
-        [sds((n, d), F32), sds((n, d)), sds((n, d)), sds((n, d)), sds((n, d))],
+        [sds((n, d))] * 5,
         [rows_of(d)] * 5,
         [pltpu.VMEM((half, d), BF), pltpu.VMEM((2 * ch, d), BF), pltpu.VMEM((2 * ch, d), BF)],
         flops=2 * n * d * (2 * half + 4 * ch), name="gate",
     )
 
 
-def k_ffn(scal, lowered, cot, up, down, part):
+def k_ffn(scal, lowered, cot, up, down, part, before=None):
     n, d = lowered.shape
     pieces = len(up) > 1
     tn = up[0].shape[1] // 4
+    rows = d // 2
 
     def body(s, low_ref, c_ref, *refs):
         step = pl.program_id(0)
         nu, nd = len(up), len(down)
-        ups, downs = refs[:nu], refs[nu : nu + nd]
-        out_ref, gl_ref, grads, acc, gl, u_scr = refs[nu + nd :]
+        ups, downs, refs = refs[:nu], refs[nu : nu + nd], refs[nu + nd :]
+        if before:
+            ins, refs = refs[:2], refs[2:]
+            held, sems = refs[-2:]
+            refs = refs[:-2]
+            copies = [pltpu.make_async_copy(ins[i], held.at[i], sems.at[i]) for i in range(2)]
+        out_ref, gl_ref, dn, up_ref, acc, gl, u_scr = refs
         if pieces:
             place(u_scr, s, ups)
             wu = u_scr
         else:
             wu = ups[0]
 
+        def split(ref, grad):
+            by_x = grad.reshape(4, 2, d // 8, tn)
+            flip = s[12] == 0
+            a, b = by_x[:, 0].reshape(rows, tn), by_x[:, 1].reshape(rows, tn)
+            ref[0] = jnp.where(flip, a, b).astype(BF)
+            ref[1] = jnp.where(flip, b, a).astype(BF)
+
         def work(wd, i):
+            if before and i == 0:
+                for c in copies:
+                    c.start()
             act, slope = silu_pair(matmul(low_ref[...], wu[...]))
             hid = act.astype(BF)
             out = matmul(hid, wd[...])
@@ -698,10 +751,15 @@
                 acc[...] = out
                 gl[...] = back
             else:
+                if before:
+                    for c in copies:
+                        c.wait()
+                    out = out + held[0].astype(F32)
+                    back = back + held[1].astype(F32)
                 out_ref[...] = (acc[...] + out).astype(BF)
                 gl_ref[...] = (gl[...] + back).astype(BF)
-            grads[0] = row_inner(c_ref[...], hid).astype(BF)
-            grads[1] = row_inner(low_ref[...], du).astype(BF)
+            split(dn, row_inner(c_ref[...], hid))
+            split(up_ref, row_inner(low_ref[...], du))
 
         for i in range(2):
 
@@ -719,17 +777,20 @@
             pl.BlockSpec((tn, d), lambda i, s: (s[first + i], 0)),
         ]
     still = pl.BlockSpec((n, d), lambda i, s: (0, 0))
-    return run(
-        body, (2,), scal, [lowered, cot, *up, *down],
-        [whole((n, d)), whole((n, d))] + specs,
-        [sds((n, d)), sds((n, d)), sds((2, d, 2 * tn))],
-        [still, still, pl.BlockSpec((2, d, tn), lambda i, s: (0, 0, s[first + i] % 2))],
-        [pltpu.VMEM((n, d), F32), pltpu.VMEM((n, d), F32), pltpu.VMEM((d, tn), BF)],
+    grads = pl.BlockSpec((2, rows, tn), lambda i, s: (0, 0, s[first + i] % 2))
+    more = list(before) if before else []
+    return run(
+        body, (2,), scal, [lowered, cot, *up, *down, *more],
+        [whole((n, d)), whole((n, d))] + specs + [pl.BlockSpec(memory_space=pl.ANY)] * len(more),
+        [sds((n, d)), sds((n, d)), sds((2, rows, 2 * tn)), sds((2, rows, 2 * tn))],
+        [still, still, grads, grads],
+        [pltpu.VMEM((n, d), F32), pltpu.VMEM((n, d), F32), pltpu.VMEM((d, tn), BF)]
+        + ([pltpu.VMEM((2, n, d), BF), pltpu.SemaphoreType.DMA((2,))] if before else []),
         flops=24 * n * d * tn, name="ffn",
     )
 
 
-def k_mid_back(scal, dls, accs, cot, mixed, fac_h, fac_f, keep, g_own, g_oth, m_own, m_oth,
+def k_mid_back(scal, dl, acc, cot, mixed, fac_h, fac_f, keep, g_own, g_oth, m_own, m_oth,
                u_own, wg_own, h_own, f_own, packs_g, packs_u, packs_h):
     n, d = cot.shape
     half = u_own.shape[0]
@@ -737,7 +798,7 @@
     ru, rh = packs_u[0].shape[0], packs_h[0].shape[0] // 2
     rg = packs_g[0].shape[0]
 
-    def body(s, l0, l1, l2, l3, o0, o1, o2, o3, c_ref, x_ref, a_ref, b_ref, k_ref, go, gt, mo, mt, uo, wo, ho, fo,
+    def body(s, l_ref, acc_ref, c_ref, x_ref, a_ref, b_ref, k_ref, go, gt, mo, mt, uo, wo, ho, fo,
              w0, w1, w2, w3, u0, u1, u2, u3, h0, h1, h2, h3, f0, f1, f2, f3,
              out_ref, dh_ref, df_ref, dir_ref, ao, at, do, dt, de_ref, u_scr, w_scr, h_scr, f_scr):
         @pl.when(pl.program_id(0) == 0)
@@ -751,10 +812,9 @@
             place(h_scr, s, (h0, h1, h2, h3), oth, 8)
             place(f_scr, s, (f0, f1, f2, f3), oth, 8)
 
-        dl = (l0[...].astype(F32) + l1[...].astype(F32)) + (l2[...].astype(F32) + l3[...].astype(F32))
-        out = (o0[...].astype(F32) + o1[...].astype(F32)) + (o2[...].astype(F32) + o3[...].astype(F32))
-        m = x_ref[...]
-        out_ref[...] = (m + out).astype(BF)
+        dl = l_ref[...].astype(F32)
+        m = x_ref[...].astype(F32)
+        out_ref[...] = (m + acc_ref[...].astype(F32)).astype(BF)
         r = lax.rsqrt(jnp.mean(m * m, axis=-1, keepdims=True) + norm_eps)
         n2 = m * r
         dm = c_ref[...].astype(F32) + r * (dl - n2 * jnp.mean(dl * n2, axis=-1, keepdims=True))
@@ -770,85 +830,75 @@
             low = (dg * m_ref[...].astype(F32)).astype(BF)
             d_out[...] = low
             de = de + col_inner(low, w[...])
-        de_ref[...] = de
-
-    ins = [*dls, *accs, cot, mixed, fac_h, fac_f, keep, g_own, g_oth, m_own, m_oth, u_own, wg_own, h_own, f_own]
+        de_ref[...] = de.astype(BF)
+
+    ins = [dl, acc, cot, mixed, fac_h, fac_f, keep, g_own, g_oth, m_own, m_oth, u_own, wg_own, h_own, f_own]
     ins += [*packs_g, *packs_u, *packs_h, *packs_h]
-    specs = [rows_of(d)] * 13 + [rows_of(half)] * 4
+    specs = [rows_of(d)] * 7 + [rows_of(half)] * 4
     specs += [whole((half, d)), whole((d, half)), whole((ch, d)), whole((ch, d))]
     specs += [piece_whole(rg, half, 0)] * 4 + [piece_whole(ru, d, 0)] * 4
     specs += [piece_whole(rh, d, 0)] * 4 + [piece_whole(rh, d, 1)] * 4
     return run(
         body, (n // ROWS,), scal, ins, specs,
-        [sds((n, d))] * 4 + [sds((n, half))] * 4 + [sds((n, d), F32)],
+        [sds((n, d))] * 4 + [sds((n, half))] * 4 + [sds((n, d))],
         [rows_of(d)] * 4 + [rows_of(half)] * 4 + [rows_of(d)],
         [pltpu.VMEM((half, d), BF), pltpu.VMEM((d, half), BF), pltpu.VMEM((2 * ch, d), BF), pltpu.VMEM((2 * ch, d), BF)],
         flops=2 * n * d * (4 * half + 4 * ch), name="mid_back",
     )
 
 
-def k_value_back(scal, p, da_own, da_oth, vs_own, vs_oth):
-    n = p.shape[0]
-    half = da_own.shape[1]
-    blocks = n // ROWS
-
-    def body(s, p_ref, ao, at, so, st, oo, ot):
-        for j in range(blocks):
-
-            @pl.when(pl.program_id(0) == j)
-            def _(j=j):
-                pj = p_ref[j * ROWS :, :]
-                oo[...] = (row_inner(pj, ao[j * ROWS :, :]) * so[...].astype(F32)).astype(BF)
-                ot[...] = (row_inner(pj, at[j * ROWS :, :]) * st[...].astype(F32)).astype(BF)
-
-    return run(
-        body, (blocks,), scal, [p, da_own, da_oth, vs_own, vs_oth],
-        [cols_of(n, ROWS), whole((n, half)), whole((n, half)), rows_of(half), rows_of(half)],
-        [sds((n, half))] * 2,
-        [rows_of(half)] * 2,
-        flops=n * n * 2 * half * 1.25, name="value_back",
-    )
-
-
-def k_score_back(scal, p, da_own, da_oth, v_own, v_oth, q, k, z_pre, gain):
+def k_attend_back(scal, p, da_own, da_oth, v_own, v_oth, vs_own, vs_oth, q, k, z_pre, gain):
     n, zw = q.shape
     half = da_own.shape[1]
     blocks = n // ROWS
     scale = zw ** (-0.5)
 
-    def body(s, p_ref, ao, at, vo, vt, q_ref, k_ref, z_ref, g_ref, dz_ref, st_ref, ds, dq):
-        for i in range(blocks):
-
-            @pl.when(pl.program_id(0) == i)
+    def body(s, p_ref, ao, at, vo, vt, so, st, q_ref, k_ref, z_ref, g_ref, oo, ot, dz_ref, sum_ref, dvo, dvt, dks):
+        for step, i in enumerate(reversed(range(blocks))):
+
+            @pl.when(pl.program_id(0) == step)
             def _(i=i):
                 seen = (i + 1) * ROWS
-                pr = p_ref[:, 0:seen].astype(F32)
+                lo = i * ROWS
+                last = i == blocks - 1
+                pb = p_ref[:, 0:seen]
+                pr = pb.astype(F32)
                 dp = col_inner(ao[...], vo[0:seen, :]) + col_inner(at[...], vt[0:seen, :])
-                d = (pr * (dp - jnp.sum(pr * dp, axis=-1, keepdims=True))).astype(BF)
-                ds[i * ROWS : (i + 1) * ROWS, 0:seen] = d
-                dq[i * ROWS : (i + 1) * ROWS, :] = matmul(d, k_ref[0:seen, :]) * scale
-                if i == blocks - 1:
-                    sums = [jnp.zeros((1, zw), F32)] * 4
-                    for j in range(blocks):
-                        at_j = slice(j * ROWS, (j + 1) * ROWS)
-                        dk = row_inner(ds[j * ROWS :, at_j], q_ref[j * ROWS :, :]) * scale
-                        dqj = dq[at_j, :]
-                        act, slope = silu_pair(z_ref[at_j, :])
-                        dz_ref[at_j, :] = (slope * (dqj * g_ref[0:1, :] + dk * g_ref[1:2, :])).astype(BF)
-                        for n_, v in enumerate((dqj * act, dk * act, dqj, dk)):
-                            sums[n_] = sums[n_] + jnp.sum(v, axis=0, keepdims=True)
-                    for n_ in range(4):
-                        st_ref[n_ : n_ + 1, :] = sums[n_]
-                    st_ref[4:8, :] = jnp.zeros((4, zw), F32)
-
-    return run(
-        body, (blocks,), scal, [p, da_own, da_oth, v_own, v_oth, q, k, z_pre, gain],
-        [rows_of(n), rows_of(half), rows_of(half), whole((n, half)), whole((n, half)), whole((n, zw)),
-         whole((n, zw)), whole((n, zw)), whole((2, zw))],
-        [sds((n, zw)), sds((8, zw), F32)],
-        [pl.BlockSpec((n, zw), lambda i, s: (0, 0)), pl.BlockSpec((8, zw), lambda i, s: (0, 0))],
-        [pltpu.VMEM((n, n), BF), pltpu.VMEM((n, zw), F32)],
-        flops=n * n * 2 * half * 1.25, name="score_back",
+                ds = (pr * (dp - jnp.sum(pr * dp, axis=-1, keepdims=True))).astype(BF)
+                dq = matmul(ds, k_ref[0:seen, :]) * scale
+                dk = row_inner(ds, q_ref[...]) * scale
+                if not last:
+                    dk = dk + dks[0:seen, :]
+                for a_ref, acc, sl, o_ref in ((ao, dvo, so, oo), (at, dvt, st, ot)):
+                    dv = row_inner(pb, a_ref[...])
+                    if not last:
+                        dv = dv + acc[0:seen, :]
+                    if i:
+                        acc[0:lo, :] = dv[0:lo]
+                    o_ref[...] = (dv[lo:seen] * sl[...].astype(F32)).astype(BF)
+                if i:
+                    dks[0:lo, :] = dk[0:lo]
+                dk = dk[lo:seen]
+                act, slope = silu_pair(z_ref[...])
+                dz_ref[...] = (slope * (dq * g_ref[0:1, :] + dk * g_ref[1:2, :])).astype(BF)
+                for j, v in enumerate((dq * act, dk * act, dq, dk)):
+                    part = jnp.sum(v, axis=0, keepdims=True)
+                    sum_ref[j : j + 1, :] = part if last else sum_ref[j : j + 1, :] + part
+                if last:
+                    sum_ref[4:8, :] = jnp.zeros((4, zw), F32)
+
+    def back_rows(cols):
+        return pl.BlockSpec((ROWS, cols), lambda i, s: (blocks - 1 - i, 0))
+
+    low = n - ROWS
+    return run(
+        body, (blocks,), scal, [p, da_own, da_oth, v_own, v_oth, vs_own, vs_oth, q, k, z_pre, gain],
+        [back_rows(n), back_rows(half), back_rows(half), whole((n, half)), whole((n, half)), back_rows(half),
+         back_rows(half), back_rows(zw), whole((n, zw)), back_rows(zw), whole((2, zw))],
+        [sds((n, half)), sds((n, half)), sds((n, zw)), sds((8, zw), F32)],
+        [back_rows(half), back_rows(half), back_rows(zw), pl.BlockSpec((8, zw), lambda i, s: (0, 0))],
+        [pltpu.VMEM((low, half), F32), pltpu.VMEM((low, half), F32), pltpu.VMEM((low, zw), F32)],
+        flops=n * n * 4 * half * 1.25, name="attend_back",
     )
 
 
@@ -877,88 +927,107 @@
     )[0]
 
 
-def k_weight(scal, left, right, at, cols, tn, adds=(), name="weight"):
-    n, d = left.shape
-    steps = cols // tn
-
-    def body(s, l_ref, r_ref, *refs):
-        total = row_inner(l_ref[...], r_ref[...])
-        for ref in refs[:-1]:
-            total = total + ref[...].astype(F32)
-        refs[-1][...] = total.astype(BF)
-
-    ins = [left, right] + [a for a, _ in adds]
-    specs = [whole((n, d)), pl.BlockSpec((n, tn), lambda i, s: (0, at(s) * steps + i))]
-    specs += [pl.BlockSpec((d, tn), lambda i, s, o=o: (0, o * steps + i)) for _, o in adds]
-    return run(
-        body, (steps,), scal, ins, specs, [sds((d, cols))], [cols_of(d, tn)],
-        flops=2 * n * d * cols, name=name,
-    )[0]
+def split_rows(s, grad):
+    d, c = grad.shape
+    by_x = grad.reshape(4, 2, d // 8, c)
+    flip = s[12] == 0
+    a, b = by_x[:, 0].reshape(d // 2, c), by_x[:, 1].reshape(d // 2, c)
+    return jnp.where(flip, a, b), jnp.where(flip, b, a)
 
 
 def k_weight_mid(scal, ema_low, dh, df, gated_own, gated_oth, dg_own, dg_oth, part, got=None):
     n, d = ema_low.shape
     half = gated_own.shape[1] // 2
-    qe = d // 4
+    tn = d // 4
+    rows = d // 2
 
     def body(s, e_ref, h_ref, f_ref, go, gt, do, dt, eo, et, *refs):
-        adds = refs[:-2]
-        own, oth = refs[-2:]
-
-        def put(out, k, at, width, value):
-            if adds:
-                value = value + adds[k][:, at : at + width].astype(F32)
-            out[:, at : at + width] = value.astype(BF)
-
         for i in range(3):
 
             @pl.when(pl.program_id(0) == i)
             def _(i=i):
-                for k, (out, g, dg, e) in enumerate(((own, go, do, eo), (oth, gt, dt, et))):
-                    if i == 0:
-                        put(out, k, 0, half, row_inner(h_ref[...], g[...]))
-                    elif i == 1:
-                        put(out, k, 0, half, row_inner(e_ref[...], dg[...]))
+                for k, (g, dg, e) in enumerate(((go, do, eo), (gt, dt, et))):
+                    a = row_inner(h_ref[...], g[...] if i < 2 else e[...])
+                    b = row_inner(e_ref[...], dg[...]) if i < 2 else row_inner(f_ref[...], e[...])
+                    a, b = split_rows(s, a), split_rows(s, b)
+                    if got is None:
+                        for j in range(2):
+                            refs[0][k, j] = a[j].astype(BF)
+                            refs[1][k, j] = b[j].astype(BF)
                     else:
-                        put(out, k, 0, qe, row_inner(h_ref[...], e[...]))
-                        put(out, k, qe, qe, row_inner(f_ref[...], e[...]))
-
-    at = pl.BlockSpec((n, half), lambda i, s: (0, s[part]), pipeline_mode=pl.Buffered(1))
-    e_own = pl.BlockSpec((n, qe), lambda i, s: (0, s[6] * 2 + s[part]), pipeline_mode=pl.Buffered(1))
-    e_oth = pl.BlockSpec((n, qe), lambda i, s: (0, s[7] * 2 + s[part]), pipeline_mode=pl.Buffered(1))
+                        a = [a[j] + refs[0][k, j].astype(F32) for j in range(2)]
+                        b = [b[j] + refs[1][k, j].astype(F32) for j in range(2)]
+                        refs[2][k] = a[1].astype(BF)
+                        refs[3][k] = a[0].astype(BF)
+                        for j in range(2):
+                            refs[4 + k][j] = b[j].astype(BF)
+
+    at = pl.BlockSpec((n, tn), lambda i, s: (0, s[part] * 2 + jnp.minimum(i, 1)))
+    e_own = pl.BlockSpec((n, tn), lambda i, s: (0, s[6] * 2 + s[part]), pipeline_mode=pl.Buffered(1))
+    e_oth = pl.BlockSpec((n, tn), lambda i, s: (0, s[7] * 2 + s[part]), pipeline_mode=pl.Buffered(1))
+    four = pl.BlockSpec((2, 2, rows, tn), lambda i, s: (0, 0, 0, i))
+    two = pl.BlockSpec((2, rows, tn), lambda i, s: (0, 0, i))
     adds = list(got) if got is not None else []
     return run(
         body, (3,), scal, [ema_low, dh, df, gated_own, gated_oth, dg_own, dg_oth, ema_low, ema_low] + adds,
-        [whole((n, d))] * 3 + [at] * 4 + [e_own, e_oth] + [cols_of(d, half)] * len(adds),
-        [sds((d, 3 * half))] * 2, [cols_of(d, half)] * 2,
+        [whole((n, d))] * 3 + [at] * 4 + [e_own, e_oth] + [four] * len(adds),
+        [sds((2, rows, 3 * tn))] * 4 if adds else [sds((2, 2, rows, 3 * tn))] * 2,
+        [two] * 4 if adds else [four] * 2,
         flops=2 * n * d * 6 * half, name="weight_mid",
     )
 
 
 def k_weight_value(scal, normed, dv_own, dv_oth, part, got=None):
     n, d = normed.shape
-    half = dv_own.shape[1] // 2
+    tn = dv_own.shape[1] // 4
+    rows = d // 2
 
     def body(s, x_ref, vo, vt, *refs):
-        adds = refs[:-2]
-        for i, v in enumerate((vo, vt)):
+        for i in range(2):
 
             @pl.when(pl.program_id(0) == i)
-            def _(i=i, v=v):
-                total = row_inner(x_ref[...], v[...])
-                if adds:
-                    total = total + adds[i][...].astype(F32)
-                refs[-2 + i][...] = total.astype(BF)
-
-    at = pl.BlockSpec((n, half), lambda i, s: (0, s[part]), pipeline_mode=pl.Buffered(1))
-    adds = list(got) if got is not None else []
-    still = pl.BlockSpec((d, half), lambda i, s: (0, 0))
+            def _(i=i):
+                for k, v in enumerate((vo, vt)):
+                    a = split_rows(s, row_inner(x_ref[...], v[...]))
+                    if got is None:
+                        for j in range(2):
+                            refs[0][k, j] = a[j].astype(BF)
+                    else:
+                        a = [a[j] + refs[0][k, j].astype(F32) for j in range(2)]
+                        if i == 0:
+                            refs[1][k] = a[1].astype(BF)
+                            refs[2][k] = a[0].astype(BF)
+                        else:
+                            for j in range(2):
+                                refs[3 + k][j] = a[j].astype(BF)
+
+    at = pl.BlockSpec((n, tn), lambda i, s: (0, s[part] * 2 + i))
+    four = pl.BlockSpec((2, 2, rows, tn), lambda i, s: (0, 0, 0, i))
+    still = pl.BlockSpec((2, rows, tn), lambda i, s: (0, 0, 0))
+    adds = [got] if got is not None else []
     return run(
         body, (2,), scal, [normed, dv_own, dv_oth] + adds,
-        [whole((n, d)), at, at] + [whole((d, half))] * len(adds),
-        [sds((d, half))] * 2, [still] * 2,
-        flops=2 * n * d * 2 * half, name="weight_value",
-    )
+        [whole((n, d)), at, at] + [four] * len(adds),
+        [sds((2, rows, tn))] * 4 if adds else [sds((2, 2, rows, 2 * tn))],
+        [still] * 4 if adds else [four],
+        flops=2 * n * d * 4 * tn, name="weight_value",
+    )
+
+
+def k_weight_z(scal, ema_low, dz):
+    n, d = ema_low.shape
+    zw = dz.shape[1]
+
+    def body(s, e_ref, z_ref, o_ref):
+        a = split_rows(s, row_inner(e_ref[...], z_ref[...]))
+        for j in range(2):
+            o_ref[j] = a[j].astype(BF)
+
+    return run(
+        body, (1,), scal, [ema_low, dz], [whole((n, d)), whole((n, zw))],
+        [sds((2, d // 2, zw))], [pl.BlockSpec((2, d // 2, zw), lambda i, s: (0, 0, 0))],
+        flops=2 * n * d * zw, name="weight_z",
+    )[0]
 
 
 def swap(values, axis, bit, size):
@@ -982,7 +1051,7 @@
     z_pos = me // 4
     kx = core * 2 + x_pos
     kz = core * 2 + z_pos % 2
-    scal = jnp.stack([kx, kx ^ 1, kx ^ 2, kx ^ 3, core, 1 - core, t, 1 - t, kz, kz ^ 1, kz ^ 2, kz ^ 3])
+    scal = jnp.stack([kx, kx ^ 1, kx ^ 2, kx ^ 3, core, 1 - core, t, 1 - t, kz, kz ^ 1, kz ^ 2, kz ^ 3, x_pos])
 
     def held(values, *deps):
         return lax.optimization_barrier((values, deps))[0]
@@ -1007,69 +1076,52 @@
         return lax.dynamic_slice_in_dim(w, k * rows, rows, 0)
 
     own_params = jnp.concatenate(
-        [a.T for a in (alpha_logit, delta_logit, ema_beta, ema_eta)] + [ema_omega[None]], axis=0
+        [alpha_logit, delta_logit, ema_beta, ema_eta, ema_omega[:, None],
+         jnp.zeros((ema_omega.shape[0], 128 - 4 * H - 1), F32)], axis=1
     )
     oth_params = over_tensor(own_params)
     pv = [over_tensor(my_rows(w_v, kx))]
-    params = jnp.where(
-        t == 0,
-        jnp.concatenate([own_params, oth_params], axis=1),
-        jnp.concatenate([oth_params, own_params], axis=1),
-    )
-    al, de, be, et = (params[i * H : (i + 1) * H] for i in range(4))
-    alpha_rate = jax.nn.sigmoid(al)
-    decay = (1.0 - alpha_rate * jax.nn.sigmoid(de)).reshape(-1, 128)
-    coef = (alpha_rate * be * et).reshape(-1, 128)
-    omega = params[4 * H].reshape(-1, 128)
-
     normed, v_own, vs_own = k_value_own(scal, tokens, w_v)
     pg = [over_tensor(held(my_rows(w_gamma, kz), v_own))]
+    decay, coef, omega = k_ema_params(after(v_own), own_params, oth_params)
     blocks = n // 128
     ema_a = k_ema_forward(after(v_own), normed, decay, coef, omega, 0, blocks // 2)
     pv.append(over_x(held(pv[0], ema_a[0])))
+    pu = [over_tensor(held(my_rows(u_h, kx), ema_a[0]))]
     ema_low, e_slope, state = k_ema_forward(
         after(ema_a[0]), normed, decay, coef, omega, blocks // 2, blocks // 2, (ema_a[2], ema_a[0], ema_a[1])
     )
     pg.append(over_z(held(pg[0], state)))
-    pu = [over_tensor(held(my_rows(u_h, kx), state))]
+    ph = [over_tensor(held(jnp.concatenate([my_rows(w_h, kz), my_rows(w_phi, kz)], axis=0), state))]
     z_pre, query, key = k_query_key(scal, ema_low, w_z, qk_gain, qk_bias)
     pv += [over_core(v) for v in held((pv[0], pv[1]), query)]
-    g_own, gs_own = k_act_own(after(query), ema_low, w_gamma, 512)
-    pg += [over_core(v) for v in held((pg[0], pg[1]), g_own)]
-    pu.append(over_x(held(pu[0], g_own)))
-    ph = [over_tensor(held(jnp.concatenate([my_rows(w_h, kz), my_rows(w_phi, kz)], axis=0), g_own))]
-    v_oth, vs_oth = k_act_other(after(g_own), normed, pv, 0, 512)
-    pup = [over_tensor(held(my_rows(w_up, kx), v_oth))]
-    g_oth, gs_oth = k_act_other(after(v_oth), ema_low, pg, 8, 512)
-    ph.append(over_z(held(ph[0], g_oth)))
-    pu += [over_core(v) for v in held((pu[0], pu[1]), g_oth)]
-    gated_own, gated_oth, m_own, m_oth, probs = k_attend(
-        after(g_oth), query, key, v_own, v_oth, g_own, g_oth, gs_own, gs_oth
-    )
+    pu.append(over_x(held(pu[0], query)))
+    pup = [over_tensor(held(my_rows(w_up, kx), query))]
+    v_oth, vs_oth = k_act_other(after(query), normed, pv, 0, 512)
+    pg += [over_core(v) for v in held((pg[0], pg[1]), v_oth)]
+    ph.append(over_z(held(ph[0], v_oth)))
+    pdn = [over_tensor(held(my_rows(w_down, kz), v_oth))]
+    gated_own, gated_oth, g_own, g_oth, m_own, m_oth, probs = k_attend(
+        after(v_oth), query, key, v_own, v_oth, ema_low, w_gamma, pg
+    )
+    pu += [over_core(v) for v in held((pu[0], pu[1]), probs)]
     ph += [over_core(v) for v in held((ph[0], ph[1]), probs)]
-    pdn = [over_tensor(held(my_rows(w_down, kz), probs))]
+    pup.append(over_x(held(pup[0], probs)))
     mixed, lowered, fac_h, fac_f, keep = k_gate(
         after(probs), gated_own, gated_oth, ema_low, tokens, u_h, w_h, w_phi, pu, ph
     )
-    pup.append(over_x(held(pup[0], mixed)))
-    acc0, dl0, sent_o = k_ffn(after(mixed), lowered, cotangent, [w_up], [w_down], 1)
-    pdn.append(over_z(held(pdn[0], acc0)))
-    got_o = over_core(sent_o)
-    acc1, dl1, kept_o = k_ffn(after(acc0), lowered, cotangent, [w_up], [w_down], 0)
-    pup += [over_core(v) for v in held((pup[0], pup[1]), acc1)]
-    pdn += [over_core(v) for v in held((pdn[0], pdn[1]), acc1)]
+    acc, dl, *sent_o = k_ffn(after(mixed), lowered, cotangent, [w_up], [w_down], 1)
+    pup += [over_core(v) for v in held((pup[0], pup[1]), acc)]
+    pdn.append(over_z(held(pdn[0], acc)))
+    dno_got, upo_got = [over_core(v) for v in sent_o]
+    acc, dl, dno, upo = k_ffn(after(acc), lowered, cotangent, [w_up], [w_down], 0, (acc, dl))
+    pdn += [over_core(v) for v in held((pdn[0], pdn[1]), acc)]
 
     def add(*values):
-        total = values[0].astype(F32)
+        value = values[0].astype(F32)
         for v in values[1:]:
-            total = total + v.astype(F32)
-        return total.astype(BF)
-
-    def x_mine(v):
-        return pick(v.reshape(4, 2, d // 8, v.shape[-1]), x_pos, 1)
-
-    def x_theirs(v):
-        return pick(v.reshape(4, 2, d // 8, v.shape[-1]), 1 - x_pos, 1)
+            value = value + v.astype(F32)
+        return value.astype(BF)
 
     def z_first(terms):
         by_z = [v.reshape(2, 2, d // 8, v.shape[-1]) for v in terms]
@@ -1100,140 +1152,119 @@
             core == 0, jnp.concatenate([kept, got], axis=1), jnp.concatenate([got, kept], axis=1)
         )
 
-    dn_x1 = add(x_theirs(kept_o[0]), x_theirs(got_o[0]))
+    dn_x1 = add(dno[1], dno_got[1])
     dn_got_x1 = over_x(dn_x1)
-    acc2, dl2, sent_t = k_ffn(after(acc1, dn_x1), lowered, cotangent, pup, pdn, 1)
-    got_t = over_core(sent_t)
-    acc3, dl3, kept_t = k_ffn(after(acc2), lowered, cotangent, pup, pdn, 0)
-    dn_x2 = add(x_theirs(kept_t[0]), x_theirs(got_t[0]))
-    up_y1 = add(kept_t[1], got_t[1])
+    acc, dl, *sent_t = k_ffn(after(acc, dn_x1), lowered, cotangent, pup, pdn, 1, (acc, dl))
+    dnt_got, upt_got = [over_core(v) for v in sent_t]
+    acc, dl, dnt, upt = k_ffn(after(acc), lowered, cotangent, pup, pdn, 0, (acc, dl))
+    dn_x2 = add(dnt[1], dnt_got[1])
+    up_y1 = add(upt, upt_got)
     dn_got_x2 = over_x(dn_x2)
     up_got_y = over_tensor(up_y1)
     output, dh, df, direct, da_own, da_oth, dg_own, dg_oth, de_part = k_mid_back(
-        after(acc3, dn_x2, up_y1), [dl0, dl1, dl2, dl3], [acc0, acc1, acc2, acc3], cotangent, mixed, fac_h, fac_f, keep,
+        after(acc, dn_x2, up_y1), dl, acc, cotangent, mixed, fac_h, fac_f, keep,
         g_own, g_oth, m_own, m_oth, u_h, w_gamma, w_h, w_phi, pg, pu, ph,
     )
     dn_got_x2 = held(dn_got_x2, dh)
-    dn_y = add(x_mine(kept_t[0]), x_mine(got_t[0]), dn_got_x2)
+    dn_y = add(dnt[0], dnt_got[0], dn_got_x2)
     dn_got_y = over_tensor(dn_y)
     mid_sent = k_weight_mid(after(dh, dn_y), ema_low, dh, df, gated_own, gated_oth, dg_own, dg_oth, 5)
     mid_got = [over_core(v) for v in mid_sent]
-    dv_own, dv_oth = k_value_back(after(*mid_sent), probs, da_own, da_oth, vs_own, vs_oth)
+    dv_own, dv_oth, dz, stats = k_attend_back(
+        after(*mid_sent), probs, da_own, da_oth, v_own, v_oth, vs_own, vs_oth, query, key, z_pre, qk_gain
+    )
     up_got_y = held(up_got_y, dv_own)
-    up_terms = [kept_o[1], got_o[1], up_got_y]
-    up_x = add(*[x_theirs(v) for v in up_terms])
+    up_x = add(upo[1], upo_got[1], up_got_y[1])
     up_got_x = over_x(up_x)
-    val_sent = k_weight_value(after(dv_own, up_x), normed, dv_own, dv_oth, 5)
-    val_got = [over_core(v) for v in val_sent]
-    mid_own, mid_oth = k_weight_mid(
-        after(*val_sent), ema_low, dh, df, gated_own, gated_oth, dg_own, dg_oth, 4, mid_got
-    )
-    c = mid_own.shape[1] // 2
-    ma_own, ma_oth, mb_own, mb_oth = mid_own[:, :c], mid_oth[:, :c], mid_own[:, c:], mid_oth[:, c:]
-    ma_x = (x_theirs(ma_own), x_theirs(ma_oth))
-    ma_got_x = [over_x(v) for v in ma_x]
+    val_sent = k_weight_value(after(dv_own, up_x), normed, dv_own, dv_oth, 5)[0]
+    val_got = over_core(val_sent)
+    ma_theirs, ma_mine, mb_own, mb_oth = k_weight_mid(
+        after(val_sent), ema_low, dh, df, gated_own, gated_oth, dg_own, dg_oth, 4, mid_got
+    )
+    ma_got_x = over_x(ma_theirs)
     mb_got_y = over_tensor(mb_oth)
-    dz, stats = k_score_back(
-        after(mid_own, ma_x), probs, da_own, da_oth, v_own, v_oth, query, key, z_pre, qk_gain
-    )
-    dn_got_y, up_got_x = held((dn_got_y, up_got_x), dz)
-    ffn_terms = [
-        jnp.concatenate([x_mine(a), x_mine(b)], axis=-1)
-        for a, b in ((kept_o[0], kept_o[1]), (got_o[0], got_o[1]))
-    ] + [
-        jnp.concatenate([dn_got_x1, x_mine(up_got_y)], axis=-1),
-        jnp.concatenate([dn_got_y, up_got_x], axis=-1),
-    ]
-    ffn_z1, ffn_terms = z_first(ffn_terms)
-    ffn_got_z1 = over_z(ffn_z1)
-    z_own = k_weight(after(dz, ffn_z1), ema_low, dz, lambda s: 0, dz.shape[1], dz.shape[1])
+    z_own = k_weight_z(after(ma_theirs), ema_low, dz)
     z_got = over_core(z_own)
-    val_own, val_oth = k_weight_value(after(z_own), normed, dv_own, dv_oth, 4, val_got)
-    c = val_own.shape[1] // 2
-    va_own, va_oth, vb_own, vb_oth = val_own[:, :c], val_oth[:, :c], val_own[:, c:], val_oth[:, c:]
-    va_x = (x_theirs(va_own), x_theirs(va_oth))
-    va_got_x = [over_x(v) for v in va_x]
+    va_theirs, va_mine, vb_own, vb_oth = k_weight_value(after(z_own), normed, dv_own, dv_oth, 4, val_got)
+    va_got_x = over_x(va_theirs)
+    vb_got_y = over_tensor(vb_oth)
+    dn_got_y, up_got_x = held((dn_got_y, up_got_x), va_theirs)
+    dn_z, dn_terms = z_first([dno[0], dno_got[0], dn_got_x1, dn_got_y])
+    up_z, up_terms = z_first([upo[0], upo_got[0], up_got_y[0], up_got_x])
+    dn_got_z, up_got_z = over_z(dn_z), over_z(up_z)
     z_sum = add(z_own, z_got)
-    vb_y = jnp.concatenate([vb_oth, z_sum], axis=1)
-    vb_got_y = over_tensor(vb_y)
+    z_got_y = over_tensor(z_sum)
     quarter = blocks // 4
-    eb = k_ema_backward(
-        after(val_own, va_x, vb_y), normed, de_part, dz, e_slope, w_z, decay, coef, omega, 0, quarter
-    )
+
+    def ema_back(dep, first, count, before=None):
+        return k_ema_backward(
+            after(*dep), normed, de_part, dz, e_slope, w_z, decay, coef, omega, first, count, before
+        )
+
+    eb = ema_back((va_theirs, dn_z, up_z, z_sum), 0, quarter)
     ma_got_x, mb_got_y = held((ma_got_x, mb_got_y), eb[1])
-    ma_y = add(x_mine(ma_oth), ma_got_x[1])
-    mb_x = add(x_theirs(mb_own), x_theirs(mb_got_y))
+    ma_y = add(ma_mine[1], ma_got_x[1])
+    mb_x = add(mb_own[1], mb_got_y[1])
     ma_got_y = over_tensor(ma_y)
     mb_got_x = over_x(mb_x)
-    eb = k_ema_backward(
-        after(eb[1], ma_y, mb_x), normed, de_part, dz, e_slope, w_z, decay, coef, omega, quarter, quarter, eb
-    )
-    ffn_got_z1 = held(ffn_got_z1, eb[1])
-    ffn_z2, ffn_terms = z_second([*ffn_terms, ffn_got_z1])
-    ffn_got_z2 = over_z2(ffn_z2)
-    va_got_x, vb_got_y = held((va_got_x, vb_got_y), eb[1])
-    va_y = add(x_mine(va_oth), va_got_x[1])
-    vb_mine = jnp.concatenate([vb_own, z_sum], axis=1)
-    vb_x = add(x_theirs(vb_mine), x_theirs(vb_got_y))
+    eb = ema_back((eb[1], ma_y, mb_x), quarter, quarter, eb)
+    dn_got_z, up_got_z, va_got_x, vb_got_y, z_got_y = held((dn_got_z, up_got_z, va_got_x, vb_got_y, z_got_y), eb[1])
+    dn_z2, dn_terms = z_second([*dn_terms, dn_got_z])
+    up_z2, up_terms = z_second([*up_terms, up_got_z])
+    va_y = add(va_mine[1], va_got_x[1])
+    zs = add(z_sum, z_got_y)
+    vb_x = jnp.concatenate([add(vb_own[1], vb_got_y[1]), zs[1]], axis=-1)
+    dn_got_z2, up_got_z2 = over_z2(dn_z2), over_z2(up_z2)
     va_got_y = over_tensor(va_y)
     vb_got_x = over_x(vb_x)
-    eb = k_ema_backward(
-        after(eb[1], ffn_z2, va_y, vb_x), normed, de_part, dz, e_slope, w_z, decay, coef, omega, 2 * quarter, quarter, eb
-    )
+    eb = ema_back((eb[1], dn_z2, up_z2, va_y, vb_x), 2 * quarter, quarter, eb)
     ma_got_y, mb_got_x = held((ma_got_y, mb_got_x), eb[1])
-    mid_terms = [
-        jnp.concatenate([x_mine(ma_own), x_mine(mb_own)], axis=-1),
-        jnp.concatenate([ma_got_x[0], x_mine(mb_got_y)], axis=-1),
-        jnp.concatenate([ma_got_y, mb_got_x], axis=-1),
-    ]
-    mid_z1, mid_terms = z_first(mid_terms)
-    mid_got_z1 = over_z(mid_z1)
-    eb = k_ema_backward(
-        after(eb[1], mid_z1), normed, de_part, dz, e_slope, w_z, decay, coef, omega, 3 * quarter, quarter, eb
-    )
+    ma_z, ma_terms = z_first([ma_mine[0], ma_got_x[0], ma_got_y])
+    mb_z, mb_terms = z_first([mb_own[0], mb_got_y[0], mb_got_x])
+    ma_got_z, mb_got_z = over_z(ma_z), over_z(mb_z)
+    eb = ema_back((eb[1], ma_z, mb_z), 3 * quarter, quarter, eb)
     d_sig, _, _, sum_a, sum_b, sum_w = eb
+    sums = jnp.concatenate([sum_a, sum_b, sum_w, stats], axis=0)
+    sums_got = over_core(sums)
     va_got_y, vb_got_x = held((va_got_y, vb_got_x), sum_a)
-    val_terms = [
-        jnp.concatenate([x_mine(va_own), x_mine(vb_mine)], axis=-1),
-        jnp.concatenate([va_got_x[0], x_mine(vb_got_y)], axis=-1),
-        jnp.concatenate([va_got_y, vb_got_x], axis=-1),
-    ]
-    val_z1, val_terms = z_first(val_terms)
-    val_got_z1 = over_z(val_z1)
-    sums = jnp.concatenate([sum_a, sum_b, sum_w, stats], axis=0)
-    sums_core = over_core(sums)
+    c = va_mine.shape[-1]
+    vb_terms = [jnp.concatenate([vb_own[0], zs[0]], axis=-1), jnp.pad(vb_got_y[0], ((0, 0), (0, zs.shape[-1]))), vb_got_x]
+    val_z, val_terms = z_first([
+        jnp.concatenate([add(va_mine[0], va_got_x[0], va_got_y), add(*vb_terms)], axis=-1)
+    ])
+    val_got_z = over_z(val_z)
     input_grad = k_input_back(
-        after(sum_a, val_z1), dv_own, dv_oth, w_v, pv, d_sig, tokens, direct
-    )
-    mid_got_z1, ffn_got_z2, val_got_z1, sums_core = held(
-        (mid_got_z1, ffn_got_z2, val_got_z1, sums_core), input_grad
-    )
-    mid_z2, mid_terms = z_second([*mid_terms, mid_got_z1])
+        after(sum_a, val_z, sums), dv_own, dv_oth, w_v, pv, d_sig, tokens, direct
+    )
+    ma_got_z, mb_got_z, val_got_z, sums_got = held((ma_got_z, mb_got_z, val_got_z, sums_got), input_grad)
+    sums = sums + sums_got
+    sums_got = over_tensor(sums)
+    mid_z2, mid_terms = z_second([
+        jnp.concatenate([add(*ma_terms, ma_got_z), add(*mb_terms, mb_got_z)], axis=-1)
+    ])
     mid_got_z2 = over_z2(mid_z2)
-    val_z2, val_terms = z_second([*val_terms, val_got_z1])
+    val_z2, val_terms = z_second([*val_terms, val_got_z])
     val_got_z2 = over_z2(val_z2)
-    sums = sums + sums_core
-    sums = sums + over_tensor(sums)
-    sums = sums + over_x(sums)
-    sums = sums + over_z(sums)
+    sums = sums + sums_got
+    others = [over_x(sums), over_z(sums), lax.ppermute(sums, "dp", [(i, i ^ 6) for i in range(dp_size)])]
+    sums = sums + others[0] + others[1] + others[2]
     sums = sums + over_z2(sums)
 
     def finish(terms):
         send, terms = core_rows(terms)
         return total(terms), over_core(send)
 
-    ffn_kept, ffn_got = finish([*ffn_terms, ffn_got_z2])
-    c = ffn_kept.shape[1] // 2
-    down_t, up = joined(ffn_kept[:, :c], ffn_got[:, :c]), joined(ffn_kept[:, c:], ffn_got[:, c:])
+    down_t = joined(*finish([*dn_terms, dn_got_z2]))
+    up = joined(*finish([*up_terms, up_got_z2]))
     mid_kept, mid_got = finish([*mid_terms, mid_got_z2])
-    half = gated_own.shape[1] // 2
-    cuts = (0, half, 2 * half, 2 * half + d // 4, 3 * half)
-    uh_t, gamma, wh_t, phi_t = (
-        joined(mid_kept[:, lo:hi], mid_got[:, lo:hi]) for lo, hi in zip(cuts[:-1], cuts[1:])
+    tn = d // 4
+    uh_t, wh_t, gamma, phi_t = (
+        joined(mid_kept[:, lo * tn : hi * tn], mid_got[:, lo * tn : hi * tn])
+        for lo, hi in ((0, 2), (2, 3), (3, 5), (5, 6))
     )
     val_kept, val_got = finish([*val_terms, val_got_z2])
-    value = joined(val_kept[:, :half], val_got[:, :half])
-    z_grad = val_kept[:, half:]
+    value = joined(val_kept[:, : 2 * c], val_got[:, : 2 * c])
+    z_grad = val_kept[:, 2 * c :]
     gh = sum_a.shape[0]
 
     def own_half(v):

time: 551 us -> 511 us (0.927)
  Pallas kernels: 323 us -> 300 us
  local copies, waits for them, and re-layouts: 58.2 us -> 44.5 us
  starting transfers between devices: 45.7 us -> 58.9 us
  other arithmetic: 45.6 us -> 33.1 us
    pallas_call x26 -> x24, Pallas kernels: 323 us -> 300 us  [run(): pl.pallas_call(body, out_shape=out_shape, grid_spec=pltpu.PrefetchScalarG...]
    ppermute x61 -> x65, starting transfers between devices: 45.7 us -> 58.9 us  [swap(): return lax.ppermute(values, axis, [(i, i ^ bit) for i in range(size)])]
    concatenate x11 -> x3, other arithmetic: 12.7 us -> 0.93 us  [the longest x1 0.81 us: one_sequence(): vb_x = jnp.concatenate([add(vb_own[1], vb_got_y[1]), zs[1]], axis=-1)]
    unnamed x173 -> x147, local copies, waits for them, and re-layouts: 19.9 us -> 12.2 us
    slice x14 -> x13, local copies, waits for them, and re-layouts: 14.3 us -> 6.8 us  [the longest x3 4.03 us: one_sequence(): up_z, up_terms = z_first([upo[0], upo_got[0], up_got_y[0], up_got_x])]
    ppermute x61 -> x65, waiting for transfers between devices: 67.5 us -> 61.7 us  [swap(): return lax.ppermute(values, axis, [(i, i ^ bit) for i in range(size)])]
    dynamic_slice x17 -> x12, local copies, waits for them, and re-layouts: 7.89 us -> 11.4 us  [pick(): return lax.dynamic_index_in_dim(values, index, axis, keepdims=False)]
    convert_element_type x16 -> x21, other arithmetic: 21.5 us -> 20.7 us  [add(): return value.astype(BF)]
  transfers between devices with their start and end apart: 61 -> 66, of which waited for: 11 -> 15; matrix products, arithmetic and copies ran while one was open for 15% -> 12% of each run, Pallas kernels for 60% -> 60%
where the time goes in v4:
time: 511 us; the launch traced here: 504 us
  Pallas kernels  300 us (59%)
  waiting for transfers between devices  64.5 us (13%)
  starting transfers between devices  58.9 us (12%)
  local copies, waits for them, and re-layouts  44.5 us (9%)
  other arithmetic  33.1 us (6%)
    pallas_call x24, Pallas kernels, run(): pl.pallas_call(body, out_shape=out_shape, grid_spec=pltpu.PrefetchScalarG...  300 us
    ppermute x65, waiting for transfers between devices, swap(): return lax.ppermute(values, axis, [(i, i ^ bit) for i in range(size)])  61.7 us
    ppermute x65, starting transfers between devices, swap(): return lax.ppermute(values, axis, [(i, i ^ bit) for i in range(size)])  58.9 us
    convert_element_type x21, other arithmetic, add(): return value.astype(BF)  20.7 us
    unnamed x147, local copies, waits for them, and re-layouts  12.2 us
    dynamic_slice x12, local copies, waits for them, and re-layouts, pick(): return lax.dynamic_index_in_dim(values, index, axis, keepdims=False)  11.4 us
  transfers between devices with their start and end apart: 66, of which 15 were waited for; matrix products, arithmetic and copies ran while one was open for 12% of the time, Pallas kernels for 60%

profile of v4, /device:TPU:0, one launch (start us, length us, event | category | flops | bytes accessed | tf_op | source)
XLA Modules:
  0.0 503.6 jit_solution(4371205851372488182)
XLA Ops:
  5.5 3.0 collective-permute-start
  10.4 8.2 %value_own.1 = (bf16[1024,1024]{1,0:T(8,128)(2,1)}, bf16[1024,1024]{1,0:T(8,128)(2,1)}, bf16[1024,1024]{1,0:T(8,128)(2,1)}) custom-call(s32[13]{0:T(128)} %stack.55.s, bf16[1024,1024]{1,0:T(8,128)(2,1)} %x_ref.5, bf16[1024,1024]{1,0:T(8,128)(2,1)} %wo.5), custom_call_target="tpu_custom_call" | custom-call | flops 21474836480 | bytes 104857600 | tf_op jit(solution)/shard_map/value_own/pallas_call | solution.py:341
  20.4 2.0 collective-permute-start.5
  25.0 2.6 ema_params.1
  27.5 8.7 %ema_forward.2 = (bf16[1024,1024]{1,0:T(8,128)(2,1)}, bf16[1024,1024]{1,0:T(8,128)(2,1)}, f32[128,128]{1,0:T(8,128)}) custom-call(s32[13]{0:T(128)} %stack.55.s, bf16[1024,1024]{1,0:T(8,128)(2,1)} %get-tuple-element.172.x_ref, f32[128,128]{1,0:T(8,128)} %get-tuple-element.173.dec_ref, f32[128,128]{1,0:T(8,128)} %get-tuple-element.174.cf_ref, ...), custom_call_target="tpu_custom_call" | custom-call | flops 99999997952 | bytes 64921600 | tf_op jit(solution)/shard_map/ema_forward/pallas_call | solution.py:341
  37.8 8.8 %ema_forward.3 = (bf16[1024,1024]{1,0:T(8,128)(2,1)}, bf16[1024,1024]{1,0:T(8,128)(2,1)}, f32[128,128]{1,0:T(8,128)}) custom-call(s32[13]{0:T(128)} %stack.55.s, bf16[1024,1024]{1,0:T(8,128)(2,1)} %get-tuple-element.172.x_ref, f32[128,128]{1,0:T(8,128)} %get-tuple-element.173.dec_ref, ...), custom_call_target="tpu_custom_call", output_to_operand_aliasing={{0}: (6, {}), {1}: (7, {})} | custom-call | flops 99999997952 | bytes 107520000 | tf_op jit(solution)/shard_map/ema_forward/pallas_call | solution.py:341
  46.5 3.7 query_key.1
  57.2 7.9 %act_other.1 = (bf16[1024,1024]{1,0:T(8,128)(2,1)}, bf16[1024,1024]{1,0:T(8,128)(2,1)}) custom-call(s32[13]{0:T(128)} %stack.55.s, bf16[1024,1024]{1,0:T(8,128)(2,1)} %get-tuple-element.172.x_ref, bf16[256,1024]{1,0:T(8,128)(2,1)} %copy-done.57, bf16[256,1024]{1,0:T(8,128)(2,1)} %copy-done.58, bf16[256,1024]{1,0:T(8,128)(2,1)} %copy-done.59, ...), custom_call_target="tpu_custom_call" | custom-call | flops 21474836480 | bytes 83886080 | tf_op jit(solution)/shard_map/act_other/pallas_call | solution.py:341
  65.1 2.5 collective-permute-done.6.w1
  70.3 7.8 %collective-permute-done.13.h0.f0 = bf16[256,1024]{1,0:T(8,128)(2,1)} collective-permute-done((bf16[256,1024]{1,0:T(8,128)(2,1)S(1)}, bf16[256,1024]{1,0:T(8,128)(2,1)}, u32[]{:S(2)}, u32[]{:S(2)}) %collective-permute-start.13) | collective-permute-done | bytes 524320 | tf_op jit(solution)/shard_map/ppermute | solution.py:1034
  80.7 16.5 %attend.1 = (bf16[1024,1024]{1,0:T(8,128)(2,1)}, bf16[1024,1024]{1,0:T(8,128)(2,1)}, bf16[1024,1024]{1,0:T(8,128)(2,1)}, bf16[1024,1024]{1,0:T(8,128)(2,1)}, bf1...) custom-call(s32[13]{0:T(128)} %stack.55.s, ...), custom_call_target="tpu_custom_call" | custom-call | flops 71470940160 | bytes 256901120 | tf_op jit(solution)/shard_map/attend/pallas_call | solution.py:341
  98.3 2.3 constant_dynamic-slice_fusion.12
  102.5 18.8 %gate.1 = (bf16[1024,1024]{1,0:T(8,128)(2,1)}, bf16[1024,1024]{1,0:T(8,128)(2,1)}, bf16[1024,1024]{1,0:T(8,128)(2,1)}, bf16[1024,1024]{1,0:T(8,128)(2,1)}, bf16[1024,1024]{1,0:T(8,128)(2,1)}) custom-call(s32[13]{0:T(128)} %stack.55.s, bf16[1024,1024]{1,0:T(8,128)(2,1)} %get-tuple-element.196.go, bf16[1024,1024]{1,0:T(8,128)(2,1)} %get-tuple-element.197.gt, ...), custom_call_target="tpu_custom_call" | custom-call | flops 85899345920 | bytes 293601280 | tf_op jit(solution)/shard_map/gate/pallas_call | solution.py:341
  121.3 20.2 %ffn.4 = (bf16[1024,1024]{1,0:T(8,128)(2,1)}, bf16[1024,1024]{1,0:T(8,128)(2,1)}, bf16[2,512,1024]{2,1,0:T(8,128)(2,1)}, bf16[2,512,1024]{2,1,0:T(8,128)(2,1)}) custom-call(s32[13]{0:T(128)} %stack.55.s, bf16[1024,1024]{1,0:T(8,128)(2,1)} %get-tuple-element.208.low_ref, bf16[1024,1024]{1,0:T(8,128)(2,1)} %c_ref.9, bf16[1024,2048]{1,0:T(8,128)(2,1)} %refs_0_.3, ...), custom_call_target="tpu_custom_call" | custom-call | flops 128849018880 | bytes 209715200 | tf_op jit(solution)/shard_map/ffn/pallas_call | solution.py:341
  142.7 20.6 %ffn.5 = (bf16[1024,1024]{1,0:T(8,128)(2,1)}, bf16[1024,1024]{1,0:T(8,128)(2,1)}, bf16[2,512,1024]{2,1,0:T(8,128)(2,1)}, bf16[2,512,1024]{2,1,0:T(8,128)(2,1)}) custom-call(s32[13]{0:T(128)} %stack.55.s, bf16[1024,1024]{1,0:T(8,128)(2,1)} %get-tuple-element.208.low_ref, bf16[1024,1024]{1,0:T(8,128)(2,1)} %c_ref.9, bf16[1024,2048]{1,0:T(8,128)(2,1)} %refs_0_.3, ...), custom_call_target="tpu_custom_call" | custom-call | flops 128849018880 | bytes 251658240 | tf_op jit(solution)/shard_map/ffn/pallas_call | solution.py:341
  163.9 2.5 collective-permute-done.23.refs_5_
  177.6 20.8 %ffn.6 = (bf16[1024,1024]{1,0:T(8,128)(2,1)}, bf16[1024,1024]{1,0:T(8,128)(2,1)}, bf16[2,512,1024]{2,1,0:T(8,128)(2,1)}, bf16[2,512,1024]{2,1,0:T(8,128)(2,1)}) custom-call(s32[13]{0:T(128)} %stack.55.s, bf16[1024,1024]{1,0:T(8,128)(2,1)} %get-tuple-element.208.low_ref, bf16[1024,1024]{1,0:T(8,128)(2,1)} %c_ref.9, ...), custom_call_target="tpu_custom_call" | custom-call | flops 128849018880 | bytes 230686720 | tf_op jit(solution)/shard_map/ffn/pallas_call | solution.py:341
  199.0 20.8 %ffn.7 = (bf16[1024,1024]{1,0:T(8,128)(2,1)}, bf16[1024,1024]{1,0:T(8,128)(2,1)}, bf16[2,512,1024]{2,1,0:T(8,128)(2,1)}, bf16[2,512,1024]{2,1,0:T(8,128)(2,1)}) custom-call(s32[13]{0:T(128)} %stack.55.s, bf16[1024,1024]{1,0:T(8,128)(2,1)} %get-tuple-element.208.low_ref, bf16[1024,1024]{1,0:T(8,128)(2,1)} %c_ref.9, ...), custom_call_target="tpu_custom_call" | custom-call | flops 128849018880 | bytes 230686720 | tf_op jit(solution)/shard_map/ffn/pallas_call | solution.py:341
  223.9 2.3 add_convert_fusion
  227.7 27.4 %mid_back.1 = (bf16[1024,1024]{1,0:T(8,128)(2,1)}, bf16[1024,1024]{1,0:T(8,128)(2,1)}, bf16[1024,1024]{1,0:T(8,128)(2,1)}, bf16[1024,1024]{1,0:T(8,128)(2,1)}, b...) custom-call(s32[13]{0:T(128)} %stack.55.s, ...), custom_call_target="tpu_custom_call" | custom-call | flops 128849018880 | bytes 566231040 | tf_op jit(solution)/shard_map/mid_back/pallas_call | solution.py:341
  256.8 13.9 %weight_mid.2 = (bf16[2,2,512,768]{3,2,1,0:T(8,128)(2,1)}, bf16[2,2,512,768]{3,2,1,0:T(8,128)(2,1)}) custom-call(s32[13]{0:T(128)} %stack.55.s, bf16[1024,1024]{1,0:T(8,128)(2,1)} %get-tuple-element.180.e_ref.eo.et, bf16[1024,1024]{1,0:T(8,128)(2,1)} %get-tuple-element.243.h_ref, bf16[1024,1024]{1,0:T(8,128)(2,1)} %get-tuple-element.246.f_ref, ...), custom_call_target="tpu_custom_call" | custom-call | flops 64424509440 | bytes 251658240 | tf_op jit(solution)/shard_map/weight_mid/pallas_call | solution.py:341
  271.6 14.7 %attend_back.1 = (bf16[1024,1024]{1,0:T(8,128)(2,1)}, bf16[1024,1024]{1,0:T(8,128)(2,1)}, bf16[1024,128]{1,0:T(8,128)(2,1)}, f32[8,128]{1,0:T(8,128)}) custom-call(s32[13]{0:T(128)} %stack.55.s, bf16[1024,1024]{1,0:T(8,128)(2,1)} %get-tuple-element.194.p_ref, bf16[1024,1024]{1,0:T(8,128)(2,1)} %get-tuple-element.252.ao, ...), custom_call_target="tpu_custom_call" | custom-call | flops 53687091200 | bytes 201902080 | tf_op jit(solution)/shard_map/attend_back/pallas_call | solution.py:341
  286.4 3.2 fusion.3
  289.6 6.3 %weight_value.2 = bf16[2,2,512,512]{3,2,1,0:T(8,128)(2,1)} custom-call(s32[13]{0:T(128)} %stack.55.s, bf16[1024,1024]{1,0:T(8,128)(2,1)} %get-tuple-element.172.x_ref, bf16[1024,1024]{1,0:T(8,128)(2,1)} %get-tuple-element.257.vo, bf16[1024,1024]{1,0:T(8,128)(2,1)} %get-tuple-element.262.vt), custom_call_target="tpu_custom_call" | custom-call | flops 21474836480 | bytes 83886080 | tf_op jit(solution)/shard_map/weight_value/pallas_call | solution.py:341
  299.5 15.7 %weight_mid.3 = (bf16[2,512,768]{2,1,0:T(8,128)(2,1)}, bf16[2,512,768]{2,1,0:T(8,128)(2,1)}, bf16[2,512,768]{2,1,0:T(8,128)(2,1)}, bf16[2,512,768]{2,1,0:T(8,128)(2,1)}) custom-call(s32[13]{0:T(128)} %stack.55.s, bf16[1024,1024]{1,0:T(8,128)(2,1)} %get-tuple-element.180.e_ref.eo.et, bf16[1024,1024]{1,0:T(8,128)(2,1)} %get-tuple-element.243.h_ref, ...), custom_call_target="tpu_custom_call" | custom-call | flops 64424509440 | bytes 314572800 | tf_op jit(solution)/shard_map/weight_mid/pallas_call | solution.py:341
  315.2 3.9 weight_z.1
  324.5 7.5 %weight_value.3 = (bf16[2,512,256]{2,1,0:T(8,128)(2,1)}, bf16[2,512,256]{2,1,0:T(8,128)(2,1)}, bf16[2,512,256]{2,1,0:T(8,128)(2,1)}, bf16[2,512,256]{2,1,0:T(8,128)(2,1)}) custom-call(s32[13]{0:T(128)} %stack.55.s, bf16[1024,1024]{1,0:T(8,128)(2,1)} %get-tuple-element.172.x_ref, bf16[1024,1024]{1,0:T(8,128)(2,1)} %get-tuple-element.257.vo, ...), custom_call_target="tpu_custom_call" | custom-call | flops 21474836480 | bytes 104857600 | tf_op jit(solution)/shard_map/weight_value/pallas_call | solution.py:341
  335.3 2.4 fusion.8
  337.7 2.3 fusion.9
  345.5 10.2 %ema_backward.4 = (f32[1024,1024]{1,0:T(8,128)}, f32[128,128]{1,0:T(8,128)}, f32[128,128]{1,0:T(8,128)}, f32[128,128]{1,0:T(8,128)}, f32[128,128]{1,0:T(8,128)}, /*index=5*/f32[8,128]{1,0:T(8,128)}) custom-call(s32[13]{0:T(128)} %stack.55.s, bf16[1024,1024]{1,0:T(8,128)(2,1)} %get-tuple-element.172.x_ref, bf16[1024,1024]{1,0:T(8,128)(2,1)} %get-tuple-element.272.de_ref, ...), custom_call_target="tpu_custom_call" | custom-call | flops 99999997952 | bytes 114114560 | tf_op jit(solution)/shard_map/ema_backward/pallas_call | solution.py:341
  358.2 2.2 collective-permute-done.39
  364.2 10.2 %ema_backward.5 = (f32[1024,1024]{1,0:T(8,128)}, f32[128,128]{1,0:T(8,128)}, f32[128,128]{1,0:T(8,128)}, f32[128,128]{1,0:T(8,128)}, f32[128,128]{1,0:T(8,128)}, /*index=5*/f32[8,128]{1,0:T(8,128)}) custom-call(s32[13]{0:T(128)} %stack.55.s, bf16[1024,1024]{1,0:T(8,128)(2,1)} %get-tuple-element.172.x_ref, ...), custom_call_target="tpu_custom_call", output_to_operand_aliasing={{0}: (14, {})} | custom-call | flops 99999997952 | bytes 158720000 | tf_op jit(solution)/shard_map/ema_backward/pallas_call | solution.py:341
  374.4 2.0 collective-permute-done.44
  379.6 2.7 collective-permute-start.64
  387.4 10.3 %ema_backward.6 = (f32[1024,1024]{1,0:T(8,128)}, f32[128,128]{1,0:T(8,128)}, f32[128,128]{1,0:T(8,128)}, f32[128,128]{1,0:T(8,128)}, f32[128,128]{1,0:T(8,128)}, /*index=5*/f32[8,128]{1,0:T(8,128)}) custom-call(s32[13]{0:T(128)} %stack.55.s, bf16[1024,1024]{1,0:T(8,128)(2,1)} %get-tuple-element.172.x_ref, ...), custom_call_target="tpu_custom_call", output_to_operand_aliasing={{0}: (14, {})} | custom-call | flops 99999997952 | bytes 158720000 | tf_op jit(solution)/shard_map/ema_backward/pallas_call | solution.py:341
  402.3 2.2 collective-permute-done.62
  408.4 10.8 %collective-permute-done.45 = bf16[512,768]{1,0:T(8,128)(2,1)S(1)} collective-permute-done((bf16[512,768]{1,0:T(8,128)(2,1)S(1)}, bf16[512,768]{1,0:T(8,128)(2,1)S(1)}, u32[]{:S(2)}, u32[]{:S(2)}) %collective-permute-start.45) | collective-permute-done | bytes 786464 | tf_op jit(solution)/shard_map/ppermute | solution.py:1034
  420.1 10.2 %ema_backward.7 = (f32[1024,1024]{1,0:T(8,128)}, f32[128,128]{1,0:T(8,128)}, f32[128,128]{1,0:T(8,128)}, f32[128,128]{1,0:T(8,128)}, f32[128,128]{1,0:T(8,128)}, /*index=5*/f32[8,128]{1,0:T(8,128)}) custom-call(s32[13]{0:T(128)} %stack.55.s, bf16[1024,1024]{1,0:T(8,128)(2,1)} %get-tuple-element.172.x_ref, ...), custom_call_target="tpu_custom_call", output_to_operand_aliasing={{0}: (14, {})} | custom-call | flops 99999997952 | bytes 158720000 | tf_op jit(solution)/shard_map/ema_backward/pallas_call | solution.py:341
  436.4 12.5 %input_back.1 = f32[1024,1024]{1,0:T(8,128)} custom-call(s32[13]{0:T(128)} %stack.55.s, bf16[1024,1024]{1,0:T(8,128)(2,1)} %get-tuple-element.257.vo, bf16[1024,1024]{1,0:T(8,128)(2,1)} %get-tuple-element.262.vt, bf16[1024,1024]{1,0:T(8,128)(2,1)} %wo.5, bf16[256,1024]{1,0:T(8,128)(2,1)} %copy-done.57, bf16[256,1024]{1,0:T(8,128)(2,1)} %copy-done.58, ...), custom_call_target="tpu_custom_call" | custom-call | flops 42949672960 | bytes 209715200 | tf_op jit(solution)/shard_map/input_back/pallas_call | solution.py:341
  448.9 3.8 collective-permute-done.50
  452.7 8.0 %collective-permute-done.49 = bf16[2,128,768]{2,1,0:T(8,128)(2,1)S(1)} collective-permute-done((bf16[2,128,768]{2,1,0:T(8,128)(2,1)S(1)}, bf16[2,128,768]{2,1,0:T(8,128)(2,1)S(1)}, u32[]{:S(2)}, u32[]{:S(2)}) %collective-permute-start.49) | collective-permute-done | bytes 393248 | tf_op jit(solution)/shard_map/ppermute | solution.py:1034
  461.0 2.6 collective-permute-start.58
  465.5 5.8 %collective-permute-done.58 = bf16[128,640]{1,0:T(8,128)(2,1)S(1)} collective-permute-done((bf16[128,640]{1,0:T(8,128)(2,1)S(1)}, bf16[128,640]{1,0:T(8,128)(2,1)S(1)}, u32[]{:S(2)}, u32[]{:S(2)}) %collective-permute-start.58) | collective-permute-done | bytes 163872 | tf_op jit(solution)/shard_map/ppermute | solution.py:1034
  473.1 3.1 collective-permute-start.55
  477.7 6.4 %collective-permute-done.55 = f32[272,128]{1,0:T(8,128)S(1)} collective-permute-done((f32[272,128]{1,0:T(8,128)S(1)}, f32[272,128]{1,0:T(8,128)S(1)}, u32[]{:S(2)}, u32[]{:S(2)}) %collective-permute-start.55) | collective-permute-done | bytes 139296 | tf_op jit(solution)/shard_map/ppermute | solution.py:1034
  484.0 2.8 collective-permute-done.56
  486.9 4.6 collective-permute-start.57
  492.5 5.7 %collective-permute-done.57 = f32[272,128]{1,0:T(8,128)S(1)} collective-permute-done((f32[272,128]{1,0:T(8,128)S(1)}, f32[272,128]{1,0:T(8,128)S(1)}, u32[]{:S(2)}, u32[]{:S(2)}) %collective-permute-start.57) | collective-permute-done | bytes 139296 | tf_op jit(solution)/shard_map/ppermute | solution.py:1034
  (348 shorter events, 108.1 us)
Async XLA Ops:
  5.5 18.7 %collective-permute-start = (f32[512,128]{1,0:T(8,128)S(1)}, f32[512,128]{1,0:T(8,128)S(1)}, u32[]{:S(2)}, u32[]{:S(2)}) collective-permute-start(f32[512,128]{1,0:T(8,128)S(1)} %concatenate.63.own_ref), channel_id=1, source_target_pairs={{0,1},{1,0},{2,3},{3,2},{4,5},{5,4},{6,7},{7,6},{8,9},{9,8},{10,11... | collective-permute-start | bytes 786440 | tf_op jit(solution)/shard_map/ppermute | solution.py:1034
  9.6 26.6 %collective-permute-start.1 = (bf16[256,1024]{1,0:T(8,128)(2,1)S(1)}, bf16[256,1024]{1,0:T(8,128)(2,1)S(1)}, u32[]{:S(2)}, u32[]{:S(2)}) collective-permute-start(bf16[256,1024]{1,0:T(8,128)(2,1)S(1)} %constant_dynamic-slice_fusion.18), channel_id=1, source_target_pairs={{0,1},{1,0},{2,3},{3,2},{4,5},{5,4},{6,7},{7,6},{8,9},{9,8},{10,11... | collective-permute-start | bytes 1572872 | tf_op jit(solution)/shard_map/ppermute | solution.py:1034
  20.4 33.6 %collective-permute-start.5 = (bf16[256,1024]{1,0:T(8,128)(2,1)}, bf16[256,1024]{1,0:T(8,128)(2,1)}, u32[]{:S(2)}, u32[]{:S(2)}) collective-permute-start(bf16[256,1024]{1,0:T(8,128)(2,1)} %constant_dynamic-slice_fusion.17), channel_id=1, source_target_pairs={{0,1},{1,0},{2,3},{3,2},{4,5},{5,4},{6,7},{7,6},{8,9},{9,8},{10,11... | collective-permute-start | bytes 1572872 | tf_op jit(solution)/shard_map/ppermute | solution.py:1034
  36.2 14.0 %collective-permute-start.2 = (bf16[256,1024]{1,0:T(8,128)(2,1)S(1)}, bf16[256,1024]{1,0:T(8,128)(2,1)S(1)}, u32[]{:S(2)}, u32[]{:S(2)}) collective-permute-start(bf16[256,1024]{1,0:T(8,128)(2,1)S(1)} %collective-permute-done.1.p0.w0), channel_id=1, source_target_pairs={{0,4},{2,6},{4,0},{6,2},{8,12},{10,14},{12,8},{14,10},{16,20},{18,... | collective-permute-start | bytes 1572872 | tf_op jit(solution)/shard_map/ppermute | solution.py:1034
  51.9 18.0 %collective-permute-start.9 = (bf16[256,1024]{1,0:T(8,128)(2,1)S(1)}, bf16[256,1024]{1,0:T(8,128)(2,1)S(1)}, u32[]{:S(2)}, u32[]{:S(2)}) collective-permute-start(bf16[256,1024]{1,0:T(8,128)(2,1)S(1)} %copy-done.44), channel_id=1, source_target_pairs={{0,1},{1,0},{2,3},{3,2},{4,5},{5,4},{6,7},{7,6},{8,9},{9,8},{10,11... | collective-permute-start | bytes 1572872 | tf_op jit(solution)/shard_map/ppermute | solution.py:1034
  52.5 25.6 %collective-permute-start.13 = (bf16[256,1024]{1,0:T(8,128)(2,1)S(1)}, bf16[256,1024]{1,0:T(8,128)(2,1)}, u32[]{:S(2)}, u32[]{:S(2)}) collective-permute-start(bf16[256,1024]{1,0:T(8,128)(2,1)S(1)} %pad_maximum_fusion.1), channel_id=1, source_target_pairs={{0,1},{1,0},{2,3},{3,2},{4,5},{5,4},{6,7},{7,6},{8,9},{9,8},{10,11... | collective-permute-start | bytes 1572872 | tf_op jit(solution)/shard_map/ppermute | solution.py:1034
  54.0 13.6 %collective-permute-start.6 = (bf16[256,1024]{1,0:T(8,128)(2,1)}, bf16[256,1024]{1,0:T(8,128)(2,1)S(1)}, u32[]{:S(2)}, u32[]{:S(2)}) collective-permute-start(bf16[256,1024]{1,0:T(8,128)(2,1)} %collective-permute-done.5.w0), channel_id=1, source_target_pairs={{0,8},{2,10},{4,12},{6,14},{8,0},{10,2},{12,4},{14,6},{16,24},{18,... | collective-permute-start | bytes 1572872 | tf_op jit(solution)/shard_map/ppermute | solution.py:1034
  67.6 12.1 %collective-permute-start.7 = (bf16[256,1024]{1,0:T(8,128)(2,1)}, bf16[256,1024]{1,0:T(8,128)(2,1)S(1)}, u32[]{:S(2)}, u32[]{:S(2)}) collective-permute-start(bf16[256,1024]{1,0:T(8,128)(2,1)} %collective-permute-done.5.w0), channel_id=1, source_target_pairs={{0,2},{2,0},{4,6},{6,4},{8,10},{10,8},{12,14},{14,12},{16,18},{18,... | collective-permute-start | bytes 1572872 | tf_op jit(solution)/shard_map/ppermute | solution.py:1034
  67.6 12.1 %collective-permute-start.8 = (bf16[256,1024]{1,0:T(8,128)(2,1)S(1)}, bf16[256,1024]{1,0:T(8,128)(2,1)S(1)}, u32[]{:S(2)}, u32[]{:S(2)}) collective-permute-start(bf16[256,1024]{1,0:T(8,128)(2,1)S(1)} %collective-permute-done.6.w1), channel_id=1, source_target_pairs={{0,2},{2,0},{4,6},{6,4},{8,10},{10,8},{12,14},{14,12},{16,18},{18,... | collective-permute-start | bytes 1572872 | tf_op jit(solution)/shard_map/ppermute | solution.py:1034
  69.4 31.2 %collective-permute-start.18 = (bf16[256,2048]{1,0:T(8,128)(2,1)S(1)}, bf16[256,2048]{1,0:T(8,128)(2,1)}, u32[]{:S(2)}, u32[]{:S(2)}) collective-permute-start(bf16[256,2048]{1,0:T(8,128)(2,1)S(1)} %constant_dynamic-slice_fusion.13), channel_id=1, source_target_pairs={{0,1},{1,0},{2,3},{3,2},{4,5},{5,4},{6,7},{7,6},{8,9},{9,8},{10,11... | collective-permute-start | bytes 3145736 | tf_op jit(solution)/shard_map/ppermute | solution.py:1034
  70.0 27.8 %collective-permute-start.10 = (bf16[256,1024]{1,0:T(8,128)(2,1)S(1)}, bf16[256,1024]{1,0:T(8,128)(2,1)S(1)}, u32[]{:S(2)}, u32[]{:S(2)}) collective-permute-start(bf16[256,1024]{1,0:T(8,128)(2,1)S(1)} %collective-permute-done.9.u0), channel_id=1, source_target_pairs={{0,4},{2,6},{4,0},{6,2},{8,12},{10,14},{12,8},{14,10},{16,20},{18,... | collective-permute-start | bytes 1572872 | tf_op jit(solution)/shard_map/ppermute | solution.py:1034
  78.1 19.0 %collective-permute-start.14 = (bf16[256,1024]{1,0:T(8,128)(2,1)}, bf16[256,1024]{1,0:T(8,128)(2,1)}, u32[]{:S(2)}, u32[]{:S(2)}) collective-permute-start(bf16[256,1024]{1,0:T(8,128)(2,1)} %collective-permute-done.13.h0.f0), channel_id=1, source_target_pairs={{0,8},{2,10},{4,12},{6,14},{8,0},{10,2},{12,4},{14,6},{16,24},{18,... | collective-permute-start | bytes 1572872 | tf_op jit(solution)/shard_map/ppermute | solution.py:1034
  100.6 40.9 %collective-permute-start.22 = (bf16[512,1024]{1,0:T(8,128)(2,1)}, bf16[512,1024]{1,0:T(8,128)(2,1)}, u32[]{:S(2)}, u32[]{:S(2)}) collective-permute-start(bf16[512,1024]{1,0:T(8,128)(2,1)} %constant_dynamic-slice_fusion.12), channel_id=1, source_target_pairs={{0,1},{1,0},{2,3},{3,2},{4,5},{5,4},{6,7},{7,6},{8,9},{9,8},{10,11... | collective-permute-start | bytes 3145736 | tf_op jit(solution)/shard_map/ppermute | solution.py:1034
  101.1 62.2 %collective-permute-start.19 = (bf16[256,2048]{1,0:T(8,128)(2,1)}, bf16[256,2048]{1,0:T(8,128)(2,1)}, u32[]{:S(2)}, u32[]{:S(2)}) collective-permute-start(bf16[256,2048]{1,0:T(8,128)(2,1)} %collective-permute-done.18.refs_0_), channel_id=1, source_target_pairs={{0,4},{2,6},{4,0},{6,2},{8,12},{10,14},{12,8},{14,10},{16,20},{18,... | collective-permute-start | bytes 3145736 | tf_op jit(solution)/shard_map/ppermute | solution.py:1034
  141.5 24.9 %collective-permute-start.23 = (bf16[512,1024]{1,0:T(8,128)(2,1)}, bf16[512,1024]{1,0:T(8,128)(2,1)S(1)}, u32[]{:S(2)}, u32[]{:S(2)}) collective-permute-start(bf16[512,1024]{1,0:T(8,128)(2,1)} %collective-permute-done.22.refs_4_), channel_id=1, source_target_pairs={{0,8},{2,10},{4,12},{6,14},{8,0},{10,2},{12,4},{14,6},{16,24},{18,... | collective-permute-start | bytes 3145736 | tf_op jit(solution)/shard_map/ppermute | solution.py:1034
  142.2 24.2 %collective-permute-start.17 = (bf16[2,512,1024]{2,1,0:T(8,128)(2,1)}, bf16[2,512,1024]{2,1,0:T(8,128)(2,1)S(1)}, u32[]{:S(2)}, u32[]{:S(2)}) collective-permute-start(bf16[2,512,1024]{2,1,0:T(8,128)(2,1)} %get-tuple-element.214), channel_id=1, source_target_pairs={{0,2},{2,0},{4,6},{6,4},{8,10},{10,8},{12,14},{14,12},{16,18},{18,... | collective-permute-start | bytes 6291464 | tf_op jit(solution)/shard_map/ppermute | solution.py:1034
  142.2 30.7 %collective-permute-start.29 = (bf16[2,512,1024]{2,1,0:T(8,128)(2,1)}, bf16[2,512,1024]{2,1,0:T(8,128)(2,1)}, u32[]{:S(2)}, u32[]{:S(2)}) collective-permute-start(bf16[2,512,1024]{2,1,0:T(8,128)(2,1)} %get-tuple-element.259), channel_id=1, source_target_pairs={{0,2},{2,0},{4,6},{6,4},{8,10},{10,8},{12,14},{14,12},{16,18},{18,... | collective-permute-start | bytes 6291464 | tf_op jit(solution)/shard_map/ppermute | solution.py:1034
  163.3 14.3 %collective-permute-start.20 = (bf16[256,2048]{1,0:T(8,128)(2,1)}, bf16[256,2048]{1,0:T(8,128)(2,1)}, u32[]{:S(2)}, u32[]{:S(2)}) collective-permute-start(bf16[256,2048]{1,0:T(8,128)(2,1)} %collective-permute-done.18.refs_0_), channel_id=1, source_target_pairs={{0,2},{2,0},{4,6},{6,4},{8,10},{10,8},{12,14},{14,12},{16,18},{18,... | collective-permute-start | bytes 3145736 | tf_op jit(solution)/shard_map/ppermute | solution.py:1034
  163.4 14.2 %collective-permute-start.21 = (bf16[256,2048]{1,0:T(8,128)(2,1)}, bf16[256,2048]{1,0:T(8,128)(2,1)}, u32[]{:S(2)}, u32[]{:S(2)}) collective-permute-start(bf16[256,2048]{1,0:T(8,128)(2,1)} %collective-permute-done.19.refs_1_), channel_id=1, source_target_pairs={{0,2},{2,0},{4,6},{6,4},{8,10},{10,8},{12,14},{14,12},{16,18},{18,... | collective-permute-start | bytes 3145736 | tf_op jit(solution)/shard_map/ppermute | solution.py:1034
  172.9 46.9 %collective-permute-start.34 = (bf16[512,1024]{1,0:T(8,128)(2,1)}, bf16[512,1024]{1,0:T(8,128)(2,1)}, u32[]{:S(2)}, u32[]{:S(2)}) collective-permute-start(bf16[512,1024]{1,0:T(8,128)(2,1)} %fusion.1), channel_id=1, source_target_pairs={{0,4},{2,6},{4,0},{6,2},{8,12},{10,14},{12,8},{14,10},{16,20},{18,... | collective-permute-start | bytes 3145736 | tf_op jit(solution)/shard_map/ppermute | solution.py:1034
  198.4 25.5 %collective-permute-start.27 = (bf16[2,512,1024]{2,1,0:T(8,128)(2,1)}, bf16[2,512,1024]{2,1,0:T(8,128)(2,1)S(1)}, u32[]{:S(2)}, u32[]{:S(2)}) collective-permute-start(bf16[2,512,1024]{2,1,0:T(8,128)(2,1)} %get-tuple-element.232), channel_id=1, source_target_pairs={{0,2},{2,0},{4,6},{6,4},{8,10},{10,8},{12,14},{14,12},{16,18},{18,... | collective-permute-start | bytes 6291464 | tf_op jit(solution)/shard_map/ppermute | solution.py:1034
  198.5 23.2 %collective-permute-start.26 = (bf16[2,512,1024]{2,1,0:T(8,128)(2,1)}, bf16[2,512,1024]{2,1,0:T(8,128)(2,1)S(1)}, u32[]{:S(2)}, u32[]{:S(2)}) collective-permute-start(bf16[2,512,1024]{2,1,0:T(8,128)(2,1)} %get-tuple-element.230), channel_id=1, source_target_pairs={{0,2},{2,0},{4,6},{6,4},{8,10},{10,8},{12,14},{14,12},{16,18},{18,... | collective-permute-start | bytes 6291464 | tf_op jit(solution)/shard_map/ppermute | solution.py:1034
  223.3 31.8 %collective-permute-start.28 = (bf16[512,1024]{1,0:T(8,128)(2,1)S(1)}, bf16[512,1024]{1,0:T(8,128)(2,1)S(1)}, u32[]{:S(2)}, u32[]{:S(2)}) collective-permute-start(bf16[512,1024]{1,0:T(8,128)(2,1)S(1)} %fusion.2), channel_id=1, source_target_pairs={{0,4},{2,6},{4,0},{6,2},{8,12},{10,14},{12,8},{14,10},{16,20},{18,... | collective-permute-start | bytes 3145736 | tf_op jit(solution)/shard_map/ppermute | solution.py:1034
  226.2 60.1 %collective-permute-start.30 = (bf16[2,512,1024]{2,1,0:T(8,128)(2,1)}, bf16[2,512,1024]{2,1,0:T(8,128)(2,1)}, u32[]{:S(2)}, u32[]{:S(2)}) collective-permute-start(bf16[2,512,1024]{2,1,0:T(8,128)(2,1)} %add_convert_fusion), channel_id=1, source_target_pairs={{0,1},{1,0},{2,3},{3,2},{4,5},{5,4},{6,7},{7,6},{8,9},{9,8},{10,11... | collective-permute-start | bytes 6291464 | tf_op jit(solution)/shard_map/ppermute | solution.py:1034
  270.6 28.8 %collective-permute-start.31 = (bf16[2,2,512,768]{3,2,1,0:T(8,128)(2,1)}, bf16[2,2,512,768]{3,2,1,0:T(8,128)(2,1)}, u32[]{:S(2)}, u32[]{:S(2)}) collective-permute-start(bf16[2,2,512,768]{3,2,1,0:T(8,128)(2,1)} %get-tuple-element.249), channel_id=1, source_target_pairs={{0,2},{2,0},{4,6},{6,4},{8,10},{10,8},{12,14},{14,12},{16,18},{18,... | collective-permute-start | bytes 9437192 | tf_op jit(solution)/shard_map/ppermute | solution.py:1034
  270.6 28.8 %collective-permute-start.32 = (bf16[2,2,512,768]{3,2,1,0:T(8,128)(2,1)}, bf16[2,2,512,768]{3,2,1,0:T(8,128)(2,1)}, u32[]{:S(2)}, u32[]{:S(2)}) collective-permute-start(bf16[2,2,512,768]{3,2,1,0:T(8,128)(2,1)} %get-tuple-element.250), channel_id=1, source_target_pairs={{0,2},{2,0},{4,6},{6,4},{8,10},{10,8},{12,14},{14,12},{16,18},{18,... | collective-permute-start | bytes 9437192 | tf_op jit(solution)/shard_map/ppermute | solution.py:1034
  271.1 60.9 %collective-permute-start.35 = (bf16[512,1024]{1,0:T(8,128)(2,1)}, bf16[512,1024]{1,0:T(8,128)(2,1)}, u32[]{:S(2)}, u32[]{:S(2)}) collective-permute-start(bf16[512,1024]{1,0:T(8,128)(2,1)} %fusion), channel_id=1, source_target_pairs={{0,1},{1,0},{2,3},{3,2},{4,5},{5,4},{6,7},{7,6},{8,9},{9,8},{10,11... | collective-permute-start | bytes 3145736 | tf_op jit(solution)/shard_map/ppermute | solution.py:1034
  295.9 25.8 %collective-permute-start.33 = (bf16[2,2,512,512]{3,2,1,0:T(8,128)(2,1)}, bf16[2,2,512,512]{3,2,1,0:T(8,128)(2,1)S(1)}, u32[]{:S(2)}, u32[]{:S(2)}) collective-permute-start(bf16[2,2,512,512]{3,2,1,0:T(8,128)(2,1)} %weight_value.2), channel_id=1, source_target_pairs={{0,2},{2,0},{4,6},{6,4},{8,10},{10,8},{12,14},{14,12},{16,18},{18,... | collective-permute-start | bytes 6291464 | tf_op jit(solution)/shard_map/ppermute | solution.py:1034
  295.9 37.7 %collective-permute-start.36 = (bf16[512,1024]{1,0:T(8,128)(2,1)}, bf16[512,1024]{1,0:T(8,128)(2,1)}, u32[]{:S(2)}, u32[]{:S(2)}) collective-permute-start(bf16[512,1024]{1,0:T(8,128)(2,1)} %fusion.3), channel_id=1, source_target_pairs={{0,4},{2,6},{4,0},{6,2},{8,12},{10,14},{12,8},{14,10},{16,20},{18,... | collective-permute-start | bytes 3145736 | tf_op jit(solution)/shard_map/ppermute | solution.py:1034
  319.1 23.9 %collective-permute-start.37 = (bf16[2,512,128]{2,1,0:T(8,128)(2,1)}, bf16[2,512,128]{2,1,0:T(8,128)(2,1)}, u32[]{:S(2)}, u32[]{:S(2)}) collective-permute-start(bf16[2,512,128]{2,1,0:T(8,128)(2,1)} %weight_z.1), channel_id=1, source_target_pairs={{0,2},{2,0},{4,6},{6,4},{8,10},{10,8},{12,14},{14,12},{16,18},{18,... | collective-permute-start | bytes 786440 | tf_op jit(solution)/shard_map/ppermute | solution.py:1034
  319.3 37.4 %collective-permute-start.38 = (bf16[2,512,768]{2,1,0:T(8,128)(2,1)}, bf16[2,512,768]{2,1,0:T(8,128)(2,1)S(1)}, u32[]{:S(2)}, u32[]{:S(2)}) collective-permute-start(bf16[2,512,768]{2,1,0:T(8,128)(2,1)} %get-tuple-element.264), channel_id=1, source_target_pairs={{0,4},{2,6},{4,0},{6,2},{8,12},{10,14},{12,8},{14,10},{16,20},{18,... | collective-permute-start | bytes 4718600 | tf_op jit(solution)/shard_map/ppermute | solution.py:1034
  323.0 37.5 %collective-permute-start.39 = (bf16[2,512,768]{2,1,0:T(8,128)(2,1)}, bf16[2,512,768]{2,1,0:T(8,128)(2,1)S(1)}, u32[]{:S(2)}, u32[]{:S(2)}) collective-permute-start(bf16[2,512,768]{2,1,0:T(8,128)(2,1)} %get-tuple-element.276), channel_id=1, source_target_pairs={{0,1},{1,0},{2,3},{3,2},{4,5},{5,4},{6,7},{7,6},{8,9},{9,8},{10,11... | collective-permute-start | bytes 4718600 | tf_op jit(solution)/shard_map/ppermute | solution.py:1034
  332.0 45.9 %collective-permute-start.42 = (bf16[2,512,256]{2,1,0:T(8,128)(2,1)}, bf16[2,512,256]{2,1,0:T(8,128)(2,1)}, u32[]{:S(2)}, u32[]{:S(2)}) collective-permute-start(bf16[2,512,256]{2,1,0:T(8,128)(2,1)} %get-tuple-element.268), channel_id=1, source_target_pairs={{0,4},{2,6},{4,0},{6,2},{8,12},{10,14},{12,8},{14,10},{16,20},{18,... | collective-permute-start | bytes 1572872 | tf_op jit(solution)/shard_map/ppermute | solution.py:1034
  341.7 36.2 %collective-permute-start.41 = (bf16[2,128,1024]{2,1,0:T(8,128)(2,1)}, bf16[2,128,1024]{2,1,0:T(8,128)(2,1)}, u32[]{:S(2)}, u32[]{:S(2)}) collective-permute-start(bf16[2,128,1024]{2,1,0:T(8,128)(2,1)} %fusion.9), channel_id=1, source_target_pairs={{0,8},{2,10},{4,12},{6,14},{8,0},{10,2},{12,4},{14,6},{16,24},{18,... | collective-permute-start | bytes 1572872 | tf_op jit(solution)/shard_map/ppermute | solution.py:1034
  343.0 34.9 %collective-permute-start.40 = (bf16[2,128,1024]{2,1,0:T(8,128)(2,1)}, bf16[2,128,1024]{2,1,0:T(8,128)(2,1)}, u32[]{:S(2)}, u32[]{:S(2)}) collective-permute-start(bf16[2,128,1024]{2,1,0:T(8,128)(2,1)} %fusion.8), channel_id=1, source_target_pairs={{0,8},{2,10},{4,12},{6,14},{8,0},{10,2},{12,4},{14,6},{16,24},{18,... | collective-permute-start | bytes 1572872 | tf_op jit(solution)/shard_map/ppermute | solution.py:1034
  356.7 21.2 %collective-permute-start.43 = (bf16[2,512,256]{2,1,0:T(8,128)(2,1)S(1)}, bf16[2,512,256]{2,1,0:T(8,128)(2,1)S(1)}, u32[]{:S(2)}, u32[]{:S(2)}) collective-permute-start(bf16[2,512,256]{2,1,0:T(8,128)(2,1)S(1)} %copy-done.68), channel_id=1, source_target_pairs={{0,1},{1,0},{2,3},{3,2},{4,5},{5,4},{6,7},{7,6},{8,9},{9,8},{10,11... | collective-permute-start | bytes 1572872 | tf_op jit(solution)/shard_map/ppermute | solution.py:1034
  360.5 15.9 %collective-permute-start.44 = (bf16[2,512,128]{2,1,0:T(8,128)(2,1)S(1)}, bf16[2,512,128]{2,1,0:T(8,128)(2,1)S(1)}, u32[]{:S(2)}, u32[]{:S(2)}) collective-permute-start(bf16[2,512,128]{2,1,0:T(8,128)(2,1)S(1)} %add_convert_fusion.14), channel_id=1, source_target_pairs={{0,1},{1,0},{2,3},{3,2},{4,5},{5,4},{6,7},{7,6},{8,9},{9,8},{10,11... | collective-permute-start | bytes 786440 | tf_op jit(solution)/shard_map/ppermute | solution.py:1034
  376.4 32.0 %collective-permute-start.46 = (bf16[512,768]{1,0:T(8,128)(2,1)S(1)}, bf16[512,768]{1,0:T(8,128)(2,1)S(1)}, u32[]{:S(2)}, u32[]{:S(2)}) collective-permute-start(bf16[512,768]{1,0:T(8,128)(2,1)S(1)} %copy-done.37), channel_id=1, source_target_pairs={{0,4},{2,6},{4,0},{6,2},{8,12},{10,14},{12,8},{14,10},{16,20},{18,... | collective-permute-start | bytes 2359304 | tf_op jit(solution)/shard_map/ppermute | solution.py:1034
  379.6 22.3 %collective-permute-start.64 = (bf16[128,1024]{1,0:T(8,128)(2,1)S(1)}, bf16[128,1024]{1,0:T(8,128)(2,1)S(1)}, u32[]{:S(2)}, u32[]{:S(2)}) collective-permute-start(bf16[128,1024]{1,0:T(8,128)(2,1)S(1)} %fusion.12), channel_id=1, source_target_pairs={{0,16},{2,18},{4,20},{6,22},{8,24},{10,26},{12,28},{14,30},{16,0},... | collective-permute-start | bytes 786440 | tf_op jit(solution)/shard_map/ppermute | solution.py:1034
  383.8 20.8 %collective-permute-start.62 = (bf16[128,1024]{1,0:T(8,128)(2,1)S(1)}, bf16[128,1024]{1,0:T(8,128)(2,1)S(1)}, u32[]{:S(2)}, u32[]{:S(2)}) collective-permute-start(bf16[128,1024]{1,0:T(8,128)(2,1)S(1)} %fusion.11), channel_id=1, source_target_pairs={{0,16},{2,18},{4,20},{6,22},{8,24},{10,26},{12,28},{14,30},{16,0},... | collective-permute-start | bytes 786440 | tf_op jit(solution)/shard_map/ppermute | solution.py:1034
  385.8 45.4 %collective-permute-start.48 = (bf16[512,384]{1,0:T(8,128)(2,1)}, bf16[512,384]{1,0:T(8,128)(2,1)}, u32[]{:S(2)}, u32[]{:S(2)}) collective-permute-start(bf16[512,384]{1,0:T(8,128)(2,1)} %pad_maximum_fusion.2), channel_id=1, source_target_pairs={{0,4},{2,6},{4,0},{6,2},{8,12},{10,14},{12,8},{14,10},{16,20},{18,... | collective-permute-start | bytes 1179656 | tf_op jit(solution)/shard_map/ppermute | solution.py:1034
  398.8 20.4 %collective-permute-start.45 = (bf16[512,768]{1,0:T(8,128)(2,1)S(1)}, bf16[512,768]{1,0:T(8,128)(2,1)S(1)}, u32[]{:S(2)}, u32[]{:S(2)}) collective-permute-start(bf16[512,768]{1,0:T(8,128)(2,1)S(1)} %copy-done.36), channel_id=1, source_target_pairs={{0,1},{1,0},{2,3},{3,2},{4,5},{5,4},{6,7},{7,6},{8,9},{9,8},{10,11... | collective-permute-start | bytes 2359304 | tf_op jit(solution)/shard_map/ppermute | solution.py:1034
  405.0 26.3 %collective-permute-start.47 = (bf16[512,256]{1,0:T(8,128)(2,1)S(1)}, bf16[512,256]{1,0:T(8,128)(2,1)S(1)}, u32[]{:S(2)}, u32[]{:S(2)}) collective-permute-start(bf16[512,256]{1,0:T(8,128)(2,1)S(1)} %fusion.20), channel_id=1, source_target_pairs={{0,1},{1,0},{2,3},{3,2},{4,5},{5,4},{6,7},{7,6},{8,9},{9,8},{10,11... | collective-permute-start | bytes 786440 | tf_op jit(solution)/shard_map/ppermute | solution.py:1034
  433.7 15.3 %collective-permute-start.52 = (f32[272,128]{1,0:T(8,128)S(1)}, f32[272,128]{1,0:T(8,128)S(1)}, u32[]{:S(2)}, u32[]{:S(2)}) collective-permute-start(f32[272,128]{1,0:T(8,128)S(1)} %constant_dynamic-update-slice_fusion), channel_id=1, source_target_pairs={{0,2},{2,0},{4,6},{6,4},{8,10},{10,8},{12,14},{14,12},{16,18},{18,... | collective-permute-start | bytes 417800 | tf_op jit(solution)/shard_map/ppermute | solution.py:1034
  433.7 15.2 %collective-permute-start.51 = (bf16[2,128,640]{2,1,0:T(8,128)(2,1)S(1)}, bf16[2,128,640]{2,1,0:T(8,128)(2,1)S(1)}, u32[]{:S(2)}, u32[]{:S(2)}) collective-permute-start(bf16[2,128,640]{2,1,0:T(8,128)(2,1)S(1)} %dynamic-slice_bitcast_fusion), channel_id=1, source_target_pairs={{0,8},{2,10},{4,12},{6,14},{8,0},{10,2},{12,4},{14,6},{16,24},{18,... | collective-permute-start | bytes 983048 | tf_op jit(solution)/shard_map/ppermute | solution.py:1034
  434.4 18.4 %collective-permute-start.50 = (bf16[2,128,768]{2,1,0:T(8,128)(2,1)S(1)}, bf16[2,128,768]{2,1,0:T(8,128)(2,1)S(1)}, u32[]{:S(2)}, u32[]{:S(2)}) collective-permute-start(bf16[2,128,768]{2,1,0:T(8,128)(2,1)S(1)} %fusion.15), channel_id=1, source_target_pairs={{0,8},{2,10},{4,12},{6,14},{8,0},{10,2},{12,4},{14,6},{16,24},{18,... | collective-permute-start | bytes 1179656 | tf_op jit(solution)/shard_map/ppermute | solution.py:1034
  435.8 24.9 %collective-permute-start.49 = (bf16[2,128,768]{2,1,0:T(8,128)(2,1)S(1)}, bf16[2,128,768]{2,1,0:T(8,128)(2,1)S(1)}, u32[]{:S(2)}, u32[]{:S(2)}) collective-permute-start(bf16[2,128,768]{2,1,0:T(8,128)(2,1)S(1)} %fusion.14), channel_id=1, source_target_pairs={{0,8},{2,10},{4,12},{6,14},{8,0},{10,2},{12,4},{14,6},{16,24},{18,... | collective-permute-start | bytes 1179656 | tf_op jit(solution)/shard_map/ppermute | solution.py:1034
  471.4 20.9 %collective-permute-start.60 = (bf16[128,1536]{1,0:T(8,128)(2,1)S(1)}, bf16[128,1536]{1,0:T(8,128)(2,1)S(1)}, u32[]{:S(2)}, u32[]{:S(2)}) collective-permute-start(bf16[128,1536]{1,0:T(8,128)(2,1)S(1)} %get-tuple-element.330), channel_id=1, source_target_pairs={{0,16},{2,18},{4,20},{6,22},{8,24},{10,26},{12,28},{14,30},{16,0},... | collective-permute-start | bytes 1179656 | tf_op jit(solution)/shard_map/ppermute | solution.py:1034
  (88 other events, 719.4 us)

commit v5 on v4

--- a/solution.py
+++ b/solution.py
@@ -312,11 +312,12 @@
     )
 
 
-CP = pltpu.CompilerParams(vmem_limit_bytes=56 * 1024 * 1024)
+MIB = 1024 * 1024
 BF = jnp.bfloat16
 F32 = jnp.float32
 ROWS = 256
-hint = 10
+hints = dict()
+opt = dict(dn=0, m2=3, v2=5, z2=3, z1m=5, z1v=6)
 
 
 def sds(shape, dtype=BF):
@@ -335,9 +336,18 @@
     return pl.BlockSpec((rows, cols), lambda i, s: (0, i))
 
 
-def run(body, grid, scal, ins, in_specs, out_shape, out_specs, scratch=(), flops=0, name=None, aliases=None):
+def run(body, grid, scal, ins, in_specs, out_shape, out_specs, scratch=(), flops=0, name=None, aliases=None, spare=12):
     moved = sum(a.size * a.dtype.itemsize for a in ins)
     moved += sum(math.prod(o.shape) * jnp.dtype(o.dtype).itemsize for o in out_shape)
+    def held_bytes(spec, a):
+        if spec.block_shape is None:
+            return 0
+        return math.prod(spec.block_shape) * jnp.dtype(a.dtype).itemsize * (1 if spec.pipeline_mode else 2)
+
+    if name in ("attend", "gate", "ffn", "mid_back", "pack_params", "ema_params", "pieces"):
+        spare = 56
+    vmem = sum(map(held_bytes, in_specs, ins)) + sum(map(held_bytes, out_specs, out_shape))
+    vmem += sum(math.prod(r.shape) * jnp.dtype(r.dtype).itemsize for r in scratch if r.memory_space == pltpu.VMEM)
     return pl.pallas_call(
         body,
         out_shape=out_shape,
@@ -348,8 +358,8 @@
             out_specs=out_specs,
             scratch_shapes=list(scratch),
         ),
-        compiler_params=CP,
-        cost_estimate=pl.CostEstimate(flops=int(flops * hint), bytes_accessed=int(moved * hint), transcendentals=0),
+        compiler_params=pltpu.CompilerParams(vmem_limit_bytes=min(vmem + spare * MIB, 56 * MIB)),
+        cost_estimate=pl.CostEstimate(flops=int(flops * hints.get(name, 10)), bytes_accessed=int(moved * hints.get(name, 10)), transcendentals=0),
         name=name,
         input_output_aliases=aliases or {},
     )(scal, *ins)
@@ -460,29 +470,70 @@
     )
 
 
+def k_pack_params(scal, arrays, omega):
+    ch = omega.shape[1]
+
+    def body(s, a0, a1, a2, a3, w_ref, o_ref):
+        for i, ref in enumerate((a0, a1, a2, a3)):
+            o_ref[i * H : (i + 1) * H, :] = ref[...]
+        o_ref[4 * H : 4 * H + 8, :] = jnp.broadcast_to(w_ref[...], (8, ch))
+
+    return run(
+        body, (1,), scal, [*arrays, omega], [whole((H, ch))] * 4 + [whole((1, ch))],
+        [sds((4 * H + 8, ch), F32)], [pl.BlockSpec((4 * H + 8, ch), lambda i, s: (0, 0))], flops=1e7, name="pack_params",
+    )[0]
+
+
 def k_ema_params(scal, own, oth):
-    ch, width = own.shape
+    height, ch = own.shape
     groups = 2 * ch // 128
 
-    def body(s, own_ref, oth_ref, dec_ref, cf_ref, om_ref, scr):
-        scr[pl.ds(pl.multiple_of(s[6] * ch, ch), ch), :] = own_ref[...]
-        scr[pl.ds(pl.multiple_of(s[7] * ch, ch), ch), :] = oth_ref[...]
-        v = scr[...].T
-        rate = sig(v[0:H])
-        dec = 1.0 - rate * sig(v[H : 2 * H])
-        cf = rate * v[2 * H : 3 * H] * v[3 * H : 4 * H]
-        for g in range(groups):
-            lanes = slice(g * 128, (g + 1) * 128)
-            dec_ref[pl.ds(g, H, stride=groups), :] = dec[:, lanes]
-            cf_ref[pl.ds(g, H, stride=groups), :] = cf[:, lanes]
-            om_ref[g : g + 1, :] = v[4 * H : 4 * H + 1, lanes]
+    def body(s, own_ref, oth_ref, dec_ref, cf_ref, om_ref):
+        for j in range(2):
+            for src, ref in ((0, own_ref), (1, oth_ref)):
+
+                @pl.when(s[6 + src] == j)
+                def _(j=j, ref=ref):
+                    v = ref[...]
+                    rate = sig(v[0:H])
+                    dec = 1.0 - rate * sig(v[H : 2 * H])
+                    cf = rate * v[2 * H : 3 * H] * v[3 * H : 4 * H]
+                    for g in range(groups // 2):
+                        lanes = slice(g * 128, (g + 1) * 128)
+                        at = j * (groups // 2) + g
+                        dec_ref[pl.ds(at, H, stride=groups), :] = dec[:, lanes]
+                        cf_ref[pl.ds(at, H, stride=groups), :] = cf[:, lanes]
+                        om_ref[at : at + 1, :] = v[4 * H : 4 * H + 1, lanes]
 
     par = (H * groups, 128)
     return run(
-        body, (1,), scal, [own, oth], [whole((ch, width))] * 2,
+        body, (1,), scal, [own, oth], [whole((height, ch))] * 2,
         [sds(par, F32), sds(par, F32), sds((groups, 128), F32)],
         [pl.BlockSpec(par, lambda i, s: (0, 0))] * 2 + [pl.BlockSpec((groups, 128), lambda i, s: (0, 0))],
-        [pltpu.VMEM((2 * ch, width), F32)], flops=1e8, name="ema_params",
+        flops=1e8, name="ema_params",
+    )
+
+
+def k_pieces(scal, takes):
+    parts = [(w, at) for take in takes for w, at in take]
+
+    def body(s, *refs):
+        ins, outs = refs[: len(parts)], refs[len(parts) :]
+        n = 0
+        for take, out in zip(takes, outs):
+            low = 0
+            for w, _ in take:
+                rows = w.shape[0] // 4
+                out[low : low + rows, :] = ins[n][...]
+                low += rows
+                n += 1
+
+    return run(
+        body, (1,), scal, [w for w, _ in parts],
+        [pl.BlockSpec((w.shape[0] // 4, w.shape[1]), lambda i, s, at=at: (s[at], 0)) for w, at in parts],
+        [sds((sum(w.shape[0] // 4 for w, _ in take), take[0][0].shape[1])) for take in takes],
+        [pl.BlockSpec((sum(w.shape[0] // 4 for w, _ in take), take[0][0].shape[1]), lambda i, s: (0, 0)) for take in takes],
+        flops=1e7, name="pieces",
     )
 
 
@@ -532,7 +583,7 @@
     return run(
         body, (count,), scal, [normed, decay, coef, omega, *more],
         [at, whole(par), whole(par), whole((groups, 128))]
-        + ([whole(par), pl.BlockSpec(memory_space=pl.ANY), pl.BlockSpec(memory_space=pl.ANY)] if before else []),
+        + ([whole(par), pl.BlockSpec(memory_space=pltpu.HBM), pl.BlockSpec(memory_space=pltpu.HBM)] if before else []),
         [sds((n, d)), sds((n, d)), sds(par, F32)],
         [at, at, pl.BlockSpec(par, lambda i, s: (0, 0))],
         [pltpu.VMEM((tb * groups, 128), F32), pltpu.VMEM((tb * groups, 128), F32)],
@@ -615,7 +666,7 @@
         body, (count,), scal, [normed, de_part, dz, slope, w_z, decay, coef, omega, *more],
         [back_rows, back_rows, pl.BlockSpec((tb, zw), lambda i, s: (top - i, 0)), back_rows, whole((d, zw)),
          whole(par), whole(par), whole(small)]
-        + ([whole(par)] * 4 + [whole(small), pl.BlockSpec(memory_space=pl.ANY)] if before else []),
+        + ([whole(par)] * 4 + [whole(small), pl.BlockSpec(memory_space=pltpu.HBM)] if before else []),
         [sds((n, d), F32)] + [sds(par, F32)] * 4 + [sds(small, F32)],
         [back_rows, const, const, const, const, pl.BlockSpec(small, lambda i, s: (0, 0))],
         [pltpu.VMEM((tb * groups, 128), F32)] * 3,
@@ -709,7 +760,25 @@
     )
 
 
-def k_ffn(scal, lowered, cot, up, down, part, before=None):
+def split_rows(s, grad):
+    d, c = grad.shape
+    by_x = grad.reshape(4, 2, d // 8, c)
+    flip = s[12] == 0
+    a, b = by_x[:, 0].reshape(d // 2, c), by_x[:, 1].reshape(d // 2, c)
+    return jnp.where(flip, a, b), jnp.where(flip, b, a)
+
+
+def put_rows(s, ref, value, lead=(), add=None):
+    rows = value.shape[0] // 4
+    for z in range(4):
+        at = pl.ds(pl.multiple_of((s[13] ^ z) * rows, rows), rows)
+        part = value[z * rows : (z + 1) * rows]
+        if add is not None:
+            part = part + add[0][(*add[1], at, slice(None))].astype(F32)
+        ref[(*lead, at, slice(None))] = part.astype(BF)
+
+
+def k_ffn(scal, lowered, cot, up, down, part, before=None, form="sent"):
     n, d = lowered.shape
     pieces = len(up) > 1
     tn = up[0].shape[1] // 4
@@ -717,26 +786,19 @@
 
     def body(s, low_ref, c_ref, *refs):
         step = pl.program_id(0)
-        nu, nd = len(up), len(down)
-        ups, downs, refs = refs[:nu], refs[nu : nu + nd], refs[nu + nd :]
+        nu = len(up)
+        ups, wd, refs = refs[:nu], refs[nu], refs[nu + 1 :]
         if before:
             ins, refs = refs[:2], refs[2:]
             held, sems = refs[-2:]
             refs = refs[:-2]
             copies = [pltpu.make_async_copy(ins[i], held.at[i], sems.at[i]) for i in range(2)]
-        out_ref, gl_ref, dn, up_ref, acc, gl, u_scr = refs
+        out_ref, gl_ref, *grads, acc, gl, u_scr = refs
         if pieces:
             place(u_scr, s, ups)
             wu = u_scr
         else:
             wu = ups[0]
-
-        def split(ref, grad):
-            by_x = grad.reshape(4, 2, d // 8, tn)
-            flip = s[12] == 0
-            a, b = by_x[:, 0].reshape(rows, tn), by_x[:, 1].reshape(rows, tn)
-            ref[0] = jnp.where(flip, a, b).astype(BF)
-            ref[1] = jnp.where(flip, b, a).astype(BF)
 
         def work(wd, i):
             if before and i == 0:
@@ -758,32 +820,42 @@
                     back = back + held[1].astype(F32)
                 out_ref[...] = (acc[...] + out).astype(BF)
                 gl_ref[...] = (gl[...] + back).astype(BF)
-            split(dn, row_inner(c_ref[...], hid))
-            split(up_ref, row_inner(low_ref[...], du))
+            for k, grad in enumerate((row_inner(c_ref[...], hid), row_inner(low_ref[...], du))):
+                for j, rows_j in enumerate(split_rows(s, grad)):
+                    if form == "sent":
+                        put_rows(s, grads[0], rows_j, (k, j))
+                    elif form == "own" or k == 0:
+                        put_rows(s, grads[2 * k + j], rows_j)
+                    else:
+                        put_rows(s, grads[2], rows_j, (j,))
 
         for i in range(2):
 
             @pl.when(step == i)
             def _(i=i):
-                work(downs[i % nd], i)
-
-    first = 8 + 2 * part
+                work(wd, i)
+
     if pieces:
-        down = down[2 * part : 2 * part + 2]
-        specs = [pl.BlockSpec((d // 4, tn), lambda i, s: (0, s[first + i]))] * 4 + [whole((tn, d))] * 2
+        down = [down[part]]
+        specs = [pl.BlockSpec((d // 4, tn), lambda i, s: (0, s[4 + part] * 2 + i))] * 4
+        specs += [pl.BlockSpec((tn, d), lambda i, s: (i, 0))]
     else:
         specs = [
-            pl.BlockSpec((d, tn), lambda i, s: (0, s[first + i])),
-            pl.BlockSpec((tn, d), lambda i, s: (s[first + i], 0)),
+            pl.BlockSpec((d, tn), lambda i, s: (0, s[4 + part] * 2 + i)),
+            pl.BlockSpec((tn, d), lambda i, s: (s[4 + part] * 2 + i, 0)),
         ]
     still = pl.BlockSpec((n, d), lambda i, s: (0, 0))
-    grads = pl.BlockSpec((2, rows, tn), lambda i, s: (0, 0, s[first + i] % 2))
+    one = pl.BlockSpec((rows, tn), lambda i, s: (0, i))
+    two = pl.BlockSpec((2, rows, tn), lambda i, s: (0, 0, i))
+    four = pl.BlockSpec((2, 2, rows, tn), lambda i, s: (0, 0, 0, i))
+    grad_specs = dict(sent=[four], own=[one] * 4, other=[one, one, two])[form]
+    grad_shapes = [sds((*g.block_shape[:-1], 2 * tn)) for g in grad_specs]
     more = list(before) if before else []
     return run(
         body, (2,), scal, [lowered, cot, *up, *down, *more],
-        [whole((n, d)), whole((n, d))] + specs + [pl.BlockSpec(memory_space=pl.ANY)] * len(more),
-        [sds((n, d)), sds((n, d)), sds((2, rows, 2 * tn)), sds((2, rows, 2 * tn))],
-        [still, still, grads, grads],
+        [whole((n, d)), whole((n, d))] + specs + [pl.BlockSpec(memory_space=pltpu.HBM)] * len(more),
+        [sds((n, d)), sds((n, d)), *grad_shapes],
+        [still, still, *grad_specs],
         [pltpu.VMEM((n, d), F32), pltpu.VMEM((n, d), F32), pltpu.VMEM((d, tn), BF)]
         + ([pltpu.VMEM((2, n, d), BF), pltpu.SemaphoreType.DMA((2,))] if before else []),
         flops=24 * n * d * tn, name="ffn",
@@ -902,12 +974,14 @@
     )
 
 
-def k_input_back(scal, dv_own, dv_oth, w_own, packs, d_sig, tokens, direct):
+def k_input_back(scal, dv_own, dv_oth, w_own, packs, d_sig, tokens, direct, first, count, before=None):
     n, d = tokens.shape
     rp = packs[0].shape[0]
     half = dv_own.shape[1]
 
-    def body(s, vo, vt, wo, w0, w1, w2, w3, sg, x_ref, dir_ref, o_ref, w_scr):
+    def body(s, vo, vt, wo, w0, w1, w2, w3, sg, x_ref, dir_ref, *refs):
+        o_ref, w_scr = refs[-2:]
+
         @pl.when(pl.program_id(0) == 0)
         def _():
             place(w_scr, s, (w0, w1, w2, w3))
@@ -918,116 +992,100 @@
         n1 = x * r
         o_ref[...] = dir_ref[...].astype(F32) + r * (dn - n1 * jnp.mean(dn * n1, axis=-1, keepdims=True))
 
-    return run(
-        body, (n // ROWS,), scal, [dv_own, dv_oth, w_own, *packs, d_sig, tokens, direct],
-        [rows_of(half), rows_of(half), whole((d, half))] + [piece_whole(rp, half, 0)] * 4 + [rows_of(d)] * 3,
-        [sds((n, d), F32)], [rows_of(d)],
+    def at(cols):
+        return pl.BlockSpec((ROWS, cols), lambda i, s: (first + i, 0))
+
+    more = [before] if before is not None else []
+    return run(
+        body, (count,), scal, [dv_own, dv_oth, w_own, *packs, d_sig, tokens, direct, *more],
+        [at(half), at(half), whole((d, half))] + [piece_whole(rp, half, 0)] * 4 + [at(d)] * 3
+        + [pl.BlockSpec(memory_space=pltpu.HBM)] * len(more),
+        [sds((n, d), F32)], [at(d)],
         [pltpu.VMEM((d, half), BF)],
-        flops=4 * n * d * half, name="input_back",
+        flops=4 * ROWS * count * d * half, name="input_back", aliases={11: 0} if more else {},
     )[0]
 
 
-def split_rows(s, grad):
-    d, c = grad.shape
-    by_x = grad.reshape(4, 2, d // 8, c)
-    flip = s[12] == 0
-    a, b = by_x[:, 0].reshape(d // 2, c), by_x[:, 1].reshape(d // 2, c)
-    return jnp.where(flip, a, b), jnp.where(flip, b, a)
-
-
-def k_weight_mid(scal, ema_low, dh, df, gated_own, gated_oth, dg_own, dg_oth, part, got=None):
+def k_weight_mid(scal, ema_low, left, right_own, right_oth, gate, part, got=None):
     n, d = ema_low.shape
-    half = gated_own.shape[1] // 2
     tn = d // 4
     rows = d // 2
 
-    def body(s, e_ref, h_ref, f_ref, go, gt, do, dt, eo, et, *refs):
+    def body(s, *refs):
+        if gate:
+            e_ref, *refs = refs
+        l_ref, ro, rt, eo, et, *refs = refs
         for i in range(3):
 
             @pl.when(pl.program_id(0) == i)
             def _(i=i):
-                for k, (g, dg, e) in enumerate(((go, do, eo), (gt, dt, et))):
-                    a = row_inner(h_ref[...], g[...] if i < 2 else e[...])
-                    b = row_inner(e_ref[...], dg[...]) if i < 2 else row_inner(f_ref[...], e[...])
-                    a, b = split_rows(s, a), split_rows(s, b)
-                    if got is None:
-                        for j in range(2):
-                            refs[0][k, j] = a[j].astype(BF)
-                            refs[1][k, j] = b[j].astype(BF)
-                    else:
-                        a = [a[j] + refs[0][k, j].astype(F32) for j in range(2)]
-                        b = [b[j] + refs[1][k, j].astype(F32) for j in range(2)]
-                        refs[2][k] = a[1].astype(BF)
-                        refs[3][k] = a[0].astype(BF)
-                        for j in range(2):
-                            refs[4 + k][j] = b[j].astype(BF)
+                for k, (r, e) in enumerate(((ro, eo), (rt, et))):
+                    lhs = e_ref if gate and i < 2 else l_ref
+                    grad = split_rows(s, row_inner(lhs[...], r[...] if i < 2 else e[...]))
+                    for j in range(2):
+                        if got is None:
+                            put_rows(s, refs[0], grad[j], (k, j))
+                        elif gate:
+                            put_rows(s, refs[1 + k], grad[j], (j,), (refs[0], (k, j)))
+                        else:
+                            put_rows(s, refs[2 - j], grad[j], (k,), (refs[0], (k, j)))
 
     at = pl.BlockSpec((n, tn), lambda i, s: (0, s[part] * 2 + jnp.minimum(i, 1)))
     e_own = pl.BlockSpec((n, tn), lambda i, s: (0, s[6] * 2 + s[part]), pipeline_mode=pl.Buffered(1))
     e_oth = pl.BlockSpec((n, tn), lambda i, s: (0, s[7] * 2 + s[part]), pipeline_mode=pl.Buffered(1))
     four = pl.BlockSpec((2, 2, rows, tn), lambda i, s: (0, 0, 0, i))
     two = pl.BlockSpec((2, rows, tn), lambda i, s: (0, 0, i))
-    adds = list(got) if got is not None else []
-    return run(
-        body, (3,), scal, [ema_low, dh, df, gated_own, gated_oth, dg_own, dg_oth, ema_low, ema_low] + adds,
-        [whole((n, d))] * 3 + [at] * 4 + [e_own, e_oth] + [four] * len(adds),
-        [sds((2, rows, 3 * tn))] * 4 if adds else [sds((2, 2, rows, 3 * tn))] * 2,
-        [two] * 4 if adds else [four] * 2,
-        flops=2 * n * d * 6 * half, name="weight_mid",
-    )
-
-
-def k_weight_value(scal, normed, dv_own, dv_oth, part, got=None):
+    adds = [got] if got is not None else []
+    lead = [ema_low] if gate else []
+    return run(
+        body, (3,), scal, [*lead, left, right_own, right_oth, ema_low, ema_low] + adds,
+        [whole((n, d))] * (1 + len(lead)) + [at] * 2 + [e_own, e_oth] + [four] * len(adds),
+        [sds((2, rows, 3 * tn))] * 2 if adds else [sds((2, 2, rows, 3 * tn))],
+        [two] * 2 if adds else [four],
+        flops=2 * n * d * 6 * tn, name="weight_mid",
+    )
+
+
+def k_weight_value(scal, normed, dv_own, dv_oth, ema_low, dz, part, got=None):
     n, d = normed.shape
     tn = dv_own.shape[1] // 4
+    zw = dz.shape[1]
     rows = d // 2
 
-    def body(s, x_ref, vo, vt, *refs):
-        for i in range(2):
-
-            @pl.when(pl.program_id(0) == i)
-            def _(i=i):
-                for k, v in enumerate((vo, vt)):
-                    a = split_rows(s, row_inner(x_ref[...], v[...]))
-                    if got is None:
-                        for j in range(2):
-                            refs[0][k, j] = a[j].astype(BF)
-                    else:
-                        a = [a[j] + refs[0][k, j].astype(F32) for j in range(2)]
-                        if i == 0:
-                            refs[1][k] = a[1].astype(BF)
-                            refs[2][k] = a[0].astype(BF)
-                        else:
-                            for j in range(2):
-                                refs[3 + k][j] = a[j].astype(BF)
-
-    at = pl.BlockSpec((n, tn), lambda i, s: (0, s[part] * 2 + i))
-    four = pl.BlockSpec((2, 2, rows, tn), lambda i, s: (0, 0, 0, i))
-    still = pl.BlockSpec((2, rows, tn), lambda i, s: (0, 0, 0))
+    def body(s, x_ref, vo, vt, e_ref, z_ref, *refs):
+        for k, v in enumerate((vo, vt)):
+            grad = split_rows(s, row_inner(x_ref[...], v[...]))
+            for j in range(2):
+                if got is None:
+                    put_rows(s, refs[0].at[:, :, :, 0 : 2 * tn], grad[j], (k, j))
+                else:
+                    add = (refs[0].at[:, :, :, 0 : 2 * tn], (k, j))
+                    put_rows(s, refs[5], grad[j], (j,), add)
+                    whole_rows = refs[5][j]
+                    refs[2 - j][k] = whole_rows[:, 0:tn]
+                    refs[3 + k][j, :, 0:tn] = whole_rows[:, tn:]
+        grad = split_rows(s, row_inner(e_ref[...], z_ref[...]))
+        for j in range(2):
+            for k in range(2):
+                if got is None:
+                    put_rows(s, refs[0].at[:, :, :, 2 * tn :], grad[j], (k, j))
+                else:
+                    put_rows(s, refs[3 + k].at[:, :, tn:], grad[j], (j,), (refs[0].at[:, :, :, 2 * tn :], (k, j)))
+
+    at = pl.BlockSpec((n, 2 * tn), lambda i, s: (0, s[part]))
     adds = [got] if got is not None else []
-    return run(
-        body, (2,), scal, [normed, dv_own, dv_oth] + adds,
-        [whole((n, d)), at, at] + [four] * len(adds),
-        [sds((2, rows, tn))] * 4 if adds else [sds((2, 2, rows, 2 * tn))],
-        [still] * 4 if adds else [four],
-        flops=2 * n * d * 4 * tn, name="weight_value",
-    )
-
-
-def k_weight_z(scal, ema_low, dz):
-    n, d = ema_low.shape
-    zw = dz.shape[1]
-
-    def body(s, e_ref, z_ref, o_ref):
-        a = split_rows(s, row_inner(e_ref[...], z_ref[...]))
-        for j in range(2):
-            o_ref[j] = a[j].astype(BF)
-
-    return run(
-        body, (1,), scal, [ema_low, dz], [whole((n, d)), whole((n, zw))],
-        [sds((2, d // 2, zw))], [pl.BlockSpec((2, d // 2, zw), lambda i, s: (0, 0, 0))],
-        flops=2 * n * d * zw, name="weight_z",
-    )[0]
+    if adds:
+        shapes = [(2, rows, tn)] * 2 + [(2, rows, tn + zw)] * 2
+    else:
+        shapes = [(2, 2, rows, 2 * tn + zw)]
+    return run(
+        body, (1,), scal, [normed, dv_own, dv_oth, ema_low, dz] + adds,
+        [whole((n, d)), at, at, whole((n, d)), whole((n, zw))] + [whole(a.shape) for a in adds],
+        [sds(o) for o in shapes],
+        [pl.BlockSpec(o, lambda i, s, r=len(o): (0,) * r) for o in shapes],
+        [pltpu.VMEM((2, rows, 2 * tn), BF)] if adds else [],
+        flops=2 * n * d * (4 * tn + zw), name="weight_value",
+    )
 
 
 def swap(values, axis, bit, size):
@@ -1051,7 +1109,9 @@
     z_pos = me // 4
     kx = core * 2 + x_pos
     kz = core * 2 + z_pos % 2
-    scal = jnp.stack([kx, kx ^ 1, kx ^ 2, kx ^ 3, core, 1 - core, t, 1 - t, kz, kz ^ 1, kz ^ 2, kz ^ 3, x_pos])
+    scal = jnp.stack(
+        [kx, kx ^ 1, kx ^ 2, kx ^ 3, core, 1 - core, t, 1 - t, kz, kz ^ 1, kz ^ 2, kz ^ 3, x_pos, z_pos, 2 * core, 2 * core + 1]
+    )
 
     def held(values, *deps):
         return lax.optimization_barrier((values, deps))[0]
@@ -1075,32 +1135,36 @@
         rows = w.shape[0] // 4
         return lax.dynamic_slice_in_dim(w, k * rows, rows, 0)
 
-    own_params = jnp.concatenate(
-        [alpha_logit, delta_logit, ema_beta, ema_eta, ema_omega[:, None],
-         jnp.zeros((ema_omega.shape[0], 128 - 4 * H - 1), F32)], axis=1
+    piece_v = my_rows(w_v, kx)
+    pv = [over_tensor(piece_v)]
+    own_params = k_pack_params(
+        after(piece_v), [a.T for a in (alpha_logit, delta_logit, ema_beta, ema_eta)], ema_omega[None]
     )
     oth_params = over_tensor(own_params)
-    pv = [over_tensor(my_rows(w_v, kx))]
-    normed, v_own, vs_own = k_value_own(scal, tokens, w_v)
-    pg = [over_tensor(held(my_rows(w_gamma, kz), v_own))]
+    piece_g, piece_u, piece_h, piece_up, piece_dn = k_pieces(
+        after(own_params),
+        [[(w_gamma, 8)], [(u_h, 0)], [(w_h, 8), (w_phi, 8)], [(w_up, 0)], [(w_down, 14), (w_down, 15)]],
+    )
+    normed, v_own, vs_own = k_value_own(after(piece_g), tokens, w_v)
+    pg = [over_tensor(held(piece_g, v_own))]
     decay, coef, omega = k_ema_params(after(v_own), own_params, oth_params)
     blocks = n // 128
     ema_a = k_ema_forward(after(v_own), normed, decay, coef, omega, 0, blocks // 2)
     pv.append(over_x(held(pv[0], ema_a[0])))
-    pu = [over_tensor(held(my_rows(u_h, kx), ema_a[0]))]
+    pu = [over_tensor(held(piece_u, ema_a[0]))]
     ema_low, e_slope, state = k_ema_forward(
         after(ema_a[0]), normed, decay, coef, omega, blocks // 2, blocks // 2, (ema_a[2], ema_a[0], ema_a[1])
     )
     pg.append(over_z(held(pg[0], state)))
-    ph = [over_tensor(held(jnp.concatenate([my_rows(w_h, kz), my_rows(w_phi, kz)], axis=0), state))]
+    ph = [over_tensor(held(piece_h, state))]
     z_pre, query, key = k_query_key(scal, ema_low, w_z, qk_gain, qk_bias)
     pv += [over_core(v) for v in held((pv[0], pv[1]), query)]
     pu.append(over_x(held(pu[0], query)))
-    pup = [over_tensor(held(my_rows(w_up, kx), query))]
+    pup = [over_tensor(held(piece_up, query))]
     v_oth, vs_oth = k_act_other(after(query), normed, pv, 0, 512)
     pg += [over_core(v) for v in held((pg[0], pg[1]), v_oth)]
     ph.append(over_z(held(ph[0], v_oth)))
-    pdn = [over_tensor(held(my_rows(w_down, kz), v_oth))]
+    pdn = [over_tensor(held(piece_dn, v_oth))]
     gated_own, gated_oth, g_own, g_oth, m_own, m_oth, probs = k_attend(
         after(v_oth), query, key, v_own, v_oth, ema_low, w_gamma, pg
     )
@@ -1110,41 +1174,38 @@
     mixed, lowered, fac_h, fac_f, keep = k_gate(
         after(probs), gated_own, gated_oth, ema_low, tokens, u_h, w_h, w_phi, pu, ph
     )
-    acc, dl, *sent_o = k_ffn(after(mixed), lowered, cotangent, [w_up], [w_down], 1)
+    acc, dl, sent_o = k_ffn(after(mixed), lowered, cotangent, [w_up], [w_down], 1)
     pup += [over_core(v) for v in held((pup[0], pup[1]), acc)]
-    pdn.append(over_z(held(pdn[0], acc)))
-    dno_got, upo_got = [over_core(v) for v in sent_o]
-    acc, dl, dno, upo = k_ffn(after(acc), lowered, cotangent, [w_up], [w_down], 0, (acc, dl))
-    pdn += [over_core(v) for v in held((pdn[0], pdn[1]), acc)]
-
-    def add(*values):
+    got_o = over_core(sent_o)
+    acc, dl, dno, dno_x, upo, upo_x = k_ffn(
+        after(acc), lowered, cotangent, [w_up], [w_down], 0, (acc, dl), "own"
+    )
+    pdn.append(over_core(held(pdn[0], acc)))
+
+    def total(*values):
         value = values[0].astype(F32)
         for v in values[1:]:
             value = value + v.astype(F32)
-        return value.astype(BF)
-
-    def z_first(terms):
-        by_z = [v.reshape(2, 2, d // 8, v.shape[-1]) for v in terms]
-        send = add(*[pick(v, 1 - z_pos % 2, 1) for v in by_z])
-        return send, [pick(v, z_pos % 2, 1) for v in by_z]
-
-    def z_second(terms):
-        send = add(*[pick(v, 1 - z_pos // 2, 0) for v in terms])
-        return send, [pick(v, z_pos // 2, 0) for v in terms]
+        return value
+
+    def add(*values):
+        return total(*values).astype(BF)
+
+    def by_z(v):
+        return v.reshape(2, 2, d // 8, v.shape[-1])
+
+    def z_send(terms):
+        return add(*[by_z(v)[:, 1] for v in terms])
+
+    def z_keep(terms):
+        return [by_z(v)[:, 0] for v in terms]
 
     def over_z2(v):
         return swap(v, "dp", 8, dp_size)
 
-    def core_rows(terms):
-        by_core = [v.reshape(2, d // 16, v.shape[-1]) for v in terms]
-        send = add(*[pick(v, 1 - core, 0) for v in by_core])
-        return send, [pick(v, core, 0) for v in by_core]
-
-    def total(terms):
-        value = terms[0].astype(F32)
-        for v in terms[1:]:
-            value = value + v.astype(F32)
-        return value
+    def core_split(value):
+        rows = value.reshape(2, d // 16, value.shape[-1])
+        return pick(rows, 1 - core, 0).astype(BF), pick(rows, core, 0)
 
     def joined(kept, got):
         kept, got = kept.astype(F32), got.astype(F32)
@@ -1152,48 +1213,51 @@
             core == 0, jnp.concatenate([kept, got], axis=1), jnp.concatenate([got, kept], axis=1)
         )
 
-    dn_x1 = add(dno[1], dno_got[1])
+    dn_x1 = add(dno_x, got_o[0, 1])
     dn_got_x1 = over_x(dn_x1)
-    acc, dl, *sent_t = k_ffn(after(acc, dn_x1), lowered, cotangent, pup, pdn, 1, (acc, dl))
-    dnt_got, upt_got = [over_core(v) for v in sent_t]
-    acc, dl, dnt, upt = k_ffn(after(acc), lowered, cotangent, pup, pdn, 0, (acc, dl))
-    dn_x2 = add(dnt[1], dnt_got[1])
-    up_y1 = add(upt, upt_got)
+    acc, dl, sent_t = k_ffn(after(acc, dn_x1), lowered, cotangent, pup, pdn, 1, (acc, dl))
+    got_t = over_core(sent_t)
+    acc, dl, dnt, dnt_x, upt = k_ffn(after(acc), lowered, cotangent, pup, pdn, 0, (acc, dl), "other")
+    dn_x2 = add(dnt_x, got_t[0, 1])
+    up_y1 = add(upt, got_t[1])
     dn_got_x2 = over_x(dn_x2)
     up_got_y = over_tensor(up_y1)
     output, dh, df, direct, da_own, da_oth, dg_own, dg_oth, de_part = k_mid_back(
-        after(acc, dn_x2, up_y1), dl, acc, cotangent, mixed, fac_h, fac_f, keep,
+        after(acc, dn_x2, up_y1, dn_got_x1), dl, acc, cotangent, mixed, fac_h, fac_f, keep,
         g_own, g_oth, m_own, m_oth, u_h, w_gamma, w_h, w_phi, pg, pu, ph,
     )
-    dn_got_x2 = held(dn_got_x2, dh)
-    dn_y = add(dnt[0], dnt_got[0], dn_got_x2)
-    dn_got_y = over_tensor(dn_y)
-    mid_sent = k_weight_mid(after(dh, dn_y), ema_low, dh, df, gated_own, gated_oth, dg_own, dg_oth, 5)
-    mid_got = [over_core(v) for v in mid_sent]
+    dn_y = {}
+
+    def start_dn(place, dep):
+        if opt["dn"] == place:
+            dn_y[0] = add(dnt, got_t[0, 0], held(dn_got_x2, dep))
+            dn_y[1] = over_tensor(dn_y[0])
+            return (dn_y[0],)
+        return ()
+
+    ma_sent = k_weight_mid(after(dh, *start_dn(0, dh)), ema_low, dh, gated_own, gated_oth, False, 5)[0]
+    ma_got = over_core(ma_sent)
+    mb_sent = k_weight_mid(after(ma_sent, *start_dn(1, ma_sent)), ema_low, df, dg_own, dg_oth, True, 5)[0]
+    mb_got = over_core(mb_sent)
     dv_own, dv_oth, dz, stats = k_attend_back(
-        after(*mid_sent), probs, da_own, da_oth, v_own, v_oth, vs_own, vs_oth, query, key, z_pre, qk_gain
+        after(mb_sent, *start_dn(2, mb_sent)), probs, da_own, da_oth, v_own, v_oth, vs_own, vs_oth, query, key, z_pre, qk_gain
     )
     up_got_y = held(up_got_y, dv_own)
-    up_x = add(upo[1], upo_got[1], up_got_y[1])
+    up_x = add(upo_x, got_o[1, 1], up_got_y[1])
     up_got_x = over_x(up_x)
-    val_sent = k_weight_value(after(dv_own, up_x), normed, dv_own, dv_oth, 5)[0]
+    val_sent = k_weight_value(after(dv_own, up_x), normed, dv_own, dv_oth, ema_low, dz, 5)[0]
     val_got = over_core(val_sent)
-    ma_theirs, ma_mine, mb_own, mb_oth = k_weight_mid(
-        after(val_sent), ema_low, dh, df, gated_own, gated_oth, dg_own, dg_oth, 4, mid_got
-    )
+    ma_theirs, ma_mine = k_weight_mid(after(val_sent), ema_low, dh, gated_own, gated_oth, False, 4, ma_got)
     ma_got_x = over_x(ma_theirs)
+    mb_own, mb_oth = k_weight_mid(after(ma_theirs), ema_low, df, dg_own, dg_oth, True, 4, mb_got)
     mb_got_y = over_tensor(mb_oth)
-    z_own = k_weight_z(after(ma_theirs), ema_low, dz)
-    z_got = over_core(z_own)
-    va_theirs, va_mine, vb_own, vb_oth = k_weight_value(after(z_own), normed, dv_own, dv_oth, 4, val_got)
-    va_got_x = over_x(va_theirs)
-    vb_got_y = over_tensor(vb_oth)
-    dn_got_y, up_got_x = held((dn_got_y, up_got_x), va_theirs)
-    dn_z, dn_terms = z_first([dno[0], dno_got[0], dn_got_x1, dn_got_y])
-    up_z, up_terms = z_first([upo[0], upo_got[0], up_got_y[0], up_got_x])
-    dn_got_z, up_got_z = over_z(dn_z), over_z(up_z)
-    z_sum = add(z_own, z_got)
-    z_got_y = over_tensor(z_sum)
+    dn_got_y = dn_y[1]
+    up_got_x, dn_got_y = held((up_got_x, dn_got_y), mb_own)
+    dn_terms = [dno, got_o[0, 0], dn_got_x1, dn_got_y]
+    up_terms = [upo, got_o[1, 0], up_got_y[0], up_got_x]
+    ffn_z = jnp.stack([z_send(dn_terms), z_send(up_terms)])
+    dn_terms, up_terms = z_keep(dn_terms), z_keep(up_terms)
+    ffn_got_z = over_z(ffn_z)
     quarter = blocks // 4
 
     def ema_back(dep, first, count, before=None):
@@ -1201,68 +1265,102 @@
             after(*dep), normed, de_part, dz, e_slope, w_z, decay, coef, omega, first, count, before
         )
 
-    eb = ema_back((va_theirs, dn_z, up_z, z_sum), 0, quarter)
-    ma_got_x, mb_got_y = held((ma_got_x, mb_got_y), eb[1])
-    ma_y = add(ma_mine[1], ma_got_x[1])
-    mb_x = add(mb_own[1], mb_got_y[1])
-    ma_got_y = over_tensor(ma_y)
-    mb_got_x = over_x(mb_x)
-    eb = ema_back((eb[1], ma_y, mb_x), quarter, quarter, eb)
-    dn_got_z, up_got_z, va_got_x, vb_got_y, z_got_y = held((dn_got_z, up_got_z, va_got_x, vb_got_y, z_got_y), eb[1])
-    dn_z2, dn_terms = z_second([*dn_terms, dn_got_z])
-    up_z2, up_terms = z_second([*up_terms, up_got_z])
-    va_y = add(va_mine[1], va_got_x[1])
-    zs = add(z_sum, z_got_y)
-    vb_x = jnp.concatenate([add(vb_own[1], vb_got_y[1]), zs[1]], axis=-1)
-    dn_got_z2, up_got_z2 = over_z2(dn_z2), over_z2(up_z2)
-    va_got_y = over_tensor(va_y)
-    vb_got_x = over_x(vb_x)
-    eb = ema_back((eb[1], dn_z2, up_z2, va_y, vb_x), 2 * quarter, quarter, eb)
-    ma_got_y, mb_got_x = held((ma_got_y, mb_got_x), eb[1])
-    ma_z, ma_terms = z_first([ma_mine[0], ma_got_x[0], ma_got_y])
-    mb_z, mb_terms = z_first([mb_own[0], mb_got_y[0], mb_got_x])
-    ma_got_z, mb_got_z = over_z(ma_z), over_z(mb_z)
-    eb = ema_back((eb[1], ma_z, mb_z), 3 * quarter, quarter, eb)
+    eb = ema_back((mb_own, ffn_z), 0, quarter)
+    va_theirs, va_mine, vb_own, vb_oth = k_weight_value(
+        after(eb[1]), normed, dv_own, dv_oth, ema_low, dz, 4, val_got
+    )
+    va_got_x = over_x(va_theirs)
+    vb_got_y = over_tensor(vb_oth)
+    eb = ema_back((va_theirs,), quarter, quarter, eb)
+    done = {}
+
+    def second(place, dep):
+        forced = []
+        if opt["m2"] == place:
+            gx, gy = held((ma_got_x, mb_got_y), dep)
+            ma_y, mb_x = add(ma_mine[1], gx[1]), add(mb_own[1], gy[1])
+            done["m"] = (gx, gy, over_tensor(ma_y), over_x(mb_x))
+            forced += [ma_y, mb_x]
+        if opt.get("z2", opt["m2"]) == place:
+            gz = held(ffn_got_z, dep)
+            done["z"] = [*dn_terms, gz[0]], [*up_terms, gz[1]]
+            ffn_z2 = jnp.stack([add(*[v[1] for v in ts]) for ts in done["z"]])
+            done["z2"] = over_z2(ffn_z2)
+            forced.append(ffn_z2)
+        if opt["v2"] == place:
+            gx, gy = held((va_got_x, vb_got_y), dep)
+            va_y, vb_x = add(va_mine[1], gx[1]), add(vb_own[1], gy[1])
+            done["v"] = (gx, gy, over_tensor(va_y), over_x(vb_x))
+            forced += [va_y, vb_x]
+        if opt.get("z1m", 6) == place:
+            gy, gx = held((done["m"][2], done["m"][3]), dep)
+            a_terms = [ma_mine[0], done["m"][0][0], gy]
+            b_terms = [mb_own[0], done["m"][1][0], gx]
+            mid_z = jnp.stack([z_send(a_terms), z_send(b_terms)])
+            done["mz"] = (z_keep(a_terms), z_keep(b_terms), over_z(mid_z))
+            forced.append(mid_z)
+        if opt.get("z1v", 6) == place:
+            gy, gx = held((done["v"][2], done["v"][3]), dep)
+            a_terms = [va_mine[0], done["v"][0][0], gy]
+            b_terms = [vb_own[0], done["v"][1][0], gx]
+            val_z = jnp.concatenate([z_send(a_terms), z_send(b_terms)], axis=-1)
+            done["vz"] = (z_keep(a_terms), z_keep(b_terms), over_z(val_z))
+            forced.append(val_z)
+        return forced
+
+    f2 = second(2, eb[1])
+    eb = ema_back((eb[1], *f2), 2 * quarter, quarter, eb)
+    f3 = second(3, eb[1])
+    eb = ema_back((eb[1], *f3), 3 * quarter, quarter, eb)
     d_sig, _, _, sum_a, sum_b, sum_w = eb
+    f4 = second(4, sum_a)
     sums = jnp.concatenate([sum_a, sum_b, sum_w, stats], axis=0)
-    sums_got = over_core(sums)
-    va_got_y, vb_got_x = held((va_got_y, vb_got_x), sum_a)
+    others = over_core(sums)
+    halves = n // ROWS // 2
+    part = k_input_back(
+        after(sum_a, sums, *f4), dv_own, dv_oth, w_v, pv, d_sig, tokens, direct, 0, halves
+    )
+    f5 = second(5, part)
+    sums = sums + held(others, part)
+    others = over_tensor(sums)
+    input_grad = k_input_back(
+        after(part, sums, *f5), dv_own, dv_oth, w_v, pv, d_sig, tokens, direct, halves, halves, part
+    )
+    second(6, input_grad)
+    sums = sums + held(others, input_grad)
+    sums = sums + over_x(sums)
+    sums = sums + over_z(sums)
+    sums = sums + over_z2(sums)
     c = va_mine.shape[-1]
-    vb_terms = [jnp.concatenate([vb_own[0], zs[0]], axis=-1), jnp.pad(vb_got_y[0], ((0, 0), (0, zs.shape[-1]))), vb_got_x]
-    val_z, val_terms = z_first([
-        jnp.concatenate([add(va_mine[0], va_got_x[0], va_got_y), add(*vb_terms)], axis=-1)
-    ])
-    val_got_z = over_z(val_z)
-    input_grad = k_input_back(
-        after(sum_a, val_z, sums), dv_own, dv_oth, w_v, pv, d_sig, tokens, direct
-    )
-    ma_got_z, mb_got_z, val_got_z, sums_got = held((ma_got_z, mb_got_z, val_got_z, sums_got), input_grad)
-    sums = sums + sums_got
-    sums_got = over_tensor(sums)
-    mid_z2, mid_terms = z_second([
-        jnp.concatenate([add(*ma_terms, ma_got_z), add(*mb_terms, mb_got_z)], axis=-1)
-    ])
+    dn_terms, up_terms = done["z"]
+    ffn_got_z2 = done["z2"]
+    ma_terms, mb_terms, mid_got_z = done["mz"]
+    va_terms, vb_terms, val_got_z = done["vz"]
+    ma_terms, mb_terms = [*ma_terms, mid_got_z[0]], [*mb_terms, mid_got_z[1]]
+    mid_z2 = jnp.stack([add(*[v[1] for v in ma_terms]), add(*[v[1] for v in mb_terms])])
     mid_got_z2 = over_z2(mid_z2)
-    val_z2, val_terms = z_second([*val_terms, val_got_z])
+    va_terms, vb_terms = [*va_terms, val_got_z[..., :c]], [*vb_terms, val_got_z[..., c:]]
+    val_z2 = jnp.concatenate([add(*[v[1] for v in ts]) for ts in (va_terms, vb_terms)], axis=-1)
     val_got_z2 = over_z2(val_z2)
-    sums = sums + sums_got
-    others = [over_x(sums), over_z(sums), lax.ppermute(sums, "dp", [(i, i ^ 6) for i in range(dp_size)])]
-    sums = sums + others[0] + others[1] + others[2]
-    sums = sums + over_z2(sums)
-
-    def finish(terms):
-        send, terms = core_rows(terms)
-        return total(terms), over_core(send)
-
-    down_t = joined(*finish([*dn_terms, dn_got_z2]))
-    up = joined(*finish([*up_terms, up_got_z2]))
-    mid_kept, mid_got = finish([*mid_terms, mid_got_z2])
+
+    def last(terms):
+        return total(*[v[0] for v in terms])
+
+    ffn_total = jnp.stack([total(last(dn_terms), ffn_got_z2[0]), total(last(up_terms), ffn_got_z2[1])])
+    ffn_rows = ffn_total.reshape(2, 2, d // 16, -1)
+    ffn_got = over_core(pick(ffn_rows, 1 - core, 1).astype(BF))
+    ffn_kept = pick(ffn_rows, core, 1)
+    mid_total = jnp.stack([total(last(ma_terms), mid_got_z2[0]), total(last(mb_terms), mid_got_z2[1])])
+    mid_rows = mid_total.reshape(2, 2, d // 16, -1)
+    mid_got = over_core(pick(mid_rows, 1 - core, 1).astype(BF))
+    mid_kept = pick(mid_rows, core, 1)
+    val_total = jnp.concatenate([last(va_terms), last(vb_terms)], axis=-1) + val_got_z2.astype(F32)
+    val_sent, val_kept = core_split(val_total)
+    val_got = over_core(val_sent)
+    down_t, up = joined(ffn_kept[0], ffn_got[0]), joined(ffn_kept[1], ffn_got[1])
     tn = d // 4
-    uh_t, wh_t, gamma, phi_t = (
-        joined(mid_kept[:, lo * tn : hi * tn], mid_got[:, lo * tn : hi * tn])
-        for lo, hi in ((0, 2), (2, 3), (3, 5), (5, 6))
-    )
-    val_kept, val_got = finish([*val_terms, val_got_z2])
+    uh_t, gamma = (joined(mid_kept[i][:, : 2 * tn], mid_got[i][:, : 2 * tn]) for i in range(2))
+    wh_t, phi_t = (joined(mid_kept[i][:, 2 * tn :], mid_got[i][:, 2 * tn :]) for i in range(2))
     value = joined(val_kept[:, : 2 * c], val_got[:, : 2 * c])
     z_grad = val_kept[:, 2 * c :]
     gh = sum_a.shape[0]

time: 511 us -> 477 us (0.933)
  Pallas kernels: 300 us -> 270 us
  starting transfers between devices: 58.9 us -> 48.6 us
  other arithmetic: 33.1 us -> 38.7 us
    pallas_call x24 -> x28, Pallas kernels: 300 us -> 270 us  [run(): pl.pallas_call(body, out_shape=out_shape, grid_spec=pltpu.PrefetchScalarG...]
    unnamed x147 -> x227, local copies, waits for them, and re-layouts: 12.2 us -> 26.9 us
    dynamic_slice x12 -> x0, local copies, waits for them, and re-layouts: 11.4 us -> none  [pick(): return lax.dynamic_index_in_dim(values, index, axis, keepdims=False)]
    ppermute x65 -> x55, starting transfers between devices: 58.9 us -> 48.6 us  [swap(): return lax.ppermute(values, axis, [(i, i ^ bit) for i in range(size)])]
    dynamic_slice x6 -> x1, local copies, waits for them, and re-layouts: 9.46 us -> 1.08 us  [my_rows(): return lax.dynamic_slice_in_dim(w, k * rows, rows, 0)]
    add x3 -> x5, other arithmetic: 0.6 us -> 7.53 us  [total(): value = value + v.astype(F32)]
    slice x11 -> x14, local copies, waits for them, and re-layouts: 6.17 us -> 12.3 us  [the longest x1 3.14 us: one_sequence(): dn_terms = [dno, got_o[0, 0], dn_got_x1, dn_got_y]]
    ppermute x65 -> x55, waiting for transfers between devices: 61.7 us -> 65 us  [swap(): return lax.ppermute(values, axis, [(i, i ^ bit) for i in range(size)])]
  transfers between devices with their start and end apart: 66 -> 55, of which waited for: 15 -> 14; matrix products, arithmetic and copies ran while one was open for 12% -> 11% of each run, Pallas kernels for 60% -> 57%
where the time goes in v5:
time: 477 us; the launch traced here: 470 us
  Pallas kernels  270 us (57%)
  waiting for transfers between devices  65 us (14%)
  starting transfers between devices  48.6 us (10%)
  local copies, waits for them, and re-layouts  45.7 us (10%)
  other arithmetic  38.7 us (8%)
    pallas_call x28, Pallas kernels, run(): pl.pallas_call(body, out_shape=out_shape, grid_spec=pltpu.PrefetchScalarG...  270 us
    ppermute x55, waiting for transfers between devices, swap(): return lax.ppermute(values, axis, [(i, i ^ bit) for i in range(size)])  65 us
    ppermute x55, starting transfers between devices, swap(): return lax.ppermute(values, axis, [(i, i ^ bit) for i in range(size)])  48.6 us
    unnamed x227, local copies, waits for them, and re-layouts  26.9 us
    convert_element_type x16, other arithmetic, add(): return total(*values).astype(BF)  22 us
  transfers between devices with their start and end apart: 55, of which 14 were waited for; matrix products, arithmetic and copies ran while one was open for 11% of the time, Pallas kernels for 57%

profile of v5, /device:TPU:0, one launch (start us, length us, event | category | flops | bytes accessed | tf_op | source)
XLA Modules:
  0.0 470.5 jit_solution(16552294803450408946)
XLA Ops:
  1.8 3.0 collective-permute-start.1
  5.5 2.1 pack_params.1.own_ref
  7.8 5.7 %pieces.1 = (bf16[256,1024]{1,0:T(8,128)(2,1)}, bf16[256,1024]{1,0:T(8,128)(2,1)}, bf16[256,1024]{1,0:T(8,128)(2,1)}, bf16[256,2048]{1,0:T(8,128)(2,1)}, bf16[1024,1024]{1,0:T(8,128)(2,1)}) custom-call(s32[16]{0:T(128)} %stack.105.s, bf16[1024,1024]{1,0:T(8,128)(2,1)} %wo.5, bf16[1024,1024]{1,0:T(8,128)(2,1)} %uo.3, bf16[512,1024]{1,0:T(8,128)(2,1)} %ho.3, ...), custom_call_target="tpu_custom_call" | custom-call | flops 100000000 | bytes 235929600 | tf_op jit(solution)/shard_map/pieces/pallas_call | solution.py:351
  13.5 5.2 %value_own.1 = (bf16[1024,1024]{1,0:T(8,128)(2,1)S(1)}, bf16[1024,1024]{1,0:T(8,128)(2,1)S(1)}, bf16[1024,1024]{1,0:T(8,128)(2,1)S(1)}) custom-call(s32[16]{0:T(128)S(1)} %copy-done.6, bf16[1024,1024]{1,0:T(8,128)(2,1)S(1)} %copy-done.9, bf16[1024,1024]{1,0:T(8,128)(2,1)S(1)} %copy-done.4), custom_call_target="tpu_custom_call" | custom-call | flops 21474836480 | bytes 104857600 | tf_op jit(solution)/shard_map/value_own/pallas_call | solution.py:351
  23.6 2.4 ema_params.1
  28.4 6.8 %ema_forward.2 = (bf16[1024,1024]{1,0:T(8,128)(2,1)S(1)}, bf16[1024,1024]{1,0:T(8,128)(2,1)S(1)}, f32[128,128]{1,0:T(8,128)S(1)}) custom-call(s32[16]{0:T(128)S(1)} %copy-done.7, bf16[1024,1024]{1,0:T(8,128)(2,1)S(1)} %get-tuple-element.179.x_ref, f32[128,128]{1,0:T(8,128)S(1)} %copy-done.26, f32[128,128]{1,0:T(8,128)S(1)} %copy-done.29, f32[8,128]{1,0:T(8,128)S(1)} %copy-done.51), custom_call_target="tpu_custom_call" | custom-call | flops 99999997952 | bytes 64921600 | tf_op jit(solution)/shard_map/ema_forward/pallas_call | solution.py:351
  36.8 7.2 %ema_forward.3 = (bf16[1024,1024]{1,0:T(8,128)(2,1)S(1)}, bf16[1024,1024]{1,0:T(8,128)(2,1)S(1)}, f32[128,128]{1,0:T(8,128)}) custom-call(s32[16]{0:T(128)S(1)} %copy-done.7, bf16[1024,1024]{1,0:T(8,128)(2,1)S(1)} %get-tuple-element.179.x_ref, f32[128,128]{1,0:T(8,128)S(1)} %copy-done.27, ...), custom_call_target="tpu_custom_call", output_to_operand_aliasing={{0}: (6, {}), {1}: (7, {})} | custom-call | flops 99999997952 | bytes 107520000 | tf_op jit(solution)/shard_map/ema_forward/pallas_call | solution.py:351
  52.2 4.8 %act_other.1 = (bf16[1024,1024]{1,0:T(8,128)(2,1)S(1)}, bf16[1024,1024]{1,0:T(8,128)(2,1)S(1)}) custom-call(s32[16]{0:T(128)S(1)} %copy-done.7, bf16[1024,1024]{1,0:T(8,128)(2,1)S(1)} %get-tuple-element.179.x_ref, bf16[256,1024]{1,0:T(8,128)(2,1)S(1)} %collective-permute-done.1.p0.w0, bf16[256,1024]{1,0:T(8,128)(2,1)S(1)} %collective-permute-done.2.p1.w1, ...), custom_call_target="tpu_custom_call" | custom-call | flops 21474836480 | bytes 83886080 | tf_op jit(solution)/shard_map/act_other/pallas_call | solution.py:351
  59.8 4.3 collective-permute-done.6.w1
  67.1 7.5 %collective-permute-done.13.h0.f0 = bf16[256,1024]{1,0:T(8,128)(2,1)S(1)} collective-permute-done((bf16[256,1024]{1,0:T(8,128)(2,1)S(1)}, bf16[256,1024]{1,0:T(8,128)(2,1)S(1)}, u32[]{:S(2)}, u32[]{:S(2)}) %collective-permute-start.13) | collective-permute-done | bytes 524320 | tf_op jit(solution)/shard_map/ppermute | solution.py:1092
  77.2 16.7 %attend.1 = (bf16[1024,1024]{1,0:T(8,128)(2,1)}, bf16[1024,1024]{1,0:T(8,128)(2,1)}, bf16[1024,1024]{1,0:T(8,128)(2,1)}, bf16[1024,1024]{1,0:T(8,128)(2,1)}, bf1...) custom-call(s32[16]{0:T(128)} %stack.105.s, bf16[1024,128]{1,0:T(8,128)(2,1)} %copy-done.31, ...), custom_call_target="tpu_custom_call" | custom-call | flops 71470940160 | bytes 256901120 | tf_op jit(solution)/shard_map/attend/pallas_call | solution.py:351
  99.8 18.8 %gate.1 = (bf16[1024,1024]{1,0:T(8,128)(2,1)}, bf16[1024,1024]{1,0:T(8,128)(2,1)}, bf16[1024,1024]{1,0:T(8,128)(2,1)}, bf16[1024,1024]{1,0:T(8,128)(2,1)}, bf16[1024,1024]{1,0:T(8,128)(2,1)}) custom-call(s32[16]{0:T(128)} %stack.105.s, bf16[1024,1024]{1,0:T(8,128)(2,1)} %get-tuple-element.203.go.refs_1_, bf16[1024,1024]{1,0:T(8,128)(2,1)} %get-tuple-element.204.gt.refs_2_, ...), custom_call_target="tpu_custom_call" | custom-call | flops 85899345920 | bytes 293601280 | tf_op jit(solution)/shard_map/gate/pallas_call | solution.py:351
  118.6 20.3 %ffn.4 = (bf16[1024,1024]{1,0:T(8,128)(2,1)}, bf16[1024,1024]{1,0:T(8,128)(2,1)}, bf16[2,2,512,1024]{3,2,1,0:T(8,128)(2,1)}) custom-call(s32[16]{0:T(128)} %stack.105.s, bf16[1024,1024]{1,0:T(8,128)(2,1)} %get-tuple-element.217.low_ref, bf16[1024,1024]{1,0:T(8,128)(2,1)} %c_ref.9, bf16[1024,2048]{1,0:T(8,128)(2,1)} %refs_0_.5, bf16[2048,1024]{1,0:T(8,128)(2,1)} %refs_1_.5), custom_call_target="tpu_custom_call" | custom-call | flops 128849018880 | bytes 209715200 | tf_op jit(solution)/shard_map/ffn/pallas_call | solution.py:351
  139.0 20.8 %ffn.5 = (bf16[1024,1024]{1,0:T(8,128)(2,1)}, bf16[1024,1024]{1,0:T(8,128)(2,1)}, bf16[512,1024]{1,0:T(8,128)(2,1)}, bf16[512,1024]{1,0:T(8,128)(2,1)}, bf16[512...) custom-call(s32[16]{0:T(128)} %stack.105.s, bf16[1024,1024]{1,0:T(8,128)(2,1)} %get-tuple-element.217.low_ref, ...), custom_call_target="tpu_custom_call" | custom-call | flops 128849018880 | bytes 251658240 | tf_op jit(solution)/shard_map/ffn/pallas_call | solution.py:351
  160.9 3.0 fusion.5
  168.8 21.2 %ffn.6 = (bf16[1024,1024]{1,0:T(8,128)(2,1)}, bf16[1024,1024]{1,0:T(8,128)(2,1)}, bf16[2,2,512,1024]{3,2,1,0:T(8,128)(2,1)}) custom-call(s32[16]{0:T(128)} %stack.105.s, bf16[1024,1024]{1,0:T(8,128)(2,1)} %get-tuple-element.217.low_ref, bf16[1024,1024]{1,0:T(8,128)(2,1)} %c_ref.9, bf16[256,2048]{1,0:T(8,128)(2,1)} %collective-permute-done.18.refs_0_, ...), custom_call_target="tpu_custom_call" | custom-call | flops 128849018880 | bytes 230686720 | tf_op jit(solution)/shard_map/ffn/pallas_call | solution.py:351
  190.4 21.1 %ffn.7 = (bf16[1024,1024]{1,0:T(8,128)(2,1)}, bf16[1024,1024]{1,0:T(8,128)(2,1)}, bf16[512,1024]{1,0:T(8,128)(2,1)}, bf16[512,1024]{1,0:T(8,128)(2,1)}, bf16[2,512,1024]{2,1,0:T(8,128)(2,1)}) custom-call(s32[16]{0:T(128)} %stack.105.s, bf16[1024,1024]{1,0:T(8,128)(2,1)} %get-tuple-element.217.low_ref, bf16[1024,1024]{1,0:T(8,128)(2,1)} %c_ref.9, ...), custom_call_target="tpu_custom_call" | custom-call | flops 128849018880 | bytes 230686720 | tf_op jit(solution)/shard_map/ffn/pallas_call | solution.py:351
  211.5 3.1 fusion.38
  215.8 2.0 copy-done.83
  217.8 2.3 fusion
  221.2 27.0 %mid_back.1 = (bf16[1024,1024]{1,0:T(8,128)(2,1)}, bf16[1024,1024]{1,0:T(8,128)(2,1)}, bf16[1024,1024]{1,0:T(8,128)(2,1)}, bf16[1024,1024]{1,0:T(8,128)(2,1)}, b...) custom-call(s32[16]{0:T(128)} %stack.105.s, ...), custom_call_target="tpu_custom_call" | custom-call | flops 128849018880 | bytes 566231040 | tf_op jit(solution)/shard_map/mid_back/pallas_call | solution.py:351
  248.3 3.3 fusion.3
  254.8 5.5 %weight_mid.4 = bf16[2,2,512,768]{3,2,1,0:T(8,128)(2,1)S(1)} custom-call(s32[16]{0:T(128)S(1)} %copy-done.8, bf16[1024,1024]{1,0:T(8,128)(2,1)S(1)} %copy-done.64, bf16[1024,1024]{1,0:T(8,128)(2,1)S(1)} %copy-done.60, bf16[1024,1024]{1,0:T(8,128)(2,1)S(1)} %copy-done.62, bf16[1024,1024]{1,0:T(8,128)(2,1)S(1)} %copy-done.25, bf16[1024,1024]{1,0:T(8,128)(2,1)S(1)} %copy-done.25), custom_call_target="tpu_custom_call" | custom-call | flops 32212254720 | bytes 136314880 | tf_op jit(solution)/shard_map/weight_mid/pallas_call | solution.py:351
  260.4 5.9 %weight_mid.5 = bf16[2,2,512,768]{3,2,1,0:T(8,128)(2,1)S(1)} custom-call(s32[16]{0:T(128)S(1)} %copy-done.8, bf16[1024,1024]{1,0:T(8,128)(2,1)S(1)} %copy-done.25, bf16[1024,1024]{1,0:T(8,128)(2,1)S(1)} %copy-done.54, bf16[1024,1024]{1,0:T(8,128)(2,1)S(1)} %copy-done.56, bf16[1024,1024]{1,0:T(8,128)(2,1)S(1)} %copy-done.58, ...), custom_call_target="tpu_custom_call" | custom-call | flops 32212254720 | bytes 157286400 | tf_op jit(solution)/shard_map/weight_mid/pallas_call | solution.py:351
  269.5 9.6 %attend_back.1 = (bf16[1024,1024]{1,0:T(8,128)(2,1)S(1)}, bf16[1024,1024]{1,0:T(8,128)(2,1)S(1)}, bf16[1024,128]{1,0:T(8,128)(2,1)S(1)}, f32[8,128]{1,0:T(8,128)S(1)}) custom-call(s32[16]{0:T(128)S(1)} %copy-done.8, bf16[1024,1024]{1,0:T(8,128)(2,1)S(1)} %copy-done.66, bf16[1024,1024]{1,0:T(8,128)(2,1)S(1)} %copy-done.67, bf16[1024,1024]{1,0:T(8,128)(2,1)S(1)} %copy-done.68, ...), custom_call_target="tpu_custom_call" | custom-call | flops 53687091200 | bytes 201902080 | tf_op jit(solution)/shard_map/attend_back/pallas_call | solution.py:351
  279.2 5.1 %fusion.1 = bf16[512,1024]{1,0:T(8,128)(2,1)} fusion(bf16[512,1024]{1,0:T(8,128)(2,1)} %get-tuple-element.266, bf16[2,2,512,1024]{3,2,1,0:T(8,128)(2,1)} %collective-permute-done.17, bf16[2,512,1024]{2,1,0:T(8,128)(2,1)} %collective-permute-done.27), kind=kLoop, calls=%fused_computation.4 | loop fusion | flops 3145728 | bytes 4194304 | tf_op jit(solution)/shard_map/convert_element_type | solution.py:1192
  285.0 5.2 %weight_value.2 = bf16[2,2,512,640]{3,2,1,0:T(8,128)(2,1)} custom-call(s32[16]{0:T(128)S(1)} %copy-done.8, bf16[1024,1024]{1,0:T(8,128)(2,1)S(1)} %copy-done.41, bf16[1024,1024]{1,0:T(8,128)(2,1)S(1)} %get-tuple-element.265.vo, bf16[1024,1024]{1,0:T(8,128)(2,1)S(1)} %get-tuple-element.269.vt, bf16[1024,1024]{1,0:T(8,128)(2,1)S(1)} %copy-done.25, ...), custom_call_target="tpu_custom_call" | custom-call | flops 24159191040 | bytes 112721920 | tf_op jit(solution)/shard_map/weight_value/pallas_call | solution.py:351
  291.6 2.0 copy-done.61
  295.4 6.4 %weight_mid.6 = (bf16[2,512,768]{2,1,0:T(8,128)(2,1)}, bf16[2,512,768]{2,1,0:T(8,128)(2,1)S(1)}) custom-call(s32[16]{0:T(128)S(1)} %copy-done.8, bf16[1024,1024]{1,0:T(8,128)(2,1)S(1)} %copy-done.65, bf16[1024,1024]{1,0:T(8,128)(2,1)S(1)} %copy-done.61, bf16[1024,1024]{1,0:T(8,128)(2,1)S(1)} %copy-done.63, bf16[1024,1024]{1,0:T(8,128)(2,1)S(1)} %copy-done.25, ...), custom_call_target="tpu_custom_call" | custom-call | flops 32212254720 | bytes 167772160 | tf_op jit(solution)/shard_map/weight_mid/pallas_call | solution.py:351
  301.8 2.1 copy-done.57
  304.0 6.9 %weight_mid.7 = (bf16[2,512,768]{2,1,0:T(8,128)(2,1)S(1)}, bf16[2,512,768]{2,1,0:T(8,128)(2,1)}) custom-call(s32[16]{0:T(128)S(1)} %copy-done.8, bf16[1024,1024]{1,0:T(8,128)(2,1)S(1)} %copy-done.25, bf16[1024,1024]{1,0:T(8,128)(2,1)S(1)} %copy-done.55, bf16[1024,1024]{1,0:T(8,128)(2,1)S(1)} %copy-done.57, bf16[1024,1024]{1,0:T(8,128)(2,1)S(1)} %copy-done.59, ...), custom_call_target="tpu_custom_call" | custom-call | flops 32212254720 | bytes 188743680 | tf_op jit(solution)/shard_map/weight_mid/pallas_call | solution.py:351
  311.0 2.5 fusion.8
  318.3 7.8 %ema_backward.4 = (f32[1024,1024]{1,0:T(8,128)S(1)}, f32[128,128]{1,0:T(8,128)S(1)}, f32[128,128]{1,0:T(8,128)S(1)}, f32[128,128]{1,0:T(8,128)S(1)}, f32[128,128]{1,0:T(8,128)S(1)}, /*index=5*/f32[8,128]{1,0:T(8,128)S(1)}) custom-call(s32[16]{0:T(128)S(1)} %copy-done.8, bf16[1024,1024]{1,0:T(8,128)(2,1)S(1)} %copy-done.41, ...), custom_call_target="tpu_custom_call" | custom-call | flops 99999997952 | bytes 114114560 | tf_op jit(solution)/shard_map/ema_backward/pallas_call | solution.py:351
  329.2 6.9 %weight_value.3 = (bf16[2,512,256]{2,1,0:T(8,128)(2,1)}, bf16[2,512,256]{2,1,0:T(8,128)(2,1)S(1)}, bf16[2,512,384]{2,1,0:T(8,128)(2,1)S(1)}, bf16[2,512,384]{2,1,0:T(8,128)(2,1)}) custom-call(s32[16]{0:T(128)S(1)} %copy-done.8, bf16[1024,1024]{1,0:T(8,128)(2,1)S(1)} %copy-done.42, bf16[1024,1024]{1,0:T(8,128)(2,1)S(1)} %get-tuple-element.265.vo, ...), custom_call_target="tpu_custom_call" | custom-call | flops 24159191040 | bytes 138936320 | tf_op jit(solution)/shard_map/weight_value/pallas_call | solution.py:351
  336.6 7.8 %ema_backward.5 = (f32[1024,1024]{1,0:T(8,128)S(1)}, f32[128,128]{1,0:T(8,128)S(1)}, f32[128,128]{1,0:T(8,128)S(1)}, f32[128,128]{1,0:T(8,128)S(1)}, f32[128,128]{1,0:T(8,128)S(1)}, /*index=5*/f32[8,128]{1,0:T(8,128)S(1)}) custom-call(s32[16]{0:T(128)S(1)} %copy-done.8, bf16[1024,1024]{1,0:T(8,128)(2,1)S(1)} %copy-done.42, ...), custom_call_target="tpu_custom_call", output_to_operand_aliasing={{0}: (14, {})} | custom-call | flops 99999997952 | bytes 158720000 | tf_op jit(solution)/shard_map/ema_backward/pallas_call | solution.py:351
  345.4 8.1 %ema_backward.6 = (f32[1024,1024]{1,0:T(8,128)S(1)}, f32[128,128]{1,0:T(8,128)S(1)}, f32[128,128]{1,0:T(8,128)S(1)}, f32[128,128]{1,0:T(8,128)S(1)}, f32[128,128]{1,0:T(8,128)S(1)}, /*index=5*/f32[8,128]{1,0:T(8,128)S(1)}) custom-call(s32[16]{0:T(128)S(1)} %copy-done.8, bf16[1024,1024]{1,0:T(8,128)(2,1)S(1)} %copy-done.42, ...), custom_call_target="tpu_custom_call", output_to_operand_aliasing={{0}: (14, {})} | custom-call | flops 99999997952 | bytes 158720000 | tf_op jit(solution)/shard_map/ema_backward/pallas_call | solution.py:351
  356.9 2.7 collective-permute-start.53
  359.5 5.2 %collective-permute-done.34 = bf16[2,512,768]{2,1,0:T(8,128)(2,1)} collective-permute-done((bf16[2,512,768]{2,1,0:T(8,128)(2,1)}, bf16[2,512,768]{2,1,0:T(8,128)(2,1)}, u32[]{:S(2)}, u32[]{:S(2)}) %collective-permute-start.34) | collective-permute-done | bytes 1572896 | tf_op jit(solution)/shard_map/ppermute | solution.py:1092
  369.1 8.3 %ema_backward.7 = (f32[1024,1024]{1,0:T(8,128)S(1)}, f32[128,128]{1,0:T(8,128)}, f32[128,128]{1,0:T(8,128)}, f32[128,128]{1,0:T(8,128)S(1)}, f32[128,128]{1,0:T(8,128)S(1)}, /*index=5*/f32[8,128]{1,0:T(8,128)S(1)}) custom-call(s32[16]{0:T(128)S(1)} %copy-done.8, bf16[1024,1024]{1,0:T(8,128)(2,1)S(1)} %copy-done.42, ...), custom_call_target="tpu_custom_call", output_to_operand_aliasing={{0}: (14, {})} | custom-call | flops 99999997952 | bytes 158720000 | tf_op jit(solution)/shard_map/ema_backward/pallas_call | solution.py:351
  377.6 4.9 %input_back.2.refs_0_ = f32[1024,1024]{1,0:T(8,128)} custom-call(s32[16]{0:T(128)S(1)} %copy-done.8, bf16[1024,1024]{1,0:T(8,128)(2,1)S(1)} %copy-done.37, bf16[1024,1024]{1,0:T(8,128)(2,1)S(1)} %copy-done.39, bf16[1024,1024]{1,0:T(8,128)(2,1)S(1)} %copy-done.5, bf16[256,1024]{1,0:T(8,128)(2,1)S(1)} %copy-done.12, bf16[256,1024]{1,0:T(8,128)(2,1)S(1)} %copy-done.14, ...), custom_call_target="tpu_custom_call" | custom-call | flops 21474836480 | bytes 209715200 | tf_op jit(solution)/shard_map/input_back/pallas_call | solution.py:351
  395.4 2.9 collective-permute-done.39
  399.6 4.9 %input_back.3 = f32[1024,1024]{1,0:T(8,128)} custom-call(s32[16]{0:T(128)S(1)} %copy-done.8, bf16[1024,1024]{1,0:T(8,128)(2,1)S(1)} %copy-done.37, bf16[1024,1024]{1,0:T(8,128)(2,1)S(1)} %copy-done.39, bf16[1024,1024]{1,0:T(8,128)(2,1)S(1)} %copy-done.5, bf16[256,1024]{1,0:T(8,128)(2,1)S(1)} %copy-done.12, ...), custom_call_target="tpu_custom_call", output_to_operand_aliasing={{}: (11, {})} | custom-call | flops 21474836480 | bytes 251658240 | tf_op jit(solution)/shard_map/input_back/pallas_call | solution.py:351
  406.5 4.5 collective-permute-done.42
  414.2 4.9 %collective-permute-done.43 = f32[272,128]{1,0:T(8,128)S(1)} collective-permute-done((f32[272,128]{1,0:T(8,128)S(1)}, f32[272,128]{1,0:T(8,128)S(1)}, u32[]{:S(2)}, u32[]{:S(2)}) %collective-permute-start.43) | collective-permute-done | bytes 139296 | tf_op jit(solution)/shard_map/ppermute | solution.py:1092
  419.2 2.6 collective-permute-start.44
  423.7 11.8 %collective-permute-done.44 = f32[272,128]{1,0:T(8,128)S(1)} collective-permute-done((f32[272,128]{1,0:T(8,128)S(1)}, f32[272,128]{1,0:T(8,128)S(1)}, u32[]{:S(2)}, u32[]{:S(2)}) %collective-permute-start.44) | collective-permute-done | bytes 139296 | tf_op jit(solution)/shard_map/ppermute | solution.py:1092
  443.7 3.4 collective-permute-start.51
  448.5 16.8 %collective-permute-done.51 = bf16[2,128,768]{2,1,0:T(8,128)(2,1)S(1)} collective-permute-done((bf16[2,128,768]{2,1,0:T(8,128)(2,1)S(1)}, bf16[2,128,768]{2,1,0:T(8,128)(2,1)S(1)}, u32[]{:S(2)}, u32[]{:S(2)}) %collective-permute-start.51) | collective-permute-done | bytes 393248 | tf_op jit(solution)/shard_map/ppermute | solution.py:1092
  (395 shorter events, 104.3 us)
Async XLA Ops:
  1.8 33.4 %collective-permute-start.1 = (bf16[256,1024]{1,0:T(8,128)(2,1)S(1)}, bf16[256,1024]{1,0:T(8,128)(2,1)S(1)}, u32[]{:S(2)}, u32[]{:S(2)}) collective-permute-start(bf16[256,1024]{1,0:T(8,128)(2,1)S(1)} %constant_dynamic-slice_fusion), channel_id=1, source_target_pairs={{0,1},{1,0},{2,3},{3,2},{4,5},{5,4},{6,7},{7,6},{8,9},{9,8},{10,11... | collective-permute-start | bytes 1572872 | tf_op jit(solution)/shard_map/ppermute | solution.py:1092
  7.6 15.3 %collective-permute-start = (f32[72,512]{1,0:T(8,128)}, f32[72,512]{1,0:T(8,128)S(1)}, u32[]{:S(2)}, u32[]{:S(2)}) collective-permute-start(f32[72,512]{1,0:T(8,128)} %pack_params.1.own_ref), channel_id=1, source_target_pairs={{0,1},{1,0},{2,3},{3,2},{4,5},{5,4},{6,7},{7,6},{8,9},{9,8},{10,11... | collective-permute-start | bytes 442376 | tf_op jit(solution)/shard_map/ppermute | solution.py:1092
  21.5 29.1 %collective-permute-start.5 = (bf16[256,1024]{1,0:T(8,128)(2,1)}, bf16[256,1024]{1,0:T(8,128)(2,1)}, u32[]{:S(2)}, u32[]{:S(2)}) collective-permute-start(bf16[256,1024]{1,0:T(8,128)(2,1)} %get-tuple-element.196), channel_id=1, source_target_pairs={{0,1},{1,0},{2,3},{3,2},{4,5},{5,4},{6,7},{7,6},{8,9},{9,8},{10,11... | collective-permute-start | bytes 1572872 | tf_op jit(solution)/shard_map/ppermute | solution.py:1092
  35.2 12.9 %collective-permute-start.2 = (bf16[256,1024]{1,0:T(8,128)(2,1)S(1)}, bf16[256,1024]{1,0:T(8,128)(2,1)S(1)}, u32[]{:S(2)}, u32[]{:S(2)}) collective-permute-start(bf16[256,1024]{1,0:T(8,128)(2,1)S(1)} %collective-permute-done.1.p0.w0), channel_id=1, source_target_pairs={{0,4},{2,6},{4,0},{6,2},{8,12},{10,14},{12,8},{14,10},{16,20},{18,... | collective-permute-start | bytes 1572872 | tf_op jit(solution)/shard_map/ppermute | solution.py:1092
  48.6 17.0 %collective-permute-start.9 = (bf16[256,1024]{1,0:T(8,128)(2,1)S(1)}, bf16[256,1024]{1,0:T(8,128)(2,1)S(1)}, u32[]{:S(2)}, u32[]{:S(2)}) collective-permute-start(bf16[256,1024]{1,0:T(8,128)(2,1)S(1)} %copy-done.110), channel_id=1, source_target_pairs={{0,1},{1,0},{2,3},{3,2},{4,5},{5,4},{6,7},{7,6},{8,9},{9,8},{10,11... | collective-permute-start | bytes 1572872 | tf_op jit(solution)/shard_map/ppermute | solution.py:1092
  49.5 25.1 %collective-permute-start.13 = (bf16[256,1024]{1,0:T(8,128)(2,1)S(1)}, bf16[256,1024]{1,0:T(8,128)(2,1)S(1)}, u32[]{:S(2)}, u32[]{:S(2)}) collective-permute-start(bf16[256,1024]{1,0:T(8,128)(2,1)S(1)} %copy-done.109), channel_id=1, source_target_pairs={{0,1},{1,0},{2,3},{3,2},{4,5},{5,4},{6,7},{7,6},{8,9},{9,8},{10,11... | collective-permute-start | bytes 1572872 | tf_op jit(solution)/shard_map/ppermute | solution.py:1092
  50.6 13.5 %collective-permute-start.6 = (bf16[256,1024]{1,0:T(8,128)(2,1)}, bf16[256,1024]{1,0:T(8,128)(2,1)S(1)}, u32[]{:S(2)}, u32[]{:S(2)}) collective-permute-start(bf16[256,1024]{1,0:T(8,128)(2,1)} %collective-permute-done.5.w0), channel_id=1, source_target_pairs={{0,8},{2,10},{4,12},{6,14},{8,0},{10,2},{12,4},{14,6},{16,24},{18,... | collective-permute-start | bytes 1572872 | tf_op jit(solution)/shard_map/ppermute | solution.py:1092
  64.1 12.1 %collective-permute-start.7 = (bf16[256,1024]{1,0:T(8,128)(2,1)}, bf16[256,1024]{1,0:T(8,128)(2,1)S(1)}, u32[]{:S(2)}, u32[]{:S(2)}) collective-permute-start(bf16[256,1024]{1,0:T(8,128)(2,1)} %collective-permute-done.5.w0), channel_id=1, source_target_pairs={{0,2},{2,0},{4,6},{6,4},{8,10},{10,8},{12,14},{14,12},{16,18},{18,... | collective-permute-start | bytes 1572872 | tf_op jit(solution)/shard_map/ppermute | solution.py:1092
  64.1 12.1 %collective-permute-start.8 = (bf16[256,1024]{1,0:T(8,128)(2,1)S(1)}, bf16[256,1024]{1,0:T(8,128)(2,1)S(1)}, u32[]{:S(2)}, u32[]{:S(2)}) collective-permute-start(bf16[256,1024]{1,0:T(8,128)(2,1)S(1)} %collective-permute-done.6.w1), channel_id=1, source_target_pairs={{0,2},{2,0},{4,6},{6,4},{8,10},{10,8},{12,14},{14,12},{16,18},{18,... | collective-permute-start | bytes 1572872 | tf_op jit(solution)/shard_map/ppermute | solution.py:1092
  64.6 31.6 %collective-permute-start.18 = (bf16[256,2048]{1,0:T(8,128)(2,1)S(1)}, bf16[256,2048]{1,0:T(8,128)(2,1)}, u32[]{:S(2)}, u32[]{:S(2)}) collective-permute-start(bf16[256,2048]{1,0:T(8,128)(2,1)S(1)} %copy-done.97), channel_id=1, source_target_pairs={{0,1},{1,0},{2,3},{3,2},{4,5},{5,4},{6,7},{7,6},{8,9},{9,8},{10,11... | collective-permute-start | bytes 3145736 | tf_op jit(solution)/shard_map/ppermute | solution.py:1092
  65.6 28.9 %collective-permute-start.10 = (bf16[256,1024]{1,0:T(8,128)(2,1)S(1)}, bf16[256,1024]{1,0:T(8,128)(2,1)S(1)}, u32[]{:S(2)}, u32[]{:S(2)}) collective-permute-start(bf16[256,1024]{1,0:T(8,128)(2,1)S(1)} %collective-permute-done.9.u0), channel_id=1, source_target_pairs={{0,4},{2,6},{4,0},{6,2},{8,12},{10,14},{12,8},{14,10},{16,20},{18,... | collective-permute-start | bytes 1572872 | tf_op jit(solution)/shard_map/ppermute | solution.py:1092
  74.6 19.3 %collective-permute-start.14 = (bf16[256,1024]{1,0:T(8,128)(2,1)S(1)}, bf16[256,1024]{1,0:T(8,128)(2,1)S(1)}, u32[]{:S(2)}, u32[]{:S(2)}) collective-permute-start(bf16[256,1024]{1,0:T(8,128)(2,1)S(1)} %collective-permute-done.13.h0.f0), channel_id=1, source_target_pairs={{0,8},{2,10},{4,12},{6,14},{8,0},{10,2},{12,4},{14,6},{16,24},{18,... | collective-permute-start | bytes 1572872 | tf_op jit(solution)/shard_map/ppermute | solution.py:1092
  96.2 63.5 %collective-permute-start.22 = (bf16[1024,1024]{1,0:T(8,128)(2,1)}, bf16[1024,1024]{1,0:T(8,128)(2,1)}, u32[]{:S(2)}, u32[]{:S(2)}) collective-permute-start(bf16[1024,1024]{1,0:T(8,128)(2,1)} %get-tuple-element.231), channel_id=1, source_target_pairs={{0,1},{1,0},{2,3},{3,2},{4,5},{5,4},{6,7},{7,6},{8,9},{9,8},{10,11... | collective-permute-start | bytes 6291464 | tf_op jit(solution)/shard_map/ppermute | solution.py:1092
  97.2 63.2 %collective-permute-start.19 = (bf16[256,2048]{1,0:T(8,128)(2,1)}, bf16[256,2048]{1,0:T(8,128)(2,1)}, u32[]{:S(2)}, u32[]{:S(2)}) collective-permute-start(bf16[256,2048]{1,0:T(8,128)(2,1)} %collective-permute-done.18.refs_0_), channel_id=1, source_target_pairs={{0,4},{2,6},{4,0},{6,2},{8,12},{10,14},{12,8},{14,10},{16,20},{18,... | collective-permute-start | bytes 3145736 | tf_op jit(solution)/shard_map/ppermute | solution.py:1092
  139.0 21.9 %collective-permute-start.17 = (bf16[2,2,512,1024]{3,2,1,0:T(8,128)(2,1)}, bf16[2,2,512,1024]{3,2,1,0:T(8,128)(2,1)}, u32[]{:S(2)}, u32[]{:S(2)}) collective-permute-start(bf16[2,2,512,1024]{3,2,1,0:T(8,128)(2,1)} %get-tuple-element.223), channel_id=1, source_target_pairs={{0,2},{2,0},{4,6},{6,4},{8,10},{10,8},{12,14},{14,12},{16,18},{18,... | collective-permute-start | bytes 12582920 | tf_op jit(solution)/shard_map/ppermute | solution.py:1092
  159.8 7.7 %collective-permute-start.23 = (bf16[1024,1024]{1,0:T(8,128)(2,1)}, bf16[1024,1024]{1,0:T(8,128)(2,1)S(1)}, u32[]{:S(2)}, u32[]{:S(2)}) collective-permute-start(bf16[1024,1024]{1,0:T(8,128)(2,1)} %collective-permute-done.22.refs_4_), channel_id=1, source_target_pairs={{0,2},{2,0},{4,6},{6,4},{8,10},{10,8},{12,14},{14,12},{16,18},{18,... | collective-permute-start | bytes 6291464 | tf_op jit(solution)/shard_map/ppermute | solution.py:1092
  160.3 5.5 %collective-permute-start.20 = (bf16[256,2048]{1,0:T(8,128)(2,1)}, bf16[256,2048]{1,0:T(8,128)(2,1)}, u32[]{:S(2)}, u32[]{:S(2)}) collective-permute-start(bf16[256,2048]{1,0:T(8,128)(2,1)} %collective-permute-done.18.refs_0_), channel_id=1, source_target_pairs={{0,2},{2,0},{4,6},{6,4},{8,10},{10,8},{12,14},{14,12},{16,18},{18,... | collective-permute-start | bytes 3145736 | tf_op jit(solution)/shard_map/ppermute | solution.py:1092
  160.4 7.0 %collective-permute-start.21 = (bf16[256,2048]{1,0:T(8,128)(2,1)}, bf16[256,2048]{1,0:T(8,128)(2,1)}, u32[]{:S(2)}, u32[]{:S(2)}) collective-permute-start(bf16[256,2048]{1,0:T(8,128)(2,1)} %collective-permute-done.19.refs_1_), channel_id=1, source_target_pairs={{0,2},{2,0},{4,6},{6,4},{8,10},{10,8},{12,14},{14,12},{16,18},{18,... | collective-permute-start | bytes 3145736 | tf_op jit(solution)/shard_map/ppermute | solution.py:1092
  163.8 57.3 %collective-permute-start.25 = (bf16[512,1024]{1,0:T(8,128)(2,1)}, bf16[512,1024]{1,0:T(8,128)(2,1)}, u32[]{:S(2)}, u32[]{:S(2)}) collective-permute-start(bf16[512,1024]{1,0:T(8,128)(2,1)} %fusion.5), channel_id=1, source_target_pairs={{0,4},{2,6},{4,0},{6,2},{8,12},{10,14},{12,8},{14,10},{16,20},{18,... | collective-permute-start | bytes 3145736 | tf_op jit(solution)/shard_map/ppermute | solution.py:1092
  190.0 24.7 %collective-permute-start.24 = (bf16[2,2,512,1024]{3,2,1,0:T(8,128)(2,1)}, bf16[2,2,512,1024]{3,2,1,0:T(8,128)(2,1)S(1)}, u32[]{:S(2)}, u32[]{:S(2)}) collective-permute-start(bf16[2,2,512,1024]{3,2,1,0:T(8,128)(2,1)} %get-tuple-element.239), channel_id=1, source_target_pairs={{0,2},{2,0},{4,6},{6,4},{8,10},{10,8},{12,14},{14,12},{16,18},{18,... | collective-permute-start | bytes 12582920 | tf_op jit(solution)/shard_map/ppermute | solution.py:1092
  215.1 33.1 %collective-permute-start.26 = (bf16[512,1024]{1,0:T(8,128)(2,1)S(1)}, bf16[512,1024]{1,0:T(8,128)(2,1)}, u32[]{:S(2)}, u32[]{:S(2)}) collective-permute-start(bf16[512,1024]{1,0:T(8,128)(2,1)S(1)} %fusion.4), channel_id=1, source_target_pairs={{0,4},{2,6},{4,0},{6,2},{8,12},{10,14},{12,8},{14,10},{16,20},{18,... | collective-permute-start | bytes 3145736 | tf_op jit(solution)/shard_map/ppermute | solution.py:1092
  220.1 59.1 %collective-permute-start.27 = (bf16[2,512,1024]{2,1,0:T(8,128)(2,1)}, bf16[2,512,1024]{2,1,0:T(8,128)(2,1)}, u32[]{:S(2)}, u32[]{:S(2)}) collective-permute-start(bf16[2,512,1024]{2,1,0:T(8,128)(2,1)} %fusion), channel_id=1, source_target_pairs={{0,1},{1,0},{2,3},{3,2},{4,5},{5,4},{6,7},{7,6},{8,9},{9,8},{10,11... | collective-permute-start | bytes 6291464 | tf_op jit(solution)/shard_map/ppermute | solution.py:1092
  260.2 31.4 %collective-permute-start.28 = (bf16[2,2,512,768]{3,2,1,0:T(8,128)(2,1)S(1)}, bf16[2,2,512,768]{3,2,1,0:T(8,128)(2,1)S(1)}, u32[]{:S(2)}, u32[]{:S(2)}) collective-permute-start(bf16[2,2,512,768]{3,2,1,0:T(8,128)(2,1)S(1)} %weight_mid.4), channel_id=1, source_target_pairs={{0,2},{2,0},{4,6},{6,4},{8,10},{10,8},{12,14},{14,12},{16,18},{18,... | collective-permute-start | bytes 9437192 | tf_op jit(solution)/shard_map/ppermute | solution.py:1092
  266.3 35.5 %collective-permute-start.29 = (bf16[2,2,512,768]{3,2,1,0:T(8,128)(2,1)S(1)}, bf16[2,2,512,768]{3,2,1,0:T(8,128)(2,1)S(1)}, u32[]{:S(2)}, u32[]{:S(2)}) collective-permute-start(bf16[2,2,512,768]{3,2,1,0:T(8,128)(2,1)S(1)} %weight_mid.5), channel_id=1, source_target_pairs={{0,2},{2,0},{4,6},{6,4},{8,10},{10,8},{12,14},{14,12},{16,18},{18,... | collective-permute-start | bytes 9437192 | tf_op jit(solution)/shard_map/ppermute | solution.py:1092
  266.9 44.1 %collective-permute-start.31 = (bf16[512,1024]{1,0:T(8,128)(2,1)}, bf16[512,1024]{1,0:T(8,128)(2,1)}, u32[]{:S(2)}, u32[]{:S(2)}) collective-permute-start(bf16[512,1024]{1,0:T(8,128)(2,1)} %fusion.3), channel_id=1, source_target_pairs={{0,1},{1,0},{2,3},{3,2},{4,5},{5,4},{6,7},{7,6},{8,9},{9,8},{10,11... | collective-permute-start | bytes 3145736 | tf_op jit(solution)/shard_map/ppermute | solution.py:1092
  284.3 26.6 %collective-permute-start.30 = (bf16[512,1024]{1,0:T(8,128)(2,1)}, bf16[512,1024]{1,0:T(8,128)(2,1)S(1)}, u32[]{:S(2)}, u32[]{:S(2)}) collective-permute-start(bf16[512,1024]{1,0:T(8,128)(2,1)} %fusion.1), channel_id=1, source_target_pairs={{0,4},{2,6},{4,0},{6,2},{8,12},{10,14},{12,8},{14,10},{16,20},{18,... | collective-permute-start | bytes 3145736 | tf_op jit(solution)/shard_map/ppermute | solution.py:1092
  291.5 37.6 %collective-permute-start.32 = (bf16[2,2,512,640]{3,2,1,0:T(8,128)(2,1)}, bf16[2,2,512,640]{3,2,1,0:T(8,128)(2,1)}, u32[]{:S(2)}, u32[]{:S(2)}) collective-permute-start(bf16[2,2,512,640]{3,2,1,0:T(8,128)(2,1)} %weight_value.2), channel_id=1, source_target_pairs={{0,2},{2,0},{4,6},{6,4},{8,10},{10,8},{12,14},{14,12},{16,18},{18,... | collective-permute-start | bytes 7864328 | tf_op jit(solution)/shard_map/ppermute | solution.py:1092
  315.2 39.7 %collective-permute-start.35 = (bf16[2,2,128,1024]{3,2,1,0:T(8,128)(2,1)}, bf16[2,2,128,1024]{3,2,1,0:T(8,128)(2,1)}, u32[]{:S(2)}, u32[]{:S(2)}) collective-permute-start(bf16[2,2,128,1024]{3,2,1,0:T(8,128)(2,1)} %pad_maximum_fusion), channel_id=1, source_target_pairs={{0,8},{2,10},{4,12},{6,14},{8,0},{10,2},{12,4},{14,6},{16,24},{18,... | collective-permute-start | bytes 3145736 | tf_op jit(solution)/shard_map/ppermute | solution.py:1092
  316.7 48.0 %collective-permute-start.33 = (bf16[2,512,768]{2,1,0:T(8,128)(2,1)}, bf16[2,512,768]{2,1,0:T(8,128)(2,1)}, u32[]{:S(2)}, u32[]{:S(2)}) collective-permute-start(bf16[2,512,768]{2,1,0:T(8,128)(2,1)} %get-tuple-element.272), channel_id=1, source_target_pairs={{0,4},{2,6},{4,0},{6,2},{8,12},{10,14},{12,8},{14,10},{16,20},{18,... | collective-permute-start | bytes 4718600 | tf_op jit(solution)/shard_map/ppermute | solution.py:1092
  327.1 37.6 %collective-permute-start.34 = (bf16[2,512,768]{2,1,0:T(8,128)(2,1)}, bf16[2,512,768]{2,1,0:T(8,128)(2,1)}, u32[]{:S(2)}, u32[]{:S(2)}) collective-permute-start(bf16[2,512,768]{2,1,0:T(8,128)(2,1)} %get-tuple-element.300), channel_id=1, source_target_pairs={{0,1},{1,0},{2,3},{3,2},{4,5},{5,4},{6,7},{7,6},{8,9},{9,8},{10,11... | collective-permute-start | bytes 4718600 | tf_op jit(solution)/shard_map/ppermute | solution.py:1092
  336.0 50.7 %collective-permute-start.37 = (bf16[2,512,256]{2,1,0:T(8,128)(2,1)}, bf16[2,512,256]{2,1,0:T(8,128)(2,1)}, u32[]{:S(2)}, u32[]{:S(2)}) collective-permute-start(bf16[2,512,256]{2,1,0:T(8,128)(2,1)} %get-tuple-element.284), channel_id=1, source_target_pairs={{0,4},{2,6},{4,0},{6,2},{8,12},{10,14},{12,8},{14,10},{16,20},{18,... | collective-permute-start | bytes 1572872 | tf_op jit(solution)/shard_map/ppermute | solution.py:1092
  344.4 43.0 %collective-permute-start.38 = (bf16[2,512,384]{2,1,0:T(8,128)(2,1)}, bf16[2,512,384]{2,1,0:T(8,128)(2,1)}, u32[]{:S(2)}, u32[]{:S(2)}) collective-permute-start(bf16[2,512,384]{2,1,0:T(8,128)(2,1)} %get-tuple-element.319), channel_id=1, source_target_pairs={{0,1},{1,0},{2,3},{3,2},{4,5},{5,4},{6,7},{7,6},{8,9},{9,8},{10,11... | collective-permute-start | bytes 2359304 | tf_op jit(solution)/shard_map/ppermute | solution.py:1092
  356.9 28.0 %collective-permute-start.53 = (bf16[2,128,1024]{2,1,0:T(8,128)(2,1)S(1)}, bf16[2,128,1024]{2,1,0:T(8,128)(2,1)S(1)}, u32[]{:S(2)}, u32[]{:S(2)}) collective-permute-start(bf16[2,128,1024]{2,1,0:T(8,128)(2,1)S(1)} %pad_maximum_fusion.2), channel_id=1, source_target_pairs={{0,16},{2,18},{4,20},{6,22},{8,24},{10,26},{12,28},{14,30},{16,0},... | collective-permute-start | bytes 1572872 | tf_op jit(solution)/shard_map/ppermute | solution.py:1092
  367.4 26.9 %collective-permute-start.40 = (bf16[512,768]{1,0:T(8,128)(2,1)S(1)}, bf16[512,768]{1,0:T(8,128)(2,1)S(1)}, u32[]{:S(2)}, u32[]{:S(2)}) collective-permute-start(bf16[512,768]{1,0:T(8,128)(2,1)S(1)} %fusion.7), channel_id=1, source_target_pairs={{0,4},{2,6},{4,0},{6,2},{8,12},{10,14},{12,8},{14,10},{16,20},{18,... | collective-permute-start | bytes 2359304 | tf_op jit(solution)/shard_map/ppermute | solution.py:1092
  367.9 30.4 %collective-permute-start.39 = (bf16[512,768]{1,0:T(8,128)(2,1)S(1)}, bf16[512,768]{1,0:T(8,128)(2,1)S(1)}, u32[]{:S(2)}, u32[]{:S(2)}) collective-permute-start(bf16[512,768]{1,0:T(8,128)(2,1)S(1)} %fusion.6), channel_id=1, source_target_pairs={{0,1},{1,0},{2,3},{3,2},{4,5},{5,4},{6,7},{7,6},{8,9},{9,8},{10,11... | collective-permute-start | bytes 2359304 | tf_op jit(solution)/shard_map/ppermute | solution.py:1092
  384.9 8.4 %collective-permute-start.36 = (f32[272,128]{1,0:T(8,128)S(1)}, f32[272,128]{1,0:T(8,128)S(1)}, u32[]{:S(2)}, u32[]{:S(2)}) collective-permute-start(f32[272,128]{1,0:T(8,128)S(1)} %constant_dynamic-update-slice_fusion), channel_id=1, source_target_pairs={{0,2},{2,0},{4,6},{6,4},{8,10},{10,8},{12,14},{14,12},{16,18},{18,... | collective-permute-start | bytes 417800 | tf_op jit(solution)/shard_map/ppermute | solution.py:1092
  386.8 19.7 %collective-permute-start.54 = (bf16[2,64,1024]{2,1,0:T(8,128)(2,1)S(1)}, bf16[2,64,1024]{2,1,0:T(8,128)(2,1)S(1)}, u32[]{:S(2)}, u32[]{:S(2)}) collective-permute-start(bf16[2,64,1024]{2,1,0:T(8,128)(2,1)S(1)} %fusion.23), channel_id=1, source_target_pairs={{0,2},{2,0},{4,6},{6,4},{8,10},{10,8},{12,14},{14,12},{16,18},{18,... | collective-permute-start | bytes 786440 | tf_op jit(solution)/shard_map/ppermute | solution.py:1092
  389.5 15.0 %collective-permute-start.46 = (bf16[512,384]{1,0:T(8,128)(2,1)S(1)}, bf16[512,384]{1,0:T(8,128)(2,1)S(1)}, u32[]{:S(2)}, u32[]{:S(2)}) collective-permute-start(bf16[512,384]{1,0:T(8,128)(2,1)S(1)} %fusion.14), channel_id=1, source_target_pairs={{0,4},{2,6},{4,0},{6,2},{8,12},{10,14},{12,8},{14,10},{16,20},{18,... | collective-permute-start | bytes 1179656 | tf_op jit(solution)/shard_map/ppermute | solution.py:1092
  393.2 11.2 %collective-permute-start.45 = (bf16[512,256]{1,0:T(8,128)(2,1)S(1)}, bf16[512,256]{1,0:T(8,128)(2,1)S(1)}, u32[]{:S(2)}, u32[]{:S(2)}) collective-permute-start(bf16[512,256]{1,0:T(8,128)(2,1)S(1)} %fusion.20), channel_id=1, source_target_pairs={{0,1},{1,0},{2,3},{3,2},{4,5},{5,4},{6,7},{7,6},{8,9},{9,8},{10,11... | collective-permute-start | bytes 786440 | tf_op jit(solution)/shard_map/ppermute | solution.py:1092
  394.3 11.6 %collective-permute-start.41 = (f32[272,128]{1,0:T(8,128)S(1)}, f32[272,128]{1,0:T(8,128)S(1)}, u32[]{:S(2)}, u32[]{:S(2)}) collective-permute-start(f32[272,128]{1,0:T(8,128)S(1)} %add.656), channel_id=1, source_target_pairs={{0,1},{1,0},{2,3},{3,2},{4,5},{5,4},{6,7},{7,6},{8,9},{9,8},{10,11... | collective-permute-start | bytes 417800 | tf_op jit(solution)/shard_map/ppermute | solution.py:1092
  404.7 17.1 %collective-permute-start.47 = (bf16[2,128,640]{2,1,0:T(8,128)(2,1)S(1)}, bf16[2,128,640]{2,1,0:T(8,128)(2,1)S(1)}, u32[]{:S(2)}, u32[]{:S(2)}) collective-permute-start(bf16[2,128,640]{2,1,0:T(8,128)(2,1)S(1)} %pad_maximum_fusion.4), channel_id=1, source_target_pairs={{0,8},{2,10},{4,12},{6,14},{8,0},{10,2},{12,4},{14,6},{16,24},{18,... | collective-permute-start | bytes 983048 | tf_op jit(solution)/shard_map/ppermute | solution.py:1092
  405.9 5.1 %collective-permute-start.42 = (f32[272,128]{1,0:T(8,128)S(1)}, f32[272,128]{1,0:T(8,128)S(1)}, u32[]{:S(2)}, u32[]{:S(2)}) collective-permute-start(f32[272,128]{1,0:T(8,128)S(1)} %add.663), channel_id=1, source_target_pairs={{0,4},{2,6},{4,0},{6,2},{8,12},{10,14},{12,8},{14,10},{16,20},{18,... | collective-permute-start | bytes 417800 | tf_op jit(solution)/shard_map/ppermute | solution.py:1092
  411.0 8.2 %collective-permute-start.43 = (f32[272,128]{1,0:T(8,128)S(1)}, f32[272,128]{1,0:T(8,128)S(1)}, u32[]{:S(2)}, u32[]{:S(2)}) collective-permute-start(f32[272,128]{1,0:T(8,128)S(1)} %add.664), channel_id=1, source_target_pairs={{0,8},{2,10},{4,12},{6,14},{8,0},{10,2},{12,4},{14,6},{16,24},{18,... | collective-permute-start | bytes 417800 | tf_op jit(solution)/shard_map/ppermute | solution.py:1092
  413.2 29.1 %collective-permute-start.50 = (bf16[2,2,128,768]{3,2,1,0:T(8,128)(2,1)}, bf16[2,2,128,768]{3,2,1,0:T(8,128)(2,1)}, u32[]{:S(2)}, u32[]{:S(2)}) collective-permute-start(bf16[2,2,128,768]{3,2,1,0:T(8,128)(2,1)} %pad_maximum_fusion.1), channel_id=1, source_target_pairs={{0,8},{2,10},{4,12},{6,14},{8,0},{10,2},{12,4},{14,6},{16,24},{18,... | collective-permute-start | bytes 2359304 | tf_op jit(solution)/shard_map/ppermute | solution.py:1092
  419.2 16.4 %collective-permute-start.44 = (f32[272,128]{1,0:T(8,128)S(1)}, f32[272,128]{1,0:T(8,128)S(1)}, u32[]{:S(2)}, u32[]{:S(2)}) collective-permute-start(f32[272,128]{1,0:T(8,128)S(1)} %add.665), channel_id=1, source_target_pairs={{0,16},{2,18},{4,20},{6,22},{8,24},{10,26},{12,28},{14,30},{16,0},... | collective-permute-start | bytes 417800 | tf_op jit(solution)/shard_map/ppermute | solution.py:1092
  423.3 17.8 %collective-permute-start.48 = (bf16[128,640]{1,0:T(8,128)(2,1)}, bf16[128,640]{1,0:T(8,128)(2,1)}, u32[]{:S(2)}, u32[]{:S(2)}) collective-permute-start(bf16[128,640]{1,0:T(8,128)(2,1)} %pad_maximum_fusion.5), channel_id=1, source_target_pairs={{0,16},{2,18},{4,20},{6,22},{8,24},{10,26},{12,28},{14,30},{16,0},... | collective-permute-start | bytes 491528 | tf_op jit(solution)/shard_map/ppermute | solution.py:1092
  442.1 5.7 %collective-permute-start.49 = (bf16[64,640]{1,0:T(8,128)(2,1)S(1)}, bf16[64,640]{1,0:T(8,128)(2,1)S(1)}, u32[]{:S(2)}, u32[]{:S(2)}) collective-permute-start(bf16[64,640]{1,0:T(8,128)(2,1)S(1)} %fusion.36), channel_id=1, source_target_pairs={{0,2},{2,0},{4,6},{6,4},{8,10},{10,8},{12,14},{14,12},{16,18},{18,... | collective-permute-start | bytes 245768 | tf_op jit(solution)/shard_map/ppermute | solution.py:1092
  443.7 21.6 %collective-permute-start.51 = (bf16[2,128,768]{2,1,0:T(8,128)(2,1)S(1)}, bf16[2,128,768]{2,1,0:T(8,128)(2,1)S(1)}, u32[]{:S(2)}, u32[]{:S(2)}) collective-permute-start(bf16[2,128,768]{2,1,0:T(8,128)(2,1)S(1)} %pad_maximum_fusion.3), channel_id=1, source_target_pairs={{0,16},{2,18},{4,20},{6,22},{8,24},{10,26},{12,28},{14,30},{16,0},... | collective-permute-start | bytes 1179656 | tf_op jit(solution)/shard_map/ppermute | solution.py:1092
  (119 other events, 961.7 us)

commit v6 on v5

--- a/solution.py
+++ b/solution.py
@@ -317,7 +317,7 @@
 F32 = jnp.float32
 ROWS = 256
 hints = dict()
-opt = dict(dn=0, m2=3, v2=5, z2=3, z1m=5, z1v=6)
+opt = dict(dn=0, m2=3, v2=4, z2=3, z1m=5)
 
 
 def sds(shape, dtype=BF):
@@ -1048,44 +1048,32 @@
 
 def k_weight_value(scal, normed, dv_own, dv_oth, ema_low, dz, part, got=None):
     n, d = normed.shape
-    tn = dv_own.shape[1] // 4
+    width = dv_own.shape[1] // 2
     zw = dz.shape[1]
-    rows = d // 2
+    shape = (2, 2, d // 2, width + zw)
 
     def body(s, x_ref, vo, vt, e_ref, z_ref, *refs):
+        def put(lanes, value, k, j):
+            add = (refs[0].at[:, :, :, lanes], (k, j)) if got is not None else None
+            put_rows(s, refs[-1].at[:, :, :, lanes], value, (k, j), add)
+
         for k, v in enumerate((vo, vt)):
             grad = split_rows(s, row_inner(x_ref[...], v[...]))
             for j in range(2):
-                if got is None:
-                    put_rows(s, refs[0].at[:, :, :, 0 : 2 * tn], grad[j], (k, j))
-                else:
-                    add = (refs[0].at[:, :, :, 0 : 2 * tn], (k, j))
-                    put_rows(s, refs[5], grad[j], (j,), add)
-                    whole_rows = refs[5][j]
-                    refs[2 - j][k] = whole_rows[:, 0:tn]
-                    refs[3 + k][j, :, 0:tn] = whole_rows[:, tn:]
+                put(slice(0, width), grad[j], k, j)
         grad = split_rows(s, row_inner(e_ref[...], z_ref[...]))
         for j in range(2):
             for k in range(2):
-                if got is None:
-                    put_rows(s, refs[0].at[:, :, :, 2 * tn :], grad[j], (k, j))
-                else:
-                    put_rows(s, refs[3 + k].at[:, :, tn:], grad[j], (j,), (refs[0].at[:, :, :, 2 * tn :], (k, j)))
-
-    at = pl.BlockSpec((n, 2 * tn), lambda i, s: (0, s[part]))
+                put(slice(width, width + zw), grad[j], k, j)
+
+    at = pl.BlockSpec((n, width), lambda i, s: (0, s[part]))
     adds = [got] if got is not None else []
-    if adds:
-        shapes = [(2, rows, tn)] * 2 + [(2, rows, tn + zw)] * 2
-    else:
-        shapes = [(2, 2, rows, 2 * tn + zw)]
     return run(
         body, (1,), scal, [normed, dv_own, dv_oth, ema_low, dz] + adds,
-        [whole((n, d)), at, at, whole((n, d)), whole((n, zw))] + [whole(a.shape) for a in adds],
-        [sds(o) for o in shapes],
-        [pl.BlockSpec(o, lambda i, s, r=len(o): (0,) * r) for o in shapes],
-        [pltpu.VMEM((2, rows, 2 * tn), BF)] if adds else [],
-        flops=2 * n * d * (4 * tn + zw), name="weight_value",
-    )
+        [whole((n, d)), at, at, whole((n, d)), whole((n, zw))] + [whole(shape)] * len(adds),
+        [sds(shape)], [pl.BlockSpec(shape, lambda i, s: (0, 0, 0, 0))],
+        flops=2 * n * d * (2 * width + zw), name="weight_value",
+    )[0]
 
 
 def swap(values, axis, bit, size):
@@ -1245,14 +1233,14 @@
     up_got_y = held(up_got_y, dv_own)
     up_x = add(upo_x, got_o[1, 1], up_got_y[1])
     up_got_x = over_x(up_x)
-    val_sent = k_weight_value(after(dv_own, up_x), normed, dv_own, dv_oth, ema_low, dz, 5)[0]
-    val_got = over_core(val_sent)
-    ma_theirs, ma_mine = k_weight_mid(after(val_sent), ema_low, dh, gated_own, gated_oth, False, 4, ma_got)
+    ma_theirs, ma_mine = k_weight_mid(after(dv_own, up_x), ema_low, dh, gated_own, gated_oth, False, 4, ma_got)
     ma_got_x = over_x(ma_theirs)
     mb_own, mb_oth = k_weight_mid(after(ma_theirs), ema_low, df, dg_own, dg_oth, True, 4, mb_got)
     mb_got_y = over_tensor(mb_oth)
+    val_sent = k_weight_value(after(mb_own), normed, dv_own, dv_oth, ema_low, dz, 5)
+    val_got = over_core(val_sent)
     dn_got_y = dn_y[1]
-    up_got_x, dn_got_y = held((up_got_x, dn_got_y), mb_own)
+    up_got_x, dn_got_y = held((up_got_x, dn_got_y), val_sent)
     dn_terms = [dno, got_o[0, 0], dn_got_x1, dn_got_y]
     up_terms = [upo, got_o[1, 0], up_got_y[0], up_got_x]
     ffn_z = jnp.stack([z_send(dn_terms), z_send(up_terms)])
@@ -1265,13 +1253,15 @@
             after(*dep), normed, de_part, dz, e_slope, w_z, decay, coef, omega, first, count, before
         )
 
-    eb = ema_back((mb_own, ffn_z), 0, quarter)
-    va_theirs, va_mine, vb_own, vb_oth = k_weight_value(
+    eb = ema_back((val_sent, ffn_z), 0, quarter)
+    val = k_weight_value(
         after(eb[1]), normed, dv_own, dv_oth, ema_low, dz, 4, val_got
     )
-    va_got_x = over_x(va_theirs)
-    vb_got_y = over_tensor(vb_oth)
-    eb = ema_back((va_theirs,), quarter, quarter, eb)
+    val = val.reshape(2, 2, 2, 2, d // 8, val.shape[-1])
+    val_z1 = val[:, :, :, 1]
+    val_kept = val[:, :, :, 0]
+    val_got_z1 = over_z(val_z1)
+    eb = ema_back((val_z1,), quarter, quarter, eb)
     done = {}
 
     def second(place, dep):
@@ -1288,10 +1278,10 @@
             done["z2"] = over_z2(ffn_z2)
             forced.append(ffn_z2)
         if opt["v2"] == place:
-            gx, gy = held((va_got_x, vb_got_y), dep)
-            va_y, vb_x = add(va_mine[1], gx[1]), add(vb_own[1], gy[1])
-            done["v"] = (gx, gy, over_tensor(va_y), over_x(vb_x))
-            forced += [va_y, vb_x]
+            gz = held(val_got_z1, dep)
+            val_x = add(val_kept[:, 1], gz[:, 1])
+            done["v"] = (gz, over_x(val_x))
+            forced.append(val_x)
         if opt.get("z1m", 6) == place:
             gy, gx = held((done["m"][2], done["m"][3]), dep)
             a_terms = [ma_mine[0], done["m"][0][0], gy]
@@ -1299,13 +1289,6 @@
             mid_z = jnp.stack([z_send(a_terms), z_send(b_terms)])
             done["mz"] = (z_keep(a_terms), z_keep(b_terms), over_z(mid_z))
             forced.append(mid_z)
-        if opt.get("z1v", 6) == place:
-            gy, gx = held((done["v"][2], done["v"][3]), dep)
-            a_terms = [va_mine[0], done["v"][0][0], gy]
-            b_terms = [vb_own[0], done["v"][1][0], gx]
-            val_z = jnp.concatenate([z_send(a_terms), z_send(b_terms)], axis=-1)
-            done["vz"] = (z_keep(a_terms), z_keep(b_terms), over_z(val_z))
-            forced.append(val_z)
         return forced
 
     f2 = second(2, eb[1])
@@ -1315,54 +1298,44 @@
     d_sig, _, _, sum_a, sum_b, sum_w = eb
     f4 = second(4, sum_a)
     sums = jnp.concatenate([sum_a, sum_b, sum_w, stats], axis=0)
-    others = over_core(sums)
+    others = over_z(sums)
     halves = n // ROWS // 2
     part = k_input_back(
-        after(sum_a, sums, *f4), dv_own, dv_oth, w_v, pv, d_sig, tokens, direct, 0, halves
-    )
+        after(sum_a, sums, done["z2"], *f4), dv_own, dv_oth, w_v, pv, d_sig, tokens, direct, 0, halves
+    )
+    ffn_got_z2 = held(done["z2"], part)
+    ffn_total = jnp.stack([total(*[v[0] for v in ts], ffn_got_z2[i]) for i, ts in enumerate(done["z"])])
+    ffn_rows = ffn_total.reshape(2, 2, d // 16, -1)
+    ffn_got = over_core(pick(ffn_rows, 1 - core, 1).astype(BF))
+    ffn_kept = pick(ffn_rows, core, 1)
     f5 = second(5, part)
     sums = sums + held(others, part)
-    others = over_tensor(sums)
+    others = over_z2(sums)
     input_grad = k_input_back(
         after(part, sums, *f5), dv_own, dv_oth, w_v, pv, d_sig, tokens, direct, halves, halves, part
     )
-    second(6, input_grad)
+    gz, gx = held(done["v"], input_grad)
+    val_y = add(val_kept[1, 0], gz[1, 0], gx[1])
+    val_terms = [val_kept[0, 0], gz[0, 0], gx[0], over_tensor(val_y)]
+    dn_terms, up_terms = done["z"]
+    ma_terms, mb_terms, mid_got_z = done["mz"]
+
+    def last(terms):
+        return total(*[v[0] for v in terms])
+
     sums = sums + held(others, input_grad)
+    sums = sums + over_core(sums)
     sums = sums + over_x(sums)
-    sums = sums + over_z(sums)
-    sums = sums + over_z2(sums)
-    c = va_mine.shape[-1]
-    dn_terms, up_terms = done["z"]
-    ffn_got_z2 = done["z2"]
-    ma_terms, mb_terms, mid_got_z = done["mz"]
-    va_terms, vb_terms, val_got_z = done["vz"]
+    mid_got_z = held(mid_got_z, sums)
     ma_terms, mb_terms = [*ma_terms, mid_got_z[0]], [*mb_terms, mid_got_z[1]]
     mid_z2 = jnp.stack([add(*[v[1] for v in ma_terms]), add(*[v[1] for v in mb_terms])])
     mid_got_z2 = over_z2(mid_z2)
-    va_terms, vb_terms = [*va_terms, val_got_z[..., :c]], [*vb_terms, val_got_z[..., c:]]
-    val_z2 = jnp.concatenate([add(*[v[1] for v in ts]) for ts in (va_terms, vb_terms)], axis=-1)
+    sums_got = over_tensor(held(sums, mid_z2))
+    val_terms[-1] = held(val_terms[-1], sums_got)
+    val_z2 = add(*[v[1] for v in val_terms])
     val_got_z2 = over_z2(val_z2)
-
-    def last(terms):
-        return total(*[v[0] for v in terms])
-
-    ffn_total = jnp.stack([total(last(dn_terms), ffn_got_z2[0]), total(last(up_terms), ffn_got_z2[1])])
-    ffn_rows = ffn_total.reshape(2, 2, d // 16, -1)
-    ffn_got = over_core(pick(ffn_rows, 1 - core, 1).astype(BF))
-    ffn_kept = pick(ffn_rows, core, 1)
-    mid_total = jnp.stack([total(last(ma_terms), mid_got_z2[0]), total(last(mb_terms), mid_got_z2[1])])
-    mid_rows = mid_total.reshape(2, 2, d // 16, -1)
-    mid_got = over_core(pick(mid_rows, 1 - core, 1).astype(BF))
-    mid_kept = pick(mid_rows, core, 1)
-    val_total = jnp.concatenate([last(va_terms), last(vb_terms)], axis=-1) + val_got_z2.astype(F32)
-    val_sent, val_kept = core_split(val_total)
-    val_got = over_core(val_sent)
+    sums = held(sums + sums_got, val_z2)
     down_t, up = joined(ffn_kept[0], ffn_got[0]), joined(ffn_kept[1], ffn_got[1])
-    tn = d // 4
-    uh_t, gamma = (joined(mid_kept[i][:, : 2 * tn], mid_got[i][:, : 2 * tn]) for i in range(2))
-    wh_t, phi_t = (joined(mid_kept[i][:, 2 * tn :], mid_got[i][:, 2 * tn :]) for i in range(2))
-    value = joined(val_kept[:, : 2 * c], val_got[:, : 2 * c])
-    z_grad = val_kept[:, 2 * c :]
     gh = sum_a.shape[0]
 
     def own_half(v):
@@ -1379,9 +1352,25 @@
     decay_grad = feed * ema_eta * tot_b
     alpha_grad = (feed_grad * ema_beta - decay_grad * damp) * rate * (1.0 - rate)
     delta_grad = -decay_grad * rate * damp * (1.0 - damp)
+    params = (alpha_grad, delta_grad, feed_grad * rate, feed * tot_a, omega_grad)
+    down_grad = down_t.T
+    mid_got_z2, val_got_z2 = held((mid_got_z2, val_got_z2), params, down_grad, up)
+    mid_total = jnp.stack([total(last(ma_terms), mid_got_z2[0]), total(last(mb_terms), mid_got_z2[1])])
+    mid_rows = mid_total.reshape(2, 2, d // 16, -1)
+    mid_got = over_core(pick(mid_rows, 1 - core, 1).astype(BF))
+    mid_kept = pick(mid_rows, core, 1)
+    val_total = last(val_terms) + val_got_z2.astype(F32)
+    val_sent, val_rows = core_split(val_total)
+    zw = dz.shape[1]
+    val_got = over_core(val_sent)
+    tn = d // 4
+    uh_t, gamma = (joined(mid_kept[i][:, : 2 * tn], mid_got[i][:, : 2 * tn]) for i in range(2))
+    wh_t, phi_t = (joined(mid_kept[i][:, 2 * tn :], mid_got[i][:, 2 * tn :]) for i in range(2))
+    value = joined(val_rows[:, :-zw], val_got[:, :-zw])
+    z_grad = val_rows[:, -zw:]
     return (
-        output, input_grad, alpha_grad, delta_grad, feed_grad * rate, feed * tot_a, omega_grad,
-        z_grad, zsum[0:2], zsum[2:4], value, gamma, uh_t.T, wh_t.T, phi_t.T, up, down_t.T,
+        output, input_grad, *params,
+        z_grad, zsum[0:2], zsum[2:4], value, gamma, uh_t.T, wh_t.T, phi_t.T, up, down_grad,
     )
 
 

time: 477 us -> 460 us (0.964)
  waiting for transfers between devices: 65 us -> 55.8 us
  Pallas kernels: 270 us -> 265 us
    ppermute x55 -> x53, waiting for transfers between devices: 65 us -> 55.8 us  [swap(): return lax.ppermute(values, axis, [(i, i ^ bit) for i in range(size)])]
    unnamed x227, local copies, waits for them, and re-layouts: 26.9 us -> 20.9 us
    convert_element_type x16 -> x13, other arithmetic: 22 us -> 24.5 us  [add(): return total(*values).astype(BF)]
    ppermute x55 -> x53, starting transfers between devices: 48.6 us -> 46.9 us  [swap(): return lax.ppermute(values, axis, [(i, i ^ bit) for i in range(size)])]
  transfers between devices with their start and end apart: 55 -> 53, of which waited for: 14 -> 14; matrix products, arithmetic and copies ran while one was open for 11% -> 12% of each run, Pallas kernels for 57% -> 58%
where the time goes in v6:
time: 460 us; the launch traced here: 453 us
  Pallas kernels  265 us (58%)
  waiting for transfers between devices  55.8 us (12%)
  starting transfers between devices  46.9 us (10%)
  local copies, waits for them, and re-layouts  41.5 us (9%)
  other arithmetic  41.4 us (9%)
    pallas_call x28, Pallas kernels, run(): pl.pallas_call(body, out_shape=out_shape, grid_spec=pltpu.PrefetchScalarG...  265 us
    ppermute x53, waiting for transfers between devices, swap(): return lax.ppermute(values, axis, [(i, i ^ bit) for i in range(size)])  55.8 us
    ppermute x53, starting transfers between devices, swap(): return lax.ppermute(values, axis, [(i, i ^ bit) for i in range(size)])  46.9 us
    convert_element_type x13, other arithmetic, add(): return total(*values).astype(BF)  24.5 us
    unnamed x227, local copies, waits for them, and re-layouts  20.9 us
  transfers between devices with their start and end apart: 53, of which 14 were waited for; matrix products, arithmetic and copies ran while one was open for 12% of the time, Pallas kernels for 58%

profile of v6, /device:TPU:0, one launch (start us, length us, event | category | flops | bytes accessed | tf_op | source)
XLA Modules:
  0.0 453.4 jit_solution(2957610862123389668)
XLA Ops:
  1.8 3.0 collective-permute-start.1
  5.5 2.1 pack_params.1.own_ref
  7.7 5.7 %pieces.1 = (bf16[256,1024]{1,0:T(8,128)(2,1)}, bf16[256,1024]{1,0:T(8,128)(2,1)}, bf16[256,1024]{1,0:T(8,128)(2,1)}, bf16[256,2048]{1,0:T(8,128)(2,1)}, bf16[1024,1024]{1,0:T(8,128)(2,1)}) custom-call(s32[16]{0:T(128)} %stack.105.s, bf16[1024,1024]{1,0:T(8,128)(2,1)} %wo.5, bf16[1024,1024]{1,0:T(8,128)(2,1)} %uo.3, bf16[512,1024]{1,0:T(8,128)(2,1)} %ho.3, ...), custom_call_target="tpu_custom_call" | custom-call | flops 100000000 | bytes 235929600 | tf_op jit(solution)/shard_map/pieces/pallas_call | solution.py:351
  13.4 5.3 %value_own.1 = (bf16[1024,1024]{1,0:T(8,128)(2,1)S(1)}, bf16[1024,1024]{1,0:T(8,128)(2,1)S(1)}, bf16[1024,1024]{1,0:T(8,128)(2,1)S(1)}) custom-call(s32[16]{0:T(128)S(1)} %copy-done.6, bf16[1024,1024]{1,0:T(8,128)(2,1)S(1)} %copy-done.9, bf16[1024,1024]{1,0:T(8,128)(2,1)S(1)} %copy-done.4), custom_call_target="tpu_custom_call" | custom-call | flops 21474836480 | bytes 104857600 | tf_op jit(solution)/shard_map/value_own/pallas_call | solution.py:351
  23.6 2.4 ema_params.1
  28.3 6.8 %ema_forward.2 = (bf16[1024,1024]{1,0:T(8,128)(2,1)S(1)}, bf16[1024,1024]{1,0:T(8,128)(2,1)S(1)}, f32[128,128]{1,0:T(8,128)S(1)}) custom-call(s32[16]{0:T(128)S(1)} %copy-done.7, bf16[1024,1024]{1,0:T(8,128)(2,1)S(1)} %get-tuple-element.181.x_ref, f32[128,128]{1,0:T(8,128)S(1)} %copy-done.26, f32[128,128]{1,0:T(8,128)S(1)} %copy-done.29, f32[8,128]{1,0:T(8,128)S(1)} %copy-done.50), custom_call_target="tpu_custom_call" | custom-call | flops 99999997952 | bytes 64921600 | tf_op jit(solution)/shard_map/ema_forward/pallas_call | solution.py:351
  36.7 7.2 %ema_forward.3 = (bf16[1024,1024]{1,0:T(8,128)(2,1)S(1)}, bf16[1024,1024]{1,0:T(8,128)(2,1)S(1)}, f32[128,128]{1,0:T(8,128)}) custom-call(s32[16]{0:T(128)S(1)} %copy-done.7, bf16[1024,1024]{1,0:T(8,128)(2,1)S(1)} %get-tuple-element.181.x_ref, f32[128,128]{1,0:T(8,128)S(1)} %copy-done.27, ...), custom_call_target="tpu_custom_call", output_to_operand_aliasing={{0}: (6, {}), {1}: (7, {})} | custom-call | flops 99999997952 | bytes 107520000 | tf_op jit(solution)/shard_map/ema_forward/pallas_call | solution.py:351
  52.2 4.8 %act_other.1 = (bf16[1024,1024]{1,0:T(8,128)(2,1)S(1)}, bf16[1024,1024]{1,0:T(8,128)(2,1)S(1)}) custom-call(s32[16]{0:T(128)S(1)} %copy-done.7, bf16[1024,1024]{1,0:T(8,128)(2,1)S(1)} %get-tuple-element.181.x_ref, bf16[256,1024]{1,0:T(8,128)(2,1)S(1)} %collective-permute-done.1.p0.w0, bf16[256,1024]{1,0:T(8,128)(2,1)S(1)} %collective-permute-done.2.p1.w1, ...), custom_call_target="tpu_custom_call" | custom-call | flops 21474836480 | bytes 83886080 | tf_op jit(solution)/shard_map/act_other/pallas_call | solution.py:351
  59.7 4.4 collective-permute-done.6.w1
  67.0 7.5 %collective-permute-done.13.h0.f0 = bf16[256,1024]{1,0:T(8,128)(2,1)S(1)} collective-permute-done((bf16[256,1024]{1,0:T(8,128)(2,1)S(1)}, bf16[256,1024]{1,0:T(8,128)(2,1)S(1)}, u32[]{:S(2)}, u32[]{:S(2)}) %collective-permute-start.13) | collective-permute-done | bytes 524320 | tf_op jit(solution)/shard_map/ppermute | solution.py:1080
  77.1 16.7 %attend.1 = (bf16[1024,1024]{1,0:T(8,128)(2,1)}, bf16[1024,1024]{1,0:T(8,128)(2,1)}, bf16[1024,1024]{1,0:T(8,128)(2,1)}, bf16[1024,1024]{1,0:T(8,128)(2,1)}, bf1...) custom-call(s32[16]{0:T(128)} %stack.105.s, bf16[1024,128]{1,0:T(8,128)(2,1)} %copy-done.31, ...), custom_call_target="tpu_custom_call" | custom-call | flops 71470940160 | bytes 256901120 | tf_op jit(solution)/shard_map/attend/pallas_call | solution.py:351
  99.8 18.8 %gate.1 = (bf16[1024,1024]{1,0:T(8,128)(2,1)}, bf16[1024,1024]{1,0:T(8,128)(2,1)}, bf16[1024,1024]{1,0:T(8,128)(2,1)}, bf16[1024,1024]{1,0:T(8,128)(2,1)}, bf16[1024,1024]{1,0:T(8,128)(2,1)}) custom-call(s32[16]{0:T(128)} %stack.105.s, bf16[1024,1024]{1,0:T(8,128)(2,1)} %get-tuple-element.205.go.refs_1_, bf16[1024,1024]{1,0:T(8,128)(2,1)} %get-tuple-element.206.gt.refs_2_, ...), custom_call_target="tpu_custom_call" | custom-call | flops 85899345920 | bytes 293601280 | tf_op jit(solution)/shard_map/gate/pallas_call | solution.py:351
  118.7 20.3 %ffn.4 = (bf16[1024,1024]{1,0:T(8,128)(2,1)}, bf16[1024,1024]{1,0:T(8,128)(2,1)}, bf16[2,2,512,1024]{3,2,1,0:T(8,128)(2,1)}) custom-call(s32[16]{0:T(128)} %stack.105.s, bf16[1024,1024]{1,0:T(8,128)(2,1)} %get-tuple-element.219.low_ref, bf16[1024,1024]{1,0:T(8,128)(2,1)} %c_ref.9, bf16[1024,2048]{1,0:T(8,128)(2,1)} %refs_0_.5, bf16[2048,1024]{1,0:T(8,128)(2,1)} %refs_1_.5), custom_call_target="tpu_custom_call" | custom-call | flops 128849018880 | bytes 209715200 | tf_op jit(solution)/shard_map/ffn/pallas_call | solution.py:351
  139.0 20.7 %ffn.5 = (bf16[1024,1024]{1,0:T(8,128)(2,1)}, bf16[1024,1024]{1,0:T(8,128)(2,1)}, bf16[512,1024]{1,0:T(8,128)(2,1)}, bf16[512,1024]{1,0:T(8,128)(2,1)}, bf16[512...) custom-call(s32[16]{0:T(128)} %stack.105.s, bf16[1024,1024]{1,0:T(8,128)(2,1)} %get-tuple-element.219.low_ref, ...), custom_call_target="tpu_custom_call" | custom-call | flops 128849018880 | bytes 251658240 | tf_op jit(solution)/shard_map/ffn/pallas_call | solution.py:351
  160.8 2.9 fusion.5
  168.8 21.2 %ffn.6 = (bf16[1024,1024]{1,0:T(8,128)(2,1)}, bf16[1024,1024]{1,0:T(8,128)(2,1)}, bf16[2,2,512,1024]{3,2,1,0:T(8,128)(2,1)}) custom-call(s32[16]{0:T(128)} %stack.105.s, bf16[1024,1024]{1,0:T(8,128)(2,1)} %get-tuple-element.219.low_ref, bf16[1024,1024]{1,0:T(8,128)(2,1)} %c_ref.9, bf16[256,2048]{1,0:T(8,128)(2,1)} %collective-permute-done.18.refs_0_, ...), custom_call_target="tpu_custom_call" | custom-call | flops 128849018880 | bytes 230686720 | tf_op jit(solution)/shard_map/ffn/pallas_call | solution.py:351
  190.4 21.1 %ffn.7 = (bf16[1024,1024]{1,0:T(8,128)(2,1)}, bf16[1024,1024]{1,0:T(8,128)(2,1)}, bf16[512,1024]{1,0:T(8,128)(2,1)}, bf16[512,1024]{1,0:T(8,128)(2,1)}, bf16[2,512,1024]{2,1,0:T(8,128)(2,1)}) custom-call(s32[16]{0:T(128)} %stack.105.s, bf16[1024,1024]{1,0:T(8,128)(2,1)} %get-tuple-element.219.low_ref, bf16[1024,1024]{1,0:T(8,128)(2,1)} %c_ref.9, ...), custom_call_target="tpu_custom_call" | custom-call | flops 128849018880 | bytes 230686720 | tf_op jit(solution)/shard_map/ffn/pallas_call | solution.py:351
  211.5 3.1 fusion.36
  215.7 2.1 copy-done.81
  217.7 2.3 fusion
  221.1 27.1 %mid_back.1 = (bf16[1024,1024]{1,0:T(8,128)(2,1)}, bf16[1024,1024]{1,0:T(8,128)(2,1)}, bf16[1024,1024]{1,0:T(8,128)(2,1)}, bf16[1024,1024]{1,0:T(8,128)(2,1)}, b...) custom-call(s32[16]{0:T(128)} %stack.105.s, ...), custom_call_target="tpu_custom_call" | custom-call | flops 128849018880 | bytes 566231040 | tf_op jit(solution)/shard_map/mid_back/pallas_call | solution.py:351
  248.3 3.3 fusion.3
  254.8 5.5 %weight_mid.4 = bf16[2,2,512,768]{3,2,1,0:T(8,128)(2,1)S(1)} custom-call(s32[16]{0:T(128)S(1)} %copy-done.8, bf16[1024,1024]{1,0:T(8,128)(2,1)S(1)} %copy-done.63, bf16[1024,1024]{1,0:T(8,128)(2,1)S(1)} %copy-done.59, bf16[1024,1024]{1,0:T(8,128)(2,1)S(1)} %copy-done.61, bf16[1024,1024]{1,0:T(8,128)(2,1)S(1)} %copy-done.25, bf16[1024,1024]{1,0:T(8,128)(2,1)S(1)} %copy-done.25), custom_call_target="tpu_custom_call" | custom-call | flops 32212254720 | bytes 136314880 | tf_op jit(solution)/shard_map/weight_mid/pallas_call | solution.py:351
  260.4 5.9 %weight_mid.5 = bf16[2,2,512,768]{3,2,1,0:T(8,128)(2,1)S(1)} custom-call(s32[16]{0:T(128)S(1)} %copy-done.8, bf16[1024,1024]{1,0:T(8,128)(2,1)S(1)} %copy-done.25, bf16[1024,1024]{1,0:T(8,128)(2,1)S(1)} %copy-done.53, bf16[1024,1024]{1,0:T(8,128)(2,1)S(1)} %copy-done.55, bf16[1024,1024]{1,0:T(8,128)(2,1)S(1)} %copy-done.57, ...), custom_call_target="tpu_custom_call" | custom-call | flops 32212254720 | bytes 157286400 | tf_op jit(solution)/shard_map/weight_mid/pallas_call | solution.py:351
  269.5 9.7 %attend_back.1 = (bf16[1024,1024]{1,0:T(8,128)(2,1)S(1)}, bf16[1024,1024]{1,0:T(8,128)(2,1)S(1)}, bf16[1024,128]{1,0:T(8,128)(2,1)S(1)}, f32[8,128]{1,0:T(8,128)S(1)}) custom-call(s32[16]{0:T(128)S(1)} %copy-done.8, bf16[1024,1024]{1,0:T(8,128)(2,1)S(1)} %copy-done.65, bf16[1024,1024]{1,0:T(8,128)(2,1)S(1)} %copy-done.66, bf16[1024,1024]{1,0:T(8,128)(2,1)S(1)} %copy-done.67, ...), custom_call_target="tpu_custom_call" | custom-call | flops 53687091200 | bytes 201902080 | tf_op jit(solution)/shard_map/attend_back/pallas_call | solution.py:351
  279.2 4.0 fusion.1
  285.2 6.4 %weight_mid.6 = (bf16[2,512,768]{2,1,0:T(8,128)(2,1)}, bf16[2,512,768]{2,1,0:T(8,128)(2,1)S(1)}) custom-call(s32[16]{0:T(128)S(1)} %copy-done.8, bf16[1024,1024]{1,0:T(8,128)(2,1)S(1)} %copy-done.64, bf16[1024,1024]{1,0:T(8,128)(2,1)S(1)} %copy-done.60, bf16[1024,1024]{1,0:T(8,128)(2,1)S(1)} %copy-done.62, bf16[1024,1024]{1,0:T(8,128)(2,1)S(1)} %copy-done.25, ...), custom_call_target="tpu_custom_call" | custom-call | flops 32212254720 | bytes 167772160 | tf_op jit(solution)/shard_map/weight_mid/pallas_call | solution.py:351
  293.1 6.8 %weight_mid.7 = (bf16[2,512,768]{2,1,0:T(8,128)(2,1)S(1)}, bf16[2,512,768]{2,1,0:T(8,128)(2,1)}) custom-call(s32[16]{0:T(128)S(1)} %copy-done.8, bf16[1024,1024]{1,0:T(8,128)(2,1)S(1)} %copy-done.25, bf16[1024,1024]{1,0:T(8,128)(2,1)S(1)} %copy-done.54, bf16[1024,1024]{1,0:T(8,128)(2,1)S(1)} %copy-done.56, bf16[1024,1024]{1,0:T(8,128)(2,1)S(1)} %copy-done.58, ...), custom_call_target="tpu_custom_call" | custom-call | flops 32212254720 | bytes 188743680 | tf_op jit(solution)/shard_map/weight_mid/pallas_call | solution.py:351
  300.0 3.7 weight_value.2
  303.8 5.5 %collective-permute-done.30 = bf16[512,1024]{1,0:T(8,128)(2,1)S(1)} collective-permute-done((bf16[512,1024]{1,0:T(8,128)(2,1)S(1)}, bf16[512,1024]{1,0:T(8,128)(2,1)S(1)}, u32[]{:S(2)}, u32[]{:S(2)}) %collective-permute-start.30) | collective-permute-done | bytes 1048608 | tf_op jit(solution)/shard_map/ppermute | solution.py:1080
  309.3 1.9 fusion.10
  314.5 7.8 %ema_backward.4 = (f32[1024,1024]{1,0:T(8,128)S(1)}, f32[128,128]{1,0:T(8,128)S(1)}, f32[128,128]{1,0:T(8,128)S(1)}, f32[128,128]{1,0:T(8,128)S(1)}, f32[128,128]{1,0:T(8,128)S(1)}, /*index=5*/f32[8,128]{1,0:T(8,128)S(1)}) custom-call(s32[16]{0:T(128)S(1)} %copy-done.8, bf16[1024,1024]{1,0:T(8,128)(2,1)S(1)} %copy-done.41, ...), custom_call_target="tpu_custom_call" | custom-call | flops 99999997952 | bytes 114114560 | tf_op jit(solution)/shard_map/ema_backward/pallas_call | solution.py:351
  325.2 3.9 weight_value.3
  332.1 7.8 %ema_backward.5 = (f32[1024,1024]{1,0:T(8,128)S(1)}, f32[128,128]{1,0:T(8,128)S(1)}, f32[128,128]{1,0:T(8,128)S(1)}, f32[128,128]{1,0:T(8,128)S(1)}, f32[128,128]{1,0:T(8,128)S(1)}, /*index=5*/f32[8,128]{1,0:T(8,128)S(1)}) custom-call(s32[16]{0:T(128)S(1)} %copy-done.8, bf16[1024,1024]{1,0:T(8,128)(2,1)S(1)} %copy-done.41, ...), custom_call_target="tpu_custom_call", output_to_operand_aliasing={{0}: (14, {})} | custom-call | flops 99999997952 | bytes 158720000 | tf_op jit(solution)/shard_map/ema_backward/pallas_call | solution.py:351
  339.9 7.8 %ema_backward.6 = (f32[1024,1024]{1,0:T(8,128)S(1)}, f32[128,128]{1,0:T(8,128)S(1)}, f32[128,128]{1,0:T(8,128)S(1)}, f32[128,128]{1,0:T(8,128)S(1)}, f32[128,128]{1,0:T(8,128)S(1)}, /*index=5*/f32[8,128]{1,0:T(8,128)S(1)}) custom-call(s32[16]{0:T(128)S(1)} %copy-done.8, bf16[1024,1024]{1,0:T(8,128)(2,1)S(1)} %copy-done.41, ...), custom_call_target="tpu_custom_call", output_to_operand_aliasing={{0}: (14, {})} | custom-call | flops 99999997952 | bytes 158720000 | tf_op jit(solution)/shard_map/ema_backward/pallas_call | solution.py:351
  347.8 9.5 %collective-permute-done.34 = bf16[2,512,768]{2,1,0:T(8,128)(2,1)} collective-permute-done((bf16[2,512,768]{2,1,0:T(8,128)(2,1)}, bf16[2,512,768]{2,1,0:T(8,128)(2,1)}, u32[]{:S(2)}, u32[]{:S(2)}) %collective-permute-start.34) | collective-permute-done | bytes 1572896 | tf_op jit(solution)/shard_map/ppermute | solution.py:1080
  361.9 2.7 collective-permute-start.36
  366.2 8.3 %ema_backward.7 = (f32[1024,1024]{1,0:T(8,128)S(1)}, f32[128,128]{1,0:T(8,128)}, f32[128,128]{1,0:T(8,128)}, f32[128,128]{1,0:T(8,128)S(1)}, f32[128,128]{1,0:T(8,128)S(1)}, /*index=5*/f32[8,128]{1,0:T(8,128)S(1)}) custom-call(s32[16]{0:T(128)S(1)} %copy-done.8, bf16[1024,1024]{1,0:T(8,128)(2,1)S(1)} %copy-done.41, ...), custom_call_target="tpu_custom_call", output_to_operand_aliasing={{0}: (14, {})} | custom-call | flops 99999997952 | bytes 158720000 | tf_op jit(solution)/shard_map/ema_backward/pallas_call | solution.py:351
  374.5 2.2 slice.483
  376.7 2.2 slice.488
  384.6 5.1 %input_back.2.refs_0_ = f32[1024,1024]{1,0:T(8,128)} custom-call(s32[16]{0:T(128)S(1)} %copy-done.8, bf16[1024,1024]{1,0:T(8,128)(2,1)S(1)} %copy-done.37, bf16[1024,1024]{1,0:T(8,128)(2,1)S(1)} %copy-done.39, bf16[1024,1024]{1,0:T(8,128)(2,1)S(1)} %copy-done.5, bf16[256,1024]{1,0:T(8,128)(2,1)S(1)} %copy-done.12, bf16[256,1024]{1,0:T(8,128)(2,1)S(1)} %copy-done.14, ...), custom_call_target="tpu_custom_call" | custom-call | flops 21474836480 | bytes 209715200 | tf_op jit(solution)/shard_map/input_back/pallas_call | solution.py:351
  389.9 1.8 fusion.16
  393.0 3.6 collective-permute-start.44
  398.5 4.9 %input_back.3 = f32[1024,1024]{1,0:T(8,128)} custom-call(s32[16]{0:T(128)S(1)} %copy-done.8, bf16[1024,1024]{1,0:T(8,128)(2,1)S(1)} %copy-done.37, bf16[1024,1024]{1,0:T(8,128)(2,1)S(1)} %copy-done.39, bf16[1024,1024]{1,0:T(8,128)(2,1)S(1)} %copy-done.5, bf16[256,1024]{1,0:T(8,128)(2,1)S(1)} %copy-done.12, ...), custom_call_target="tpu_custom_call", output_to_operand_aliasing={{}: (11, {})} | custom-call | flops 21474836480 | bytes 251658240 | tf_op jit(solution)/shard_map/input_back/pallas_call | solution.py:351
  405.7 5.3 %collective-permute-done.43 = f32[272,128]{1,0:T(8,128)S(1)} collective-permute-done((f32[272,128]{1,0:T(8,128)S(1)}, f32[272,128]{1,0:T(8,128)S(1)}, u32[]{:S(2)}, u32[]{:S(2)}) %collective-permute-start.43) | collective-permute-done | bytes 139296 | tf_op jit(solution)/shard_map/ppermute | solution.py:1080
  419.2 5.1 %collective-permute-done.45 = f32[272,128]{1,0:T(8,128)S(1)} collective-permute-done((f32[272,128]{1,0:T(8,128)S(1)}, f32[272,128]{1,0:T(8,128)S(1)}, u32[]{:S(2)}, u32[]{:S(2)}) %collective-permute-start.45) | collective-permute-done | bytes 139296 | tf_op jit(solution)/shard_map/ppermute | solution.py:1080
  424.4 1.8 fusion.22
  434.1 10.3 %collective-permute-done.49 = bf16[128,640]{1,0:T(8,128)(2,1)} collective-permute-done((bf16[128,640]{1,0:T(8,128)(2,1)}, bf16[128,640]{1,0:T(8,128)(2,1)}, u32[]{:S(2)}, u32[]{:S(2)}) %collective-permute-start.49) | collective-permute-done | bytes 163872 | tf_op jit(solution)/shard_map/ppermute | solution.py:1080
  (385 shorter events, 102.4 us)
Async XLA Ops:
  1.8 33.3 %collective-permute-start.1 = (bf16[256,1024]{1,0:T(8,128)(2,1)S(1)}, bf16[256,1024]{1,0:T(8,128)(2,1)S(1)}, u32[]{:S(2)}, u32[]{:S(2)}) collective-permute-start(bf16[256,1024]{1,0:T(8,128)(2,1)S(1)} %constant_dynamic-slice_fusion), channel_id=1, source_target_pairs={{0,1},{1,0},{2,3},{3,2},{4,5},{5,4},{6,7},{7,6},{8,9},{9,8},{10,11... | collective-permute-start | bytes 1572872 | tf_op jit(solution)/shard_map/ppermute | solution.py:1080
  7.6 15.3 %collective-permute-start = (f32[72,512]{1,0:T(8,128)}, f32[72,512]{1,0:T(8,128)S(1)}, u32[]{:S(2)}, u32[]{:S(2)}) collective-permute-start(f32[72,512]{1,0:T(8,128)} %pack_params.1.own_ref), channel_id=1, source_target_pairs={{0,1},{1,0},{2,3},{3,2},{4,5},{5,4},{6,7},{7,6},{8,9},{9,8},{10,11... | collective-permute-start | bytes 442376 | tf_op jit(solution)/shard_map/ppermute | solution.py:1080
  21.4 29.1 %collective-permute-start.5 = (bf16[256,1024]{1,0:T(8,128)(2,1)}, bf16[256,1024]{1,0:T(8,128)(2,1)}, u32[]{:S(2)}, u32[]{:S(2)}) collective-permute-start(bf16[256,1024]{1,0:T(8,128)(2,1)} %get-tuple-element.198), channel_id=1, source_target_pairs={{0,1},{1,0},{2,3},{3,2},{4,5},{5,4},{6,7},{7,6},{8,9},{9,8},{10,11... | collective-permute-start | bytes 1572872 | tf_op jit(solution)/shard_map/ppermute | solution.py:1080
  35.1 12.9 %collective-permute-start.2 = (bf16[256,1024]{1,0:T(8,128)(2,1)S(1)}, bf16[256,1024]{1,0:T(8,128)(2,1)S(1)}, u32[]{:S(2)}, u32[]{:S(2)}) collective-permute-start(bf16[256,1024]{1,0:T(8,128)(2,1)S(1)} %collective-permute-done.1.p0.w0), channel_id=1, source_target_pairs={{0,4},{2,6},{4,0},{6,2},{8,12},{10,14},{12,8},{14,10},{16,20},{18,... | collective-permute-start | bytes 1572872 | tf_op jit(solution)/shard_map/ppermute | solution.py:1080
  48.0 4.1 collective-permute-start.4
  48.5 17.0 %collective-permute-start.9 = (bf16[256,1024]{1,0:T(8,128)(2,1)S(1)}, bf16[256,1024]{1,0:T(8,128)(2,1)S(1)}, u32[]{:S(2)}, u32[]{:S(2)}) collective-permute-start(bf16[256,1024]{1,0:T(8,128)(2,1)S(1)} %copy-done.110), channel_id=1, source_target_pairs={{0,1},{1,0},{2,3},{3,2},{4,5},{5,4},{6,7},{7,6},{8,9},{9,8},{10,11... | collective-permute-start | bytes 1572872 | tf_op jit(solution)/shard_map/ppermute | solution.py:1080
  49.5 25.1 %collective-permute-start.13 = (bf16[256,1024]{1,0:T(8,128)(2,1)S(1)}, bf16[256,1024]{1,0:T(8,128)(2,1)S(1)}, u32[]{:S(2)}, u32[]{:S(2)}) collective-permute-start(bf16[256,1024]{1,0:T(8,128)(2,1)S(1)} %copy-done.109), channel_id=1, source_target_pairs={{0,1},{1,0},{2,3},{3,2},{4,5},{5,4},{6,7},{7,6},{8,9},{9,8},{10,11... | collective-permute-start | bytes 1572872 | tf_op jit(solution)/shard_map/ppermute | solution.py:1080
  50.6 13.5 %collective-permute-start.6 = (bf16[256,1024]{1,0:T(8,128)(2,1)}, bf16[256,1024]{1,0:T(8,128)(2,1)S(1)}, u32[]{:S(2)}, u32[]{:S(2)}) collective-permute-start(bf16[256,1024]{1,0:T(8,128)(2,1)} %collective-permute-done.5.w0), channel_id=1, source_target_pairs={{0,8},{2,10},{4,12},{6,14},{8,0},{10,2},{12,4},{14,6},{16,24},{18,... | collective-permute-start | bytes 1572872 | tf_op jit(solution)/shard_map/ppermute | solution.py:1080
  64.0 12.1 %collective-permute-start.7 = (bf16[256,1024]{1,0:T(8,128)(2,1)}, bf16[256,1024]{1,0:T(8,128)(2,1)S(1)}, u32[]{:S(2)}, u32[]{:S(2)}) collective-permute-start(bf16[256,1024]{1,0:T(8,128)(2,1)} %collective-permute-done.5.w0), channel_id=1, source_target_pairs={{0,2},{2,0},{4,6},{6,4},{8,10},{10,8},{12,14},{14,12},{16,18},{18,... | collective-permute-start | bytes 1572872 | tf_op jit(solution)/shard_map/ppermute | solution.py:1080
  64.0 12.1 %collective-permute-start.8 = (bf16[256,1024]{1,0:T(8,128)(2,1)S(1)}, bf16[256,1024]{1,0:T(8,128)(2,1)S(1)}, u32[]{:S(2)}, u32[]{:S(2)}) collective-permute-start(bf16[256,1024]{1,0:T(8,128)(2,1)S(1)} %collective-permute-done.6.w1), channel_id=1, source_target_pairs={{0,2},{2,0},{4,6},{6,4},{8,10},{10,8},{12,14},{14,12},{16,18},{18,... | collective-permute-start | bytes 1572872 | tf_op jit(solution)/shard_map/ppermute | solution.py:1080
  64.6 31.6 %collective-permute-start.18 = (bf16[256,2048]{1,0:T(8,128)(2,1)S(1)}, bf16[256,2048]{1,0:T(8,128)(2,1)}, u32[]{:S(2)}, u32[]{:S(2)}) collective-permute-start(bf16[256,2048]{1,0:T(8,128)(2,1)S(1)} %copy-done.97), channel_id=1, source_target_pairs={{0,1},{1,0},{2,3},{3,2},{4,5},{5,4},{6,7},{7,6},{8,9},{9,8},{10,11... | collective-permute-start | bytes 3145736 | tf_op jit(solution)/shard_map/ppermute | solution.py:1080
  65.5 28.9 %collective-permute-start.10 = (bf16[256,1024]{1,0:T(8,128)(2,1)S(1)}, bf16[256,1024]{1,0:T(8,128)(2,1)S(1)}, u32[]{:S(2)}, u32[]{:S(2)}) collective-permute-start(bf16[256,1024]{1,0:T(8,128)(2,1)S(1)} %collective-permute-done.9.u0), channel_id=1, source_target_pairs={{0,4},{2,6},{4,0},{6,2},{8,12},{10,14},{12,8},{14,10},{16,20},{18,... | collective-permute-start | bytes 1572872 | tf_op jit(solution)/shard_map/ppermute | solution.py:1080
  74.6 19.2 %collective-permute-start.14 = (bf16[256,1024]{1,0:T(8,128)(2,1)S(1)}, bf16[256,1024]{1,0:T(8,128)(2,1)S(1)}, u32[]{:S(2)}, u32[]{:S(2)}) collective-permute-start(bf16[256,1024]{1,0:T(8,128)(2,1)S(1)} %collective-permute-done.13.h0.f0), channel_id=1, source_target_pairs={{0,8},{2,10},{4,12},{6,14},{8,0},{10,2},{12,4},{14,6},{16,24},{18,... | collective-permute-start | bytes 1572872 | tf_op jit(solution)/shard_map/ppermute | solution.py:1080
  93.9 4.8 %collective-permute-start.16 = (bf16[256,1024]{1,0:T(8,128)(2,1)S(1)}, bf16[256,1024]{1,0:T(8,128)(2,1)S(1)}, u32[]{:S(2)}, u32[]{:S(2)}) collective-permute-start(bf16[256,1024]{1,0:T(8,128)(2,1)S(1)} %collective-permute-done.14.h1.f1), channel_id=1, source_target_pairs={{0,2},{2,0},{4,6},{6,4},{8,10},{10,8},{12,14},{14,12},{16,18},{18,... | collective-permute-start | bytes 1572872 | tf_op jit(solution)/shard_map/ppermute | solution.py:1080
  94.4 4.3 collective-permute-start.11
  94.5 4.1 collective-permute-start.12
  96.2 63.6 %collective-permute-start.22 = (bf16[1024,1024]{1,0:T(8,128)(2,1)}, bf16[1024,1024]{1,0:T(8,128)(2,1)}, u32[]{:S(2)}, u32[]{:S(2)}) collective-permute-start(bf16[1024,1024]{1,0:T(8,128)(2,1)} %get-tuple-element.233), channel_id=1, source_target_pairs={{0,1},{1,0},{2,3},{3,2},{4,5},{5,4},{6,7},{7,6},{8,9},{9,8},{10,11... | collective-permute-start | bytes 6291464 | tf_op jit(solution)/shard_map/ppermute | solution.py:1080
  97.1 63.2 %collective-permute-start.19 = (bf16[256,2048]{1,0:T(8,128)(2,1)}, bf16[256,2048]{1,0:T(8,128)(2,1)}, u32[]{:S(2)}, u32[]{:S(2)}) collective-permute-start(bf16[256,2048]{1,0:T(8,128)(2,1)} %collective-permute-done.18.refs_0_), channel_id=1, source_target_pairs={{0,4},{2,6},{4,0},{6,2},{8,12},{10,14},{12,8},{14,10},{16,20},{18,... | collective-permute-start | bytes 3145736 | tf_op jit(solution)/shard_map/ppermute | solution.py:1080
  139.0 21.8 %collective-permute-start.17 = (bf16[2,2,512,1024]{3,2,1,0:T(8,128)(2,1)}, bf16[2,2,512,1024]{3,2,1,0:T(8,128)(2,1)}, u32[]{:S(2)}, u32[]{:S(2)}) collective-permute-start(bf16[2,2,512,1024]{3,2,1,0:T(8,128)(2,1)} %get-tuple-element.225), channel_id=1, source_target_pairs={{0,2},{2,0},{4,6},{6,4},{8,10},{10,8},{12,14},{14,12},{16,18},{18,... | collective-permute-start | bytes 12582920 | tf_op jit(solution)/shard_map/ppermute | solution.py:1080
  159.8 7.7 %collective-permute-start.23 = (bf16[1024,1024]{1,0:T(8,128)(2,1)}, bf16[1024,1024]{1,0:T(8,128)(2,1)S(1)}, u32[]{:S(2)}, u32[]{:S(2)}) collective-permute-start(bf16[1024,1024]{1,0:T(8,128)(2,1)} %collective-permute-done.22.refs_4_), channel_id=1, source_target_pairs={{0,2},{2,0},{4,6},{6,4},{8,10},{10,8},{12,14},{14,12},{16,18},{18,... | collective-permute-start | bytes 6291464 | tf_op jit(solution)/shard_map/ppermute | solution.py:1080
  160.3 5.5 %collective-permute-start.20 = (bf16[256,2048]{1,0:T(8,128)(2,1)}, bf16[256,2048]{1,0:T(8,128)(2,1)}, u32[]{:S(2)}, u32[]{:S(2)}) collective-permute-start(bf16[256,2048]{1,0:T(8,128)(2,1)} %collective-permute-done.18.refs_0_), channel_id=1, source_target_pairs={{0,2},{2,0},{4,6},{6,4},{8,10},{10,8},{12,14},{14,12},{16,18},{18,... | collective-permute-start | bytes 3145736 | tf_op jit(solution)/shard_map/ppermute | solution.py:1080
  160.4 7.0 %collective-permute-start.21 = (bf16[256,2048]{1,0:T(8,128)(2,1)}, bf16[256,2048]{1,0:T(8,128)(2,1)}, u32[]{:S(2)}, u32[]{:S(2)}) collective-permute-start(bf16[256,2048]{1,0:T(8,128)(2,1)} %collective-permute-done.19.refs_1_), channel_id=1, source_target_pairs={{0,2},{2,0},{4,6},{6,4},{8,10},{10,8},{12,14},{14,12},{16,18},{18,... | collective-permute-start | bytes 3145736 | tf_op jit(solution)/shard_map/ppermute | solution.py:1080
  163.8 57.4 %collective-permute-start.25 = (bf16[512,1024]{1,0:T(8,128)(2,1)}, bf16[512,1024]{1,0:T(8,128)(2,1)}, u32[]{:S(2)}, u32[]{:S(2)}) collective-permute-start(bf16[512,1024]{1,0:T(8,128)(2,1)} %fusion.5), channel_id=1, source_target_pairs={{0,4},{2,6},{4,0},{6,2},{8,12},{10,14},{12,8},{14,10},{16,20},{18,... | collective-permute-start | bytes 3145736 | tf_op jit(solution)/shard_map/ppermute | solution.py:1080
  190.0 24.7 %collective-permute-start.24 = (bf16[2,2,512,1024]{3,2,1,0:T(8,128)(2,1)}, bf16[2,2,512,1024]{3,2,1,0:T(8,128)(2,1)S(1)}, u32[]{:S(2)}, u32[]{:S(2)}) collective-permute-start(bf16[2,2,512,1024]{3,2,1,0:T(8,128)(2,1)} %get-tuple-element.241), channel_id=1, source_target_pairs={{0,2},{2,0},{4,6},{6,4},{8,10},{10,8},{12,14},{14,12},{16,18},{18,... | collective-permute-start | bytes 12582920 | tf_op jit(solution)/shard_map/ppermute | solution.py:1080
  215.1 33.2 %collective-permute-start.26 = (bf16[512,1024]{1,0:T(8,128)(2,1)S(1)}, bf16[512,1024]{1,0:T(8,128)(2,1)}, u32[]{:S(2)}, u32[]{:S(2)}) collective-permute-start(bf16[512,1024]{1,0:T(8,128)(2,1)S(1)} %fusion.4), channel_id=1, source_target_pairs={{0,4},{2,6},{4,0},{6,2},{8,12},{10,14},{12,8},{14,10},{16,20},{18,... | collective-permute-start | bytes 3145736 | tf_op jit(solution)/shard_map/ppermute | solution.py:1080
  220.1 59.1 %collective-permute-start.27 = (bf16[2,512,1024]{2,1,0:T(8,128)(2,1)}, bf16[2,512,1024]{2,1,0:T(8,128)(2,1)}, u32[]{:S(2)}, u32[]{:S(2)}) collective-permute-start(bf16[2,512,1024]{2,1,0:T(8,128)(2,1)} %fusion), channel_id=1, source_target_pairs={{0,1},{1,0},{2,3},{3,2},{4,5},{5,4},{6,7},{7,6},{8,9},{9,8},{10,11... | collective-permute-start | bytes 6291464 | tf_op jit(solution)/shard_map/ppermute | solution.py:1080
  260.2 24.9 %collective-permute-start.28 = (bf16[2,2,512,768]{3,2,1,0:T(8,128)(2,1)S(1)}, bf16[2,2,512,768]{3,2,1,0:T(8,128)(2,1)S(1)}, u32[]{:S(2)}, u32[]{:S(2)}) collective-permute-start(bf16[2,2,512,768]{3,2,1,0:T(8,128)(2,1)S(1)} %weight_mid.4), channel_id=1, source_target_pairs={{0,2},{2,0},{4,6},{6,4},{8,10},{10,8},{12,14},{14,12},{16,18},{18,... | collective-permute-start | bytes 9437192 | tf_op jit(solution)/shard_map/ppermute | solution.py:1080
  266.3 26.8 %collective-permute-start.29 = (bf16[2,2,512,768]{3,2,1,0:T(8,128)(2,1)S(1)}, bf16[2,2,512,768]{3,2,1,0:T(8,128)(2,1)S(1)}, u32[]{:S(2)}, u32[]{:S(2)}) collective-permute-start(bf16[2,2,512,768]{3,2,1,0:T(8,128)(2,1)S(1)} %weight_mid.5), channel_id=1, source_target_pairs={{0,2},{2,0},{4,6},{6,4},{8,10},{10,8},{12,14},{14,12},{16,18},{18,... | collective-permute-start | bytes 9437192 | tf_op jit(solution)/shard_map/ppermute | solution.py:1080
  266.8 37.0 %collective-permute-start.31 = (bf16[512,1024]{1,0:T(8,128)(2,1)}, bf16[512,1024]{1,0:T(8,128)(2,1)}, u32[]{:S(2)}, u32[]{:S(2)}) collective-permute-start(bf16[512,1024]{1,0:T(8,128)(2,1)} %fusion.3), channel_id=1, source_target_pairs={{0,1},{1,0},{2,3},{3,2},{4,5},{5,4},{6,7},{7,6},{8,9},{9,8},{10,11... | collective-permute-start | bytes 3145736 | tf_op jit(solution)/shard_map/ppermute | solution.py:1080
  283.2 26.1 %collective-permute-start.30 = (bf16[512,1024]{1,0:T(8,128)(2,1)S(1)}, bf16[512,1024]{1,0:T(8,128)(2,1)S(1)}, u32[]{:S(2)}, u32[]{:S(2)}) collective-permute-start(bf16[512,1024]{1,0:T(8,128)(2,1)S(1)} %fusion.1), channel_id=1, source_target_pairs={{0,4},{2,6},{4,0},{6,2},{8,12},{10,14},{12,8},{14,10},{16,20},{18,... | collective-permute-start | bytes 3145736 | tf_op jit(solution)/shard_map/ppermute | solution.py:1080
  291.6 65.7 %collective-permute-start.33 = (bf16[2,512,768]{2,1,0:T(8,128)(2,1)}, bf16[2,512,768]{2,1,0:T(8,128)(2,1)}, u32[]{:S(2)}, u32[]{:S(2)}) collective-permute-start(bf16[2,512,768]{2,1,0:T(8,128)(2,1)} %get-tuple-element.271), channel_id=1, source_target_pairs={{0,4},{2,6},{4,0},{6,2},{8,12},{10,14},{12,8},{14,10},{16,20},{18,... | collective-permute-start | bytes 4718600 | tf_op jit(solution)/shard_map/ppermute | solution.py:1080
  303.7 21.4 %collective-permute-start.32 = (bf16[2,2,512,640]{3,2,1,0:T(8,128)(2,1)S(1)}, bf16[2,2,512,640]{3,2,1,0:T(8,128)(2,1)S(1)}, u32[]{:S(2)}, u32[]{:S(2)}) collective-permute-start(bf16[2,2,512,640]{3,2,1,0:T(8,128)(2,1)S(1)} %weight_value.2), channel_id=1, source_target_pairs={{0,2},{2,0},{4,6},{6,4},{8,10},{10,8},{12,14},{14,12},{16,18},{18,... | collective-permute-start | bytes 7864328 | tf_op jit(solution)/shard_map/ppermute | solution.py:1080
  312.9 47.2 %collective-permute-start.35 = (bf16[2,2,128,1024]{3,2,1,0:T(8,128)(2,1)}, bf16[2,2,128,1024]{3,2,1,0:T(8,128)(2,1)}, u32[]{:S(2)}, u32[]{:S(2)}) collective-permute-start(bf16[2,2,128,1024]{3,2,1,0:T(8,128)(2,1)} %pad_maximum_fusion), channel_id=1, source_target_pairs={{0,8},{2,10},{4,12},{6,14},{8,0},{10,2},{12,4},{14,6},{16,24},{18,... | collective-permute-start | bytes 3145736 | tf_op jit(solution)/shard_map/ppermute | solution.py:1080
  323.2 34.1 %collective-permute-start.34 = (bf16[2,512,768]{2,1,0:T(8,128)(2,1)}, bf16[2,512,768]{2,1,0:T(8,128)(2,1)}, u32[]{:S(2)}, u32[]{:S(2)}) collective-permute-start(bf16[2,512,768]{2,1,0:T(8,128)(2,1)} %get-tuple-element.301), channel_id=1, source_target_pairs={{0,1},{1,0},{2,3},{3,2},{4,5},{5,4},{6,7},{7,6},{8,9},{9,8},{10,11... | collective-permute-start | bytes 4718600 | tf_op jit(solution)/shard_map/ppermute | solution.py:1080
  330.8 49.6 %collective-permute-start.37 = (bf16[2,2,2,128,640]{4,3,2,1,0:T(8,128)(2,1)}, bf16[2,2,2,128,640]{4,3,2,1,0:T(8,128)(2,1)}, u32[]{:S(2)}, u32[]{:S(2)}) collective-permute-start(bf16[2,2,2,128,640]{4,3,2,1,0:T(8,128)(2,1)} %get-tuple-element.336), channel_id=1, source_target_pairs={{0,8},{2,10},{4,12},{6,14},{8,0},{10,2},{12,4},{14,6},{16,24},{18,... | collective-permute-start | bytes 3932168 | tf_op jit(solution)/shard_map/ppermute | solution.py:1080
  361.9 22.7 %collective-permute-start.36 = (bf16[2,128,1024]{2,1,0:T(8,128)(2,1)S(1)}, bf16[2,128,1024]{2,1,0:T(8,128)(2,1)S(1)}, u32[]{:S(2)}, u32[]{:S(2)}) collective-permute-start(bf16[2,128,1024]{2,1,0:T(8,128)(2,1)S(1)} %pad_maximum_fusion.2), channel_id=1, source_target_pairs={{0,16},{2,18},{4,20},{6,22},{8,24},{10,26},{12,28},{14,30},{16,0},... | collective-permute-start | bytes 1572872 | tf_op jit(solution)/shard_map/ppermute | solution.py:1080
  364.5 25.3 %collective-permute-start.40 = (bf16[512,768]{1,0:T(8,128)(2,1)S(1)}, bf16[512,768]{1,0:T(8,128)(2,1)S(1)}, u32[]{:S(2)}, u32[]{:S(2)}) collective-permute-start(bf16[512,768]{1,0:T(8,128)(2,1)S(1)} %fusion.7), channel_id=1, source_target_pairs={{0,4},{2,6},{4,0},{6,2},{8,12},{10,14},{12,8},{14,10},{16,20},{18,... | collective-permute-start | bytes 2359304 | tf_op jit(solution)/shard_map/ppermute | solution.py:1080
  365.1 24.7 %collective-permute-start.39 = (bf16[512,768]{1,0:T(8,128)(2,1)S(1)}, bf16[512,768]{1,0:T(8,128)(2,1)S(1)}, u32[]{:S(2)}, u32[]{:S(2)}) collective-permute-start(bf16[512,768]{1,0:T(8,128)(2,1)S(1)} %fusion.6), channel_id=1, source_target_pairs={{0,1},{1,0},{2,3},{3,2},{4,5},{5,4},{6,7},{7,6},{8,9},{9,8},{10,11... | collective-permute-start | bytes 2359304 | tf_op jit(solution)/shard_map/ppermute | solution.py:1080
  378.9 10.9 %collective-permute-start.38 = (f32[272,128]{1,0:T(8,128)S(1)}, f32[272,128]{1,0:T(8,128)S(1)}, u32[]{:S(2)}, u32[]{:S(2)}) collective-permute-start(f32[272,128]{1,0:T(8,128)S(1)} %constant_dynamic-update-slice_fusion), channel_id=1, source_target_pairs={{0,8},{2,10},{4,12},{6,14},{8,0},{10,2},{12,4},{14,6},{16,24},{18,... | collective-permute-start | bytes 417800 | tf_op jit(solution)/shard_map/ppermute | solution.py:1080
  381.7 29.4 %collective-permute-start.46 = (bf16[2,2,128,640]{3,2,1,0:T(8,128)(2,1)S(1)}, bf16[2,2,128,640]{3,2,1,0:T(8,128)(2,1)S(1)}, u32[]{:S(2)}, u32[]{:S(2)}) collective-permute-start(bf16[2,2,128,640]{3,2,1,0:T(8,128)(2,1)S(1)} %fusion.8), channel_id=1, source_target_pairs={{0,4},{2,6},{4,0},{6,2},{8,12},{10,14},{12,8},{14,10},{16,20},{18,... | collective-permute-start | bytes 1966088 | tf_op jit(solution)/shard_map/ppermute | solution.py:1080
  389.9 13.6 %collective-permute-start.41 = (f32[272,128]{1,0:T(8,128)S(1)}, f32[272,128]{1,0:T(8,128)S(1)}, u32[]{:S(2)}, u32[]{:S(2)}) collective-permute-start(f32[272,128]{1,0:T(8,128)S(1)} %add.618), channel_id=1, source_target_pairs={{0,16},{2,18},{4,20},{6,22},{8,24},{10,26},{12,28},{14,30},{16,0},... | collective-permute-start | bytes 417800 | tf_op jit(solution)/shard_map/ppermute | solution.py:1080
  393.0 20.3 %collective-permute-start.44 = (bf16[2,2,128,768]{3,2,1,0:T(8,128)(2,1)S(1)}, bf16[2,2,128,768]{3,2,1,0:T(8,128)(2,1)S(1)}, u32[]{:S(2)}, u32[]{:S(2)}) collective-permute-start(bf16[2,2,128,768]{3,2,1,0:T(8,128)(2,1)S(1)} %pad_maximum_fusion.1), channel_id=1, source_target_pairs={{0,8},{2,10},{4,12},{6,14},{8,0},{10,2},{12,4},{14,6},{16,24},{18,... | collective-permute-start | bytes 2359304 | tf_op jit(solution)/shard_map/ppermute | solution.py:1080
  398.4 7.3 %collective-permute-start.50 = (bf16[2,64,1024]{2,1,0:T(8,128)(2,1)S(1)}, bf16[2,64,1024]{2,1,0:T(8,128)(2,1)S(1)}, u32[]{:S(2)}, u32[]{:S(2)}) collective-permute-start(bf16[2,64,1024]{2,1,0:T(8,128)(2,1)S(1)} %fusion.25), channel_id=1, source_target_pairs={{0,2},{2,0},{4,6},{6,4},{8,10},{10,8},{12,14},{14,12},{16,18},{18,... | collective-permute-start | bytes 786440 | tf_op jit(solution)/shard_map/ppermute | solution.py:1080
  405.0 6.0 %collective-permute-start.43 = (f32[272,128]{1,0:T(8,128)S(1)}, f32[272,128]{1,0:T(8,128)S(1)}, u32[]{:S(2)}, u32[]{:S(2)}) collective-permute-start(f32[272,128]{1,0:T(8,128)S(1)} %add.624), channel_id=1, source_target_pairs={{0,4},{2,6},{4,0},{6,2},{8,12},{10,14},{12,8},{14,10},{16,20},{18,... | collective-permute-start | bytes 417800 | tf_op jit(solution)/shard_map/ppermute | solution.py:1080
  412.1 12.2 %collective-permute-start.47 = (bf16[2,128,640]{2,1,0:T(8,128)(2,1)S(1)}, bf16[2,128,640]{2,1,0:T(8,128)(2,1)S(1)}, u32[]{:S(2)}, u32[]{:S(2)}) collective-permute-start(bf16[2,128,640]{2,1,0:T(8,128)(2,1)S(1)} %fusion.9), channel_id=1, source_target_pairs={{0,1},{1,0},{2,3},{3,2},{4,5},{5,4},{6,7},{7,6},{8,9},{9,8},{10,11... | collective-permute-start | bytes 983048 | tf_op jit(solution)/shard_map/ppermute | solution.py:1080
  415.6 8.7 %collective-permute-start.45 = (f32[272,128]{1,0:T(8,128)S(1)}, f32[272,128]{1,0:T(8,128)S(1)}, u32[]{:S(2)}, u32[]{:S(2)}) collective-permute-start(f32[272,128]{1,0:T(8,128)S(1)} %add.625), channel_id=1, source_target_pairs={{0,1},{1,0},{2,3},{3,2},{4,5},{5,4},{6,7},{7,6},{8,9},{9,8},{10,11... | collective-permute-start | bytes 417800 | tf_op jit(solution)/shard_map/ppermute | solution.py:1080
  417.7 26.7 %collective-permute-start.48 = (bf16[2,128,768]{2,1,0:T(8,128)(2,1)}, bf16[2,128,768]{2,1,0:T(8,128)(2,1)}, u32[]{:S(2)}, u32[]{:S(2)}) collective-permute-start(bf16[2,128,768]{2,1,0:T(8,128)(2,1)} %pad_maximum_fusion.3), channel_id=1, source_target_pairs={{0,16},{2,18},{4,20},{6,22},{8,24},{10,26},{12,28},{14,30},{16,0},... | collective-permute-start | bytes 1179656 | tf_op jit(solution)/shard_map/ppermute | solution.py:1080
  426.3 18.1 %collective-permute-start.49 = (bf16[128,640]{1,0:T(8,128)(2,1)}, bf16[128,640]{1,0:T(8,128)(2,1)}, u32[]{:S(2)}, u32[]{:S(2)}) collective-permute-start(bf16[128,640]{1,0:T(8,128)(2,1)} %fusion.22), channel_id=1, source_target_pairs={{0,16},{2,18},{4,20},{6,22},{8,24},{10,26},{12,28},{14,30},{16,0},... | collective-permute-start | bytes 491528 | tf_op jit(solution)/shard_map/ppermute | solution.py:1080
  (117 other events, 1003.4 us)

commit v7 on v6

--- a/solution.py
+++ b/solution.py
@@ -316,7 +316,7 @@
 BF = jnp.bfloat16
 F32 = jnp.float32
 ROWS = 256
-hints = dict()
+hints = dict(ema_backward2=0.3, weight_value=0.3)
 opt = dict(dn=0, m2=3, v2=4, z2=3, z1m=5)
 
 
@@ -670,7 +670,7 @@
         [sds((n, d), F32)] + [sds(par, F32)] * 4 + [sds(small, F32)],
         [back_rows, const, const, const, const, pl.BlockSpec(small, lambda i, s: (0, 0))],
         [pltpu.VMEM((tb * groups, 128), F32)] * 3,
-        flops=5e9 * count, name="ema_backward", aliases={14: 0} if before else {},
+        flops=5e9 * count, name=f"ema_backward{first}", aliases={14: 0} if before else {},
     )
 
 
@@ -1143,13 +1143,13 @@
     ema_low, e_slope, state = k_ema_forward(
         after(ema_a[0]), normed, decay, coef, omega, blocks // 2, blocks // 2, (ema_a[2], ema_a[0], ema_a[1])
     )
-    pg.append(over_z(held(pg[0], state)))
+    pg.append(over_z(held(pg[0], ema_a[0])))
     ph = [over_tensor(held(piece_h, state))]
     z_pre, query, key = k_query_key(scal, ema_low, w_z, qk_gain, qk_bias)
     pv += [over_core(v) for v in held((pv[0], pv[1]), query)]
     pu.append(over_x(held(pu[0], query)))
     pup = [over_tensor(held(piece_up, query))]
-    v_oth, vs_oth = k_act_other(after(query), normed, pv, 0, 512)
+    v_oth, vs_oth = k_act_other(after(query, pu[0], pg[1]), normed, pv, 0, 512)
     pg += [over_core(v) for v in held((pg[0], pg[1]), v_oth)]
     ph.append(over_z(held(ph[0], v_oth)))
     pdn = [over_tensor(held(piece_dn, v_oth))]

time: 460 us -> 444 us (0.965)
  other arithmetic: 41.4 us -> 34.9 us
  waiting for transfers between devices: 55.8 us -> 49.6 us
    ppermute x53, waiting for transfers between devices: 55.8 us -> 49.6 us  [swap(): return lax.ppermute(values, axis, [(i, i ^ bit) for i in range(size)])]
    convert_element_type x13, other arithmetic: 24.5 us -> 19.3 us  [add(): return total(*values).astype(BF)]
    unnamed x227 -> x221, local copies, waits for them, and re-layouts: 20.9 us -> 20.1 us
  transfers between devices with their start and end apart: 53 -> 53, of which waited for: 14 -> 14; matrix products, arithmetic and copies ran while one was open for 12% -> 10% of each run, Pallas kernels for 58% -> 61%
where the time goes in v7:
time: 444 us; the launch traced here: 438 us
  Pallas kernels  265 us (60%)
  waiting for transfers between devices  49.6 us (11%)
  starting transfers between devices  46.4 us (10%)
  local copies, waits for them, and re-layouts  38.6 us (9%)
  other arithmetic  34.9 us (8%)
    pallas_call x28, Pallas kernels, run(): pl.pallas_call(body, out_shape=out_shape, grid_spec=pltpu.PrefetchScalarG...  265 us
    ppermute x53, waiting for transfers between devices, swap(): return lax.ppermute(values, axis, [(i, i ^ bit) for i in range(size)])  49.6 us
    ppermute x53, starting transfers between devices, swap(): return lax.ppermute(values, axis, [(i, i ^ bit) for i in range(size)])  46.4 us
    unnamed x221, local copies, waits for them, and re-layouts  20.1 us
    convert_element_type x13, other arithmetic, add(): return total(*values).astype(BF)  19.3 us
  transfers between devices with their start and end apart: 53, of which 14 were waited for; matrix products, arithmetic and copies ran while one was open for 10% of the time, Pallas kernels for 61%

profile of v7, /device:TPU:0, one launch (start us, length us, event | category | flops | bytes accessed | tf_op | source)
XLA Modules:
  0.0 437.6 jit_solution(9609012360649300325)
XLA Ops:
  0.7 1.9 constant_dynamic-slice_fusion
  2.6 3.0 collective-permute-start.4
  6.2 2.1 pack_params.1.own_ref
  8.4 5.7 %pieces.1 = (bf16[256,1024]{1,0:T(8,128)(2,1)}, bf16[256,1024]{1,0:T(8,128)(2,1)}, bf16[256,1024]{1,0:T(8,128)(2,1)}, bf16[256,2048]{1,0:T(8,128)(2,1)}, bf16[1024,1024]{1,0:T(8,128)(2,1)}) custom-call(s32[16]{0:T(128)} %stack.105.s, bf16[1024,1024]{1,0:T(8,128)(2,1)} %wo.5, bf16[1024,1024]{1,0:T(8,128)(2,1)} %uo.3, bf16[512,1024]{1,0:T(8,128)(2,1)} %ho.3, ...), custom_call_target="tpu_custom_call" | custom-call | flops 100000000 | bytes 235929600 | tf_op jit(solution)/shard_map/pieces/pallas_call | solution.py:351
  14.1 5.2 %value_own.1 = (bf16[1024,1024]{1,0:T(8,128)(2,1)S(1)}, bf16[1024,1024]{1,0:T(8,128)(2,1)S(1)}, bf16[1024,1024]{1,0:T(8,128)(2,1)S(1)}) custom-call(s32[16]{0:T(128)S(1)} %copy-done.17, bf16[1024,1024]{1,0:T(8,128)(2,1)S(1)} %copy-done.23, bf16[1024,1024]{1,0:T(8,128)(2,1)S(1)} %copy-done.9), custom_call_target="tpu_custom_call" | custom-call | flops 21474836480 | bytes 104857600 | tf_op jit(solution)/shard_map/value_own/pallas_call | solution.py:351
  24.3 2.4 ema_params.1
  29.0 6.8 %ema_forward.2 = (bf16[1024,1024]{1,0:T(8,128)(2,1)S(1)}, bf16[1024,1024]{1,0:T(8,128)(2,1)S(1)}, f32[128,128]{1,0:T(8,128)S(1)}) custom-call(s32[16]{0:T(128)S(1)} %copy-done.18, bf16[1024,1024]{1,0:T(8,128)(2,1)S(1)} %get-tuple-element.179.x_ref, f32[128,128]{1,0:T(8,128)S(1)} %copy-done.11, f32[128,128]{1,0:T(8,128)S(1)} %copy-done.14, ...), custom_call_target="tpu_custom_call" | custom-call | flops 99999997952 | bytes 64921600 | tf_op jit(solution)/shard_map/ema_forward/pallas_call | solution.py:351
  39.7 7.2 %ema_forward.3 = (bf16[1024,1024]{1,0:T(8,128)(2,1)S(1)}, bf16[1024,1024]{1,0:T(8,128)(2,1)S(1)}, f32[128,128]{1,0:T(8,128)}) custom-call(s32[16]{0:T(128)S(1)} %copy-done.18, bf16[1024,1024]{1,0:T(8,128)(2,1)S(1)} %get-tuple-element.179.x_ref, f32[128,128]{1,0:T(8,128)S(1)} %copy-done.12, ...), custom_call_target="tpu_custom_call", output_to_operand_aliasing={{0}: (6, {}), {1}: (7, {})} | custom-call | flops 99999997952 | bytes 107520000 | tf_op jit(solution)/shard_map/ema_forward/pallas_call | solution.py:351
  52.6 4.7 %act_other.1 = (bf16[1024,1024]{1,0:T(8,128)(2,1)S(1)}, bf16[1024,1024]{1,0:T(8,128)(2,1)S(1)}) custom-call(s32[16]{0:T(128)S(1)} %copy-done.18, bf16[1024,1024]{1,0:T(8,128)(2,1)S(1)} %get-tuple-element.179.x_ref, bf16[256,1024]{1,0:T(8,128)(2,1)S(1)} %collective-permute-done.4.p0.w0, bf16[256,1024]{1,0:T(8,128)(2,1)S(1)} %collective-permute-done.5.p1.w1, ...), custom_call_target="tpu_custom_call" | custom-call | flops 21474836480 | bytes 83886080 | tf_op jit(solution)/shard_map/act_other/pallas_call | solution.py:351
  62.7 2.5 collective-permute-done.13.h0.f0
  67.3 16.7 %attend.1 = (bf16[1024,1024]{1,0:T(8,128)(2,1)}, bf16[1024,1024]{1,0:T(8,128)(2,1)}, bf16[1024,1024]{1,0:T(8,128)(2,1)}, bf16[1024,1024]{1,0:T(8,128)(2,1)}, bf1...) custom-call(s32[16]{0:T(128)} %stack.105.s, bf16[1024,128]{1,0:T(8,128)(2,1)} %copy-done.36, ...), custom_call_target="tpu_custom_call" | custom-call | flops 71470940160 | bytes 256901120 | tf_op jit(solution)/shard_map/attend/pallas_call | solution.py:351
  90.2 18.9 %gate.1 = (bf16[1024,1024]{1,0:T(8,128)(2,1)}, bf16[1024,1024]{1,0:T(8,128)(2,1)}, bf16[1024,1024]{1,0:T(8,128)(2,1)}, bf16[1024,1024]{1,0:T(8,128)(2,1)}, bf16[1024,1024]{1,0:T(8,128)(2,1)}) custom-call(s32[16]{0:T(128)} %stack.105.s, bf16[1024,1024]{1,0:T(8,128)(2,1)} %get-tuple-element.204.go.refs_1_, bf16[1024,1024]{1,0:T(8,128)(2,1)} %get-tuple-element.205.gt.refs_2_, ...), custom_call_target="tpu_custom_call" | custom-call | flops 85899345920 | bytes 293601280 | tf_op jit(solution)/shard_map/gate/pallas_call | solution.py:351
  109.1 20.3 %ffn.4 = (bf16[1024,1024]{1,0:T(8,128)(2,1)}, bf16[1024,1024]{1,0:T(8,128)(2,1)}, bf16[2,2,512,1024]{3,2,1,0:T(8,128)(2,1)}) custom-call(s32[16]{0:T(128)} %stack.105.s, bf16[1024,1024]{1,0:T(8,128)(2,1)} %get-tuple-element.215.low_ref, bf16[1024,1024]{1,0:T(8,128)(2,1)} %c_ref.9, bf16[1024,2048]{1,0:T(8,128)(2,1)} %refs_0_.5, bf16[2048,1024]{1,0:T(8,128)(2,1)} %refs_1_.5), custom_call_target="tpu_custom_call" | custom-call | flops 128849018880 | bytes 209715200 | tf_op jit(solution)/shard_map/ffn/pallas_call | solution.py:351
  129.4 20.7 %ffn.5 = (bf16[1024,1024]{1,0:T(8,128)(2,1)}, bf16[1024,1024]{1,0:T(8,128)(2,1)}, bf16[512,1024]{1,0:T(8,128)(2,1)}, bf16[512,1024]{1,0:T(8,128)(2,1)}, bf16[512...) custom-call(s32[16]{0:T(128)} %stack.105.s, bf16[1024,1024]{1,0:T(8,128)(2,1)} %get-tuple-element.215.low_ref, ...), custom_call_target="tpu_custom_call" | custom-call | flops 128849018880 | bytes 251658240 | tf_op jit(solution)/shard_map/ffn/pallas_call | solution.py:351
  151.3 2.9 fusion.5
  159.2 21.2 %ffn.6 = (bf16[1024,1024]{1,0:T(8,128)(2,1)}, bf16[1024,1024]{1,0:T(8,128)(2,1)}, bf16[2,2,512,1024]{3,2,1,0:T(8,128)(2,1)}) custom-call(s32[16]{0:T(128)} %stack.105.s, bf16[1024,1024]{1,0:T(8,128)(2,1)} %get-tuple-element.215.low_ref, bf16[1024,1024]{1,0:T(8,128)(2,1)} %c_ref.9, bf16[256,2048]{1,0:T(8,128)(2,1)} %collective-permute-done.18.refs_0_, ...), custom_call_target="tpu_custom_call" | custom-call | flops 128849018880 | bytes 230686720 | tf_op jit(solution)/shard_map/ffn/pallas_call | solution.py:351
  180.8 21.1 %ffn.7 = (bf16[1024,1024]{1,0:T(8,128)(2,1)}, bf16[1024,1024]{1,0:T(8,128)(2,1)}, bf16[512,1024]{1,0:T(8,128)(2,1)}, bf16[512,1024]{1,0:T(8,128)(2,1)}, bf16[2,512,1024]{2,1,0:T(8,128)(2,1)}) custom-call(s32[16]{0:T(128)} %stack.105.s, bf16[1024,1024]{1,0:T(8,128)(2,1)} %get-tuple-element.215.low_ref, bf16[1024,1024]{1,0:T(8,128)(2,1)} %c_ref.9, ...), custom_call_target="tpu_custom_call" | custom-call | flops 128849018880 | bytes 230686720 | tf_op jit(solution)/shard_map/ffn/pallas_call | solution.py:351
  201.9 3.1 fusion.36
  208.2 2.3 fusion
  211.4 27.5 %mid_back.1 = (bf16[1024,1024]{1,0:T(8,128)(2,1)}, bf16[1024,1024]{1,0:T(8,128)(2,1)}, bf16[1024,1024]{1,0:T(8,128)(2,1)}, bf16[1024,1024]{1,0:T(8,128)(2,1)}, b...) custom-call(s32[16]{0:T(128)} %stack.105.s, ...), custom_call_target="tpu_custom_call" | custom-call | flops 128849018880 | bytes 566231040 | tf_op jit(solution)/shard_map/mid_back/pallas_call | solution.py:351
  238.9 3.3 fusion.3
  243.8 6.2 %weight_mid.4 = bf16[2,2,512,768]{3,2,1,0:T(8,128)(2,1)} custom-call(s32[16]{0:T(128)S(1)} %copy-done.19, bf16[1024,1024]{1,0:T(8,128)(2,1)S(1)} %copy-done.59, bf16[1024,1024]{1,0:T(8,128)(2,1)S(1)} %copy-done.55, bf16[1024,1024]{1,0:T(8,128)(2,1)S(1)} %copy-done.57, bf16[1024,1024]{1,0:T(8,128)(2,1)S(1)} %copy-done.3, bf16[1024,1024]{1,0:T(8,128)(2,1)S(1)} %copy-done.3), custom_call_target="tpu_custom_call" | custom-call | flops 32212254720 | bytes 136314880 | tf_op jit(solution)/shard_map/weight_mid/pallas_call | solution.py:351
  250.1 5.9 %weight_mid.5 = bf16[2,2,512,768]{3,2,1,0:T(8,128)(2,1)S(1)} custom-call(s32[16]{0:T(128)S(1)} %copy-done.19, bf16[1024,1024]{1,0:T(8,128)(2,1)S(1)} %copy-done.3, bf16[1024,1024]{1,0:T(8,128)(2,1)S(1)} %copy-done.49, bf16[1024,1024]{1,0:T(8,128)(2,1)S(1)} %copy-done.51, bf16[1024,1024]{1,0:T(8,128)(2,1)S(1)} %copy-done.53, ...), custom_call_target="tpu_custom_call" | custom-call | flops 32212254720 | bytes 157286400 | tf_op jit(solution)/shard_map/weight_mid/pallas_call | solution.py:351
  259.3 9.8 %attend_back.1 = (bf16[1024,1024]{1,0:T(8,128)(2,1)S(1)}, bf16[1024,1024]{1,0:T(8,128)(2,1)S(1)}, bf16[1024,128]{1,0:T(8,128)(2,1)S(1)}, f32[8,128]{1,0:T(8,128)S(1)}) custom-call(s32[16]{0:T(128)S(1)} %copy-done.19, bf16[1024,1024]{1,0:T(8,128)(2,1)S(1)} %copy-done.61, bf16[1024,1024]{1,0:T(8,128)(2,1)S(1)} %copy-done.62, ...), custom_call_target="tpu_custom_call" | custom-call | flops 53687091200 | bytes 201902080 | tf_op jit(solution)/shard_map/attend_back/pallas_call | solution.py:351
  269.2 2.3 fusion.1
  274.2 6.4 %weight_mid.6 = (bf16[2,512,768]{2,1,0:T(8,128)(2,1)}, bf16[2,512,768]{2,1,0:T(8,128)(2,1)S(1)}) custom-call(s32[16]{0:T(128)S(1)} %copy-done.19, bf16[1024,1024]{1,0:T(8,128)(2,1)S(1)} %copy-done.60, bf16[1024,1024]{1,0:T(8,128)(2,1)S(1)} %copy-done.56, bf16[1024,1024]{1,0:T(8,128)(2,1)S(1)} %copy-done.58, bf16[1024,1024]{1,0:T(8,128)(2,1)S(1)} %copy-done.3, ...), custom_call_target="tpu_custom_call" | custom-call | flops 32212254720 | bytes 167772160 | tf_op jit(solution)/shard_map/weight_mid/pallas_call | solution.py:351
  281.4 6.1 %weight_mid.7 = (bf16[2,512,768]{2,1,0:T(8,128)(2,1)S(1)}, bf16[2,512,768]{2,1,0:T(8,128)(2,1)S(1)}) custom-call(s32[16]{0:T(128)S(1)} %copy-done.19, bf16[1024,1024]{1,0:T(8,128)(2,1)S(1)} %copy-done.3, bf16[1024,1024]{1,0:T(8,128)(2,1)S(1)} %copy-done.50, bf16[1024,1024]{1,0:T(8,128)(2,1)S(1)} %copy-done.52, bf16[1024,1024]{1,0:T(8,128)(2,1)S(1)} %copy-done.54, ...), custom_call_target="tpu_custom_call" | custom-call | flops 32212254720 | bytes 188743680 | tf_op jit(solution)/shard_map/weight_mid/pallas_call | solution.py:351
  287.6 3.7 weight_value.2
  291.4 6.2 %collective-permute-done.30 = bf16[512,1024]{1,0:T(8,128)(2,1)S(1)} collective-permute-done((bf16[512,1024]{1,0:T(8,128)(2,1)S(1)}, bf16[512,1024]{1,0:T(8,128)(2,1)S(1)}, u32[]{:S(2)}, u32[]{:S(2)}) %collective-permute-start.30) | collective-permute-done | bytes 1048608 | tf_op jit(solution)/shard_map/ppermute | solution.py:1080
  297.6 1.9 fusion.10
  302.7 7.8 %ema_backward0.1 = (f32[1024,1024]{1,0:T(8,128)S(1)}, f32[128,128]{1,0:T(8,128)S(1)}, f32[128,128]{1,0:T(8,128)S(1)}, f32[128,128]{1,0:T(8,128)S(1)}, f32[128,128]{1,0:T(8,128)S(1)}, /*index=5*/f32[8,128]{1,0:T(8,128)S(1)}) custom-call(s32[16]{0:T(128)S(1)} %copy-done.19, bf16[1024,1024]{1,0:T(8,128)(2,1)S(1)} %copy-done.1, ...), custom_call_target="tpu_custom_call" | custom-call | flops 99999997952 | bytes 114114560 | tf_op jit(solution)/shard_map/ema_backward0/pallas_call | solution.py:351
  313.4 3.8 weight_value.3
  317.3 1.8 slice_bitcast_fusion.1
  320.1 7.8 %ema_backward2.1 = (f32[1024,1024]{1,0:T(8,128)S(1)}, f32[128,128]{1,0:T(8,128)S(1)}, f32[128,128]{1,0:T(8,128)S(1)}, f32[128,128]{1,0:T(8,128)S(1)}, f32[128,128]{1,0:T(8,128)S(1)}, /*index=5*/f32[8,128]{1,0:T(8,128)S(1)}) custom-call(s32[16]{0:T(128)S(1)} %copy-done.19, bf16[1024,1024]{1,0:T(8,128)(2,1)S(1)} %copy-done.1, ...), custom_call_target="tpu_custom_call", output_to_operand_aliasing={{0}: (14, {})} | custom-call | flops 3000000000 | bytes 4761600 | tf_op jit(solution)/shard_map/ema_backward2/pallas_call | solution.py:351
  327.9 7.8 %ema_backward4.1 = (f32[1024,1024]{1,0:T(8,128)S(1)}, f32[128,128]{1,0:T(8,128)S(1)}, f32[128,128]{1,0:T(8,128)S(1)}, f32[128,128]{1,0:T(8,128)S(1)}, f32[128,128]{1,0:T(8,128)S(1)}, /*index=5*/f32[8,128]{1,0:T(8,128)S(1)}) custom-call(s32[16]{0:T(128)S(1)} %copy-done.19, bf16[1024,1024]{1,0:T(8,128)(2,1)S(1)} %copy-done.1, ...), custom_call_target="tpu_custom_call", output_to_operand_aliasing={{0}: (14, {})} | custom-call | flops 99999997952 | bytes 158720000 | tf_op jit(solution)/shard_map/ema_backward4/pallas_call | solution.py:351
  335.7 9.5 %collective-permute-done.34 = bf16[2,512,768]{2,1,0:T(8,128)(2,1)S(1)} collective-permute-done((bf16[2,512,768]{2,1,0:T(8,128)(2,1)S(1)}, bf16[2,512,768]{2,1,0:T(8,128)(2,1)S(1)}, u32[]{:S(2)}, u32[]{:S(2)}) %collective-permute-start.34) | collective-permute-done | bytes 1572896 | tf_op jit(solution)/shard_map/ppermute | solution.py:1080
  349.4 2.6 collective-permute-start.36
  353.7 8.3 %ema_backward6.1 = (f32[1024,1024]{1,0:T(8,128)S(1)}, f32[128,128]{1,0:T(8,128)}, f32[128,128]{1,0:T(8,128)}, f32[128,128]{1,0:T(8,128)S(1)}, f32[128,128]{1,0:T(8,128)S(1)}, /*index=5*/f32[8,128]{1,0:T(8,128)S(1)}) custom-call(s32[16]{0:T(128)S(1)} %copy-done.19, bf16[1024,1024]{1,0:T(8,128)(2,1)S(1)} %copy-done.1, ...), custom_call_target="tpu_custom_call", output_to_operand_aliasing={{0}: (14, {})} | custom-call | flops 99999997952 | bytes 158720000 | tf_op jit(solution)/shard_map/ema_backward6/pallas_call | solution.py:351
  367.5 4.7 %collective-permute-done.36 = bf16[2,128,1024]{2,1,0:T(8,128)(2,1)S(1)} collective-permute-done((bf16[2,128,1024]{2,1,0:T(8,128)(2,1)S(1)}, bf16[2,128,1024]{2,1,0:T(8,128)(2,1)S(1)}, u32[]{:S(2)}, u32[]{:S(2)}) %collective-permute-start.36) | collective-permute-done | bytes 524320 | tf_op jit(solution)/shard_map/ppermute | solution.py:1080
  372.2 5.1 %input_back.2.refs_0_ = f32[1024,1024]{1,0:T(8,128)} custom-call(s32[16]{0:T(128)S(1)} %copy-done.19, bf16[1024,1024]{1,0:T(8,128)(2,1)S(1)} %get-tuple-element.263.vo, bf16[1024,1024]{1,0:T(8,128)(2,1)S(1)} %get-tuple-element.271.vt, bf16[1024,1024]{1,0:T(8,128)(2,1)S(1)} %copy-done.10, bf16[256,1024]{1,0:T(8,128)(2,1)S(1)} %copy-done.26, ...), custom_call_target="tpu_custom_call" | custom-call | flops 21474836480 | bytes 209715200 | tf_op jit(solution)/shard_map/input_back/pallas_call | solution.py:351
  379.2 2.8 collective-permute-start.44
  382.1 1.8 bitcast_add_fusion.1
  383.9 4.9 %input_back.3 = f32[1024,1024]{1,0:T(8,128)} custom-call(s32[16]{0:T(128)S(1)} %copy-done.19, bf16[1024,1024]{1,0:T(8,128)(2,1)S(1)} %get-tuple-element.263.vo, bf16[1024,1024]{1,0:T(8,128)(2,1)S(1)} %get-tuple-element.271.vt, bf16[1024,1024]{1,0:T(8,128)(2,1)S(1)} %copy-done.10, bf16[256,1024]{1,0:T(8,128)(2,1)S(1)} %copy-done.26, ...), custom_call_target="tpu_custom_call", output_to_operand_aliasing={{}: (11, {})} | custom-call | flops 21474836480 | bytes 251658240 | tf_op jit(solution)/shard_map/input_back/pallas_call | solution.py:351
  391.1 5.4 %collective-permute-done.43 = f32[272,128]{1,0:T(8,128)S(1)} collective-permute-done((f32[272,128]{1,0:T(8,128)S(1)}, f32[272,128]{1,0:T(8,128)S(1)}, u32[]{:S(2)}, u32[]{:S(2)}) %collective-permute-start.43) | collective-permute-done | bytes 139296 | tf_op jit(solution)/shard_map/ppermute | solution.py:1080
  402.0 1.9 collective-permute-start.48
  404.0 5.8 %collective-permute-done.45 = f32[272,128]{1,0:T(8,128)S(1)} collective-permute-done((f32[272,128]{1,0:T(8,128)S(1)}, f32[272,128]{1,0:T(8,128)S(1)}, u32[]{:S(2)}, u32[]{:S(2)}) %collective-permute-start.45) | collective-permute-done | bytes 139296 | tf_op jit(solution)/shard_map/ppermute | solution.py:1080
  409.9 1.8 fusion.22
  420.2 8.4 %collective-permute-done.49 = bf16[128,640]{1,0:T(8,128)(2,1)} collective-permute-done((bf16[128,640]{1,0:T(8,128)(2,1)}, bf16[128,640]{1,0:T(8,128)(2,1)}, u32[]{:S(2)}, u32[]{:S(2)}) %collective-permute-start.49) | collective-permute-done | bytes 163872 | tf_op jit(solution)/shard_map/ppermute | solution.py:1080
  (379 shorter events, 94.8 us)
Async XLA Ops:
  2.6 34.0 %collective-permute-start.4 = (bf16[256,1024]{1,0:T(8,128)(2,1)}, bf16[256,1024]{1,0:T(8,128)(2,1)S(1)}, u32[]{:S(2)}, u32[]{:S(2)}) collective-permute-start(bf16[256,1024]{1,0:T(8,128)(2,1)} %constant_dynamic-slice_fusion), channel_id=1, source_target_pairs={{0,1},{1,0},{2,3},{3,2},{4,5},{5,4},{6,7},{7,6},{8,9},{9,8},{10,11... | collective-permute-start | bytes 1572872 | tf_op jit(solution)/shard_map/ppermute | solution.py:1080
  8.3 15.3 %collective-permute-start = (f32[72,512]{1,0:T(8,128)}, f32[72,512]{1,0:T(8,128)S(1)}, u32[]{:S(2)}, u32[]{:S(2)}) collective-permute-start(f32[72,512]{1,0:T(8,128)} %pack_params.1.own_ref), channel_id=1, source_target_pairs={{0,1},{1,0},{2,3},{3,2},{4,5},{5,4},{6,7},{7,6},{8,9},{9,8},{10,11... | collective-permute-start | bytes 442376 | tf_op jit(solution)/shard_map/ppermute | solution.py:1080
  22.1 14.5 %collective-permute-start.2 = (bf16[256,1024]{1,0:T(8,128)(2,1)}, bf16[256,1024]{1,0:T(8,128)(2,1)S(1)}, u32[]{:S(2)}, u32[]{:S(2)}) collective-permute-start(bf16[256,1024]{1,0:T(8,128)(2,1)} %get-tuple-element.191), channel_id=1, source_target_pairs={{0,1},{1,0},{2,3},{3,2},{4,5},{5,4},{6,7},{7,6},{8,9},{9,8},{10,11... | collective-permute-start | bytes 1572872 | tf_op jit(solution)/shard_map/ppermute | solution.py:1080
  35.8 16.0 %collective-permute-start.1 = (bf16[256,1024]{1,0:T(8,128)(2,1)S(1)}, bf16[256,1024]{1,0:T(8,128)(2,1)S(1)}, u32[]{:S(2)}, u32[]{:S(2)}) collective-permute-start(bf16[256,1024]{1,0:T(8,128)(2,1)S(1)} %copy-done.107), channel_id=1, source_target_pairs={{0,1},{1,0},{2,3},{3,2},{4,5},{5,4},{6,7},{7,6},{8,9},{9,8},{10,11... | collective-permute-start | bytes 1572872 | tf_op jit(solution)/shard_map/ppermute | solution.py:1080
  36.6 13.3 %collective-permute-start.5 = (bf16[256,1024]{1,0:T(8,128)(2,1)S(1)}, bf16[256,1024]{1,0:T(8,128)(2,1)S(1)}, u32[]{:S(2)}, u32[]{:S(2)}) collective-permute-start(bf16[256,1024]{1,0:T(8,128)(2,1)S(1)} %collective-permute-done.4.p0.w0), channel_id=1, source_target_pairs={{0,4},{2,6},{4,0},{6,2},{8,12},{10,14},{12,8},{14,10},{16,20},{18,... | collective-permute-start | bytes 1572872 | tf_op jit(solution)/shard_map/ppermute | solution.py:1080
  38.1 13.7 %collective-permute-start.3 = (bf16[256,1024]{1,0:T(8,128)(2,1)S(1)}, bf16[256,1024]{1,0:T(8,128)(2,1)S(1)}, u32[]{:S(2)}, u32[]{:S(2)}) collective-permute-start(bf16[256,1024]{1,0:T(8,128)(2,1)S(1)} %collective-permute-done.2.w0), channel_id=1, source_target_pairs={{0,8},{2,10},{4,12},{6,14},{8,0},{10,2},{12,4},{14,6},{16,24},{18,... | collective-permute-start | bytes 1572872 | tf_op jit(solution)/shard_map/ppermute | solution.py:1080
  50.4 14.8 %collective-permute-start.13 = (bf16[256,1024]{1,0:T(8,128)(2,1)S(1)}, bf16[256,1024]{1,0:T(8,128)(2,1)S(1)}, u32[]{:S(2)}, u32[]{:S(2)}) collective-permute-start(bf16[256,1024]{1,0:T(8,128)(2,1)S(1)} %copy-done.106), channel_id=1, source_target_pairs={{0,1},{1,0},{2,3},{3,2},{4,5},{5,4},{6,7},{7,6},{8,9},{9,8},{10,11... | collective-permute-start | bytes 1572872 | tf_op jit(solution)/shard_map/ppermute | solution.py:1080
  60.0 6.3 %collective-permute-start.8 = (bf16[256,1024]{1,0:T(8,128)(2,1)S(1)}, bf16[256,1024]{1,0:T(8,128)(2,1)S(1)}, u32[]{:S(2)}, u32[]{:S(2)}) collective-permute-start(bf16[256,1024]{1,0:T(8,128)(2,1)S(1)} %collective-permute-done.2.w0), channel_id=1, source_target_pairs={{0,2},{2,0},{4,6},{6,4},{8,10},{10,8},{12,14},{14,12},{16,18},{18,... | collective-permute-start | bytes 1572872 | tf_op jit(solution)/shard_map/ppermute | solution.py:1080
  60.2 6.2 %collective-permute-start.9 = (bf16[256,1024]{1,0:T(8,128)(2,1)S(1)}, bf16[256,1024]{1,0:T(8,128)(2,1)S(1)}, u32[]{:S(2)}, u32[]{:S(2)}) collective-permute-start(bf16[256,1024]{1,0:T(8,128)(2,1)S(1)} %collective-permute-done.3.w1), channel_id=1, source_target_pairs={{0,2},{2,0},{4,6},{6,4},{8,10},{10,8},{12,14},{14,12},{16,18},{18,... | collective-permute-start | bytes 1572872 | tf_op jit(solution)/shard_map/ppermute | solution.py:1080
  60.6 26.4 %collective-permute-start.18 = (bf16[256,2048]{1,0:T(8,128)(2,1)S(1)}, bf16[256,2048]{1,0:T(8,128)(2,1)}, u32[]{:S(2)}, u32[]{:S(2)}) collective-permute-start(bf16[256,2048]{1,0:T(8,128)(2,1)S(1)} %copy-done.93), channel_id=1, source_target_pairs={{0,1},{1,0},{2,3},{3,2},{4,5},{5,4},{6,7},{7,6},{8,9},{9,8},{10,11... | collective-permute-start | bytes 3145736 | tf_op jit(solution)/shard_map/ppermute | solution.py:1080
  61.9 22.7 %collective-permute-start.10 = (bf16[256,1024]{1,0:T(8,128)(2,1)S(1)}, bf16[256,1024]{1,0:T(8,128)(2,1)S(1)}, u32[]{:S(2)}, u32[]{:S(2)}) collective-permute-start(bf16[256,1024]{1,0:T(8,128)(2,1)S(1)} %collective-permute-done.1.u0), channel_id=1, source_target_pairs={{0,4},{2,6},{4,0},{6,2},{8,12},{10,14},{12,8},{14,10},{16,20},{18,... | collective-permute-start | bytes 1572872 | tf_op jit(solution)/shard_map/ppermute | solution.py:1080
  65.2 18.8 %collective-permute-start.14 = (bf16[256,1024]{1,0:T(8,128)(2,1)S(1)}, bf16[256,1024]{1,0:T(8,128)(2,1)S(1)}, u32[]{:S(2)}, u32[]{:S(2)}) collective-permute-start(bf16[256,1024]{1,0:T(8,128)(2,1)S(1)} %collective-permute-done.13.h0.f0), channel_id=1, source_target_pairs={{0,8},{2,10},{4,12},{6,14},{8,0},{10,2},{12,4},{14,6},{16,24},{18,... | collective-permute-start | bytes 1572872 | tf_op jit(solution)/shard_map/ppermute | solution.py:1080
  84.1 4.2 collective-permute-start.15
  84.1 4.9 %collective-permute-start.16 = (bf16[256,1024]{1,0:T(8,128)(2,1)S(1)}, bf16[256,1024]{1,0:T(8,128)(2,1)S(1)}, u32[]{:S(2)}, u32[]{:S(2)}) collective-permute-start(bf16[256,1024]{1,0:T(8,128)(2,1)S(1)} %collective-permute-done.14.h1.f1), channel_id=1, source_target_pairs={{0,2},{2,0},{4,6},{6,4},{8,10},{10,8},{12,14},{14,12},{16,18},{18,... | collective-permute-start | bytes 1572872 | tf_op jit(solution)/shard_map/ppermute | solution.py:1080
  84.6 4.4 %collective-permute-start.11 = (bf16[256,1024]{1,0:T(8,128)(2,1)S(1)}, bf16[256,1024]{1,0:T(8,128)(2,1)S(1)}, u32[]{:S(2)}, u32[]{:S(2)}) collective-permute-start(bf16[256,1024]{1,0:T(8,128)(2,1)S(1)} %collective-permute-done.1.u0), channel_id=1, source_target_pairs={{0,2},{2,0},{4,6},{6,4},{8,10},{10,8},{12,14},{14,12},{16,18},{18,... | collective-permute-start | bytes 1572872 | tf_op jit(solution)/shard_map/ppermute | solution.py:1080
  84.8 4.3 collective-permute-start.12
  86.9 63.2 %collective-permute-start.22 = (bf16[1024,1024]{1,0:T(8,128)(2,1)}, bf16[1024,1024]{1,0:T(8,128)(2,1)}, u32[]{:S(2)}, u32[]{:S(2)}) collective-permute-start(bf16[1024,1024]{1,0:T(8,128)(2,1)} %get-tuple-element.229), channel_id=1, source_target_pairs={{0,1},{1,0},{2,3},{3,2},{4,5},{5,4},{6,7},{7,6},{8,9},{9,8},{10,11... | collective-permute-start | bytes 6291464 | tf_op jit(solution)/shard_map/ppermute | solution.py:1080
  88.3 62.5 %collective-permute-start.19 = (bf16[256,2048]{1,0:T(8,128)(2,1)}, bf16[256,2048]{1,0:T(8,128)(2,1)}, u32[]{:S(2)}, u32[]{:S(2)}) collective-permute-start(bf16[256,2048]{1,0:T(8,128)(2,1)} %collective-permute-done.18.refs_0_), channel_id=1, source_target_pairs={{0,4},{2,6},{4,0},{6,2},{8,12},{10,14},{12,8},{14,10},{16,20},{18,... | collective-permute-start | bytes 3145736 | tf_op jit(solution)/shard_map/ppermute | solution.py:1080
  129.4 21.8 %collective-permute-start.17 = (bf16[2,2,512,1024]{3,2,1,0:T(8,128)(2,1)}, bf16[2,2,512,1024]{3,2,1,0:T(8,128)(2,1)}, u32[]{:S(2)}, u32[]{:S(2)}) collective-permute-start(bf16[2,2,512,1024]{3,2,1,0:T(8,128)(2,1)} %get-tuple-element.221), channel_id=1, source_target_pairs={{0,2},{2,0},{4,6},{6,4},{8,10},{10,8},{12,14},{14,12},{16,18},{18,... | collective-permute-start | bytes 12582920 | tf_op jit(solution)/shard_map/ppermute | solution.py:1080
  150.2 7.7 %collective-permute-start.23 = (bf16[1024,1024]{1,0:T(8,128)(2,1)}, bf16[1024,1024]{1,0:T(8,128)(2,1)S(1)}, u32[]{:S(2)}, u32[]{:S(2)}) collective-permute-start(bf16[1024,1024]{1,0:T(8,128)(2,1)} %collective-permute-done.22.refs_4_), channel_id=1, source_target_pairs={{0,2},{2,0},{4,6},{6,4},{8,10},{10,8},{12,14},{14,12},{16,18},{18,... | collective-permute-start | bytes 6291464 | tf_op jit(solution)/shard_map/ppermute | solution.py:1080
  150.7 5.5 %collective-permute-start.20 = (bf16[256,2048]{1,0:T(8,128)(2,1)}, bf16[256,2048]{1,0:T(8,128)(2,1)}, u32[]{:S(2)}, u32[]{:S(2)}) collective-permute-start(bf16[256,2048]{1,0:T(8,128)(2,1)} %collective-permute-done.18.refs_0_), channel_id=1, source_target_pairs={{0,2},{2,0},{4,6},{6,4},{8,10},{10,8},{12,14},{14,12},{16,18},{18,... | collective-permute-start | bytes 3145736 | tf_op jit(solution)/shard_map/ppermute | solution.py:1080
  150.8 7.0 %collective-permute-start.21 = (bf16[256,2048]{1,0:T(8,128)(2,1)}, bf16[256,2048]{1,0:T(8,128)(2,1)}, u32[]{:S(2)}, u32[]{:S(2)}) collective-permute-start(bf16[256,2048]{1,0:T(8,128)(2,1)} %collective-permute-done.19.refs_1_), channel_id=1, source_target_pairs={{0,2},{2,0},{4,6},{6,4},{8,10},{10,8},{12,14},{14,12},{16,18},{18,... | collective-permute-start | bytes 3145736 | tf_op jit(solution)/shard_map/ppermute | solution.py:1080
  154.2 57.2 %collective-permute-start.25 = (bf16[512,1024]{1,0:T(8,128)(2,1)}, bf16[512,1024]{1,0:T(8,128)(2,1)}, u32[]{:S(2)}, u32[]{:S(2)}) collective-permute-start(bf16[512,1024]{1,0:T(8,128)(2,1)} %fusion.5), channel_id=1, source_target_pairs={{0,4},{2,6},{4,0},{6,2},{8,12},{10,14},{12,8},{14,10},{16,20},{18,... | collective-permute-start | bytes 3145736 | tf_op jit(solution)/shard_map/ppermute | solution.py:1080
  180.4 24.7 %collective-permute-start.24 = (bf16[2,2,512,1024]{3,2,1,0:T(8,128)(2,1)}, bf16[2,2,512,1024]{3,2,1,0:T(8,128)(2,1)S(1)}, u32[]{:S(2)}, u32[]{:S(2)}) collective-permute-start(bf16[2,2,512,1024]{3,2,1,0:T(8,128)(2,1)} %get-tuple-element.237), channel_id=1, source_target_pairs={{0,2},{2,0},{4,6},{6,4},{8,10},{10,8},{12,14},{14,12},{16,18},{18,... | collective-permute-start | bytes 12582920 | tf_op jit(solution)/shard_map/ppermute | solution.py:1080
  205.5 33.4 %collective-permute-start.26 = (bf16[512,1024]{1,0:T(8,128)(2,1)S(1)}, bf16[512,1024]{1,0:T(8,128)(2,1)}, u32[]{:S(2)}, u32[]{:S(2)}) collective-permute-start(bf16[512,1024]{1,0:T(8,128)(2,1)S(1)} %fusion.4), channel_id=1, source_target_pairs={{0,4},{2,6},{4,0},{6,2},{8,12},{10,14},{12,8},{14,10},{16,20},{18,... | collective-permute-start | bytes 3145736 | tf_op jit(solution)/shard_map/ppermute | solution.py:1080
  210.5 58.7 %collective-permute-start.27 = (bf16[2,512,1024]{2,1,0:T(8,128)(2,1)}, bf16[2,512,1024]{2,1,0:T(8,128)(2,1)}, u32[]{:S(2)}, u32[]{:S(2)}) collective-permute-start(bf16[2,512,1024]{2,1,0:T(8,128)(2,1)} %fusion), channel_id=1, source_target_pairs={{0,1},{1,0},{2,3},{3,2},{4,5},{5,4},{6,7},{7,6},{8,9},{9,8},{10,11... | collective-permute-start | bytes 6291464 | tf_op jit(solution)/shard_map/ppermute | solution.py:1080
  250.0 24.1 %collective-permute-start.28 = (bf16[2,2,512,768]{3,2,1,0:T(8,128)(2,1)}, bf16[2,2,512,768]{3,2,1,0:T(8,128)(2,1)S(1)}, u32[]{:S(2)}, u32[]{:S(2)}) collective-permute-start(bf16[2,2,512,768]{3,2,1,0:T(8,128)(2,1)} %weight_mid.4), channel_id=1, source_target_pairs={{0,2},{2,0},{4,6},{6,4},{8,10},{10,8},{12,14},{14,12},{16,18},{18,... | collective-permute-start | bytes 9437192 | tf_op jit(solution)/shard_map/ppermute | solution.py:1080
  256.0 25.4 %collective-permute-start.29 = (bf16[2,2,512,768]{3,2,1,0:T(8,128)(2,1)S(1)}, bf16[2,2,512,768]{3,2,1,0:T(8,128)(2,1)S(1)}, u32[]{:S(2)}, u32[]{:S(2)}) collective-permute-start(bf16[2,2,512,768]{3,2,1,0:T(8,128)(2,1)S(1)} %weight_mid.5), channel_id=1, source_target_pairs={{0,2},{2,0},{4,6},{6,4},{8,10},{10,8},{12,14},{14,12},{16,18},{18,... | collective-permute-start | bytes 9437192 | tf_op jit(solution)/shard_map/ppermute | solution.py:1080
  256.6 34.8 %collective-permute-start.31 = (bf16[512,1024]{1,0:T(8,128)(2,1)}, bf16[512,1024]{1,0:T(8,128)(2,1)}, u32[]{:S(2)}, u32[]{:S(2)}) collective-permute-start(bf16[512,1024]{1,0:T(8,128)(2,1)} %fusion.3), channel_id=1, source_target_pairs={{0,1},{1,0},{2,3},{3,2},{4,5},{5,4},{6,7},{7,6},{8,9},{9,8},{10,11... | collective-permute-start | bytes 3145736 | tf_op jit(solution)/shard_map/ppermute | solution.py:1080
  271.5 26.1 %collective-permute-start.30 = (bf16[512,1024]{1,0:T(8,128)(2,1)S(1)}, bf16[512,1024]{1,0:T(8,128)(2,1)S(1)}, u32[]{:S(2)}, u32[]{:S(2)}) collective-permute-start(bf16[512,1024]{1,0:T(8,128)(2,1)S(1)} %fusion.1), channel_id=1, source_target_pairs={{0,4},{2,6},{4,0},{6,2},{8,12},{10,14},{12,8},{14,10},{16,20},{18,... | collective-permute-start | bytes 3145736 | tf_op jit(solution)/shard_map/ppermute | solution.py:1080
  280.6 64.7 %collective-permute-start.33 = (bf16[2,512,768]{2,1,0:T(8,128)(2,1)}, bf16[2,512,768]{2,1,0:T(8,128)(2,1)}, u32[]{:S(2)}, u32[]{:S(2)}) collective-permute-start(bf16[2,512,768]{2,1,0:T(8,128)(2,1)} %get-tuple-element.267), channel_id=1, source_target_pairs={{0,4},{2,6},{4,0},{6,2},{8,12},{10,14},{12,8},{14,10},{16,20},{18,... | collective-permute-start | bytes 4718600 | tf_op jit(solution)/shard_map/ppermute | solution.py:1080
  291.3 22.1 %collective-permute-start.32 = (bf16[2,2,512,640]{3,2,1,0:T(8,128)(2,1)S(1)}, bf16[2,2,512,640]{3,2,1,0:T(8,128)(2,1)S(1)}, u32[]{:S(2)}, u32[]{:S(2)}) collective-permute-start(bf16[2,2,512,640]{3,2,1,0:T(8,128)(2,1)S(1)} %weight_value.2), channel_id=1, source_target_pairs={{0,2},{2,0},{4,6},{6,4},{8,10},{10,8},{12,14},{14,12},{16,18},{18,... | collective-permute-start | bytes 7864328 | tf_op jit(solution)/shard_map/ppermute | solution.py:1080
  301.1 45.8 %collective-permute-start.35 = (bf16[2,2,128,1024]{3,2,1,0:T(8,128)(2,1)}, bf16[2,2,128,1024]{3,2,1,0:T(8,128)(2,1)}, u32[]{:S(2)}, u32[]{:S(2)}) collective-permute-start(bf16[2,2,128,1024]{3,2,1,0:T(8,128)(2,1)} %pad_maximum_fusion), channel_id=1, source_target_pairs={{0,8},{2,10},{4,12},{6,14},{8,0},{10,2},{12,4},{14,6},{16,24},{18,... | collective-permute-start | bytes 3145736 | tf_op jit(solution)/shard_map/ppermute | solution.py:1080
  311.5 33.7 %collective-permute-start.34 = (bf16[2,512,768]{2,1,0:T(8,128)(2,1)S(1)}, bf16[2,512,768]{2,1,0:T(8,128)(2,1)S(1)}, u32[]{:S(2)}, u32[]{:S(2)}) collective-permute-start(bf16[2,512,768]{2,1,0:T(8,128)(2,1)S(1)} %get-tuple-element.297), channel_id=1, source_target_pairs={{0,1},{1,0},{2,3},{3,2},{4,5},{5,4},{6,7},{7,6},{8,9},{9,8},{10,11... | collective-permute-start | bytes 4718600 | tf_op jit(solution)/shard_map/ppermute | solution.py:1080
  319.1 45.6 %collective-permute-start.37 = (bf16[2,2,2,128,640]{4,3,2,1,0:T(8,128)(2,1)}, bf16[2,2,2,128,640]{4,3,2,1,0:T(8,128)(2,1)}, u32[]{:S(2)}, u32[]{:S(2)}) collective-permute-start(bf16[2,2,2,128,640]{4,3,2,1,0:T(8,128)(2,1)} %get-tuple-element.332), channel_id=1, source_target_pairs={{0,8},{2,10},{4,12},{6,14},{8,0},{10,2},{12,4},{14,6},{16,24},{18,... | collective-permute-start | bytes 3932168 | tf_op jit(solution)/shard_map/ppermute | solution.py:1080
  349.4 22.8 %collective-permute-start.36 = (bf16[2,128,1024]{2,1,0:T(8,128)(2,1)S(1)}, bf16[2,128,1024]{2,1,0:T(8,128)(2,1)S(1)}, u32[]{:S(2)}, u32[]{:S(2)}) collective-permute-start(bf16[2,128,1024]{2,1,0:T(8,128)(2,1)S(1)} %pad_maximum_fusion.2), channel_id=1, source_target_pairs={{0,16},{2,18},{4,20},{6,22},{8,24},{10,26},{12,28},{14,30},{16,0},... | collective-permute-start | bytes 1572872 | tf_op jit(solution)/shard_map/ppermute | solution.py:1080
  352.0 25.3 %collective-permute-start.40 = (bf16[512,768]{1,0:T(8,128)(2,1)S(1)}, bf16[512,768]{1,0:T(8,128)(2,1)S(1)}, u32[]{:S(2)}, u32[]{:S(2)}) collective-permute-start(bf16[512,768]{1,0:T(8,128)(2,1)S(1)} %fusion.7), channel_id=1, source_target_pairs={{0,4},{2,6},{4,0},{6,2},{8,12},{10,14},{12,8},{14,10},{16,20},{18,... | collective-permute-start | bytes 2359304 | tf_op jit(solution)/shard_map/ppermute | solution.py:1080
  353.0 24.3 %collective-permute-start.39 = (bf16[512,768]{1,0:T(8,128)(2,1)S(1)}, bf16[512,768]{1,0:T(8,128)(2,1)S(1)}, u32[]{:S(2)}, u32[]{:S(2)}) collective-permute-start(bf16[512,768]{1,0:T(8,128)(2,1)S(1)} %fusion.6), channel_id=1, source_target_pairs={{0,1},{1,0},{2,3},{3,2},{4,5},{5,4},{6,7},{7,6},{8,9},{9,8},{10,11... | collective-permute-start | bytes 2359304 | tf_op jit(solution)/shard_map/ppermute | solution.py:1080
  363.5 13.9 %collective-permute-start.38 = (f32[272,128]{1,0:T(8,128)S(1)}, f32[272,128]{1,0:T(8,128)S(1)}, u32[]{:S(2)}, u32[]{:S(2)}) collective-permute-start(f32[272,128]{1,0:T(8,128)S(1)} %constant_dynamic-update-slice_fusion), channel_id=1, source_target_pairs={{0,8},{2,10},{4,12},{6,14},{8,0},{10,2},{12,4},{14,6},{16,24},{18,... | collective-permute-start | bytes 417800 | tf_op jit(solution)/shard_map/ppermute | solution.py:1080
  366.1 30.4 %collective-permute-start.46 = (bf16[2,2,128,640]{3,2,1,0:T(8,128)(2,1)S(1)}, bf16[2,2,128,640]{3,2,1,0:T(8,128)(2,1)S(1)}, u32[]{:S(2)}, u32[]{:S(2)}) collective-permute-start(bf16[2,2,128,640]{3,2,1,0:T(8,128)(2,1)S(1)} %fusion.8), channel_id=1, source_target_pairs={{0,4},{2,6},{4,0},{6,2},{8,12},{10,14},{12,8},{14,10},{16,20},{18,... | collective-permute-start | bytes 1966088 | tf_op jit(solution)/shard_map/ppermute | solution.py:1080
  377.4 11.5 %collective-permute-start.41 = (f32[272,128]{1,0:T(8,128)S(1)}, f32[272,128]{1,0:T(8,128)S(1)}, u32[]{:S(2)}, u32[]{:S(2)}) collective-permute-start(f32[272,128]{1,0:T(8,128)S(1)} %add.618), channel_id=1, source_target_pairs={{0,16},{2,18},{4,20},{6,22},{8,24},{10,26},{12,28},{14,30},{16,0},... | collective-permute-start | bytes 417800 | tf_op jit(solution)/shard_map/ppermute | solution.py:1080
  379.2 19.7 %collective-permute-start.44 = (bf16[2,2,128,768]{3,2,1,0:T(8,128)(2,1)S(1)}, bf16[2,2,128,768]{3,2,1,0:T(8,128)(2,1)S(1)}, u32[]{:S(2)}, u32[]{:S(2)}) collective-permute-start(bf16[2,2,128,768]{3,2,1,0:T(8,128)(2,1)S(1)} %pad_maximum_fusion.1), channel_id=1, source_target_pairs={{0,8},{2,10},{4,12},{6,14},{8,0},{10,2},{12,4},{14,6},{16,24},{18,... | collective-permute-start | bytes 2359304 | tf_op jit(solution)/shard_map/ppermute | solution.py:1080
  383.9 7.2 %collective-permute-start.50 = (bf16[2,64,1024]{2,1,0:T(8,128)(2,1)S(1)}, bf16[2,64,1024]{2,1,0:T(8,128)(2,1)S(1)}, u32[]{:S(2)}, u32[]{:S(2)}) collective-permute-start(bf16[2,64,1024]{2,1,0:T(8,128)(2,1)S(1)} %fusion.25), channel_id=1, source_target_pairs={{0,2},{2,0},{4,6},{6,4},{8,10},{10,8},{12,14},{14,12},{16,18},{18,... | collective-permute-start | bytes 786440 | tf_op jit(solution)/shard_map/ppermute | solution.py:1080
  390.5 6.0 %collective-permute-start.43 = (f32[272,128]{1,0:T(8,128)S(1)}, f32[272,128]{1,0:T(8,128)S(1)}, u32[]{:S(2)}, u32[]{:S(2)}) collective-permute-start(f32[272,128]{1,0:T(8,128)S(1)} %add.624), channel_id=1, source_target_pairs={{0,4},{2,6},{4,0},{6,2},{8,12},{10,14},{12,8},{14,10},{16,20},{18,... | collective-permute-start | bytes 417800 | tf_op jit(solution)/shard_map/ppermute | solution.py:1080
  397.6 12.2 %collective-permute-start.47 = (bf16[2,128,640]{2,1,0:T(8,128)(2,1)S(1)}, bf16[2,128,640]{2,1,0:T(8,128)(2,1)S(1)}, u32[]{:S(2)}, u32[]{:S(2)}) collective-permute-start(bf16[2,128,640]{2,1,0:T(8,128)(2,1)S(1)} %fusion.9), channel_id=1, source_target_pairs={{0,1},{1,0},{2,3},{3,2},{4,5},{5,4},{6,7},{7,6},{8,9},{9,8},{10,11... | collective-permute-start | bytes 983048 | tf_op jit(solution)/shard_map/ppermute | solution.py:1080
  400.0 9.8 %collective-permute-start.45 = (f32[272,128]{1,0:T(8,128)S(1)}, f32[272,128]{1,0:T(8,128)S(1)}, u32[]{:S(2)}, u32[]{:S(2)}) collective-permute-start(f32[272,128]{1,0:T(8,128)S(1)} %add.625), channel_id=1, source_target_pairs={{0,1},{1,0},{2,3},{3,2},{4,5},{5,4},{6,7},{7,6},{8,9},{9,8},{10,11... | collective-permute-start | bytes 417800 | tf_op jit(solution)/shard_map/ppermute | solution.py:1080
  402.0 26.6 %collective-permute-start.48 = (bf16[2,128,768]{2,1,0:T(8,128)(2,1)}, bf16[2,128,768]{2,1,0:T(8,128)(2,1)}, u32[]{:S(2)}, u32[]{:S(2)}) collective-permute-start(bf16[2,128,768]{2,1,0:T(8,128)(2,1)} %pad_maximum_fusion.3), channel_id=1, source_target_pairs={{0,16},{2,18},{4,20},{6,22},{8,24},{10,26},{12,28},{14,30},{16,0},... | collective-permute-start | bytes 1179656 | tf_op jit(solution)/shard_map/ppermute | solution.py:1080
  411.7 16.9 %collective-permute-start.49 = (bf16[128,640]{1,0:T(8,128)(2,1)}, bf16[128,640]{1,0:T(8,128)(2,1)}, u32[]{:S(2)}, u32[]{:S(2)}) collective-permute-start(bf16[128,640]{1,0:T(8,128)(2,1)} %fusion.22), channel_id=1, source_target_pairs={{0,16},{2,18},{4,20},{6,22},{8,24},{10,26},{12,28},{14,30},{16,0},... | collective-permute-start | bytes 491528 | tf_op jit(solution)/shard_map/ppermute | solution.py:1080
  (114 other events, 916.5 us)

commit v8 on v7

--- a/solution.py
+++ b/solution.py
@@ -1240,22 +1240,22 @@
     val_sent = k_weight_value(after(mb_own), normed, dv_own, dv_oth, ema_low, dz, 5)
     val_got = over_core(val_sent)
     dn_got_y = dn_y[1]
-    up_got_x, dn_got_y = held((up_got_x, dn_got_y), val_sent)
+    quarter = blocks // 4
+
+    def ema_back(dep, first, count, before=None):
+        return k_ema_backward(
+            after(*dep), normed, de_part, dz, e_slope, w_z, decay, coef, omega, first, count, before
+        )
+
+    eb = ema_back((val_sent,), 0, quarter)
+    up_got_x, dn_got_y = held((up_got_x, dn_got_y), eb[1])
     dn_terms = [dno, got_o[0, 0], dn_got_x1, dn_got_y]
     up_terms = [upo, got_o[1, 0], up_got_y[0], up_got_x]
     ffn_z = jnp.stack([z_send(dn_terms), z_send(up_terms)])
     dn_terms, up_terms = z_keep(dn_terms), z_keep(up_terms)
     ffn_got_z = over_z(ffn_z)
-    quarter = blocks // 4
-
-    def ema_back(dep, first, count, before=None):
-        return k_ema_backward(
-            after(*dep), normed, de_part, dz, e_slope, w_z, decay, coef, omega, first, count, before
-        )
-
-    eb = ema_back((val_sent, ffn_z), 0, quarter)
     val = k_weight_value(
-        after(eb[1]), normed, dv_own, dv_oth, ema_low, dz, 4, val_got
+        after(eb[1], ffn_z), normed, dv_own, dv_oth, ema_low, dz, 4, val_got
     )
     val = val.reshape(2, 2, 2, 2, d // 8, val.shape[-1])
     val_z1 = val[:, :, :, 1]

time: 444 us -> 443 us (level)
    unnamed x221 -> x211, local copies, waits for them, and re-layouts: 20.1 us -> 19.5 us
  transfers between devices with their start and end apart: 53 -> 53, of which waited for: 14 -> 13; matrix products, arithmetic and copies ran while one was open for 10% -> 11% of each run, Pallas kernels for 61% -> 61%
where the time goes in v8:
time: 443 us; the launch traced here: 437 us
  Pallas kernels  265 us (60%)
  waiting for transfers between devices  51.1 us (12%)
  starting transfers between devices  43.5 us (10%)
  local copies, waits for them, and re-layouts  38.8 us (9%)
  other arithmetic  35.6 us (8%)
    pallas_call x28, Pallas kernels, run(): pl.pallas_call(body, out_shape=out_shape, grid_spec=pltpu.PrefetchScalarG...  265 us
    ppermute x53, waiting for transfers between devices, swap(): return lax.ppermute(values, axis, [(i, i ^ bit) for i in range(size)])  51.1 us
    ppermute x53, starting transfers between devices, swap(): return lax.ppermute(values, axis, [(i, i ^ bit) for i in range(size)])  43.5 us
    convert_element_type x13, other arithmetic, add(): return total(*values).astype(BF)  20.2 us
    unnamed x211, local copies, waits for them, and re-layouts  19.5 us
  transfers between devices with their start and end apart: 53, of which 13 were waited for; matrix products, arithmetic and copies ran while one was open for 11% of the time, Pallas kernels for 61%

profile of v8, /device:TPU:0, one launch (start us, length us, event | category | flops | bytes accessed | tf_op | source)
XLA Modules:
  0.0 436.9 jit_solution(7822521625650626471)
XLA Ops:
  0.7 1.9 constant_dynamic-slice_fusion
  2.6 3.0 collective-permute-start.4
  6.2 2.1 pack_params.1.own_ref
  8.4 5.7 %pieces.1 = (bf16[256,1024]{1,0:T(8,128)(2,1)}, bf16[256,1024]{1,0:T(8,128)(2,1)}, bf16[256,1024]{1,0:T(8,128)(2,1)}, bf16[256,2048]{1,0:T(8,128)(2,1)}, bf16[1024,1024]{1,0:T(8,128)(2,1)}) custom-call(s32[16]{0:T(128)} %stack.105.s, bf16[1024,1024]{1,0:T(8,128)(2,1)} %wo.5, bf16[1024,1024]{1,0:T(8,128)(2,1)} %uo.3, bf16[512,1024]{1,0:T(8,128)(2,1)} %ho.3, ...), custom_call_target="tpu_custom_call" | custom-call | flops 100000000 | bytes 235929600 | tf_op jit(solution)/shard_map/pieces/pallas_call | solution.py:351
  14.1 5.2 %value_own.1 = (bf16[1024,1024]{1,0:T(8,128)(2,1)S(1)}, bf16[1024,1024]{1,0:T(8,128)(2,1)S(1)}, bf16[1024,1024]{1,0:T(8,128)(2,1)S(1)}) custom-call(s32[16]{0:T(128)S(1)} %copy-done.17, bf16[1024,1024]{1,0:T(8,128)(2,1)S(1)} %copy-done.23, bf16[1024,1024]{1,0:T(8,128)(2,1)S(1)} %copy-done.9), custom_call_target="tpu_custom_call" | custom-call | flops 21474836480 | bytes 104857600 | tf_op jit(solution)/shard_map/value_own/pallas_call | solution.py:351
  24.3 2.4 ema_params.1
  29.0 6.8 %ema_forward.2 = (bf16[1024,1024]{1,0:T(8,128)(2,1)S(1)}, bf16[1024,1024]{1,0:T(8,128)(2,1)S(1)}, f32[128,128]{1,0:T(8,128)S(1)}) custom-call(s32[16]{0:T(128)S(1)} %copy-done.18, bf16[1024,1024]{1,0:T(8,128)(2,1)S(1)} %get-tuple-element.179.x_ref, f32[128,128]{1,0:T(8,128)S(1)} %copy-done.11, f32[128,128]{1,0:T(8,128)S(1)} %copy-done.14, ...), custom_call_target="tpu_custom_call" | custom-call | flops 99999997952 | bytes 64921600 | tf_op jit(solution)/shard_map/ema_forward/pallas_call | solution.py:351
  39.7 7.2 %ema_forward.3 = (bf16[1024,1024]{1,0:T(8,128)(2,1)S(1)}, bf16[1024,1024]{1,0:T(8,128)(2,1)S(1)}, f32[128,128]{1,0:T(8,128)}) custom-call(s32[16]{0:T(128)S(1)} %copy-done.18, bf16[1024,1024]{1,0:T(8,128)(2,1)S(1)} %get-tuple-element.179.x_ref, f32[128,128]{1,0:T(8,128)S(1)} %copy-done.12, ...), custom_call_target="tpu_custom_call", output_to_operand_aliasing={{0}: (6, {}), {1}: (7, {})} | custom-call | flops 99999997952 | bytes 107520000 | tf_op jit(solution)/shard_map/ema_forward/pallas_call | solution.py:351
  52.5 4.7 %act_other.1 = (bf16[1024,1024]{1,0:T(8,128)(2,1)S(1)}, bf16[1024,1024]{1,0:T(8,128)(2,1)S(1)}) custom-call(s32[16]{0:T(128)S(1)} %copy-done.18, bf16[1024,1024]{1,0:T(8,128)(2,1)S(1)} %get-tuple-element.179.x_ref, bf16[256,1024]{1,0:T(8,128)(2,1)S(1)} %collective-permute-done.4.p0.w0, bf16[256,1024]{1,0:T(8,128)(2,1)S(1)} %collective-permute-done.5.p1.w1, ...), custom_call_target="tpu_custom_call" | custom-call | flops 21474836480 | bytes 83886080 | tf_op jit(solution)/shard_map/act_other/pallas_call | solution.py:351
  62.7 2.4 collective-permute-done.13.h0.f0
  67.3 16.7 %attend.1 = (bf16[1024,1024]{1,0:T(8,128)(2,1)}, bf16[1024,1024]{1,0:T(8,128)(2,1)}, bf16[1024,1024]{1,0:T(8,128)(2,1)}, bf16[1024,1024]{1,0:T(8,128)(2,1)}, bf1...) custom-call(s32[16]{0:T(128)} %stack.105.s, bf16[1024,128]{1,0:T(8,128)(2,1)} %copy-done.36, ...), custom_call_target="tpu_custom_call" | custom-call | flops 71470940160 | bytes 256901120 | tf_op jit(solution)/shard_map/attend/pallas_call | solution.py:351
  90.2 18.8 %gate.1 = (bf16[1024,1024]{1,0:T(8,128)(2,1)}, bf16[1024,1024]{1,0:T(8,128)(2,1)}, bf16[1024,1024]{1,0:T(8,128)(2,1)}, bf16[1024,1024]{1,0:T(8,128)(2,1)}, bf16[1024,1024]{1,0:T(8,128)(2,1)}) custom-call(s32[16]{0:T(128)} %stack.105.s, bf16[1024,1024]{1,0:T(8,128)(2,1)} %get-tuple-element.204.go.refs_1_, bf16[1024,1024]{1,0:T(8,128)(2,1)} %get-tuple-element.205.gt.refs_2_, ...), custom_call_target="tpu_custom_call" | custom-call | flops 85899345920 | bytes 293601280 | tf_op jit(solution)/shard_map/gate/pallas_call | solution.py:351
  109.0 20.3 %ffn.4 = (bf16[1024,1024]{1,0:T(8,128)(2,1)}, bf16[1024,1024]{1,0:T(8,128)(2,1)}, bf16[2,2,512,1024]{3,2,1,0:T(8,128)(2,1)}) custom-call(s32[16]{0:T(128)} %stack.105.s, bf16[1024,1024]{1,0:T(8,128)(2,1)} %get-tuple-element.215.low_ref, bf16[1024,1024]{1,0:T(8,128)(2,1)} %c_ref.9, bf16[1024,2048]{1,0:T(8,128)(2,1)} %refs_0_.5, bf16[2048,1024]{1,0:T(8,128)(2,1)} %refs_1_.5), custom_call_target="tpu_custom_call" | custom-call | flops 128849018880 | bytes 209715200 | tf_op jit(solution)/shard_map/ffn/pallas_call | solution.py:351
  129.3 20.6 %ffn.5 = (bf16[1024,1024]{1,0:T(8,128)(2,1)}, bf16[1024,1024]{1,0:T(8,128)(2,1)}, bf16[512,1024]{1,0:T(8,128)(2,1)}, bf16[512,1024]{1,0:T(8,128)(2,1)}, bf16[512...) custom-call(s32[16]{0:T(128)} %stack.105.s, bf16[1024,1024]{1,0:T(8,128)(2,1)} %get-tuple-element.215.low_ref, ...), custom_call_target="tpu_custom_call" | custom-call | flops 128849018880 | bytes 251658240 | tf_op jit(solution)/shard_map/ffn/pallas_call | solution.py:351
  151.1 2.9 fusion.5
  159.0 21.2 %ffn.6 = (bf16[1024,1024]{1,0:T(8,128)(2,1)}, bf16[1024,1024]{1,0:T(8,128)(2,1)}, bf16[2,2,512,1024]{3,2,1,0:T(8,128)(2,1)}) custom-call(s32[16]{0:T(128)} %stack.105.s, bf16[1024,1024]{1,0:T(8,128)(2,1)} %get-tuple-element.215.low_ref, bf16[1024,1024]{1,0:T(8,128)(2,1)} %c_ref.9, bf16[256,2048]{1,0:T(8,128)(2,1)} %collective-permute-done.18.refs_0_, ...), custom_call_target="tpu_custom_call" | custom-call | flops 128849018880 | bytes 230686720 | tf_op jit(solution)/shard_map/ffn/pallas_call | solution.py:351
  180.6 21.1 %ffn.7 = (bf16[1024,1024]{1,0:T(8,128)(2,1)}, bf16[1024,1024]{1,0:T(8,128)(2,1)}, bf16[512,1024]{1,0:T(8,128)(2,1)}, bf16[512,1024]{1,0:T(8,128)(2,1)}, bf16[2,512,1024]{2,1,0:T(8,128)(2,1)}) custom-call(s32[16]{0:T(128)} %stack.105.s, bf16[1024,1024]{1,0:T(8,128)(2,1)} %get-tuple-element.215.low_ref, bf16[1024,1024]{1,0:T(8,128)(2,1)} %c_ref.9, ...), custom_call_target="tpu_custom_call" | custom-call | flops 128849018880 | bytes 230686720 | tf_op jit(solution)/shard_map/ffn/pallas_call | solution.py:351
  201.7 3.1 fusion.36
  207.9 2.3 fusion
  211.2 27.5 %mid_back.1 = (bf16[1024,1024]{1,0:T(8,128)(2,1)}, bf16[1024,1024]{1,0:T(8,128)(2,1)}, bf16[1024,1024]{1,0:T(8,128)(2,1)}, bf16[1024,1024]{1,0:T(8,128)(2,1)}, b...) custom-call(s32[16]{0:T(128)} %stack.105.s, ...), custom_call_target="tpu_custom_call" | custom-call | flops 128849018880 | bytes 566231040 | tf_op jit(solution)/shard_map/mid_back/pallas_call | solution.py:351
  238.7 3.3 fusion.3
  243.7 6.2 %weight_mid.4 = bf16[2,2,512,768]{3,2,1,0:T(8,128)(2,1)} custom-call(s32[16]{0:T(128)S(1)} %copy-done.19, bf16[1024,1024]{1,0:T(8,128)(2,1)S(1)} %copy-done.59, bf16[1024,1024]{1,0:T(8,128)(2,1)S(1)} %copy-done.55, bf16[1024,1024]{1,0:T(8,128)(2,1)S(1)} %copy-done.57, bf16[1024,1024]{1,0:T(8,128)(2,1)S(1)} %copy-done.3, bf16[1024,1024]{1,0:T(8,128)(2,1)S(1)} %copy-done.3), custom_call_target="tpu_custom_call" | custom-call | flops 32212254720 | bytes 136314880 | tf_op jit(solution)/shard_map/weight_mid/pallas_call | solution.py:351
  250.0 5.8 %weight_mid.5 = bf16[2,2,512,768]{3,2,1,0:T(8,128)(2,1)S(1)} custom-call(s32[16]{0:T(128)S(1)} %copy-done.19, bf16[1024,1024]{1,0:T(8,128)(2,1)S(1)} %copy-done.3, bf16[1024,1024]{1,0:T(8,128)(2,1)S(1)} %copy-done.49, bf16[1024,1024]{1,0:T(8,128)(2,1)S(1)} %copy-done.51, bf16[1024,1024]{1,0:T(8,128)(2,1)S(1)} %copy-done.53, ...), custom_call_target="tpu_custom_call" | custom-call | flops 32212254720 | bytes 157286400 | tf_op jit(solution)/shard_map/weight_mid/pallas_call | solution.py:351
  259.1 9.8 %attend_back.1 = (bf16[1024,1024]{1,0:T(8,128)(2,1)S(1)}, bf16[1024,1024]{1,0:T(8,128)(2,1)S(1)}, bf16[1024,128]{1,0:T(8,128)(2,1)S(1)}, f32[8,128]{1,0:T(8,128)S(1)}) custom-call(s32[16]{0:T(128)S(1)} %copy-done.19, bf16[1024,1024]{1,0:T(8,128)(2,1)S(1)} %copy-done.61, bf16[1024,1024]{1,0:T(8,128)(2,1)S(1)} %copy-done.62, ...), custom_call_target="tpu_custom_call" | custom-call | flops 53687091200 | bytes 201902080 | tf_op jit(solution)/shard_map/attend_back/pallas_call | solution.py:351
  269.0 3.3 fusion.1
  273.5 2.3 slice.460
  275.9 6.4 %weight_mid.6 = (bf16[2,512,768]{2,1,0:T(8,128)(2,1)}, bf16[2,512,768]{2,1,0:T(8,128)(2,1)S(1)}) custom-call(s32[16]{0:T(128)S(1)} %copy-done.19, bf16[1024,1024]{1,0:T(8,128)(2,1)S(1)} %copy-done.60, bf16[1024,1024]{1,0:T(8,128)(2,1)S(1)} %copy-done.56, bf16[1024,1024]{1,0:T(8,128)(2,1)S(1)} %copy-done.58, bf16[1024,1024]{1,0:T(8,128)(2,1)S(1)} %copy-done.3, ...), custom_call_target="tpu_custom_call" | custom-call | flops 32212254720 | bytes 167772160 | tf_op jit(solution)/shard_map/weight_mid/pallas_call | solution.py:351
  282.3 6.1 %weight_mid.7 = (bf16[2,512,768]{2,1,0:T(8,128)(2,1)S(1)}, bf16[2,512,768]{2,1,0:T(8,128)(2,1)S(1)}) custom-call(s32[16]{0:T(128)S(1)} %copy-done.19, bf16[1024,1024]{1,0:T(8,128)(2,1)S(1)} %copy-done.3, bf16[1024,1024]{1,0:T(8,128)(2,1)S(1)} %copy-done.50, bf16[1024,1024]{1,0:T(8,128)(2,1)S(1)} %copy-done.52, bf16[1024,1024]{1,0:T(8,128)(2,1)S(1)} %copy-done.54, ...), custom_call_target="tpu_custom_call" | custom-call | flops 32212254720 | bytes 188743680 | tf_op jit(solution)/shard_map/weight_mid/pallas_call | solution.py:351
  288.5 3.7 weight_value.2
  293.2 7.8 %ema_backward0.1 = (f32[1024,1024]{1,0:T(8,128)S(1)}, f32[128,128]{1,0:T(8,128)S(1)}, f32[128,128]{1,0:T(8,128)S(1)}, f32[128,128]{1,0:T(8,128)S(1)}, f32[128,128]{1,0:T(8,128)S(1)}, /*index=5*/f32[8,128]{1,0:T(8,128)S(1)}) custom-call(s32[16]{0:T(128)S(1)} %copy-done.19, bf16[1024,1024]{1,0:T(8,128)(2,1)S(1)} %copy-done.1, ...), custom_call_target="tpu_custom_call" | custom-call | flops 99999997952 | bytes 114114560 | tf_op jit(solution)/shard_map/ema_backward0/pallas_call | solution.py:351
  308.8 3.9 weight_value.3
  312.7 1.8 slice_bitcast_fusion.1
  314.9 7.8 %ema_backward2.1 = (f32[1024,1024]{1,0:T(8,128)S(1)}, f32[128,128]{1,0:T(8,128)S(1)}, f32[128,128]{1,0:T(8,128)S(1)}, f32[128,128]{1,0:T(8,128)S(1)}, f32[128,128]{1,0:T(8,128)S(1)}, /*index=5*/f32[8,128]{1,0:T(8,128)S(1)}) custom-call(s32[16]{0:T(128)S(1)} %copy-done.19, bf16[1024,1024]{1,0:T(8,128)(2,1)S(1)} %copy-done.1, ...), custom_call_target="tpu_custom_call", output_to_operand_aliasing={{0}: (14, {})} | custom-call | flops 3000000000 | bytes 4761600 | tf_op jit(solution)/shard_map/ema_backward2/pallas_call | solution.py:351
  322.7 7.8 %ema_backward4.1 = (f32[1024,1024]{1,0:T(8,128)S(1)}, f32[128,128]{1,0:T(8,128)S(1)}, f32[128,128]{1,0:T(8,128)S(1)}, f32[128,128]{1,0:T(8,128)S(1)}, f32[128,128]{1,0:T(8,128)S(1)}, /*index=5*/f32[8,128]{1,0:T(8,128)S(1)}) custom-call(s32[16]{0:T(128)S(1)} %copy-done.19, bf16[1024,1024]{1,0:T(8,128)(2,1)S(1)} %copy-done.1, ...), custom_call_target="tpu_custom_call", output_to_operand_aliasing={{0}: (14, {})} | custom-call | flops 99999997952 | bytes 158720000 | tf_op jit(solution)/shard_map/ema_backward4/pallas_call | solution.py:351
  330.5 12.6 %collective-permute-done.34 = bf16[2,512,768]{2,1,0:T(8,128)(2,1)S(1)} collective-permute-done((bf16[2,512,768]{2,1,0:T(8,128)(2,1)S(1)}, bf16[2,512,768]{2,1,0:T(8,128)(2,1)S(1)}, u32[]{:S(2)}, u32[]{:S(2)}) %collective-permute-start.34) | collective-permute-done | bytes 1572896 | tf_op jit(solution)/shard_map/ppermute | solution.py:1080
  344.7 2.0 fusion.23
  346.7 2.6 collective-permute-start.36
  350.9 8.3 %ema_backward6.1 = (f32[1024,1024]{1,0:T(8,128)S(1)}, f32[128,128]{1,0:T(8,128)}, f32[128,128]{1,0:T(8,128)}, f32[128,128]{1,0:T(8,128)S(1)}, f32[128,128]{1,0:T(8,128)S(1)}, /*index=5*/f32[8,128]{1,0:T(8,128)S(1)}) custom-call(s32[16]{0:T(128)S(1)} %copy-done.19, bf16[1024,1024]{1,0:T(8,128)(2,1)S(1)} %copy-done.1, ...), custom_call_target="tpu_custom_call", output_to_operand_aliasing={{0}: (14, {})} | custom-call | flops 99999997952 | bytes 158720000 | tf_op jit(solution)/shard_map/ema_backward6/pallas_call | solution.py:351
  361.5 7.5 %collective-permute-done.37 = bf16[2,2,2,128,640]{4,3,2,1,0:T(8,128)(2,1)} collective-permute-done((bf16[2,2,2,128,640]{4,3,2,1,0:T(8,128)(2,1)}, bf16[2,2,2,128,640]{4,3,2,1,0:T(8,128)(2,1)}, u32[]{:S(2)}, u32[]{:S(2)}) %collective-permute-start.37) | collective-permute-done | bytes 1310752 | tf_op jit(solution)/shard_map/ppermute | solution.py:1080
  370.3 2.0 collective-permute-start.46
  372.4 5.1 %input_back.2.refs_0_ = f32[1024,1024]{1,0:T(8,128)} custom-call(s32[16]{0:T(128)S(1)} %copy-done.19, bf16[1024,1024]{1,0:T(8,128)(2,1)S(1)} %get-tuple-element.263.vo, bf16[1024,1024]{1,0:T(8,128)(2,1)S(1)} %get-tuple-element.271.vt, bf16[1024,1024]{1,0:T(8,128)(2,1)S(1)} %copy-done.10, bf16[256,1024]{1,0:T(8,128)(2,1)S(1)} %copy-done.26, ...), custom_call_target="tpu_custom_call" | custom-call | flops 21474836480 | bytes 209715200 | tf_op jit(solution)/shard_map/input_back/pallas_call | solution.py:351
  380.8 1.8 bitcast_add_fusion.1
  382.6 4.8 %input_back.3 = f32[1024,1024]{1,0:T(8,128)} custom-call(s32[16]{0:T(128)S(1)} %copy-done.19, bf16[1024,1024]{1,0:T(8,128)(2,1)S(1)} %get-tuple-element.263.vo, bf16[1024,1024]{1,0:T(8,128)(2,1)S(1)} %get-tuple-element.271.vt, bf16[1024,1024]{1,0:T(8,128)(2,1)S(1)} %copy-done.10, bf16[256,1024]{1,0:T(8,128)(2,1)S(1)} %copy-done.26, ...), custom_call_target="tpu_custom_call", output_to_operand_aliasing={{}: (11, {})} | custom-call | flops 21474836480 | bytes 251658240 | tf_op jit(solution)/shard_map/input_back/pallas_call | solution.py:351
  390.5 4.6 %collective-permute-done.43 = f32[272,128]{1,0:T(8,128)S(1)} collective-permute-done((f32[272,128]{1,0:T(8,128)S(1)}, f32[272,128]{1,0:T(8,128)S(1)}, u32[]{:S(2)}, u32[]{:S(2)}) %collective-permute-start.43) | collective-permute-done | bytes 139296 | tf_op jit(solution)/shard_map/ppermute | solution.py:1080
  397.3 2.7 collective-permute-done.44
  402.7 5.7 %collective-permute-done.45 = f32[272,128]{1,0:T(8,128)S(1)} collective-permute-done((f32[272,128]{1,0:T(8,128)S(1)}, f32[272,128]{1,0:T(8,128)S(1)}, u32[]{:S(2)}, u32[]{:S(2)}) %collective-permute-start.45) | collective-permute-done | bytes 139296 | tf_op jit(solution)/shard_map/ppermute | solution.py:1080
  408.5 1.8 fusion.22
  418.8 9.1 %collective-permute-done.49 = bf16[128,640]{1,0:T(8,128)(2,1)} collective-permute-done((bf16[128,640]{1,0:T(8,128)(2,1)}, bf16[128,640]{1,0:T(8,128)(2,1)}, u32[]{:S(2)}, u32[]{:S(2)}) %collective-permute-start.49) | collective-permute-done | bytes 163872 | tf_op jit(solution)/shard_map/ppermute | solution.py:1080
  (369 shorter events, 91.9 us)
Async XLA Ops:
  2.6 34.0 %collective-permute-start.4 = (bf16[256,1024]{1,0:T(8,128)(2,1)}, bf16[256,1024]{1,0:T(8,128)(2,1)S(1)}, u32[]{:S(2)}, u32[]{:S(2)}) collective-permute-start(bf16[256,1024]{1,0:T(8,128)(2,1)} %constant_dynamic-slice_fusion), channel_id=1, source_target_pairs={{0,1},{1,0},{2,3},{3,2},{4,5},{5,4},{6,7},{7,6},{8,9},{9,8},{10,11... | collective-permute-start | bytes 1572872 | tf_op jit(solution)/shard_map/ppermute | solution.py:1080
  8.3 15.3 %collective-permute-start = (f32[72,512]{1,0:T(8,128)}, f32[72,512]{1,0:T(8,128)S(1)}, u32[]{:S(2)}, u32[]{:S(2)}) collective-permute-start(f32[72,512]{1,0:T(8,128)} %pack_params.1.own_ref), channel_id=1, source_target_pairs={{0,1},{1,0},{2,3},{3,2},{4,5},{5,4},{6,7},{7,6},{8,9},{9,8},{10,11... | collective-permute-start | bytes 442376 | tf_op jit(solution)/shard_map/ppermute | solution.py:1080
  22.1 14.5 %collective-permute-start.2 = (bf16[256,1024]{1,0:T(8,128)(2,1)}, bf16[256,1024]{1,0:T(8,128)(2,1)S(1)}, u32[]{:S(2)}, u32[]{:S(2)}) collective-permute-start(bf16[256,1024]{1,0:T(8,128)(2,1)} %get-tuple-element.191), channel_id=1, source_target_pairs={{0,1},{1,0},{2,3},{3,2},{4,5},{5,4},{6,7},{7,6},{8,9},{9,8},{10,11... | collective-permute-start | bytes 1572872 | tf_op jit(solution)/shard_map/ppermute | solution.py:1080
  35.8 15.9 %collective-permute-start.1 = (bf16[256,1024]{1,0:T(8,128)(2,1)S(1)}, bf16[256,1024]{1,0:T(8,128)(2,1)S(1)}, u32[]{:S(2)}, u32[]{:S(2)}) collective-permute-start(bf16[256,1024]{1,0:T(8,128)(2,1)S(1)} %copy-done.102), channel_id=1, source_target_pairs={{0,1},{1,0},{2,3},{3,2},{4,5},{5,4},{6,7},{7,6},{8,9},{9,8},{10,11... | collective-permute-start | bytes 1572872 | tf_op jit(solution)/shard_map/ppermute | solution.py:1080
  36.6 13.2 %collective-permute-start.5 = (bf16[256,1024]{1,0:T(8,128)(2,1)S(1)}, bf16[256,1024]{1,0:T(8,128)(2,1)S(1)}, u32[]{:S(2)}, u32[]{:S(2)}) collective-permute-start(bf16[256,1024]{1,0:T(8,128)(2,1)S(1)} %collective-permute-done.4.p0.w0), channel_id=1, source_target_pairs={{0,4},{2,6},{4,0},{6,2},{8,12},{10,14},{12,8},{14,10},{16,20},{18,... | collective-permute-start | bytes 1572872 | tf_op jit(solution)/shard_map/ppermute | solution.py:1080
  38.1 13.6 %collective-permute-start.3 = (bf16[256,1024]{1,0:T(8,128)(2,1)S(1)}, bf16[256,1024]{1,0:T(8,128)(2,1)S(1)}, u32[]{:S(2)}, u32[]{:S(2)}) collective-permute-start(bf16[256,1024]{1,0:T(8,128)(2,1)S(1)} %collective-permute-done.2.w0), channel_id=1, source_target_pairs={{0,8},{2,10},{4,12},{6,14},{8,0},{10,2},{12,4},{14,6},{16,24},{18,... | collective-permute-start | bytes 1572872 | tf_op jit(solution)/shard_map/ppermute | solution.py:1080
  50.3 14.8 %collective-permute-start.13 = (bf16[256,1024]{1,0:T(8,128)(2,1)S(1)}, bf16[256,1024]{1,0:T(8,128)(2,1)S(1)}, u32[]{:S(2)}, u32[]{:S(2)}) collective-permute-start(bf16[256,1024]{1,0:T(8,128)(2,1)S(1)} %copy-done.101), channel_id=1, source_target_pairs={{0,1},{1,0},{2,3},{3,2},{4,5},{5,4},{6,7},{7,6},{8,9},{9,8},{10,11... | collective-permute-start | bytes 1572872 | tf_op jit(solution)/shard_map/ppermute | solution.py:1080
  60.0 6.3 %collective-permute-start.8 = (bf16[256,1024]{1,0:T(8,128)(2,1)S(1)}, bf16[256,1024]{1,0:T(8,128)(2,1)S(1)}, u32[]{:S(2)}, u32[]{:S(2)}) collective-permute-start(bf16[256,1024]{1,0:T(8,128)(2,1)S(1)} %collective-permute-done.2.w0), channel_id=1, source_target_pairs={{0,2},{2,0},{4,6},{6,4},{8,10},{10,8},{12,14},{14,12},{16,18},{18,... | collective-permute-start | bytes 1572872 | tf_op jit(solution)/shard_map/ppermute | solution.py:1080
  60.2 6.2 %collective-permute-start.9 = (bf16[256,1024]{1,0:T(8,128)(2,1)S(1)}, bf16[256,1024]{1,0:T(8,128)(2,1)S(1)}, u32[]{:S(2)}, u32[]{:S(2)}) collective-permute-start(bf16[256,1024]{1,0:T(8,128)(2,1)S(1)} %collective-permute-done.3.w1), channel_id=1, source_target_pairs={{0,2},{2,0},{4,6},{6,4},{8,10},{10,8},{12,14},{14,12},{16,18},{18,... | collective-permute-start | bytes 1572872 | tf_op jit(solution)/shard_map/ppermute | solution.py:1080
  60.5 26.3 %collective-permute-start.18 = (bf16[256,2048]{1,0:T(8,128)(2,1)S(1)}, bf16[256,2048]{1,0:T(8,128)(2,1)}, u32[]{:S(2)}, u32[]{:S(2)}) collective-permute-start(bf16[256,2048]{1,0:T(8,128)(2,1)S(1)} %copy-done.88), channel_id=1, source_target_pairs={{0,1},{1,0},{2,3},{3,2},{4,5},{5,4},{6,7},{7,6},{8,9},{9,8},{10,11... | collective-permute-start | bytes 3145736 | tf_op jit(solution)/shard_map/ppermute | solution.py:1080
  61.9 22.8 %collective-permute-start.10 = (bf16[256,1024]{1,0:T(8,128)(2,1)S(1)}, bf16[256,1024]{1,0:T(8,128)(2,1)S(1)}, u32[]{:S(2)}, u32[]{:S(2)}) collective-permute-start(bf16[256,1024]{1,0:T(8,128)(2,1)S(1)} %collective-permute-done.1.u0), channel_id=1, source_target_pairs={{0,4},{2,6},{4,0},{6,2},{8,12},{10,14},{12,8},{14,10},{16,20},{18,... | collective-permute-start | bytes 1572872 | tf_op jit(solution)/shard_map/ppermute | solution.py:1080
  65.1 18.9 %collective-permute-start.14 = (bf16[256,1024]{1,0:T(8,128)(2,1)S(1)}, bf16[256,1024]{1,0:T(8,128)(2,1)S(1)}, u32[]{:S(2)}, u32[]{:S(2)}) collective-permute-start(bf16[256,1024]{1,0:T(8,128)(2,1)S(1)} %collective-permute-done.13.h0.f0), channel_id=1, source_target_pairs={{0,8},{2,10},{4,12},{6,14},{8,0},{10,2},{12,4},{14,6},{16,24},{18,... | collective-permute-start | bytes 1572872 | tf_op jit(solution)/shard_map/ppermute | solution.py:1080
  84.1 4.1 collective-permute-start.15
  84.2 4.8 %collective-permute-start.16 = (bf16[256,1024]{1,0:T(8,128)(2,1)S(1)}, bf16[256,1024]{1,0:T(8,128)(2,1)S(1)}, u32[]{:S(2)}, u32[]{:S(2)}) collective-permute-start(bf16[256,1024]{1,0:T(8,128)(2,1)S(1)} %collective-permute-done.14.h1.f1), channel_id=1, source_target_pairs={{0,2},{2,0},{4,6},{6,4},{8,10},{10,8},{12,14},{14,12},{16,18},{18,... | collective-permute-start | bytes 1572872 | tf_op jit(solution)/shard_map/ppermute | solution.py:1080
  84.7 4.3 collective-permute-start.11
  84.8 4.2 collective-permute-start.12
  86.8 63.1 %collective-permute-start.22 = (bf16[1024,1024]{1,0:T(8,128)(2,1)}, bf16[1024,1024]{1,0:T(8,128)(2,1)}, u32[]{:S(2)}, u32[]{:S(2)}) collective-permute-start(bf16[1024,1024]{1,0:T(8,128)(2,1)} %get-tuple-element.229), channel_id=1, source_target_pairs={{0,1},{1,0},{2,3},{3,2},{4,5},{5,4},{6,7},{7,6},{8,9},{9,8},{10,11... | collective-permute-start | bytes 6291464 | tf_op jit(solution)/shard_map/ppermute | solution.py:1080
  88.2 62.4 %collective-permute-start.19 = (bf16[256,2048]{1,0:T(8,128)(2,1)}, bf16[256,2048]{1,0:T(8,128)(2,1)}, u32[]{:S(2)}, u32[]{:S(2)}) collective-permute-start(bf16[256,2048]{1,0:T(8,128)(2,1)} %collective-permute-done.18.refs_0_), channel_id=1, source_target_pairs={{0,4},{2,6},{4,0},{6,2},{8,12},{10,14},{12,8},{14,10},{16,20},{18,... | collective-permute-start | bytes 3145736 | tf_op jit(solution)/shard_map/ppermute | solution.py:1080
  129.3 21.7 %collective-permute-start.17 = (bf16[2,2,512,1024]{3,2,1,0:T(8,128)(2,1)}, bf16[2,2,512,1024]{3,2,1,0:T(8,128)(2,1)}, u32[]{:S(2)}, u32[]{:S(2)}) collective-permute-start(bf16[2,2,512,1024]{3,2,1,0:T(8,128)(2,1)} %get-tuple-element.221), channel_id=1, source_target_pairs={{0,2},{2,0},{4,6},{6,4},{8,10},{10,8},{12,14},{14,12},{16,18},{18,... | collective-permute-start | bytes 12582920 | tf_op jit(solution)/shard_map/ppermute | solution.py:1080
  150.0 7.7 %collective-permute-start.23 = (bf16[1024,1024]{1,0:T(8,128)(2,1)}, bf16[1024,1024]{1,0:T(8,128)(2,1)S(1)}, u32[]{:S(2)}, u32[]{:S(2)}) collective-permute-start(bf16[1024,1024]{1,0:T(8,128)(2,1)} %collective-permute-done.22.refs_4_), channel_id=1, source_target_pairs={{0,2},{2,0},{4,6},{6,4},{8,10},{10,8},{12,14},{14,12},{16,18},{18,... | collective-permute-start | bytes 6291464 | tf_op jit(solution)/shard_map/ppermute | solution.py:1080
  150.5 5.5 %collective-permute-start.20 = (bf16[256,2048]{1,0:T(8,128)(2,1)}, bf16[256,2048]{1,0:T(8,128)(2,1)}, u32[]{:S(2)}, u32[]{:S(2)}) collective-permute-start(bf16[256,2048]{1,0:T(8,128)(2,1)} %collective-permute-done.18.refs_0_), channel_id=1, source_target_pairs={{0,2},{2,0},{4,6},{6,4},{8,10},{10,8},{12,14},{14,12},{16,18},{18,... | collective-permute-start | bytes 3145736 | tf_op jit(solution)/shard_map/ppermute | solution.py:1080
  150.6 7.0 %collective-permute-start.21 = (bf16[256,2048]{1,0:T(8,128)(2,1)}, bf16[256,2048]{1,0:T(8,128)(2,1)}, u32[]{:S(2)}, u32[]{:S(2)}) collective-permute-start(bf16[256,2048]{1,0:T(8,128)(2,1)} %collective-permute-done.19.refs_1_), channel_id=1, source_target_pairs={{0,2},{2,0},{4,6},{6,4},{8,10},{10,8},{12,14},{14,12},{16,18},{18,... | collective-permute-start | bytes 3145736 | tf_op jit(solution)/shard_map/ppermute | solution.py:1080
  154.0 57.2 %collective-permute-start.25 = (bf16[512,1024]{1,0:T(8,128)(2,1)}, bf16[512,1024]{1,0:T(8,128)(2,1)}, u32[]{:S(2)}, u32[]{:S(2)}) collective-permute-start(bf16[512,1024]{1,0:T(8,128)(2,1)} %fusion.5), channel_id=1, source_target_pairs={{0,4},{2,6},{4,0},{6,2},{8,12},{10,14},{12,8},{14,10},{16,20},{18,... | collective-permute-start | bytes 3145736 | tf_op jit(solution)/shard_map/ppermute | solution.py:1080
  180.2 24.7 %collective-permute-start.24 = (bf16[2,2,512,1024]{3,2,1,0:T(8,128)(2,1)}, bf16[2,2,512,1024]{3,2,1,0:T(8,128)(2,1)S(1)}, u32[]{:S(2)}, u32[]{:S(2)}) collective-permute-start(bf16[2,2,512,1024]{3,2,1,0:T(8,128)(2,1)} %get-tuple-element.237), channel_id=1, source_target_pairs={{0,2},{2,0},{4,6},{6,4},{8,10},{10,8},{12,14},{14,12},{16,18},{18,... | collective-permute-start | bytes 12582920 | tf_op jit(solution)/shard_map/ppermute | solution.py:1080
  205.3 33.4 %collective-permute-start.26 = (bf16[512,1024]{1,0:T(8,128)(2,1)S(1)}, bf16[512,1024]{1,0:T(8,128)(2,1)}, u32[]{:S(2)}, u32[]{:S(2)}) collective-permute-start(bf16[512,1024]{1,0:T(8,128)(2,1)S(1)} %fusion.4), channel_id=1, source_target_pairs={{0,4},{2,6},{4,0},{6,2},{8,12},{10,14},{12,8},{14,10},{16,20},{18,... | collective-permute-start | bytes 3145736 | tf_op jit(solution)/shard_map/ppermute | solution.py:1080
  210.2 58.7 %collective-permute-start.27 = (bf16[2,512,1024]{2,1,0:T(8,128)(2,1)}, bf16[2,512,1024]{2,1,0:T(8,128)(2,1)}, u32[]{:S(2)}, u32[]{:S(2)}) collective-permute-start(bf16[2,512,1024]{2,1,0:T(8,128)(2,1)} %fusion), channel_id=1, source_target_pairs={{0,1},{1,0},{2,3},{3,2},{4,5},{5,4},{6,7},{7,6},{8,9},{9,8},{10,11... | collective-permute-start | bytes 6291464 | tf_op jit(solution)/shard_map/ppermute | solution.py:1080
  249.9 26.0 %collective-permute-start.28 = (bf16[2,2,512,768]{3,2,1,0:T(8,128)(2,1)}, bf16[2,2,512,768]{3,2,1,0:T(8,128)(2,1)S(1)}, u32[]{:S(2)}, u32[]{:S(2)}) collective-permute-start(bf16[2,2,512,768]{3,2,1,0:T(8,128)(2,1)} %weight_mid.4), channel_id=1, source_target_pairs={{0,2},{2,0},{4,6},{6,4},{8,10},{10,8},{12,14},{14,12},{16,18},{18,... | collective-permute-start | bytes 9437192 | tf_op jit(solution)/shard_map/ppermute | solution.py:1080
  255.8 26.4 %collective-permute-start.29 = (bf16[2,2,512,768]{3,2,1,0:T(8,128)(2,1)S(1)}, bf16[2,2,512,768]{3,2,1,0:T(8,128)(2,1)S(1)}, u32[]{:S(2)}, u32[]{:S(2)}) collective-permute-start(bf16[2,2,512,768]{3,2,1,0:T(8,128)(2,1)S(1)} %weight_mid.5), channel_id=1, source_target_pairs={{0,2},{2,0},{4,6},{6,4},{8,10},{10,8},{12,14},{14,12},{16,18},{18,... | collective-permute-start | bytes 9437192 | tf_op jit(solution)/shard_map/ppermute | solution.py:1080
  256.4 44.6 %collective-permute-start.31 = (bf16[512,1024]{1,0:T(8,128)(2,1)}, bf16[512,1024]{1,0:T(8,128)(2,1)}, u32[]{:S(2)}, u32[]{:S(2)}) collective-permute-start(bf16[512,1024]{1,0:T(8,128)(2,1)} %fusion.3), channel_id=1, source_target_pairs={{0,1},{1,0},{2,3},{3,2},{4,5},{5,4},{6,7},{7,6},{8,9},{9,8},{10,11... | collective-permute-start | bytes 3145736 | tf_op jit(solution)/shard_map/ppermute | solution.py:1080
  272.3 28.7 %collective-permute-start.30 = (bf16[512,1024]{1,0:T(8,128)(2,1)}, bf16[512,1024]{1,0:T(8,128)(2,1)}, u32[]{:S(2)}, u32[]{:S(2)}) collective-permute-start(bf16[512,1024]{1,0:T(8,128)(2,1)} %fusion.1), channel_id=1, source_target_pairs={{0,4},{2,6},{4,0},{6,2},{8,12},{10,14},{12,8},{14,10},{16,20},{18,... | collective-permute-start | bytes 3145736 | tf_op jit(solution)/shard_map/ppermute | solution.py:1080
  292.2 16.6 %collective-permute-start.32 = (bf16[2,2,512,640]{3,2,1,0:T(8,128)(2,1)S(1)}, bf16[2,2,512,640]{3,2,1,0:T(8,128)(2,1)S(1)}, u32[]{:S(2)}, u32[]{:S(2)}) collective-permute-start(bf16[2,2,512,640]{3,2,1,0:T(8,128)(2,1)S(1)} %weight_value.2), channel_id=1, source_target_pairs={{0,2},{2,0},{4,6},{6,4},{8,10},{10,8},{12,14},{14,12},{16,18},{18,... | collective-permute-start | bytes 7864328 | tf_op jit(solution)/shard_map/ppermute | solution.py:1080
  292.3 50.8 %collective-permute-start.33 = (bf16[2,512,768]{2,1,0:T(8,128)(2,1)}, bf16[2,512,768]{2,1,0:T(8,128)(2,1)}, u32[]{:S(2)}, u32[]{:S(2)}) collective-permute-start(bf16[2,512,768]{2,1,0:T(8,128)(2,1)} %get-tuple-element.267), channel_id=1, source_target_pairs={{0,4},{2,6},{4,0},{6,2},{8,12},{10,14},{12,8},{14,10},{16,20},{18,... | collective-permute-start | bytes 4718600 | tf_op jit(solution)/shard_map/ppermute | solution.py:1080
  304.3 40.3 %collective-permute-start.35 = (bf16[2,2,128,1024]{3,2,1,0:T(8,128)(2,1)S(1)}, bf16[2,2,128,1024]{3,2,1,0:T(8,128)(2,1)S(1)}, u32[]{:S(2)}, u32[]{:S(2)}) collective-permute-start(bf16[2,2,128,1024]{3,2,1,0:T(8,128)(2,1)S(1)} %pad_maximum_fusion), channel_id=1, source_target_pairs={{0,8},{2,10},{4,12},{6,14},{8,0},{10,2},{12,4},{14,6},{16,24},{18,... | collective-permute-start | bytes 3145736 | tf_op jit(solution)/shard_map/ppermute | solution.py:1080
  306.9 36.2 %collective-permute-start.34 = (bf16[2,512,768]{2,1,0:T(8,128)(2,1)S(1)}, bf16[2,512,768]{2,1,0:T(8,128)(2,1)S(1)}, u32[]{:S(2)}, u32[]{:S(2)}) collective-permute-start(bf16[2,512,768]{2,1,0:T(8,128)(2,1)S(1)} %get-tuple-element.297), channel_id=1, source_target_pairs={{0,1},{1,0},{2,3},{3,2},{4,5},{5,4},{6,7},{7,6},{8,9},{9,8},{10,11... | collective-permute-start | bytes 4718600 | tf_op jit(solution)/shard_map/ppermute | solution.py:1080
  314.5 54.5 %collective-permute-start.37 = (bf16[2,2,2,128,640]{4,3,2,1,0:T(8,128)(2,1)}, bf16[2,2,2,128,640]{4,3,2,1,0:T(8,128)(2,1)}, u32[]{:S(2)}, u32[]{:S(2)}) collective-permute-start(bf16[2,2,2,128,640]{4,3,2,1,0:T(8,128)(2,1)} %get-tuple-element.332), channel_id=1, source_target_pairs={{0,8},{2,10},{4,12},{6,14},{8,0},{10,2},{12,4},{14,6},{16,24},{18,... | collective-permute-start | bytes 3932168 | tf_op jit(solution)/shard_map/ppermute | solution.py:1080
  346.7 25.6 %collective-permute-start.36 = (bf16[2,128,1024]{2,1,0:T(8,128)(2,1)S(1)}, bf16[2,128,1024]{2,1,0:T(8,128)(2,1)S(1)}, u32[]{:S(2)}, u32[]{:S(2)}) collective-permute-start(bf16[2,128,1024]{2,1,0:T(8,128)(2,1)S(1)} %pad_maximum_fusion.2), channel_id=1, source_target_pairs={{0,16},{2,18},{4,20},{6,22},{8,24},{10,26},{12,28},{14,30},{16,0},... | collective-permute-start | bytes 1572872 | tf_op jit(solution)/shard_map/ppermute | solution.py:1080
  349.4 28.1 %collective-permute-start.40 = (bf16[512,768]{1,0:T(8,128)(2,1)S(1)}, bf16[512,768]{1,0:T(8,128)(2,1)S(1)}, u32[]{:S(2)}, u32[]{:S(2)}) collective-permute-start(bf16[512,768]{1,0:T(8,128)(2,1)S(1)} %fusion.7), channel_id=1, source_target_pairs={{0,4},{2,6},{4,0},{6,2},{8,12},{10,14},{12,8},{14,10},{16,20},{18,... | collective-permute-start | bytes 2359304 | tf_op jit(solution)/shard_map/ppermute | solution.py:1080
  349.9 27.5 %collective-permute-start.39 = (bf16[512,768]{1,0:T(8,128)(2,1)S(1)}, bf16[512,768]{1,0:T(8,128)(2,1)S(1)}, u32[]{:S(2)}, u32[]{:S(2)}) collective-permute-start(bf16[512,768]{1,0:T(8,128)(2,1)S(1)} %fusion.6), channel_id=1, source_target_pairs={{0,1},{1,0},{2,3},{3,2},{4,5},{5,4},{6,7},{7,6},{8,9},{9,8},{10,11... | collective-permute-start | bytes 2359304 | tf_op jit(solution)/shard_map/ppermute | solution.py:1080
  360.6 16.8 %collective-permute-start.38 = (f32[272,128]{1,0:T(8,128)S(1)}, f32[272,128]{1,0:T(8,128)S(1)}, u32[]{:S(2)}, u32[]{:S(2)}) collective-permute-start(f32[272,128]{1,0:T(8,128)S(1)} %constant_dynamic-update-slice_fusion), channel_id=1, source_target_pairs={{0,8},{2,10},{4,12},{6,14},{8,0},{10,2},{12,4},{14,6},{16,24},{18,... | collective-permute-start | bytes 417800 | tf_op jit(solution)/shard_map/ppermute | solution.py:1080
  370.3 24.9 %collective-permute-start.46 = (bf16[2,2,128,640]{3,2,1,0:T(8,128)(2,1)S(1)}, bf16[2,2,128,640]{3,2,1,0:T(8,128)(2,1)S(1)}, u32[]{:S(2)}, u32[]{:S(2)}) collective-permute-start(bf16[2,2,128,640]{3,2,1,0:T(8,128)(2,1)S(1)} %fusion.8), channel_id=1, source_target_pairs={{0,4},{2,6},{4,0},{6,2},{8,12},{10,14},{12,8},{14,10},{16,20},{18,... | collective-permute-start | bytes 1966088 | tf_op jit(solution)/shard_map/ppermute | solution.py:1080
  377.5 10.0 %collective-permute-start.41 = (f32[272,128]{1,0:T(8,128)S(1)}, f32[272,128]{1,0:T(8,128)S(1)}, u32[]{:S(2)}, u32[]{:S(2)}) collective-permute-start(f32[272,128]{1,0:T(8,128)S(1)} %add.618), channel_id=1, source_target_pairs={{0,16},{2,18},{4,20},{6,22},{8,24},{10,26},{12,28},{14,30},{16,0},... | collective-permute-start | bytes 417800 | tf_op jit(solution)/shard_map/ppermute | solution.py:1080
  379.3 20.7 %collective-permute-start.44 = (bf16[2,2,128,768]{3,2,1,0:T(8,128)(2,1)S(1)}, bf16[2,2,128,768]{3,2,1,0:T(8,128)(2,1)S(1)}, u32[]{:S(2)}, u32[]{:S(2)}) collective-permute-start(bf16[2,2,128,768]{3,2,1,0:T(8,128)(2,1)S(1)} %pad_maximum_fusion.1), channel_id=1, source_target_pairs={{0,8},{2,10},{4,12},{6,14},{8,0},{10,2},{12,4},{14,6},{16,24},{18,... | collective-permute-start | bytes 2359304 | tf_op jit(solution)/shard_map/ppermute | solution.py:1080
  382.6 7.9 %collective-permute-start.50 = (bf16[2,64,1024]{2,1,0:T(8,128)(2,1)S(1)}, bf16[2,64,1024]{2,1,0:T(8,128)(2,1)S(1)}, u32[]{:S(2)}, u32[]{:S(2)}) collective-permute-start(bf16[2,64,1024]{2,1,0:T(8,128)(2,1)S(1)} %fusion.25), channel_id=1, source_target_pairs={{0,2},{2,0},{4,6},{6,4},{8,10},{10,8},{12,14},{14,12},{16,18},{18,... | collective-permute-start | bytes 786440 | tf_op jit(solution)/shard_map/ppermute | solution.py:1080
  389.1 6.0 %collective-permute-start.43 = (f32[272,128]{1,0:T(8,128)S(1)}, f32[272,128]{1,0:T(8,128)S(1)}, u32[]{:S(2)}, u32[]{:S(2)}) collective-permute-start(f32[272,128]{1,0:T(8,128)S(1)} %add.624), channel_id=1, source_target_pairs={{0,4},{2,6},{4,0},{6,2},{8,12},{10,14},{12,8},{14,10},{16,20},{18,... | collective-permute-start | bytes 417800 | tf_op jit(solution)/shard_map/ppermute | solution.py:1080
  396.2 12.2 %collective-permute-start.47 = (bf16[2,128,640]{2,1,0:T(8,128)(2,1)S(1)}, bf16[2,128,640]{2,1,0:T(8,128)(2,1)S(1)}, u32[]{:S(2)}, u32[]{:S(2)}) collective-permute-start(bf16[2,128,640]{2,1,0:T(8,128)(2,1)S(1)} %fusion.9), channel_id=1, source_target_pairs={{0,1},{1,0},{2,3},{3,2},{4,5},{5,4},{6,7},{7,6},{8,9},{9,8},{10,11... | collective-permute-start | bytes 983048 | tf_op jit(solution)/shard_map/ppermute | solution.py:1080
  401.1 7.4 %collective-permute-start.45 = (f32[272,128]{1,0:T(8,128)S(1)}, f32[272,128]{1,0:T(8,128)S(1)}, u32[]{:S(2)}, u32[]{:S(2)}) collective-permute-start(f32[272,128]{1,0:T(8,128)S(1)} %add.625), channel_id=1, source_target_pairs={{0,1},{1,0},{2,3},{3,2},{4,5},{5,4},{6,7},{7,6},{8,9},{9,8},{10,11... | collective-permute-start | bytes 417800 | tf_op jit(solution)/shard_map/ppermute | solution.py:1080
  402.2 25.7 %collective-permute-start.48 = (bf16[2,128,768]{2,1,0:T(8,128)(2,1)}, bf16[2,128,768]{2,1,0:T(8,128)(2,1)}, u32[]{:S(2)}, u32[]{:S(2)}) collective-permute-start(bf16[2,128,768]{2,1,0:T(8,128)(2,1)} %pad_maximum_fusion.3), channel_id=1, source_target_pairs={{0,16},{2,18},{4,20},{6,22},{8,24},{10,26},{12,28},{14,30},{16,0},... | collective-permute-start | bytes 1179656 | tf_op jit(solution)/shard_map/ppermute | solution.py:1080
  410.3 17.6 %collective-permute-start.49 = (bf16[128,640]{1,0:T(8,128)(2,1)}, bf16[128,640]{1,0:T(8,128)(2,1)}, u32[]{:S(2)}, u32[]{:S(2)}) collective-permute-start(bf16[128,640]{1,0:T(8,128)(2,1)} %fusion.22), channel_id=1, source_target_pairs={{0,16},{2,18},{4,20},{6,22},{8,24},{10,26},{12,28},{14,30},{16,0},... | collective-permute-start | bytes 491528 | tf_op jit(solution)/shard_map/ppermute | solution.py:1080
  (109 other events, 889.4 us)
